TPU v7x, 32 devices: a whole 2x2x4 slice. The times are simulated.
32 devices in a mesh: fsdp: 32 (over z, y, x, core).
Axes of the slice: x: 2, y: 2, z: 4, core: 2. Of those that a mesh axis runs over, the one named last changes fastest.
Arguments:
- input_one: bfloat16 [32768, 1024], P('fsdp'), may hold values from -6 to 6
- input_two: bfloat16 [32768, 1024], P('fsdp'), may hold values from -6 to 6
- upstream_one: bfloat16 [32768, 1024], P('fsdp'), may hold values from -6 to 6
- upstream_two: bfloat16 [32768, 1024], P('fsdp'), may hold values from -6 to 6
- lengths: int32 [32], replicated, may hold values from 512 to 1024, as said below
- destination: int32 [32], replicated, may hold values from 0 to 31, each once
- buckets: int32 [32, 32, 1024], P('fsdp'), may hold values from 0 to 31
- w_shared: bfloat16 [1024, 1024], P('fsdp'), may hold values from -3 to 3
- w_value: bfloat16 [1024, 1024], P('fsdp'), may hold values from -0.1875 to 0.1875
- w_output: bfloat16 [1024, 1024], P('fsdp'), may hold values from -1.5 to 1.5
- w_expand: bfloat16 [1024, 4096], P('fsdp'), may hold values from -0.1875 to 0.1875
- w_reduce: bfloat16 [4096, 1024], P('fsdp'), may hold values from -0.125 to 0.125
- gain_attend: float32 [1024], P('fsdp'), may hold values from 0.25 to 1.75
- shift_attend: float32 [1024], P('fsdp'), may hold values from -2.5 to 2.5
- gain_mixing: float32 [1024], P('fsdp'), may hold values from 0.25 to 1.75
- shift_mixing: float32 [1024], P('fsdp'), may hold values from -2.5 to 2.5
- bias_output: float32 [1024], P('fsdp'), may hold values from -2.5 to 2.5
- bias_expand: float32 [4096], P('fsdp'), may hold values from -2.5 to 2.5
- bias_reduce: float32 [1024], P('fsdp'), may hold values from -2.5 to 2.5
Outputs:
- result_one: bfloat16 [32768, 1024], P('fsdp')
- result_two: bfloat16 [32768, 1024], P('fsdp')
- grad_one: bfloat16 [32768, 1024], P('fsdp')
- grad_two: bfloat16 [32768, 1024], P('fsdp')
- grad_shared: float32 [1024, 1024], P('fsdp')
- grad_value: float32 [1024, 1024], P('fsdp')
- grad_output: float32 [1024, 1024], P('fsdp')
- grad_expand: float32 [1024, 4096], P('fsdp')
- grad_reduce: float32 [4096, 1024], P('fsdp')
- grad_gain_attend: float32 [1024], P('fsdp')
- grad_shift_attend: float32 [1024], P('fsdp')
- grad_gain_mixing: float32 [1024], P('fsdp')
- grad_shift_mixing: float32 [1024], P('fsdp')
- grad_bias_output: float32 [1024], P('fsdp')
- grad_bias_expand: float32 [4096], P('fsdp')
- grad_bias_reduce: float32 [1024], P('fsdp')
Inputs may be any that keep to these rules, and one draw needn't show every extreme that they name: `lengths`: the longest sequence has exactly 1024 tokens. `destination`: each device index receives exactly one sequence.
All inputs are finite; a program needn't handle non-finite values.
Results may differ from a plain program's by a relative error of at most 0.035.
Values may be sent and summed in bfloat16 or wider, within the bound.
A program may use at most 384 MiB of HBM per device.

v0:
```python
import math

import jax
import jax.numpy as jnp
from jax import lax
from jax.sharding import PartitionSpec as P

HEADS = 8
DH = 128
GROUP = 64
ROUNDS = 4
BUCKETS = 32


EPS_NORM = 1e-05
EPS_UNIT = 1e-06
SELF_SCORE = -100000.0
MASKED_SCORE = -1000000000.0


def layer_norm(values, gain, shift):
    center = values - jnp.mean(values, axis=-1, keepdims=True)
    spread = jnp.mean(center * center, axis=-1, keepdims=True)
    return center * lax.rsqrt(spread + EPS_NORM) * gain + shift


def unit_keys(shared):
    return shared * lax.rsqrt(jnp.sum(shared * shared, axis=-1, keepdims=True) + EPS_UNIT)


def norm_back(values, gain, shift, upstream):
    outcome, pullback = jax.vjp(layer_norm, values, gain, shift)
    return pullback(upstream)


def pick_rows(table, index):
    return jnp.take(table, index, axis=0)


def arrange(table, ordering):
    over_heads = jax.vmap(pick_rows)
    return jax.vmap(over_heads, in_axes=(None, 0))(table, ordering)


def permute(table, index):
    return jax.vmap(jax.vmap(pick_rows))(table, index)


def pair_blocks(sorted_rows, blocks):
    own_rows = sorted_rows.reshape(sorted_rows.shape[:2] + (blocks, GROUP) + sorted_rows.shape[3:])
    prior_rows = jnp.concatenate([jnp.zeros_like(own_rows[:, :, :1]), own_rows[:, :, :-1]], axis=2)
    return jnp.concatenate([prior_rows, own_rows], axis=3)


def fold_pairs(paired):
    prior_rows = paired[:, :, :, :GROUP]
    moved = jnp.concatenate([prior_rows[:, :, 1:], jnp.zeros_like(prior_rows[:, :, :1])], axis=2)
    return paired[:, :, :, GROUP:] + moved


def block_scores(query_blocks, key_pairs, allowed, selfish):
    raw_scores = jnp.einsum(
        "rhcqd,rhckd->rhcqk", query_blocks, key_pairs, preferred_element_type=jnp.float32
    ) / math.sqrt(DH)
    return jnp.where(allowed, jnp.where(selfish, SELF_SCORE, raw_scores), MASKED_SCORE)


def body(
    input_one,
    input_two,
    upstream_one,
    upstream_two,
    lengths,
    destination,
    buckets,
    w_shared,
    w_value,
    w_output,
    w_expand,
    w_reduce,
    gain_attend,
    shift_attend,
    gain_mixing,
    shift_mixing,
    bias_output,
    bias_expand,
    bias_reduce,
):
    devices = lax.axis_size("fsdp")
    slots = input_one.shape[0]
    width = input_one.shape[1]
    stream_total = devices * slots
    blocks = slots // GROUP
    ends = jnp.cumsum(lengths)
    starts = ends - lengths
    owner = (
        jnp.zeros((devices,), jnp.int32).at[destination].set(jnp.arange(devices, dtype=jnp.int32))
    )
    positions = jnp.arange(slots, dtype=jnp.int32)
    columns = (
        lax.all_to_all(input_one, "fsdp", split_axis=1, concat_axis=0, tiled=True),
        lax.all_to_all(input_two, "fsdp", split_axis=1, concat_axis=0, tiled=True),
        lax.all_to_all(upstream_one, "fsdp", split_axis=1, concat_axis=0, tiled=True),
        lax.all_to_all(upstream_two, "fsdp", split_axis=1, concat_axis=0, tiled=True),
    )
    narrow = columns[0].shape[1]
    stacked = jnp.concatenate([columns[0], columns[1], columns[2], columns[3]], axis=1)
    stacked = jnp.concatenate([stacked, jnp.zeros((slots, 4 * narrow), stacked.dtype)], axis=0)

    def take_window(start_row):
        return lax.dynamic_slice_in_dim(stacked, start_row, slots, 0)

    windows = jax.vmap(take_window)(starts[owner])
    window_live = (positions[None, :] < lengths[owner][:, None])[:, :, None]
    windows = jnp.where(window_live, windows, jnp.zeros((), windows.dtype)).reshape(
        stream_total, 4 * narrow
    )
    mine = (
        lax.all_to_all(windows[:, :narrow], "fsdp", split_axis=0, concat_axis=1, tiled=True),
        lax.all_to_all(
            windows[:, narrow : 2 * narrow], "fsdp", split_axis=0, concat_axis=1, tiled=True
        ),
        lax.all_to_all(
            windows[:, 2 * narrow : 3 * narrow], "fsdp", split_axis=0, concat_axis=1, tiled=True
        ),
        lax.all_to_all(windows[:, 3 * narrow :], "fsdp", split_axis=0, concat_axis=1, tiled=True),
    )
    length = lengths[owner[lax.axis_index("fsdp")]]
    live_rows = (positions < length).astype(jnp.float32)[:, None]
    slot_one = mine[0].astype(jnp.float32)
    slot_two = mine[1].astype(jnp.float32)
    above_one = mine[2].astype(jnp.float32)
    above_two = mine[3].astype(jnp.float32)
    gathered = (
        lax.all_gather(w_shared, "fsdp", axis=0, tiled=True),
        lax.all_gather(w_value, "fsdp", axis=0, tiled=True),
        lax.all_gather(w_output, "fsdp", axis=0, tiled=True),
        lax.all_gather(w_expand, "fsdp", axis=0, tiled=True),
        lax.all_gather(w_reduce, "fsdp", axis=0, tiled=True),
        lax.all_gather(gain_attend.astype(jnp.bfloat16), "fsdp", axis=0, tiled=True).astype(
            gain_attend.dtype
        ),
        lax.all_gather(shift_attend.astype(jnp.bfloat16), "fsdp", axis=0, tiled=True).astype(
            shift_attend.dtype
        ),
        lax.all_gather(gain_mixing.astype(jnp.bfloat16), "fsdp", axis=0, tiled=True).astype(
            gain_mixing.dtype
        ),
        lax.all_gather(shift_mixing.astype(jnp.bfloat16), "fsdp", axis=0, tiled=True).astype(
            shift_mixing.dtype
        ),
        lax.all_gather(bias_output.astype(jnp.bfloat16), "fsdp", axis=0, tiled=True).astype(
            bias_output.dtype
        ),
        lax.all_gather(bias_expand.astype(jnp.bfloat16), "fsdp", axis=0, tiled=True).astype(
            bias_expand.dtype
        ),
        lax.all_gather(bias_reduce.astype(jnp.bfloat16), "fsdp", axis=0, tiled=True).astype(
            bias_reduce.dtype
        ),
    )
    (
        full_shared,
        full_value,
        full_output,
        full_expand,
        full_reduce,
        full_gain_a,
        full_shift_a,
        full_gain_m,
        full_shift_m,
        full_bias_o,
        full_bias_e,
        full_bias_r,
    ) = gathered
    normed_one = layer_norm(slot_two, full_gain_a, full_shift_a).astype(jnp.bfloat16)
    shared = jnp.dot(normed_one, full_shared, preferred_element_type=jnp.float32).astype(
        jnp.bfloat16
    )
    values = jnp.dot(normed_one, full_value, preferred_element_type=jnp.float32).astype(
        jnp.bfloat16
    )
    shared_heads = shared.reshape(slots, HEADS, DH).transpose(1, 0, 2)
    value_heads = values.reshape(slots, HEADS, DH).transpose(1, 0, 2)
    shared_float = shared_heads.astype(jnp.float32)
    unit_heads = unit_keys(shared_float).astype(jnp.bfloat16)
    bucket_of = buckets[0].reshape(ROUNDS, HEADS, slots)
    sort_key = jnp.where(
        positions < length, bucket_of * slots + positions, BUCKETS * slots + positions
    )
    ordering = jnp.argsort(sort_key, axis=-1)
    inverse = jnp.argsort(ordering, axis=-1)
    joined_heads = jnp.concatenate([shared_heads, unit_heads, value_heads], axis=-1)
    sorted_joined = arrange(joined_heads, ordering)
    query_blocks = sorted_joined[..., :DH].reshape(ROUNDS, HEADS, blocks, GROUP, DH)
    key_pairs = pair_blocks(sorted_joined[..., DH : 2 * DH], blocks)
    value_pairs = pair_blocks(sorted_joined[..., 2 * DH :], blocks)
    place_sorted = ordering.reshape(ROUNDS, HEADS, blocks, GROUP)
    prior_place = jnp.concatenate(
        [jnp.full((ROUNDS, HEADS, 1, GROUP), 2 * slots, jnp.int32), place_sorted[:, :, :-1]], axis=2
    )
    key_place = jnp.concatenate([prior_place, place_sorted], axis=3)
    key_at = key_place[..., None, :]
    query_at = place_sorted[..., :, None]
    allowed = (key_at <= query_at) & (key_at < length)
    selfish = key_at == query_at
    scores = block_scores(query_blocks, key_pairs, allowed, selfish)
    highest = jnp.max(scores, axis=-1, keepdims=True)
    log_total = highest[..., 0] + jnp.log(jnp.sum(jnp.exp(scores - highest), axis=-1))
    prob_low = jnp.exp(scores - log_total[..., None]).astype(jnp.bfloat16)
    partial_sorted = jnp.einsum(
        "rhcqk,rhckd->rhcqd", prob_low, value_pairs, preferred_element_type=jnp.float32
    )
    partials = permute(partial_sorted.reshape(ROUNDS, HEADS, slots, DH), inverse)
    log_place = jnp.take_along_axis(log_total.reshape(ROUNDS, HEADS, slots), inverse, axis=-1)
    mixing = jax.nn.softmax(log_place, axis=0)
    combined = (
        jnp.sum(mixing[..., None] * partials, axis=0).transpose(1, 0, 2).reshape(slots, width)
    )
    combined = combined.astype(jnp.bfloat16)
    attend = jnp.dot(combined, full_output, preferred_element_type=jnp.float32) + full_bias_o
    out_one = slot_one + live_rows * attend
    second = layer_norm(out_one, full_gain_m, full_shift_m).astype(jnp.bfloat16)
    pre_act = jnp.dot(second, full_expand, preferred_element_type=jnp.float32) + full_bias_e
    expand = jax.nn.gelu(pre_act, approximate=True).astype(jnp.bfloat16)
    out_two = slot_two + live_rows * (
        jnp.dot(expand, full_reduce, preferred_element_type=jnp.float32) + full_bias_r
    )
    refetched = (
        lax.all_gather(w_shared, "fsdp", axis=0, tiled=True),
        lax.all_gather(w_value, "fsdp", axis=0, tiled=True),
        lax.all_gather(w_output, "fsdp", axis=0, tiled=True),
        lax.all_gather(w_expand, "fsdp", axis=0, tiled=True),
        lax.all_gather(w_reduce, "fsdp", axis=0, tiled=True),
        lax.all_gather(gain_attend.astype(jnp.bfloat16), "fsdp", axis=0, tiled=True).astype(
            gain_attend.dtype
        ),
        lax.all_gather(shift_attend.astype(jnp.bfloat16), "fsdp", axis=0, tiled=True).astype(
            shift_attend.dtype
        ),
        lax.all_gather(gain_mixing.astype(jnp.bfloat16), "fsdp", axis=0, tiled=True).astype(
            gain_mixing.dtype
        ),
        lax.all_gather(shift_mixing.astype(jnp.bfloat16), "fsdp", axis=0, tiled=True).astype(
            shift_mixing.dtype
        ),
        lax.all_gather(bias_output.astype(jnp.bfloat16), "fsdp", axis=0, tiled=True).astype(
            bias_output.dtype
        ),
        lax.all_gather(bias_expand.astype(jnp.bfloat16), "fsdp", axis=0, tiled=True).astype(
            bias_expand.dtype
        ),
        lax.all_gather(bias_reduce.astype(jnp.bfloat16), "fsdp", axis=0, tiled=True).astype(
            bias_reduce.dtype
        ),
    )
    (
        back_shared,
        back_value,
        back_output,
        back_expand,
        back_reduce,
        back_gain_a,
        back_shift_a,
        back_gain_m,
        back_shift_m,
        unused_bias_o,
        unused_bias_e,
        unused_bias_r,
    ) = refetched
    d_reduce = (live_rows * above_two).astype(jnp.bfloat16)
    grad_reduce = jnp.einsum("sf,sd->fd", expand, d_reduce, preferred_element_type=jnp.float32)
    grad_bias_reduce = jnp.sum(d_reduce, axis=0, dtype=jnp.float32)
    d_expand = jnp.einsum("sd,fd->sf", d_reduce, back_reduce, preferred_element_type=jnp.float32)
    gelu_out, gelu_pull = jax.vjp(lambda inner: jax.nn.gelu(inner, approximate=True), pre_act)
    d_pre = gelu_pull(d_expand)[0].astype(jnp.bfloat16)
    grad_expand = jnp.einsum("sd,sf->df", second, d_pre, preferred_element_type=jnp.float32)
    grad_bias_expand = jnp.sum(d_pre, axis=0, dtype=jnp.float32)
    d_second = jnp.einsum("sf,df->sd", d_pre, back_expand, preferred_element_type=jnp.float32)
    d_one_mix, grad_gain_mixing, grad_shift_mixing = norm_back(
        out_one, back_gain_m, back_shift_m, d_second
    )
    total_one = above_one + d_one_mix
    d_attend = (live_rows * total_one).astype(jnp.bfloat16)
    grad_output = jnp.einsum("sd,se->de", combined, d_attend, preferred_element_type=jnp.float32)
    grad_bias_output = jnp.sum(d_attend, axis=0, dtype=jnp.float32)
    d_combined = jnp.einsum("se,de->sd", d_attend, back_output, preferred_element_type=jnp.float32)
    d_combined = d_combined.reshape(slots, HEADS, DH).transpose(1, 0, 2)
    d_weight = jnp.sum(d_combined[None] * partials, axis=-1)
    d_log = mixing * (d_weight - jnp.sum(mixing * d_weight, axis=0, keepdims=True))
    d_partials = (mixing[..., None] * d_combined[None]).astype(jnp.bfloat16)
    d_part_blocks = permute(d_partials, ordering).reshape(ROUNDS, HEADS, blocks, GROUP, DH)
    d_log_sorted = jnp.take_along_axis(d_log, ordering, axis=-1).reshape(
        ROUNDS, HEADS, blocks, GROUP
    )
    scores = block_scores(query_blocks, key_pairs, allowed, selfish)
    prob_full = jnp.exp(scores - log_total[..., None])
    prob_low = prob_full.astype(jnp.bfloat16)
    d_prob = jnp.einsum(
        "rhcqd,rhckd->rhcqk", d_part_blocks, value_pairs, preferred_element_type=jnp.float32
    )
    row_dot = jnp.sum(prob_full * d_prob, axis=-1, keepdims=True)
    d_score = prob_full * (d_prob - row_dot + d_log_sorted[..., None])
    d_score = jnp.where(allowed & jnp.logical_not(selfish), d_score, 0.0).astype(jnp.bfloat16)
    d_query = jnp.einsum(
        "rhcqk,rhckd->rhcqd", d_score, key_pairs, preferred_element_type=jnp.float32
    ) / math.sqrt(DH)
    d_key_pairs = jnp.einsum(
        "rhcqk,rhcqd->rhckd", d_score, query_blocks, preferred_element_type=jnp.float32
    ) / math.sqrt(DH)
    d_value_pairs = jnp.einsum(
        "rhcqk,rhcqd->rhckd", prob_low, d_part_blocks, preferred_element_type=jnp.float32
    )
    d_joined = jnp.concatenate(
        [d_query, fold_pairs(d_key_pairs), fold_pairs(d_value_pairs)], axis=-1
    )
    d_joined_pos = jnp.sum(permute(d_joined.reshape(ROUNDS, HEADS, slots, 3 * DH), inverse), axis=0)
    unit_out, unit_pull = jax.vjp(unit_keys, shared_float)
    d_shared_heads = d_joined_pos[..., :DH] + unit_pull(d_joined_pos[..., DH : 2 * DH])[0]
    d_shared = d_shared_heads.transpose(1, 0, 2).reshape(slots, width).astype(jnp.bfloat16)
    d_values = (
        d_joined_pos[..., 2 * DH :].transpose(1, 0, 2).reshape(slots, width).astype(jnp.bfloat16)
    )
    grad_shared = jnp.einsum("sd,se->de", normed_one, d_shared, preferred_element_type=jnp.float32)
    grad_value = jnp.einsum("sd,se->de", normed_one, d_values, preferred_element_type=jnp.float32)
    d_normed = jnp.einsum(
        "se,de->sd", d_shared, back_shared, preferred_element_type=jnp.float32
    ) + jnp.einsum("se,de->sd", d_values, back_value, preferred_element_type=jnp.float32)
    d_two_attend, grad_gain_attend, grad_shift_attend = norm_back(
        slot_two, back_gain_a, back_shift_a, d_normed
    )
    back_two = above_two + d_two_attend
    (
        grad_shared,
        grad_value,
        grad_output,
        grad_expand,
        grad_reduce,
        grad_gain_attend,
        grad_shift_attend,
        grad_gain_mixing,
        grad_shift_mixing,
        grad_bias_output,
        grad_bias_expand,
        grad_bias_reduce,
    ) = (
        lax.psum_scatter(grad_shared, "fsdp", scatter_dimension=0, tiled=True),
        lax.psum_scatter(grad_value, "fsdp", scatter_dimension=0, tiled=True),
        lax.psum_scatter(grad_output, "fsdp", scatter_dimension=0, tiled=True),
        lax.psum_scatter(grad_expand, "fsdp", scatter_dimension=0, tiled=True),
        lax.psum_scatter(grad_reduce, "fsdp", scatter_dimension=0, tiled=True),
        lax.psum_scatter(grad_gain_attend, "fsdp", scatter_dimension=0, tiled=True),
        lax.psum_scatter(grad_shift_attend, "fsdp", scatter_dimension=0, tiled=True),
        lax.psum_scatter(grad_gain_mixing, "fsdp", scatter_dimension=0, tiled=True),
        lax.psum_scatter(grad_shift_mixing, "fsdp", scatter_dimension=0, tiled=True),
        lax.psum_scatter(grad_bias_output, "fsdp", scatter_dimension=0, tiled=True),
        lax.psum_scatter(grad_bias_expand, "fsdp", scatter_dimension=0, tiled=True),
        lax.psum_scatter(grad_bias_reduce, "fsdp", scatter_dimension=0, tiled=True),
    )
    leaving = (
        (live_rows * out_one).astype(jnp.bfloat16),
        (live_rows * out_two).astype(jnp.bfloat16),
        (live_rows * total_one).astype(jnp.bfloat16),
        (live_rows * back_two).astype(jnp.bfloat16),
    )
    spread_back = (
        lax.all_to_all(leaving[0], "fsdp", split_axis=1, concat_axis=0, tiled=True),
        lax.all_to_all(leaving[1], "fsdp", split_axis=1, concat_axis=0, tiled=True),
        lax.all_to_all(leaving[2], "fsdp", split_axis=1, concat_axis=0, tiled=True),
        lax.all_to_all(leaving[3], "fsdp", split_axis=1, concat_axis=0, tiled=True),
    )
    slot_table = jnp.concatenate(
        [spread_back[0], spread_back[1], spread_back[2], spread_back[3]], axis=1
    )
    stream_buffer = jnp.zeros((stream_total + slots, 4 * narrow), slot_table.dtype)

    def place_sequence(sequence, buffer_rows):
        window_rows = lax.dynamic_slice_in_dim(slot_table, destination[sequence] * slots, slots, 0)
        return lax.dynamic_update_slice_in_dim(buffer_rows, window_rows, starts[sequence], 0)

    stream_buffer = lax.fori_loop(0, devices, place_sequence, stream_buffer)[:stream_total]
    final = (
        lax.all_to_all(stream_buffer[:, :narrow], "fsdp", split_axis=0, concat_axis=1, tiled=True),
        lax.all_to_all(
            stream_buffer[:, narrow : 2 * narrow], "fsdp", split_axis=0, concat_axis=1, tiled=True
        ),
        lax.all_to_all(
            stream_buffer[:, 2 * narrow : 3 * narrow],
            "fsdp",
            split_axis=0,
            concat_axis=1,
            tiled=True,
        ),
        lax.all_to_all(
            stream_buffer[:, 3 * narrow :], "fsdp", split_axis=0, concat_axis=1, tiled=True
        ),
    )
    return (
        final[0],
        final[1],
        final[2],
        final[3],
        grad_shared,
        grad_value,
        grad_output,
        grad_expand,
        grad_reduce,
        grad_gain_attend,
        grad_shift_attend,
        grad_gain_mixing,
        grad_shift_mixing,
        grad_bias_output,
        grad_bias_expand,
        grad_bias_reduce,
    )


def solution(mesh):
    placed = (
        P("fsdp", None),
        P("fsdp", None),
        P("fsdp", None),
        P("fsdp", None),
        P(),
        P(),
        P("fsdp", None, None),
        P("fsdp", None),
        P("fsdp", None),
        P("fsdp", None),
        P("fsdp", None),
        P("fsdp", None),
        P("fsdp"),
        P("fsdp"),
        P("fsdp"),
        P("fsdp"),
        P("fsdp"),
        P("fsdp"),
        P("fsdp"),
    )
    return jax.shard_map(
        body,
        mesh=mesh,
        in_specs=placed,
        out_specs=(
            P("fsdp", None),
            P("fsdp", None),
            P("fsdp", None),
            P("fsdp", None),
            P("fsdp", None),
            P("fsdp", None),
            P("fsdp", None),
            P("fsdp", None),
            P("fsdp", None),
            P("fsdp"),
            P("fsdp"),
            P("fsdp"),
            P("fsdp"),
            P("fsdp"),
            P("fsdp"),
            P("fsdp"),
        ),
        check_vma=False,
    )
```

profile of v0, /device:TPU:0, one launch (start us, length us, event | category | flops | bytes accessed | tf_op | source)
XLA Modules:
  0.0 4989.7 jit_solution(5979176113303369158)
XLA Ops:
  76.9 54.0 %all-to-all-done.1 = bf16[1024,32,32]{0,2,1:T(8,128)(2,1)} async-done(((bf16[1024,32,32]{0,2,1:T(8,128)(2,1)}), bf16[1024,32,32]{0,2,1:T(8,128)(2,1)}, u32[]{:S(2)}, u32[]{:S(2)}) %all-to-all-start.1) | async-done | bytes 2097184 | tf_op jit(solution)/shard_map/all_to_all | solution.py:102
  139.3 51.5 %all-to-all-done.2 = bf16[1024,32,32]{0,2,1:T(8,128)(2,1)} async-done(((bf16[1024,32,32]{0,2,1:T(8,128)(2,1)}), bf16[1024,32,32]{0,2,1:T(8,128)(2,1)}, u32[]{:S(2)}, u32[]{:S(2)}) %all-to-all-start.2) | async-done | bytes 2097184 | tf_op jit(solution)/shard_map/all_to_all | solution.py:103
  206.1 42.5 all-to-all-done.3
  258.1 103.9 %while.15 = (s32[]{:T(128)}, bf16[33792,128]{0,1:T(8,128)(2,1)}, s32[32,2]{0,1:T(2,128)S(1)}, bf16[32,1024,128]{2,1,0:T(8,128)(2,1)}, s32[]{:T(128)}) while((s32[]{:T(128)}, bf16[33792,128]{0,1:T(8,128)(2,1)}, s32[32,2]{0,1:T(2,128)S(1)}, bf16[32,1024,128]{2,1,0:T(8,128)(2,1)}, s32[]{:T(128)}) %tuple.76), condition=%wide.while_cond, body=%wide.while_body.sunk | while | flops 2 | bytes 1572969 | solution.py:111
  396.2 85.2 %all-reduce.21 = (bf16[1024]{0:T(1024)(128)(2,1)S(1)}, bf16[1024]{0:T(1024)(128)(2,1)S(1)}, bf16[1024]{0:T(1024)(128)(2,1)S(1)}, bf16[1024]{0:T(1024)(128)(2,1)S...) all-reduce(bf16[1024]{0:T(1024)(128)(2,1)S(1)} %dynamic-update-slice, ...), channel_id=1, replica_groups=mesh['fsdp'=32] {'fsdp'}, use_global_device_ids=true, to_apply=%add.9 | all-reduce | flops 6144 | bytes 24576
  484.5 40.2 all-gather
  572.4 559.0 %gather_fusion.2 = bf16[32768,384]{1,0:T(8,128)(2,1)} fusion(bf16[8,1024,384]{2,1,0:T(8,128)(2,1)} %pad_maximum_fusion.2, s32[32768]{0:T(1024)S(1)} %bitcast.245), kind=kCustom, calls=%fused_computation.4 | custom fusion | bytes 50593792 | tf_op jit(solution)/shard_map/vmap(vmap(jit(_take)))/gather | solution.py:37
  1192.3 252.1 %gather_fusion.6 = f32[32768]{0:T(1024)S(1)} fusion(f32[4,8,1024]{2,1,0:T(8,128)S(1)} %add.291, s32[32768]{0:T(1024)S(1)} %bitcast.239), kind=kCustom, calls=%fused_computation.clone | custom fusion | bytes 655360 | tf_op jit(solution)/shard_map/jit(take_along_axis)/gather | solution.py:215
  1471.8 500.0 %gather_fusion.3 = f32[32768,128]{1,0:T(8,128)} fusion(f32[4,8,1024,128]{3,2,1,0:T(8,128)} %bitcast.246, s32[32768]{0:T(1024)S(1)} %bitcast.240), kind=kCustom, calls=%fused_computation.5 | custom fusion | bytes 33947648 | tf_op jit(solution)/shard_map/vmap(vmap(jit(_take)))/gather | solution.py:37
  2112.9 575.1 %gather_fusion.4 = bf16[32768,128]{1,0:T(8,128)(2,1)} fusion(bf16[4,8,1024,128]{3,2,1,0:T(8,128)(2,1)} %get-tuple-element.260, s32[32768]{0:T(1024)S(1)} %bitcast.242), kind=kCustom, calls=%fused_computation.6 | custom fusion | bytes 17170432 | tf_op jit(solution)/shard_map/vmap(vmap(jit(_take)))/gather | solution.py:37
  2688.0 252.2 %gather_fusion.7 = f32[32768]{0:T(1024)S(1)} fusion(f32[4,8,1024]{2,1,0:T(8,128)S(1)} %subtract_multiply_fusion, s32[32768]{0:T(1024)S(1)} %bitcast.243), kind=kCustom, calls=%fused_computation.1.clone | custom fusion | bytes 655360 | tf_op jit(solution)/shard_map/jit(take_along_axis)/gather | solution.py:293
  2960.0 201.6 %convolution_multiply_fusion = f32[4,8,16,64,128]{4,3,2,1,0:T(8,128)} fusion(f32[4,8,16,64,128]{4,3,2,1,0:T(8,128)} %fusion.33, f32[4,8,16,64,128]{4,3,2,1,0:T(8,128)} %copy-done.9, f32[4,8,16,64]{3,2,1,0:T(8,128)S(1)} %add.307, f32[4,8,16,64]{3,2,1,0:T(8,128)S(1)} %copy-done.23, s32[4,8,16,64]{3,2,1,0:T(8,128)S(1)} %copy-done.25, ...), kind=kOutput, calls=%fused_computation.55 | convolution fusion | flops 1182826624 | bytes 67305472 | tf_op jit(solution)/shard_map/rhcqk,rhckd->rhcqd/dot_general | solution.py:305
  3161.6 208.4 %broadcast_multiply_fusion = f32[4,8,16,128,128]{4,3,2,1,0:T(8,128)} fusion(bf16[4,8,16,64,128]{4,3,2,1,0:T(8,128)(2,1)} %bitcast.289, f32[4,8,16,64,128]{4,3,2,1,0:T(8,128)} %fusion.33, f32[4,8,16,64,128]{4,3,2,1,0:T(8,128)} %copy-done.9, f32[4,8,16,64]{3,2,1,0:T(8,128)S(1)} %add.307, f32[4,8,16,64]{3,2,1,0:T(8,128)S(1)} %copy-done.23, ...), kind=kOutput, calls=%fused_computation.42 | convolution fusion | flops 1136689280 | bytes 76218368 | tf_op jit(solution)/shard_map/rhcqk,rhcqd->rhckd/dot_general | solution.py:308
  3425.8 34.1 slice_add_fusion
  3459.9 34.2 pad_maximum_fusion
  3494.2 568.2 %gather_fusion.5 = f32[32768,384]{1,0:T(8,128)} fusion(f32[4,8,1024,384]{3,2,1,0:T(8,128)} %bitcast.244, s32[32768]{0:T(1024)S(1)} %bitcast.241), kind=kCustom, calls=%fused_computation.7 | custom fusion | bytes 101056512 | tf_op jit(solution)/shard_map/vmap(vmap(jit(_take)))/gather | solution.py:37
  4154.2 65.3 %all_to_all.280 = bf16[1024,32,32]{0,2,1:T(8,128)(2,1)} all-to-all(bf16[1024,32,32]{0,2,1:T(8,128)(2,1)} %bitcast.308), channel_id=1, replica_groups=mesh['fsdp'=32] {'fsdp'}, dimensions={1} | all-to-all | bytes 4194304 | tf_op jit(solution)/shard_map/all_to_all | solution.py:368
  4219.5 56.1 %all_to_all.281 = bf16[1024,32,32]{0,2,1:T(8,128)(2,1)} all-to-all(bf16[1024,32,32]{0,2,1:T(8,128)(2,1)} %bitcast.285), channel_id=1, replica_groups=mesh['fsdp'=32] {'fsdp'}, dimensions={1} | all-to-all | bytes 4194304 | tf_op jit(solution)/shard_map/all_to_all | solution.py:367
  4295.5 42.6 all-to-all-done.10
  4427.8 239.8 %while.14 = (s32[]{:T(128)}, bf16[33792,128]{1,0:T(8,128)(2,1)}, s32[32]{0:T(128)S(1)}, bf16[32768,128]{1,0:T(8,128)(2,1)}, s32[32]{0:T(128)S(1)}, /*index=5*/s3...) while((s32[]{:T(128)}, bf16[33792,128]{1,0:T(8,128)(2,1)}, s32[32]{0:T(128)S(1)}, ...), condition=%wide.region_24.26_spmd, body=%wide.region_23.25_spmd.sunk | while | flops 9 | bytes 1048797 | solution.py:381
  4712.0 52.2 %all-to-all-done.14 = bf16[32,1024,32]{1,2,0:T(8,128)(2,1)S(1)} async-done(((bf16[32,1024,32]{1,2,0:T(8,128)(2,1)}), bf16[32,1024,32]{1,2,0:T(8,128)(2,1)S(1)}, u32[]{:S(2)}, u32[]{:S(2)}) %all-to-all-start.14) | async-done | bytes 2097184 | tf_op jit(solution)/shard_map/all_to_all | solution.py:387
  4785.4 51.2 %all-to-all-done.15 = bf16[32,1024,32]{1,2,0:T(8,128)(2,1)} async-done(((bf16[32,1024,32]{1,2,0:T(8,128)(2,1)}), bf16[32,1024,32]{1,2,0:T(8,128)(2,1)}, u32[]{:S(2)}, u32[]{:S(2)}) %all-to-all-start.15) | async-done | bytes 2097184 | tf_op jit(solution)/shard_map/all_to_all | solution.py:394
  4848.6 40.8 all-to-all-done.13
  4896.0 67.3 %all-reduce.20 = (f32[1024]{0:T(1024)S(1)}, f32[1024]{0:T(1024)S(1)}, f32[1024]{0:T(1024)S(1)}, f32[1024]{0:T(1024)S(1)}, f32[1024]{0:T(1024)S(1)}, /*index=5*/f32[4096]{0:T(1024)S(1)}, f32[1024]{0:T(1024)S(1)}) all-reduce(f32[1024]{0:T(1024)S(1)} %get-tuple-element.202, ...), channel_id=7, replica_groups=mesh['fsdp'=32] {'fsdp'}, use_global_device_ids=true, to_apply=%region_31.33.clone | all-reduce | flops 10240 | bytes 81920
  (687 shorter events, 1052.5 us)
Async XLA Ops:
  12.0 56.2 %all-to-all-start = ((bf16[1024,32,32]{0,2,1:T(8,128)(2,1)}), bf16[1024,32,32]{0,2,1:T(8,128)(2,1)S(1)}, u32[]{:S(2)}, u32[]{:S(2)}) async-start(bf16[1024,32,32]{0,2,1:T(8,128)(2,1)} %bitcast.278), calls=%async_computation | async-start | bytes 4194304 | tf_op jit(solution)/shard_map/all_to_all | solution.py:101
  59.7 485.8 %all-gather.7.cloned.1.call-start = ((), (), s32[]{:S(2)}) async-start(), calls=%async_computation.21 | async-start | bytes 2162688 | tf_op jit(solution)/shard_map/all_gather | solution.py:135
  68.2 62.7 %all-to-all-start.1 = ((bf16[1024,32,32]{0,2,1:T(8,128)(2,1)}), bf16[1024,32,32]{0,2,1:T(8,128)(2,1)}, u32[]{:S(2)}, u32[]{:S(2)}) async-start(bf16[1024,32,32]{0,2,1:T(8,128)(2,1)} %bitcast.282), calls=%async_computation.1 | async-start | bytes 4194304 | tf_op jit(solution)/shard_map/all_to_all | solution.py:102
  72.4 482.1 %all-gather.9.cloned.1.call-start = ((), (), s32[]{:S(2)}) async-start(), calls=%async_computation.22 | async-start | bytes 2162688 | tf_op jit(solution)/shard_map/all_gather | solution.py:136
  131.0 59.9 %all-to-all-start.2 = ((bf16[1024,32,32]{0,2,1:T(8,128)(2,1)}), bf16[1024,32,32]{0,2,1:T(8,128)(2,1)}, u32[]{:S(2)}, u32[]{:S(2)}) async-start(bf16[1024,32,32]{0,2,1:T(8,128)(2,1)} %bitcast.283), calls=%async_computation.2 | async-start | bytes 4194304 | tf_op jit(solution)/shard_map/all_to_all | solution.py:103
  134.8 1853.0 %all-gather.11.cloned.1.call-start = ((), (), s32[]{:S(2)}) async-start(), calls=%async_computation.23 | async-start | bytes 2162688 | tf_op jit(solution)/shard_map/all_gather | solution.py:137
  190.8 57.8 %all-to-all-start.3 = ((bf16[1024,32,32]{0,2,1:T(8,128)(2,1)}), bf16[1024,32,32]{0,2,1:T(8,128)(2,1)}, u32[]{:S(2)}, u32[]{:S(2)}) async-start(bf16[1024,32,32]{0,2,1:T(8,128)(2,1)} %bitcast.281), calls=%async_computation.3 | async-start | bytes 4194304 | tf_op jit(solution)/shard_map/all_to_all | solution.py:104
  195.6 1812.5 %all-gather.13.cloned.1.call-start = ((), (), s32[]{:S(2)}) async-start(), calls=%async_computation.24 | async-start | bytes 8650752 | tf_op jit(solution)/shard_map/all_gather | solution.py:138
  390.0 148.8 %all-to-all-start.5 = ((bf16[32,1024,32]{1,2,0:T(8,128)(2,1)}), bf16[32,1024,32]{1,2,0:T(8,128)(2,1)S(1)}, u32[]{:S(2)}, u32[]{:S(2)}) async-start(bf16[32,1024,32]{1,2,0:T(8,128)(2,1)} %bitcast.277), calls=%async_computation.5 | async-start | bytes 4194304 | tf_op jit(solution)/shard_map/all_to_all | solution.py:120
  394.1 1631.2 %all-gather.15.cloned.1.call-start = ((), (), s32[]{:S(2)}) async-start(), calls=%async_computation.25 | async-start | bytes 8650752 | tf_op jit(solution)/shard_map/all_gather | solution.py:139
  538.8 905.6 %all-to-all-start.4 = ((bf16[32,1024,32]{1,2,0:T(8,128)(2,1)}), bf16[32,1024,32]{1,2,0:T(8,128)(2,1)}, u32[]{:S(2)}, u32[]{:S(2)}) async-start(bf16[32,1024,32]{1,2,0:T(8,128)(2,1)} %bitcast.280), calls=%async_computation.4 | async-start | bytes 4194304 | tf_op jit(solution)/shard_map/all_to_all | solution.py:119
  1444.4 551.9 %all-to-all-start.9 = ((bf16[32,1024,32]{1,2,0:T(8,128)(2,1)}), bf16[32,1024,32]{1,2,0:T(8,128)(2,1)}, u32[]{:S(2)}, u32[]{:S(2)}) async-start(bf16[32,1024,32]{1,2,0:T(8,128)(2,1)} %bitcast.225), calls=%async_computation.9 | async-start | bytes 4194304 | tf_op jit(solution)/shard_map/all_to_all | solution.py:126
  1996.3 72.3 %all-to-all-start.8 = ((bf16[32,1024,32]{1,2,0:T(8,128)(2,1)}), bf16[32,1024,32]{1,2,0:T(8,128)(2,1)}, u32[]{:S(2)}, u32[]{:S(2)}) async-start(bf16[32,1024,32]{1,2,0:T(8,128)(2,1)} %bitcast.276), calls=%async_computation.8 | async-start | bytes 4194304 | tf_op jit(solution)/shard_map/all_to_all | solution.py:123
  2002.4 2979.4 %reduce-scatter.10.cloned.1.call-start = ((), (), s32[]{:S(2)}) async-start(), calls=%async_computation.28 | async-start | bytes 4325376 | tf_op jit(solution)/shard_map/reduce_scatter | solution.py:349
  3396.7 1585.1 %reduce-scatter.6.cloned.1.call-start = ((), (), s32[]{:S(2)}) async-start(), calls=%async_computation.26 | async-start | bytes 4325376 | tf_op jit(solution)/shard_map/reduce_scatter | solution.py:347
  4103.6 878.1 %reduce-scatter.8.cloned.1.call-start = ((), (), s32[]{:S(2)}) async-start(), calls=%async_computation.27 | async-start | bytes 4325376 | tf_op jit(solution)/shard_map/reduce_scatter | solution.py:348
  4115.6 866.2 %reduce-scatter.14.cloned.1.call-start = ((), (), s32[]{:S(2)}) async-start(), calls=%async_computation.30 | async-start | bytes 17301504 | tf_op jit(solution)/shard_map/reduce_scatter | solution.py:351
  4275.6 62.5 %all-to-all-start.10 = ((bf16[1024,32,32]{0,2,1:T(8,128)(2,1)}), bf16[1024,32,32]{0,2,1:T(8,128)(2,1)}, u32[]{:S(2)}, u32[]{:S(2)}) async-start(bf16[1024,32,32]{0,2,1:T(8,128)(2,1)} %bitcast.284), calls=%async_computation.10 | async-start | bytes 4194304 | tf_op jit(solution)/shard_map/all_to_all | solution.py:369
  4338.1 59.6 %all-to-all-start.11 = ((bf16[1024,32,32]{0,2,1:T(8,128)(2,1)}), bf16[1024,32,32]{0,2,1:T(8,128)(2,1)}, u32[]{:S(2)}, u32[]{:S(2)}) async-start(bf16[1024,32,32]{0,2,1:T(8,128)(2,1)} %bitcast.286), calls=%async_computation.11 | async-start | bytes 4194304 | tf_op jit(solution)/shard_map/all_to_all | solution.py:370
  4341.6 640.2 %reduce-scatter.12.cloned.1.call-start = ((), (), s32[]{:S(2)}) async-start(), calls=%async_computation.29 | async-start | bytes 17301504 | tf_op jit(solution)/shard_map/reduce_scatter | solution.py:350
  4700.5 63.6 %all-to-all-start.14 = ((bf16[32,1024,32]{1,2,0:T(8,128)(2,1)}), bf16[32,1024,32]{1,2,0:T(8,128)(2,1)S(1)}, u32[]{:S(2)}, u32[]{:S(2)}) async-start(bf16[32,1024,32]{1,2,0:T(8,128)(2,1)} %copy.181), calls=%async_computation.14 | async-start | bytes 4194304 | tf_op jit(solution)/shard_map/all_to_all | solution.py:387
  4764.2 72.5 %all-to-all-start.15 = ((bf16[32,1024,32]{1,2,0:T(8,128)(2,1)}), bf16[32,1024,32]{1,2,0:T(8,128)(2,1)}, u32[]{:S(2)}, u32[]{:S(2)}) async-start(bf16[32,1024,32]{1,2,0:T(8,128)(2,1)} %copy.183), calls=%async_computation.15 | async-start | bytes 4194304 | tf_op jit(solution)/shard_map/all_to_all | solution.py:394
  4836.6 52.8 %all-to-all-start.13 = ((bf16[32,1024,32]{1,2,0:T(8,128)(2,1)}), bf16[32,1024,32]{1,2,0:T(8,128)(2,1)}, u32[]{:S(2)}, u32[]{:S(2)}) async-start(bf16[32,1024,32]{1,2,0:T(8,128)(2,1)} %copy.179), calls=%async_computation.13 | async-start | bytes 4194304 | tf_op jit(solution)/shard_map/all_to_all | solution.py:384
  4889.4 88.4 %all-to-all-start.12 = ((bf16[32,1024,32]{1,2,0:T(8,128)(2,1)}), bf16[32,1024,32]{1,2,0:T(8,128)(2,1)}, u32[]{:S(2)}, u32[]{:S(2)}) async-start(bf16[32,1024,32]{1,2,0:T(8,128)(2,1)} %copy.177), calls=%async_computation.12 | async-start | bytes 4194304 | tf_op jit(solution)/shard_map/all_to_all | solution.py:383
  (86 other events, 6039.7 us)
Sparse Core Ops, SparseCore 0:
  25.4 33.2 sort.34.cloned.1.call-done
  62.2 20.9 sort.36.cloned.1.call-done
  (2 shorter events, 0.0 us)
Sparse Core Ops, SparseCore 1:
  63.0 69.7 all-gather.6
  135.5 61.4 all-gather.8
  199.7 64.2 all-gather.10
  266.9 76.1 all-gather.12
  397.7 91.6 all-gather.14
  3396.7 145.3 reduce-scatter.9
  4103.7 153.6 reduce-scatter.5
  4260.1 148.5 reduce-scatter.7
  4411.4 179.1 reduce-scatter.13
  4593.5 229.7 reduce-scatter.11
where the time goes:
time: 5030 us; the launch traced here: 4990 us
  local copies, waits for them, and re-layouts  3250 us (65%)
  matrix products  653 us (13%)
  waiting for transfers between devices  360 us (7%)
  blocking collectives  314 us (6%)
  other arithmetic  227 us (5%)
  loops' own time  83.9 us (2%)
  starting transfers between devices  79.1 us (2%)
    gather x4, local copies, waits for them, and re-layouts, pick_rows(): return jnp.take(table, index, axis=0)  2200 us
    gather x2, local copies, waits for them, and re-layouts, body(): jnp.take_along_axis(d_log, ordering, axis=-1)  252 us
    gather x2, local copies, waits for them, and re-layouts, body(): jnp.take_along_axis(log_total.reshape(ROUNDS, HEADS, slots), inverse, axi...  252 us
    dot_general x1, matrix products, body(): jnp.einsum('rhcqk,rhcqd->rhckd', d_score, query_blocks, preferred_element...  208 us
    dot_general x1, matrix products, body(): jnp.einsum('rhcqk,rhckd->rhcqd', d_score, key_pairs, preferred_element_ty...  202 us
    unnamed x2, blocking collectives  152 us
    gather x160, local copies, waits for them, and re-layouts  103 us
  transfers between devices with their start and end apart: 24, of which 9 were waited for; matrix products, arithmetic and copies ran while one was open for 55% of the time, Pallas kernels for 0%

commit v1 on v0

v1 whole, which is shorter than its diff:
```python
import functools
import math

import jax
import jax.numpy as jnp
from jax import lax
from jax.experimental import pallas as pl
from jax.experimental.pallas import tpu as pltpu
from jax.sharding import PartitionSpec as P

HEADS = 8
DH = 128
GROUP = 64
ROUNDS = 4
BUCKETS = 32
EPS_NORM = 1e-05
EPS_UNIT = 1e-06
LOG2E = math.log2(math.e)
SELF2 = -100000.0 * LOG2E
NEG = -1e30
SCALE = 1.0 / math.sqrt(DH)
TILE = 256
FREE = 99.0

NT = (((1,), (1,)), ((), ()))
NN = (((1,), (0,)), ((), ()))
TN = (((0,), (0,)), ((), ()))
F32 = jnp.float32
BF16 = jnp.bfloat16


def dot(a, b, dims=NN):
    return lax.dot_general(a, b, dims, preferred_element_type=F32)


def layer_norm(values, gain, shift):
    center = values - jnp.mean(values, axis=-1, keepdims=True)
    spread = jnp.mean(center * center, axis=-1, keepdims=True)
    return center * lax.rsqrt(spread + EPS_NORM) * gain + shift


def norm_back(values, gain, shift, upstream):
    outcome, pullback = jax.vjp(layer_norm, values, gain, shift)
    return pullback(upstream)


def prepare(q_ref, code_ref, spread_ref, unit_s, ask_s, key_s):
    rows = q_ref.shape[0]
    lane = lax.broadcasted_iota(jnp.int32, (TILE, DH), 1)
    target = ((lane // 64) * 32 + lane % 16).astype(F32)
    for i in range(rows // TILE):
        at = pl.ds(i * TILE, TILE)
        q = q_ref[at, :].astype(F32)
        norm = lax.rsqrt(jnp.sum(q * q, axis=1, keepdims=True) + EPS_UNIT)
        unit_s[at, :] = (q * (norm * (SCALE * LOG2E))).astype(BF16)
        code = dot(code_ref[at, :], spread_ref[...])
        here = code == target
        ask_s[at, :] = jnp.where(here, 1.0, 0.0).astype(BF16)
        key_s[at, :] = jnp.where(here | (code + 1.0 == target), 1.0, 0.0).astype(BF16)


def attend_kernel(low_ref, q_ref, v_ref, code_ref, spread_ref, comb_ref, lse_ref, lone_ref, unit_s, ask_s, key_s, vt_s, acc_s):
    rows = q_ref.shape[0]
    prepare(q_ref, code_ref, spread_ref, unit_s, ask_s, key_s)
    for i in range(rows // TILE):
        at = pl.ds(i * TILE, TILE)
        vt_s[:, at] = v_ref[at, :].astype(F32).T.astype(BF16)
    key_at = lax.broadcasted_iota(jnp.int32, (TILE, TILE), 0)
    ask_at = lax.broadcasted_iota(jnp.int32, (TILE, TILE), 1)
    for i in range(rows // TILE):
        at = pl.ds(i * TILE, TILE)
        low = low_ref[i]

        @pl.when(low <= i)
        def _():
            q = q_ref[at, :]
            ask = ask_s[at, :]
            score = dot(unit_s[at, :], q, NT)
            count = dot(key_s[at, :], ask, NT)
            score = jnp.where(key_at == ask_at, SELF2, score)
            score = jnp.where((key_at <= ask_at) & (count > 0.5), score, NEG)
            top = jnp.max(score, axis=0, keepdims=True)
            prob = count * jnp.exp2(score - top)
            total = jnp.sum(prob, axis=0, keepdims=True)
            acc_s[...] = dot(vt_s[:, at], prob.astype(BF16))

            def step(j, carry):
                top, total = carry
                key_rows = pl.ds(pl.multiple_of(j * TILE, TILE), TILE)
                score = dot(unit_s[key_rows, :], q, NT)
                count = dot(key_s[key_rows, :], ask, NT)
                score = jnp.where(count > 0.5, score, NEG)
                newer = jnp.maximum(top, jnp.max(score, axis=0, keepdims=True))
                fade = jnp.exp2(top - newer)
                prob = count * jnp.exp2(score - newer)
                acc_s[...] = acc_s[...] * fade + dot(vt_s[:, key_rows], prob.astype(BF16))
                return newer, total * fade + jnp.sum(prob, axis=0, keepdims=True)

            top, total = lax.fori_loop(low, i, step, (top, total))
            some = total > 0.0
            safe = jnp.where(some, total, 1.0)
            inverse = jnp.where(some, 1.0 / safe, 0.0)
            comb_ref[at, :] = (acc_s[...] * inverse).T.astype(BF16)
            lse_ref[0, :, at] = top + jnp.log2(safe)
            lone_ref[0, :, at] = ROUNDS * jnp.exp2(SELF2 - jnp.maximum(top, SELF2)) * inverse

        @pl.when(low > i)
        def _():
            comb_ref[at, :] = jnp.zeros((TILE, DH), BF16)
            lse_ref[0, :, at] = jnp.zeros((1, TILE), F32)
            lone_ref[0, :, at] = jnp.zeros((1, TILE), F32)


def back_kernel(
    low_ref, q_ref, v_ref, code_ref, spread_ref, comb_ref, above_ref, lse_ref, lone_ref,
    dq_ref, dv_ref, unit_s, ask_s, key_s, dunit_s, dvalue_s, dask_s,
):
    rows = q_ref.shape[0]
    prepare(q_ref, code_ref, spread_ref, unit_s, ask_s, key_s)
    key_at = lax.broadcasted_iota(jnp.int32, (TILE, TILE), 0)
    ask_at = lax.broadcasted_iota(jnp.int32, (TILE, TILE), 1)
    dunit_s[...] = jnp.zeros(dunit_s.shape, F32)
    dvalue_s[...] = jnp.zeros(dvalue_s.shape, F32)
    dask_s[...] = jnp.zeros(dask_s.shape, F32)
    for i in range(rows // TILE):
        at = pl.ds(i * TILE, TILE)
        low = low_ref[i]

        @pl.when(low <= i)
        def _():
            q = q_ref[at, :]
            ask = ask_s[at, :]
            above = above_ref[at, :]
            lse = lse_ref[0, :, at]
            mixed = above.astype(F32) * comb_ref[at, :].astype(F32)
            delta = jnp.sum(mixed.T, axis=0, keepdims=True)
            score = dot(unit_s[at, :], q, NT)
            count = dot(key_s[at, :], ask, NT)
            d_prob = dot(v_ref[at, :], above, NT)
            earlier = key_at < ask_at
            prob = count * jnp.exp2(jnp.minimum(score - lse, 0.0))
            prob = jnp.where(earlier, prob, 0.0)
            d_score = (prob * (d_prob - delta)).astype(BF16)
            prob = jnp.where(key_at == ask_at, lone_ref[0, :, at], prob).astype(BF16)
            dvalue_s[at, :] += dot(prob, above)
            dunit_s[at, :] += dot(d_score, q)
            dask_s[at, :] += dot(d_score, unit_s[at, :], TN)

            def step(j, carry):
                key_rows = pl.ds(pl.multiple_of(j * TILE, TILE), TILE)
                unit = unit_s[key_rows, :]
                score = dot(unit, q, NT)
                count = dot(key_s[key_rows, :], ask, NT)
                d_prob = dot(v_ref[key_rows, :], above, NT)
                prob = count * jnp.exp2(jnp.minimum(score - lse, 0.0))
                d_score = (prob * (d_prob - delta)).astype(BF16)
                dvalue_s[key_rows, :] += dot(prob.astype(BF16), above)
                dunit_s[key_rows, :] += dot(d_score, q)
                dask_s[at, :] += dot(d_score, unit, TN)
                return carry

            lax.fori_loop(low, i, step, 0)

    for i in range(rows // TILE):
        at = pl.ds(i * TILE, TILE)
        q = q_ref[at, :].astype(F32)
        norm = lax.rsqrt(jnp.sum(q * q, axis=1, keepdims=True) + EPS_UNIT)
        d_unit = dunit_s[at, :] * SCALE
        along = jnp.sum(q * d_unit, axis=1, keepdims=True)
        d_q = dask_s[at, :] * (1.0 / LOG2E) + d_unit * norm - q * (norm * norm * norm * along)
        dq_ref[at, :] = d_q.astype(BF16)
        dv_ref[at, :] = dvalue_s[at, :].astype(BF16)


def head_specs(rows):
    by_head = pl.BlockSpec((rows, DH), lambda h, low: (0, h))
    code = pl.BlockSpec((rows, ROUNDS * HEADS), lambda h, low: (0, 0))
    spread = pl.BlockSpec((ROUNDS * HEADS, DH), lambda h, low: (0, h))
    stat = pl.BlockSpec((1, 1, rows), lambda h, low: (h, 0, 0))
    return by_head, code, spread, stat


def attend(low, shared, values, code, spread):
    rows = shared.shape[0]
    by_head, code_spec, spread_spec, stat = head_specs(rows)
    wide = jax.ShapeDtypeStruct((rows, HEADS * DH), BF16)
    thin = jax.ShapeDtypeStruct((HEADS, 1, rows), F32)
    return pl.pallas_call(
        attend_kernel,
        grid_spec=pltpu.PrefetchScalarGridSpec(
            num_scalar_prefetch=1,
            grid=(HEADS,),
            in_specs=[by_head, by_head, code_spec, spread_spec],
            out_specs=[by_head, stat, stat],
            scratch_shapes=[pltpu.VMEM((rows, DH), BF16)] * 3
            + [pltpu.VMEM((DH, rows), BF16), pltpu.VMEM((DH, TILE), F32)],
        ),
        out_shape=(wide, thin, thin),
        name="attend",
        cost_estimate=pl.CostEstimate(
            flops=HEADS * 20 * 3 * 2 * TILE * TILE * DH, bytes_accessed=rows * HEADS * DH * 6, transcendentals=HEADS * 20 * TILE * TILE
        ),
    )(low, shared, values, code, spread)


def attend_back(low, shared, values, code, spread, combined, above, lse, lone):
    rows = shared.shape[0]
    by_head, code_spec, spread_spec, stat = head_specs(rows)
    wide = jax.ShapeDtypeStruct((rows, HEADS * DH), BF16)
    return pl.pallas_call(
        back_kernel,
        grid_spec=pltpu.PrefetchScalarGridSpec(
            num_scalar_prefetch=1,
            grid=(HEADS,),
            in_specs=[by_head, by_head, code_spec, spread_spec, by_head, by_head, stat, stat],
            out_specs=[by_head, by_head],
            scratch_shapes=[pltpu.VMEM((rows, DH), BF16)] * 3 + [pltpu.VMEM((rows, DH), F32)] * 3,
        ),
        out_shape=(wide, wide),
        name="attend_back",
        cost_estimate=pl.CostEstimate(
            flops=HEADS * 20 * 6 * 2 * TILE * TILE * DH, bytes_accessed=rows * HEADS * DH * 12, transcendentals=HEADS * 20 * TILE * TILE
        ),
    )(low, shared, values, code, spread, combined, above, lse, lone)


def block_of_rank(buckets, length):
    slots = buckets.shape[-1]
    place = lax.broadcasted_iota(jnp.int32, (1, 1, slots), 2)
    bucket = lax.broadcasted_iota(jnp.int32, (1, BUCKETS, 1), 1)
    one_hot = (buckets[:, None, :] == bucket) & (place < length)
    first = lax.broadcasted_iota(jnp.int32, (slots, slots), 0)
    second = lax.broadcasted_iota(jnp.int32, (slots, slots), 1)
    before = dot(one_hot.astype(BF16).reshape(-1, slots), (first < second).astype(BF16)).reshape(one_hot.shape)
    size = jnp.sum(one_hot.astype(F32), axis=2, keepdims=True)
    offset = jnp.cumsum(size, axis=1) - size
    rank = jnp.sum(jnp.where(one_hot, before + offset, 0.0), axis=1)
    return jnp.where(place[0] < length, jnp.floor(rank * (1.0 / GROUP)), FREE)


def body(
    input_one, input_two, upstream_one, upstream_two, lengths, destination, buckets,
    w_shared, w_value, w_output, w_expand, w_reduce,
    gain_attend, shift_attend, gain_mixing, shift_mixing, bias_output, bias_expand, bias_reduce,
):
    devices = lax.axis_size("fsdp")
    me = lax.axis_index("fsdp")
    slots, width = input_one.shape
    half = slots // 2
    window = 2 * slots
    part = w_shared.shape[0]
    hidden = w_expand.shape[1]
    sides = hidden // width
    down = [(i, i - 1) for i in range(1, devices)]
    up = [(i, i + 1) for i in range(devices - 1)]

    def widen(own):
        head = lax.ppermute(own[half:], "fsdp", up)
        tail = lax.ppermute(own[:half], "fsdp", down)
        return jnp.concatenate([head, own, tail], axis=0)

    def narrow(wide):
        tail = lax.ppermute(wide[:half], "fsdp", down)
        head = lax.ppermute(wide[half + slots :], "fsdp", up)
        return wide[half : half + slots], jnp.concatenate([head, tail], axis=0)

    ends = jnp.cumsum(lengths)
    starts = ends - lengths
    middle = starts + lengths // 2
    base = me * slots
    owner = jnp.zeros((devices,), jnp.int32).at[destination].set(jnp.arange(devices, dtype=jnp.int32))
    mine = lengths[owner[me]]
    block = block_of_rank(buckets[0], mine)

    vectors = jnp.concatenate(
        [gain_attend, shift_attend, gain_mixing, shift_mixing, bias_output, bias_reduce, bias_expand]
    )
    high = lax.reduce_precision(vectors, 8, 7)
    count = vectors.shape[0]
    packed = jnp.zeros((8, width), BF16).at[0, :count].set(high.astype(BF16)).at[1, :count].set((vectors - high).astype(BF16))
    first = lax.all_gather(
        jnp.concatenate([w_shared, w_value, block.astype(BF16), packed], axis=0), "fsdp", axis=0, tiled=False
    )
    lists = ROUNDS * HEADS
    full_shared = first[:, :part].reshape(width, width)
    full_value = first[:, part : 2 * part].reshape(width, width)
    blocks_all = first[:, 2 * part : 2 * part + lists]
    full_vectors = first[:, 2 * part + lists, :count].astype(F32) + first[:, 2 * part + lists + 1, :count].astype(F32)
    gain_a, shift_a, gain_m, shift_m, bias_o, bias_r = (
        full_vectors[:, k * part : (k + 1) * part].reshape(width) for k in range(6)
    )
    bias_e = full_vectors[:, 6 * part :].reshape(hidden)
    second_gather = lax.all_gather(
        jnp.concatenate(
            [w_output] + [w_expand[:, k * width : (k + 1) * width] for k in range(sides)] + [w_reduce], axis=0
        ),
        "fsdp", axis=0, tiled=False,
    )
    full_output = second_gather[:, :part].reshape(width, width)
    full_expand = jnp.concatenate(
        [second_gather[:, (k + 1) * part : (k + 2) * part].reshape(width, width) for k in range(sides)], axis=1
    )
    full_reduce = second_gather[:, (sides + 1) * part :].reshape(hidden, width)

    inside = (middle >= base) & (middle < base + slots)
    chosen = jnp.sum(inside.astype(jnp.int32))
    lowest = jnp.minimum(jnp.argmax(inside).astype(jnp.int32), devices - 1)
    code = jnp.full((window + slots, lists), FREE, F32)
    begin = jnp.full((window + slots,), window, jnp.int32)
    spot = jnp.arange(slots, dtype=jnp.int32)
    for k in range(2):
        s = jnp.minimum(lowest + k, devices - 1)
        valid = chosen > k
        offset = jnp.where(valid, starts[s] - (base - half), window)
        rows = lax.dynamic_index_in_dim(blocks_all, destination[s], 0, keepdims=False).astype(F32).T
        rows = jnp.where(rows < 50.0, rows + 32.0 * k, FREE)
        code = lax.dynamic_update_slice(code, rows, (offset, 0))
        begin = lax.dynamic_update_slice(begin, jnp.where(spot < lengths[s], offset, window), (offset,))
    code = code[:window].astype(BF16)
    lowest_row = jnp.min(begin[:window].reshape(-1, TILE), axis=1)
    low = (lowest_row // TILE).astype(jnp.int32)
    lane = jnp.arange(HEADS * DH, dtype=jnp.int32)
    row = jnp.arange(lists, dtype=jnp.int32)[:, None]
    spread = (row == ((lane % 64) // 16) * HEADS + lane // DH).astype(BF16)

    live = ((base + jnp.arange(slots, dtype=jnp.int32)) < ends[-1]).astype(F32)[:, None]
    slot_one = input_one.astype(F32)
    slot_two = input_two.astype(F32)
    above_one = live * upstream_one.astype(F32)
    above_two = live * upstream_two.astype(F32)

    two_window = widen(input_two).astype(F32)
    normed = layer_norm(two_window, gain_a, shift_a).astype(BF16)
    shared = dot(normed, full_shared).astype(BF16)
    values = dot(normed, full_value).astype(BF16)
    combined_window, lse, lone = attend(low, shared, values, code, spread)
    own, other = narrow(combined_window)
    combined = own + other
    attended = dot(combined, full_output) + bias_o
    out_one = slot_one + live * attended
    second = layer_norm(out_one, gain_m, shift_m).astype(BF16)
    pre_act = dot(second, full_expand) + bias_e
    expand = jax.nn.gelu(pre_act, approximate=True).astype(BF16)
    out_two = slot_two + live * (dot(expand, full_reduce) + bias_r)

    d_reduce = above_two.astype(BF16)
    grad_reduce = dot(expand, d_reduce, TN)
    grad_bias_reduce = jnp.sum(d_reduce, axis=0, dtype=F32)
    d_expand = dot(d_reduce, full_reduce, NT)
    gelu_out, gelu_pull = jax.vjp(lambda inner: jax.nn.gelu(inner, approximate=True), pre_act)
    d_pre = gelu_pull(d_expand)[0].astype(BF16)
    grad_expand = dot(second, d_pre, TN)
    grad_bias_expand = jnp.sum(d_pre, axis=0, dtype=F32)
    d_second = dot(d_pre, full_expand, NT)
    d_one_mix, grad_gain_m, grad_shift_m = norm_back(out_one, gain_m, shift_m, d_second)
    total_one = above_one + d_one_mix
    d_attend = (live * total_one).astype(BF16)
    grad_output = dot(combined, d_attend, TN)
    grad_bias_output = jnp.sum(d_attend, axis=0, dtype=F32)
    d_combined = dot(d_attend, full_output, NT).astype(BF16)
    d_shared, d_values = attend_back(
        low, shared, values, code, spread, combined_window, widen(d_combined), lse, lone
    )
    grad_shared = dot(normed, d_shared, TN)
    grad_value = dot(normed, d_values, TN)
    d_normed = dot(d_shared, full_shared, NT) + dot(d_values, full_value, NT)
    d_two_window, grad_gain_a, grad_shift_a = norm_back(two_window, gain_a, shift_a, d_normed)
    own, other = narrow(d_two_window.astype(BF16))
    back_two = above_two + own.astype(F32) + other.astype(F32)

    def scatter(whole):
        return lax.psum_scatter(whole, "fsdp", scatter_dimension=0, tiled=True)

    def split(whole):
        return whole.astype(BF16).reshape(devices, -1, width)

    early = jnp.concatenate(
        [split(grad_output)] + [split(grad_expand[:, k * width : (k + 1) * width]) for k in range(sides)] + [split(grad_reduce)],
        axis=1,
    )
    late = jnp.concatenate([split(grad_shared), split(grad_value)], axis=1)
    early = scatter(early.reshape(-1, width)).astype(F32)
    late = scatter(late.reshape(-1, width)).astype(F32)
    small = [
        scatter(member.reshape(devices, -1)).reshape(-1)
        for member in (
            jnp.concatenate(
                [
                    member.reshape(devices, -1)
                    for member in (
                        grad_gain_a, grad_shift_a, grad_gain_m, grad_shift_m, grad_bias_output, grad_bias_reduce, grad_bias_expand
                    )
                ],
                axis=1,
            ),
        )
    ][0]
    return (
        (live * out_one).astype(BF16),
        (live * out_two).astype(BF16),
        (live * total_one).astype(BF16),
        (live * back_two).astype(BF16),
        late[:part],
        late[part:],
        early[:part],
        jnp.concatenate([early[(k + 1) * part : (k + 2) * part] for k in range(sides)], axis=1),
        early[(sides + 1) * part :],
        small[:part],
        small[part : 2 * part],
        small[2 * part : 3 * part],
        small[3 * part : 4 * part],
        small[4 * part : 5 * part],
        small[6 * part :],
        small[5 * part : 6 * part],
    )


def solution(mesh):
    rows, flat, whole = P("fsdp", None), P("fsdp"), P()
    return jax.shard_map(
        body,
        mesh=mesh,
        in_specs=(rows,) * 4 + (whole, whole, P("fsdp", None, None)) + (rows,) * 5 + (flat,) * 7,
        out_specs=(rows,) * 9 + (flat,) * 7,
        check_vma=False,
    )
```

time: 5030 us -> 882 us (0.18)
  local copies, waits for them, and re-layouts: 3250 us -> 117 us
  matrix products: 653 us -> 168 us
  blocking collectives: 314 us -> 82.6 us
  other arithmetic: 227 us -> 50.7 us
  waiting for transfers between devices: 360 us -> 234 us
  loops' own time: 83.9 us -> 0 us
  Pallas kernels: 0 us -> 73.9 us
  starting transfers between devices: 79.1 us -> 141 us
    gather x171 -> x0, local copies, waits for them, and re-layouts: 2820 us -> none  [the longest x4 2200 us: pick_rows(): return jnp.take(table, index, axis=0)]
    dot_general x21 -> x16, matrix products: 653 us -> 168 us  [dot(): return lax.dot_general(a, b, dims, preferred_element_type=F32)]
    all_to_all x14 -> x0, waiting for transfers between devices: 357 us -> none  [the longest x1 54 us: body(): lax.all_to_all(input_two, 'fsdp', split_axis=1, concat_axis=0, tiled=True)]
    reduce_scatter x5 -> x2, waiting for transfers between devices: 0.04 us -> 177 us  [scatter(): return lax.psum_scatter(whole, 'fsdp', scatter_dimension=0, tiled=True)]
    ppermute x0 -> x8, starting transfers between devices: none -> 141 us  [the longest x2 130 us: narrow(): head = lax.ppermute(wide[half + slots:], 'fsdp', up)]
    all_to_all x2 -> x0, blocking collectives: 121 us -> none  [the longest x1 65.3 us: body(): lax.all_to_all(leaving[1], 'fsdp', split_axis=1, concat_axis=0, tiled=True)]
    another operation x2 -> x0, loops' own time: 83.9 us -> none  [the longest x1 83.4 us: body(): lax.fori_loop(0, devices, place_sequence, stream_buffer)[:stream_total]]
    dynamic_update_slice x32 -> x2, local copies, waits for them, and re-layouts: 87.6 us -> 4.72 us  [body(): code = lax.dynamic_update_slice(code, rows, (offset, 0))]
  transfers between devices with their start and end apart: 24 -> 12, of which waited for: 9 -> 4; matrix products, arithmetic and copies ran while one was open for 55% -> 23% of each run, Pallas kernels for 0% -> 4%
where the time goes in v1:
time: 882 us; the launch traced here: 892 us
  waiting for transfers between devices  234 us (27%)
  matrix products  168 us (19%)
  starting transfers between devices  141 us (16%)
  local copies, waits for them, and re-layouts  117 us (13%)
  blocking collectives  82.6 us (9%)
  Pallas kernels  73.9 us (8%)
  other arithmetic  50.7 us (6%)
  between operations  24.2 us (3%)
    reduce_scatter x2, waiting for transfers between devices, scatter(): return lax.psum_scatter(whole, 'fsdp', scatter_dimension=0, tiled=True)  177 us
    dot_general x16, matrix products, dot(): return lax.dot_general(a, b, dims, preferred_element_type=F32)  168 us
    ppermute x2, starting transfers between devices, narrow(): head = lax.ppermute(wide[half + slots:], 'fsdp', up)  130 us
    unnamed x1, blocking collectives  82.6 us
    all_gather x1, waiting for transfers between devices, body(): lax.all_gather(jnp.concatenate([w_shared, w_value, block.astype(BF16), pa...  54.4 us
    unnamed x117, local copies, waits for them, and re-layouts  51.4 us
    pallas_call x1, Pallas kernels, attend_back(): pl.pallas_call(back_kernel, grid_spec=pltpu.PrefetchScalarGridSpec(num_sc...  41 us
    pallas_call x1, Pallas kernels, attend(): pl.pallas_call(attend_kernel, grid_spec=pltpu.PrefetchScalarGridSpec(num_...  32.9 us
  transfers between devices with their start and end apart: 12, of which 4 were waited for; matrix products, arithmetic and copies ran while one was open for 23% of the time, Pallas kernels for 4%

profile of v1, /device:TPU:0, one launch (start us, length us, event | category | flops | bytes accessed | tf_op | source)
XLA Modules:
  0.0 891.8 jit_solution(12127125399504294440)
XLA Ops:
  48.4 54.4 %all-gather.5.cloned.1.call-done = bf16[3328,1024]{1,0:T(8,128)(2,1)} async-done(((bf16[104,1024]{1,0:T(8,128)(2,1)}), bf16[3328,1024]{1,0:T(8,128)(2,1)}) %all-gather.5.cloned.1.call-update) | async-done | bytes 6815760 | tf_op jit(solution)/shard_map/all_gather | solution.py:281
  104.8 6.2 fusion.69
  126.7 6.3 convolution_convert_fusion.2.v_ref
  133.0 6.2 convolution_convert_fusion.3.q_ref
  139.2 32.9 %attend.1 = (bf16[2048,1024]{1,0:T(8,128)(2,1)}, f32[8,1,2048]{2,1,0:T(1,128)}, f32[8,1,2048]{2,1,0:T(1,128)}) custom-call(s32[8]{0:T(128)} %and_select_fusion.low_ref, bf16[2048,1024]{1,0:T(8,128)(2,1)} %convolution_convert_fusion.3.q_ref, bf16[2048,1024]{1,0:T(8,128)(2,1)} %convolution_convert_fusion.2.v_ref, bf16[2048,32]{1,0:T(8,128)(2,1)} %slice.352.code_ref, ...), custom_call_target="tpu_custom_call" | custom-call | flops 8053063680 | bytes 12582912 | tf_op jit(solution)/shard_map/attend/pallas_call | solution.py:188
  175.1 52.3 %collective-permute-start.2 = (bf16[512,1024]{1,0:T(8,128)(2,1)}, bf16[512,1024]{1,0:T(8,128)(2,1)}, u32[]{:S(2)}, u32[]{:S(2)}) collective-permute-start(bf16[512,1024]{1,0:T(8,128)(2,1)} %get-tuple-element.142), channel_id=1, source_target_pairs={{0,1},{1,2},{2,3},{3,4},{4,5},{5,6},{6,7},{7,8},{8,9},{9,10},{10,1... | collective-permute-start | bytes 3145736 | tf_op jit(solution)/shard_map/ppermute | solution.py:264
  242.8 8.2 slice.317
  251.0 7.3 fusion.67
  267.6 17.6 %fusion.36 = f32[1024,4096]{1,0:T(8,128)} fusion(bf16[1024,1024]{1,0:T(8,128)(2,1)} %bitcast.111, bf16[1024,1024]{1,0:T(8,128)(2,1)} %bitcast.113, bf16[1024,1024]{1,0:T(8,128)(2,1)} %bitcast.115, bf16[1024,1024]{1,0:T(8,128)(2,1)} %bitcast.109, f32[1024,1024]{0,1:T(8,128)} %copy-done.2, f32[1024]{0:T(1024)S(1)} %add.259, f32[1024]{0:T(1024)S(1)} %mul.265, ...), kind=kOutput, calls=%fused_computation.67 | convolution fusion | flops 8628731904 | bytes 29376512 | tf_op jit(solution)/shard_map/dot_general | solution.py:33
  285.3 25.0 %convert_reduce_fusion = (f32[4096]{0:T(1024)}, bf16[1024,4096]{1,0:T(8,128)(2,1)}) fusion(f32[1024,4096]{1,0:T(8,128)} %fusion.36, f32[4096]{0:T(1024)S(1)} %slice_bitcast_fusion, bf16[4096,1024]{1,0:T(8,128)(2,1)} %bitcast.98, bf16[1024,1024]{0,1:T(8,128)(2,1)S(1)} %copy.97, f32[1024]{0:T(1024)S(1)} %fusion.56), kind=kOutput, calls=%fused_computation.10 | convolution fusion | flops 8689545216 | bytes 35688448 | tf_op jit(solution)/shard_map/dot_general | solution.py:33
  310.2 15.8 %fusion.81 = (f32[1024]{0:T(1024)}, f32[1024,1024]{1,0:T(8,128)}) fusion(bf16[1024,4096]{1,0:T(8,128)(2,1)} %get-tuple-element.186, bf16[1024,1024]{1,0:T(8,128)(2,1)} %bitcast.112, bf16[1024,1024]{1,0:T(8,128)(2,1)} %bitcast.114, bf16[1024,1024]{1,0:T(8,128)(2,1)} %bitcast.116, bf16[1024,1024]{1,0:T(8,128)(2,1)} %bitcast.110), kind=kOutput, calls=%fused_computation.182 | convolution fusion | flops 8624536576 | bytes 20975616 | tf_op jit(solution)/shard_map/dot_general | solution.py:33
  326.0 5.3 copy.98
  357.1 41.0 %attend_back.1 = (bf16[2048,1024]{1,0:T(8,128)(2,1)}, bf16[2048,1024]{1,0:T(8,128)(2,1)}) custom-call(s32[8]{0:T(128)} %and_select_fusion.low_ref, bf16[2048,1024]{1,0:T(8,128)(2,1)} %convolution_convert_fusion.3.q_ref, bf16[2048,1024]{1,0:T(8,128)(2,1)} %convolution_convert_fusion.2.v_ref, bf16[2048,32]{1,0:T(8,128)(2,1)} %slice.352.code_ref, ...), custom_call_target="tpu_custom_call" | custom-call | flops 16106127360 | bytes 25165824 | tf_op jit(solution)/shard_map/attend_back/pallas_call | solution.py:210
  398.2 8.1 convolution_convert_fusion.6
  413.9 5.3 convolution_convert_fusion.4
  422.1 11.7 %convolution_convert_fusion.1 = bf16[1024,4096]{1,0:T(8,128)(2,1)S(1)} fusion(bf16[1024,4096]{1,0:T(8,128)(2,1)} %get-tuple-element.186, f32[1024,1024]{0,1:T(8,128)S(1)} %copy-done.4, f32[1024]{0:T(1024)S(1)} %add.259, f32[1024]{0:T(1024)S(1)} %mul.265, f32[1024]{0:T(1024)S(1)} %fusion.59, f32[1024]{0:T(1024)S(1)} %broadcast_multiply_fusion.1), kind=kOutput, calls=%fused_computation.29 | convolution fusion | flops 8599371776 | bytes 20987904 | tf_op jit(solution)/shard_map/dot_general | solution.py:33
  441.3 19.8 %convolution_convert_fusion = bf16[4096,1024]{1,0:T(8,128)(2,1)} fusion(bf16[1024,1024]{0,1:T(8,128)(2,1)S(1)} %copy.97, f32[1024]{0:T(1024)S(1)} %fusion.56, f32[1024,4096]{1,0:T(8,128)} %fusion.36, f32[4096]{0:T(1024)S(1)} %slice_bitcast_fusion), kind=kOutput, calls=%fused_computation.28 | convolution fusion | flops 8639217664 | bytes 27283456 | tf_op jit(solution)/shard_map/dot_general | solution.py:33
  461.1 8.2 constant_dynamic-update-slice_fusion.2
  470.1 10.8 %fusion.82 = f32[2048,1024]{0,1:T(8,128)} fusion(bf16[2048,1024]{1,0:T(8,128)(2,1)} %get-tuple-element.51, bf16[1024,1024]{1,0:T(8,128)(2,1)} %bitcast.120), kind=kOutput, calls=%fused_computation.183 | convolution fusion | flops 4294967296 | bytes 14680064 | tf_op jit(solution)/shard_map/dot_general | solution.py:33
  481.0 8.5 fusion.66
  502.2 77.7 %collective-permute-start.6 = (bf16[512,1024]{0,1:T(8,128)(2,1)}, bf16[512,1024]{0,1:T(8,128)(2,1)S(1)}, u32[]{:S(2)}, u32[]{:S(2)}) collective-permute-start(bf16[512,1024]{0,1:T(8,128)(2,1)} %get-tuple-element.140), channel_id=1, source_target_pairs={{0,1},{1,2},{2,3},{3,4},{4,5},{5,6},{6,7},{7,8},{8,9},{9,10},{10,1... | collective-permute-start | bytes 3145736 | tf_op jit(solution)/shard_map/ppermute | solution.py:264
  581.2 17.2 %multiply_convert_fusion.3 = bf16[1024,1024]{0,1:T(8,128)(2,1)} fusion(bf16[1024,1024]{0,1:T(8,128)(2,1)S(1)} %copy-done.1, f32[1024]{0:T(1024)S(1)} %add.267, f32[1024]{0:T(1024)S(1)} %fusion.56, bf16[4096,1024]{1,0:T(8,128)(2,1)} %bitcast.99, f32[1024,4096]{1,0:T(8,128)} %fusion.36, f32[4096]{0:T(1024)S(1)} %slice_bitcast_fusion), kind=kOutput, calls=%fused_computation.42 | convolution fusion | flops 8638169088 | bytes 29384704 | tf_op jit(solution)/shard_map/dot_general | solution.py:33
  618.5 82.6 %all-reduce.1 = f32[32,320]{1,0:T(8,128)S(1)} all-reduce(f32[32,320]{1,0:T(8,128)S(1)} %concatenate.84), channel_id=6, replica_groups=mesh['fsdp'=32] {'fsdp'}, use_global_device_ids=true, to_apply=%region_25.26.clone | all-reduce | flops 10240 | bytes 81920
  703.9 176.6 %reduce-scatter.5.cloned.1.call-done = bf16[288,1024]{1,0:T(8,128)(2,1)} async-done(((bf16[9216,1024]{1,0:T(8,128)(2,1)}), bf16[288,1024]{1,0:T(8,128)(2,1)}) %reduce-scatter.5.cloned.1.call-update) | async-done | bytes 589840 | tf_op jit(solution)/shard_map/reduce_scatter | solution.py:372
  (232 shorter events, 162.5 us)
Async XLA Ops:
  7.2 95.7 %all-gather.5.cloned.1.call-start = ((), (), s32[]{:S(2)}) async-start(), calls=%async_computation.4 | async-start | bytes 7028736 | tf_op jit(solution)/shard_map/all_gather | solution.py:281
  23.9 218.9 %all-gather.7.cloned.1.call-start = ((), (), s32[]{:S(2)}) async-start(), calls=%async_computation.5 | async-start | bytes 19464192 | tf_op jit(solution)/shard_map/all_gather | solution.py:293
  24.9 11.5 %copy-start.44 = (s32[32]{0:T(128)S(1)}, s32[32]{0:T(128)}, u32[]{:S(2)}) copy-start(s32[32]{0:T(128)} %param.28) | copy-start | bytes 388
  24.9 677.4 %reduce-scatter.3.cloned.1.call-start = ((), (), s32[]{:S(2)}) async-start(), calls=%async_computation.2 | async-start | bytes 4325376 | tf_op jit(solution)/shard_map/reduce_scatter | solution.py:372
  27.9 95.8 %copy-start = (bf16[1024,1024]{0,1:T(8,128)(2,1)}, bf16[1024,1024]{0,1:T(8,128)(2,1)S(1)}, u32[]{:S(2)}) copy-start(bf16[1024,1024]{0,1:T(8,128)(2,1)S(1)} %copy.90) | copy-start | bytes 6291460
  29.5 14.5 %collective-permute-start = (bf16[512,1024]{0,1:T(8,128)(2,1)}, bf16[512,1024]{0,1:T(8,128)(2,1)S(1)}, u32[]{:S(2)}, u32[]{:S(2)}) collective-permute-start(bf16[512,1024]{0,1:T(8,128)(2,1)} %get-tuple-element.150), channel_id=1, source_target_pairs={{0,1},{1,2},{2,3},{3,4},{4,5},{5,6},{6,7},{7,8},{8,9},{9,10},{10,1... | collective-permute-start | bytes 3145736 | tf_op jit(solution)/shard_map/ppermute | solution.py:258
  31.9 12.1 %collective-permute-start.1 = (bf16[512,1024]{0,1:T(8,128)(2,1)}, bf16[512,1024]{0,1:T(8,128)(2,1)}, u32[]{:S(2)}, u32[]{:S(2)}) collective-permute-start(bf16[512,1024]{0,1:T(8,128)(2,1)} %get-tuple-element.151), channel_id=1, source_target_pairs={{1,0},{2,1},{3,2},{4,3},{5,4},{6,5},{7,6},{8,7},{9,8},{10,9},{11,1... | collective-permute-start | bytes 3145736 | tf_op jit(solution)/shard_map/ppermute | solution.py:259
  44.0 79.7 %copy-start.6 = (bf16[512,1024]{0,1:T(8,128)(2,1)}, bf16[512,1024]{0,1:T(8,128)(2,1)S(1)}, u32[]{:S(2)}) copy-start(bf16[512,1024]{0,1:T(8,128)(2,1)S(1)} %collective-permute-done) | copy-start | bytes 3145732
  46.2 77.5 %copy-start.25 = (f32[2048]{0:T(1024)}, f32[2048]{0:T(1024)S(1)}, u32[]{:S(2)}) copy-start(f32[2048]{0:T(1024)S(1)} %broadcast_multiply_fusion) | copy-start | bytes 24580
  48.4 62.6 %copy-start.29 = (f32[2048]{0:T(1024)}, f32[2048]{0:T(1024)S(1)}, u32[]{:S(2)}) copy-start(f32[2048]{0:T(1024)S(1)} %fusion.16) | copy-start | bytes 24580
  48.4 75.2 %copy-start.27 = (f32[2048]{0:T(1024)}, f32[2048]{0:T(1024)S(1)}, u32[]{:S(2)}) copy-start(f32[2048]{0:T(1024)S(1)} %fusion.46) | copy-start | bytes 24580
  104.7 18.9 %copy-start.31 = (f32[1024]{0:T(1024)}, f32[1024]{0:T(1024)S(1)}, u32[]{:S(2)}) copy-start(f32[1024]{0:T(1024)S(1)} %mul.255) | copy-start | bytes 12292
  175.1 83.3 %collective-permute-start.2 = (bf16[512,1024]{1,0:T(8,128)(2,1)}, bf16[512,1024]{1,0:T(8,128)(2,1)}, u32[]{:S(2)}, u32[]{:S(2)}) collective-permute-start(bf16[512,1024]{1,0:T(8,128)(2,1)} %get-tuple-element.142), channel_id=1, source_target_pairs={{0,1},{1,2},{2,3},{3,4},{4,5},{5,6},{6,7},{7,8},{8,9},{9,10},{10,1... | collective-permute-start | bytes 3145736 | tf_op jit(solution)/shard_map/ppermute | solution.py:264
  227.4 31.0 %collective-permute-start.3 = (bf16[512,1024]{1,0:T(8,128)(2,1)S(1)}, bf16[512,1024]{1,0:T(8,128)(2,1)}, u32[]{:S(2)}, u32[]{:S(2)}) collective-permute-start(bf16[512,1024]{1,0:T(8,128)(2,1)S(1)} %get-tuple-element.143), channel_id=1, source_target_pairs={{1,0},{2,1},{3,2},{4,3},{5,4},{6,5},{7,6},{8,7},{9,8},{10,9},{11,1... | collective-permute-start | bytes 3145736 | tf_op jit(solution)/shard_map/ppermute | solution.py:263
  233.2 208.1 %copy-start.9 = (bf16[1024,1024]{0,1:T(8,128)(2,1)}, bf16[1024,1024]{0,1:T(8,128)(2,1)S(1)}, u32[]{:S(2)}) copy-start(bf16[1024,1024]{0,1:T(8,128)(2,1)S(1)} %copy.97) | copy-start | bytes 6291460
  346.8 5.3 collective-permute-start.4
  349.9 4.6 collective-permute-start.5
  413.9 466.7 %reduce-scatter.5.cloned.1.call-start = ((), (), s32[]{:S(2)}) async-start(), calls=%async_computation.3 | async-start | bytes 19464192 | tf_op jit(solution)/shard_map/reduce_scatter | solution.py:372
  470.0 10.9 %copy-start.19 = (bf16[32,32,1024]{2,1,0:T(8,128)(2,1)S(1)}, bf16[32,32,1024]{2,1,0:T(8,128)(2,1)}, u32[]{:S(2)}) copy-start(bf16[32,32,1024]{2,1,0:T(8,128)(2,1)} %get-tuple-element.138) | copy-start | bytes 6291460
  470.1 10.9 %copy-start.26 = (f32[2048]{0:T(1024)S(1)}, f32[2048]{0:T(1024)}, u32[]{:S(2)}) copy-start(f32[2048]{0:T(1024)} %copy-done.25) | copy-start | bytes 24580
  470.1 10.9 %copy-start.32 = (f32[1024]{0:T(1024)S(1)}, f32[1024]{0:T(1024)}, u32[]{:S(2)}) copy-start(f32[1024]{0:T(1024)} %copy-done.31) | copy-start | bytes 12292
  470.1 10.9 %copy-start.46 = (bf16[2048,1024]{1,0:T(8,128)(2,1)S(1)}, bf16[2048,1024]{1,0:T(8,128)(2,1)}, u32[]{:S(2)}) copy-start(bf16[2048,1024]{1,0:T(8,128)(2,1)} %get-tuple-element.50) | copy-start | bytes 12582916
  502.2 108.6 %collective-permute-start.6 = (bf16[512,1024]{0,1:T(8,128)(2,1)}, bf16[512,1024]{0,1:T(8,128)(2,1)S(1)}, u32[]{:S(2)}, u32[]{:S(2)}) collective-permute-start(bf16[512,1024]{0,1:T(8,128)(2,1)} %get-tuple-element.140), channel_id=1, source_target_pairs={{0,1},{1,2},{2,3},{3,4},{4,5},{5,6},{6,7},{7,8},{8,9},{9,10},{10,1... | collective-permute-start | bytes 3145736 | tf_op jit(solution)/shard_map/ppermute | solution.py:264
  579.9 30.8 %collective-permute-start.7 = (bf16[512,1024]{0,1:T(8,128)(2,1)}, bf16[512,1024]{0,1:T(8,128)(2,1)}, u32[]{:S(2)}, u32[]{:S(2)}) collective-permute-start(bf16[512,1024]{0,1:T(8,128)(2,1)} %get-tuple-element.141), channel_id=1, source_target_pairs={{1,0},{2,1},{3,2},{4,3},{5,4},{6,5},{7,6},{8,7},{9,8},{10,9},{11,1... | collective-permute-start | bytes 3145736 | tf_op jit(solution)/shard_map/ppermute | solution.py:263
  (36 other events, 220.6 us)
Sparse Core Ops, SparseCore 0:
  24.0 78.7 all-gather.4
  106.3 126.3 all-gather.6
  414.0 255.0 reduce-scatter.2
  675.3 205.1 reduce-scatter.4

commit v2 on v1

--- a/solution.py
+++ b/solution.py
@@ -21,6 +21,11 @@
 SCALE = 1.0 / math.sqrt(DH)
 TILE = 256
 FREE = 99.0
+STRIP = 512
+ROWS = 1024
+LAG = 1
+CURVE = math.sqrt(2.0 / math.pi)
+MESH = pl.DeviceIdType.MESH
 
 NT = (((1,), (1,)), ((), ()))
 NN = (((1,), (0,)), ((), ()))
@@ -224,6 +229,258 @@
     )(low, shared, values, code, spread, combined, above, lse, lone)
 
 
+def mixing_kernel(second_ref, above_ref, expand_ref, reduce_ref, bias_e_ref, bias_r_ref,
+                  out_ref, back_ref, grad_r_ref, grad_e_ref, grad_b_ref, act_s, pre_s):
+    step = pl.program_id(0)
+    rows, width = second_ref.shape
+    w_e = expand_ref[...].reshape(width, STRIP)
+    w_r = reduce_ref[...].reshape(STRIP, width)
+    bias = bias_e_ref[...]
+
+    @pl.when(step == 0)
+    def _():
+        out_ref[...] = jnp.broadcast_to(bias_r_ref[...], out_ref.shape)
+        back_ref[...] = jnp.zeros(back_ref.shape, F32)
+
+    def strip(i, total):
+        at = pl.ds(pl.multiple_of(i * ROWS, ROWS), ROWS)
+        pre = dot(second_ref[at, :], w_e) + bias
+        square = pre * pre
+        curve = jnp.tanh(CURVE * pre * (1.0 + 0.044715 * square))
+        hinge = 0.5 * (1.0 + curve)
+        act = (pre * hinge).astype(BF16)
+        slope = hinge + 0.5 * pre * (1.0 - curve * curve) * (CURVE * (1.0 + 3 * 0.044715 * square))
+        d_pre_wide = dot(above_ref[at, :], w_r, NT) * slope
+        d_pre = d_pre_wide.astype(BF16)
+        act_s[at, :] = act
+        pre_s[at, :] = d_pre
+        out_ref[at, :] += dot(act, w_r)
+        back_ref[at, :] += dot(d_pre, w_e, NT)
+        return total + jnp.sum(d_pre.astype(F32), axis=0, keepdims=True)
+
+    grad_b_ref[...] = lax.fori_loop(0, rows // ROWS, strip, jnp.zeros((1, STRIP), F32))
+    grad_r_ref[...] = dot(act_s[...], above_ref[...], TN).astype(BF16).reshape(grad_r_ref.shape)
+    grad_e_ref[...] = dot(second_ref[...], pre_s[...], TN).astype(BF16).reshape(grad_e_ref.shape)
+
+
+def mixing(second, above, gathered, bias_e, bias_r, part):
+    rows, width = second.shape
+    devices = gathered.shape[0]
+    hidden = bias_e.shape[1]
+    many = hidden // devices
+    per = width // STRIP
+    fixed = pl.BlockSpec((rows, width), lambda i: (0, 0), pipeline_mode=pl.Buffered(1))
+    return pl.pallas_call(
+        mixing_kernel,
+        grid=(hidden // STRIP,),
+        in_specs=[
+            fixed, fixed,
+            pl.BlockSpec((devices, part, STRIP), lambda i: (0, many // part + 1 + i // per, i % per)),
+            pl.BlockSpec((STRIP // many, many, width), lambda i: (i, 0, 0)),
+            pl.BlockSpec((1, STRIP), lambda i: (0, i)),
+            pl.BlockSpec((1, width), lambda i: (0, 0)),
+        ],
+        out_specs=[
+            pl.BlockSpec((rows, width), lambda i: (0, 0)),
+            pl.BlockSpec((rows, width), lambda i: (0, 0)),
+            pl.BlockSpec((STRIP // many, many, width), lambda i: (i, 0, 0)),
+            pl.BlockSpec((devices, part, STRIP), lambda i: (0, i // per, i % per)),
+            pl.BlockSpec((1, STRIP), lambda i: (0, i)),
+        ],
+        out_shape=[
+            jax.ShapeDtypeStruct((rows, width), F32),
+            jax.ShapeDtypeStruct((rows, width), F32),
+            jax.ShapeDtypeStruct((devices, many, width), BF16),
+            jax.ShapeDtypeStruct((devices, hidden // width * part, width), BF16),
+            jax.ShapeDtypeStruct((1, hidden), F32),
+        ],
+        scratch_shapes=[pltpu.VMEM((rows, STRIP), BF16)] * 2,
+        compiler_params=pltpu.CompilerParams(vmem_limit_bytes=56 << 20),
+        name="mixing",
+    )(second, above, gathered, gathered, bias_e, bias_r)
+
+
+def digits(devices):
+    side = 2
+    while 8 * side * side < devices:
+        side += 1
+    assert 8 * side * side == devices, devices
+    return 4, side, 2
+
+
+def neighbours(devices):
+    outer, side, core = digits(devices)
+    me = lax.axis_index("fsdp")
+    c = lax.rem(me, core)
+    q = lax.rem(lax.div(me, core), side)
+    p = lax.rem(lax.div(me, core * side), side)
+    o = lax.div(me, core * side * side)
+
+    def at(o_, p_, q_, c_):
+        return ((o_ * side + p_) * side + q_) * core + c_
+
+    core_peer = at(o, p, q, 1 - c)
+    q_peers = [lax.rem(q + d, side) for d in range(1, side)]
+    p_peers = [lax.rem(p + d, side) for d in range(1, side)]
+    o_peers = [lax.rem(o + d, outer) for d in range(1, outer)]
+    return (o, p, q, c), core_peer, [(k, at(o, p, k, c)) for k in q_peers], [(k, at(o, k, q, c)) for k in p_peers], [(k, at(k, p, q, c)) for k in o_peers]
+
+
+def greet(peers):
+    barrier = pltpu.get_barrier_semaphore()
+    for peer in peers:
+        pl.semaphore_signal(barrier, inc=1, device_id=(peer,), device_id_type=MESH)
+    pl.semaphore_wait(barrier, len(peers))
+
+
+def reduce_kernel(devices, plan, arrays, *refs):
+    outer, side, core = digits(devices)
+    sources, outs = refs[:arrays], refs[arrays : 2 * arrays]
+    rest = refs[2 * arrays :]
+    count = len(plan)
+    own = rest[:count]
+    landed_c = rest[count : 2 * count]
+    landed_a = rest[2 * count : 4 * count]
+    landed_b = rest[4 * count : 5 * count]
+    landed_o = rest[5 * count : 6 * count]
+    load_sem, sem_c, sem_a, sem_b, sem_o = rest[6 * count :]
+    (o, p, q, c), core_peer, q_peers, p_peers, o_peers = neighbours(devices)
+    greet([core_peer] + [d for _, d in q_peers] + [d for _, d in p_peers] + [d for _, d in o_peers])
+    width = own[0].shape[-1]
+    half = width // 2
+    columns = (pl.ds(0, half), pl.ds(half, half))
+
+    def remote(src, dst, sems, slot, device):
+        return pltpu.make_async_remote_copy(
+            src_ref=src, dst_ref=dst, send_sem=sems.at[(0,) + slot], recv_sem=sems.at[(1,) + slot],
+            device_id=(device,), device_id_type=MESH,
+        )
+
+    loads, to_core, first, second, third = {}, {}, {}, {}, {}
+    for s, (k, row, rows) in enumerate(plan):
+        at = pl.ds(row, rows)
+        to_core[s] = remote(sources[k].at[:, :, :, 1 - c, at, :], landed_c[s], sem_c, (s,), core_peer)
+        to_core[s].start()
+        loads[s] = pltpu.make_async_copy(sources[k].at[:, :, :, c, at, :], own[s], load_sem.at[s])
+        loads[s].start()
+
+    def stage_core(s):
+        loads[s].wait()
+        to_core[s].wait_recv()
+        mine, other = own[s], landed_c[s]
+
+        def add(i, carry):
+            a, b, d = i // (side * side), (i // side) % side, i % side
+            mine[a, b, d] = mine[a, b, d] + other[a, b, d]
+            return carry
+
+        lax.fori_loop(0, outer * side * side, add, 0)
+        for h in range(2):
+            for d in range(side - 1):
+                if h == 0:
+                    k, device = q_peers[d]
+                    src = mine.at[:, :, k, :, columns[h]]
+                else:
+                    k, device = p_peers[d]
+                    src = mine.at[:, k, :, :, columns[h]]
+                first[s, h, d] = remote(src, landed_a[2 * s + h].at[d], sem_a, (s, h, d), device)
+                first[s, h, d].start()
+
+    def stage_first(s):
+        mine = own[s]
+        for h in range(2):
+            box = landed_a[2 * s + h]
+            for d in range(side - 1):
+                first[s, h, d].wait_recv()
+
+            def add(i, carry):
+                a, b = i // side, i % side
+                total = mine[a, b, q, :, columns[h]] if h == 0 else mine[a, p, b, :, columns[h]]
+                for d in range(side - 1):
+                    total = total + box[d, a, b]
+                box[0, a, b] = total
+                return carry
+
+            lax.fori_loop(0, outer * side, add, 0)
+            for d in range(side - 1):
+                k, device = (p_peers if h == 0 else q_peers)[d]
+                second[s, h, d] = remote(
+                    box.at[0, :, k], landed_b[s].at[d, :, :, columns[h]], sem_b, (s, h, d), device
+                )
+                second[s, h, d].start()
+
+    def stage_second(s):
+        box = landed_b[s]
+        for h in range(2):
+            part = landed_a[2 * s + h]
+            k = p if h == 0 else q
+            for d in range(side - 1):
+                second[s, h, d].wait_recv()
+
+            def add(a, carry):
+                total = part[0, a, k]
+                for d in range(side - 1):
+                    total = total + box[d, a, :, columns[h]]
+                box[0, a, :, columns[h]] = total
+                return carry
+
+            lax.fori_loop(0, outer, add, 0)
+        for d in range(outer - 1):
+            k, device = o_peers[d]
+            third[s, d] = remote(box.at[0, k], landed_o[s].at[d], sem_o, (s, d), device)
+            third[s, d].start()
+
+    def stage_third(s):
+        k, row, rows = plan[s]
+        total = landed_b[s][0, o].astype(F32)
+        for d in range(outer - 1):
+            third[s, d].wait_recv()
+            total = total + landed_o[s][d].astype(F32)
+        outs[k][pl.ds(row, rows), :] = total
+
+    for t in range(count + 3 * LAG):
+        if t < count:
+            stage_core(t)
+        if 0 <= t - LAG < count:
+            stage_first(t - LAG)
+        if 0 <= t - 2 * LAG < count:
+            stage_second(t - 2 * LAG)
+        if 0 <= t - 3 * LAG < count:
+            stage_third(t - 3 * LAG)
+    for copies in (to_core, first, second, third):
+        for copy in copies.values():
+            copy.wait_send()
+
+
+def reduce_scatter(devices, arrays, cuts):
+    outer, side, core = digits(devices)
+    plan = []
+    for k, array in enumerate(arrays):
+        rows = array.shape[1] // cuts[k]
+        plan += [(k, i * rows, rows) for i in range(cuts[k])]
+    width = arrays[0].shape[2]
+    half = width // 2
+    count = len(plan)
+    vmem = pltpu.VMEM
+    scratch = [vmem((outer, side, side, r, width), BF16) for _, _, r in plan]
+    scratch += [vmem((outer, side, side, r, width), BF16) for _, _, r in plan]
+    for _, _, r in plan:
+        scratch += [vmem((side - 1, outer, side, r, half), BF16)] * 2
+    scratch += [vmem((side - 1, outer, r, width), BF16) for _, _, r in plan]
+    scratch += [vmem((outer - 1, r, width), BF16) for _, _, r in plan]
+    dma = pltpu.SemaphoreType.DMA
+    scratch += [dma((count,)), dma((2, count)), dma((2, count, 2, side - 1)), dma((2, count, 2, side - 1)), dma((2, count, outer - 1))]
+    return pl.pallas_call(
+        functools.partial(reduce_kernel, devices, plan, len(arrays)),
+        out_shape=tuple(jax.ShapeDtypeStruct(array.shape[1:], F32) for array in arrays),
+        in_specs=[pl.BlockSpec(memory_space=pl.ANY)] * len(arrays),
+        out_specs=tuple(pl.BlockSpec(memory_space=pltpu.VMEM) for _ in arrays),
+        scratch_shapes=scratch,
+        compiler_params=pltpu.CompilerParams(collective_id=1, has_side_effects=True, vmem_limit_bytes=56 << 20),
+        name="reduce_scatter",
+    )(*[array.reshape(outer, side, side, core, *array.shape[1:]) for array in arrays])
+
+
 def block_of_rank(buckets, length):
     slots = buckets.shape[-1]
     place = lax.broadcasted_iota(jnp.int32, (1, 1, slots), 2)
@@ -292,15 +549,11 @@
     bias_e = full_vectors[:, 6 * part :].reshape(hidden)
     second_gather = lax.all_gather(
         jnp.concatenate(
-            [w_output] + [w_expand[:, k * width : (k + 1) * width] for k in range(sides)] + [w_reduce], axis=0
+            [w_reduce, w_output] + [w_expand[:, k * width : (k + 1) * width] for k in range(sides)], axis=0
         ),
         "fsdp", axis=0, tiled=False,
     )
-    full_output = second_gather[:, :part].reshape(width, width)
-    full_expand = jnp.concatenate(
-        [second_gather[:, (k + 1) * part : (k + 2) * part].reshape(width, width) for k in range(sides)], axis=1
-    )
-    full_reduce = second_gather[:, (sides + 1) * part :].reshape(hidden, width)
+    full_output = second_gather[:, sides * part : (sides + 1) * part].reshape(width, width)
 
     inside = (middle >= base) & (middle < base + slots)
     chosen = jnp.sum(inside.astype(jnp.int32))
@@ -339,19 +592,12 @@
     attended = dot(combined, full_output) + bias_o
     out_one = slot_one + live * attended
     second = layer_norm(out_one, gain_m, shift_m).astype(BF16)
-    pre_act = dot(second, full_expand) + bias_e
-    expand = jax.nn.gelu(pre_act, approximate=True).astype(BF16)
-    out_two = slot_two + live * (dot(expand, full_reduce) + bias_r)
-
     d_reduce = above_two.astype(BF16)
-    grad_reduce = dot(expand, d_reduce, TN)
     grad_bias_reduce = jnp.sum(d_reduce, axis=0, dtype=F32)
-    d_expand = dot(d_reduce, full_reduce, NT)
-    gelu_out, gelu_pull = jax.vjp(lambda inner: jax.nn.gelu(inner, approximate=True), pre_act)
-    d_pre = gelu_pull(d_expand)[0].astype(BF16)
-    grad_expand = dot(second, d_pre, TN)
-    grad_bias_expand = jnp.sum(d_pre, axis=0, dtype=F32)
-    d_second = dot(d_pre, full_expand, NT)
+    mixed, d_second, grad_reduce, grad_expand, grad_bias_expand = mixing(
+        second, d_reduce, second_gather, bias_e[None], bias_r[None], part
+    )
+    out_two = slot_two + live * mixed
     d_one_mix, grad_gain_m, grad_shift_m = norm_back(out_one, gain_m, shift_m, d_second)
     total_one = above_one + d_one_mix
     d_attend = (live * total_one).astype(BF16)
@@ -368,49 +614,41 @@
     own, other = narrow(d_two_window.astype(BF16))
     back_two = above_two + own.astype(F32) + other.astype(F32)
 
-    def scatter(whole):
-        return lax.psum_scatter(whole, "fsdp", scatter_dimension=0, tiled=True)
-
     def split(whole):
         return whole.astype(BF16).reshape(devices, -1, width)
 
-    early = jnp.concatenate(
-        [split(grad_output)] + [split(grad_expand[:, k * width : (k + 1) * width]) for k in range(sides)] + [split(grad_reduce)],
+    small = jnp.concatenate(
+        [
+            member.reshape(devices, -1)
+            for member in (
+                grad_gain_a, grad_shift_a, grad_gain_m, grad_shift_m, grad_bias_output, grad_bias_reduce, grad_bias_expand
+            )
+        ],
         axis=1,
     )
-    late = jnp.concatenate([split(grad_shared), split(grad_value)], axis=1)
-    early = scatter(early.reshape(-1, width)).astype(F32)
-    late = scatter(late.reshape(-1, width)).astype(F32)
-    small = [
-        scatter(member.reshape(devices, -1)).reshape(-1)
-        for member in (
-            jnp.concatenate(
-                [
-                    member.reshape(devices, -1)
-                    for member in (
-                        grad_gain_a, grad_shift_a, grad_gain_m, grad_shift_m, grad_bias_output, grad_bias_reduce, grad_bias_expand
-                    )
-                ],
-                axis=1,
-            ),
-        )
-    ][0]
+    small = jnp.zeros((devices, 8, width), BF16).at[:, 0, : small.shape[1]].set(small.astype(BF16))
+    grad_reduce, grad_expand, grad_output, grad_shared, grad_value, small = reduce_scatter(
+        devices,
+        (grad_reduce, grad_expand, split(grad_output), split(grad_shared), split(grad_value), small),
+        (2, 2, 1, 1, 1, 1),
+    )
+    small = small[0]
     return (
         (live * out_one).astype(BF16),
         (live * out_two).astype(BF16),
         (live * total_one).astype(BF16),
         (live * back_two).astype(BF16),
-        late[:part],
-        late[part:],
-        early[:part],
-        jnp.concatenate([early[(k + 1) * part : (k + 2) * part] for k in range(sides)], axis=1),
-        early[(sides + 1) * part :],
+        grad_shared,
+        grad_value,
+        grad_output,
+        jnp.concatenate([grad_expand[k * part : (k + 1) * part] for k in range(sides)], axis=1),
+        grad_reduce,
         small[:part],
         small[part : 2 * part],
         small[2 * part : 3 * part],
         small[3 * part : 4 * part],
         small[4 * part : 5 * part],
-        small[6 * part :],
+        small[6 * part : 6 * part + hidden // devices],
         small[5 * part : 6 * part],
     )
 

time: 882 us -> 702 us (0.80)
  the two profiles are of different devices: /device:TPU:0 before, /device:TPU:13 now
where the time goes in v2:
time: 702 us; the launch traced here: 697 us
  Pallas kernels  344 us (49%)
  waiting for transfers between devices  124 us (18%)
  matrix products  65.4 us (9%)
  other arithmetic  53.1 us (8%)
  local copies, waits for them, and re-layouts  44.5 us (6%)
  starting transfers between devices  41.6 us (6%)
  between operations  24.3 us (3%)
    pallas_call x1, Pallas kernels, reduce_scatter(): pl.pallas_call(functools.partial(reduce_kernel, devices, plan, len(arrays...  175 us
    dot_general x10, matrix products, dot(): return lax.dot_general(a, b, dims, preferred_element_type=F32)  65.4 us
    pallas_call x1, Pallas kernels, mixing(): pl.pallas_call(mixing_kernel, grid=(hidden // STRIP,), in_specs=[fixed, f...  64.2 us
    pallas_call x1, Pallas kernels, attend_back(): pl.pallas_call(back_kernel, grid_spec=pltpu.PrefetchScalarGridSpec(num_sc...  58.1 us
    pallas_call x1, Pallas kernels, attend(): pl.pallas_call(attend_kernel, grid_spec=pltpu.PrefetchScalarGridSpec(num_...  47.8 us
    all_gather x1, waiting for transfers between devices, body(): lax.all_gather(jnp.concatenate([w_shared, w_value, block.astype(BF16), pa...  38.3 us
    ppermute x2, waiting for transfers between devices, narrow(): tail = lax.ppermute(wide[:half], 'fsdp', down)  32.6 us
    ppermute x2, starting transfers between devices, narrow(): tail = lax.ppermute(wide[:half], 'fsdp', down)  21.8 us
  transfers between devices with their start and end apart: 10, of which 8 were waited for; matrix products, arithmetic and copies ran while one was open for 10% of the time, Pallas kernels for 7%

profile of v2, /device:TPU:13, one launch (start us, length us, event | category | flops | bytes accessed | tf_op | source)
XLA Modules:
  0.0 697.1 jit_solution(9363085730583343205)
XLA Ops:
  42.2 8.4 %collective-permute-done = bf16[512,1024]{1,0:T(8,128)(2,1)S(1)} collective-permute-done((bf16[512,1024]{1,0:T(8,128)(2,1)}, bf16[512,1024]{1,0:T(8,128)(2,1)S(1)}, u32[]{:S(2)}, u32[]{:S(2)}) %collective-permute-start) | collective-permute-done | bytes 1048608 | tf_op jit(solution)/shard_map/ppermute | solution.py:515
  50.7 5.5 collective-permute-done.1
  61.6 38.3 %all-gather.5.cloned.1.call-done = bf16[3328,1024]{1,0:T(8,128)(2,1)} async-done(((bf16[104,1024]{1,0:T(8,128)(2,1)}), bf16[3328,1024]{1,0:T(8,128)(2,1)}) %all-gather.5.cloned.1.call-update) | async-done | bytes 6815760 | tf_op jit(solution)/shard_map/all_gather | solution.py:538
  103.0 6.2 fusion.53
  125.2 6.1 convolution_convert_fusion.v_ref
  131.2 6.1 convolution_convert_fusion.1.q_ref
  137.3 47.8 %attend.1 = (bf16[2048,1024]{1,0:T(8,128)(2,1)}, f32[8,1,2048]{2,1,0:T(1,128)}, f32[8,1,2048]{2,1,0:T(1,128)}) custom-call(s32[8]{0:T(128)} %and_select_fusion.low_ref, bf16[2048,1024]{1,0:T(8,128)(2,1)} %convolution_convert_fusion.1.q_ref, bf16[2048,1024]{1,0:T(8,128)(2,1)} %convolution_convert_fusion.v_ref, bf16[2048,32]{1,0:T(8,128)(2,1)} %slice.314.code_ref, ...), custom_call_target="tpu_custom_call" | custom-call | flops 8053063680 | bytes 12582912 | tf_op jit(solution)/shard_map/attend/pallas_call | solution.py:193
  190.7 19.9 %collective-permute-start.3 = (bf16[512,1024]{1,0:T(8,128)(2,1)}, bf16[512,1024]{1,0:T(8,128)(2,1)}, u32[]{:S(2)}, u32[]{:S(2)}) collective-permute-start(bf16[512,1024]{1,0:T(8,128)(2,1)} %get-tuple-element.110), channel_id=1, source_target_pairs={{1,0},{2,1},{3,2},{4,3},{5,4},{6,5},{7,6},{8,7},{9,8},{10,9},{11,1... | collective-permute-start | bytes 3145736 | tf_op jit(solution)/shard_map/ppermute | solution.py:520
  215.9 11.3 %all-gather.7.cloned.1.call-done = bf16[9216,1024]{1,0:T(8,128)(2,1)} async-done(((bf16[288,1024]{1,0:T(8,128)(2,1)}), bf16[9216,1024]{1,0:T(8,128)(2,1)}) %all-gather.7.cloned.1.call-update) | async-done | bytes 18874384 | tf_op jit(solution)/shard_map/all_gather | solution.py:550
  229.2 29.2 %collective-permute-done.3 = bf16[512,1024]{1,0:T(8,128)(2,1)} collective-permute-done((bf16[512,1024]{1,0:T(8,128)(2,1)}, bf16[512,1024]{1,0:T(8,128)(2,1)}, u32[]{:S(2)}, u32[]{:S(2)}) %collective-permute-start.3) | collective-permute-done | bytes 1048608 | tf_op jit(solution)/shard_map/ppermute | solution.py:520
  258.4 4.8 fusion.63
  265.8 64.2 %mixing.1 = (f32[1024,1024]{1,0:T(8,128)}, f32[1024,1024]{1,0:T(8,128)}, bf16[32,128,1024]{2,1,0:T(8,128)(2,1)}, bf16[32,128,1024]{2,1,0:T(8,128)(2,1)}, f32[1,4096]{1,0:T(1,128)}) custom-call(bf16[1024,1024]{1,0:T(8,128)(2,1)} %add_convert_fusion.1.second_ref, bf16[1024,1024]{1,0:T(8,128)(2,1)} %get-tuple-element.93.above_ref, ...), custom_call_target="tpu_custom_call" | custom-call | tf_op jit(solution)/shard_map/mixing/pallas_call | solution.py:273
  350.4 6.8 convolution_convert_fusion.4
  357.2 10.8 %collective-permute-done.4 = bf16[512,1024]{1,0:T(8,128)(2,1)} collective-permute-done((bf16[512,1024]{1,0:T(8,128)(2,1)}, bf16[512,1024]{1,0:T(8,128)(2,1)}, u32[]{:S(2)}, u32[]{:S(2)}) %collective-permute-start.4) | collective-permute-done | bytes 1048608 | tf_op jit(solution)/shard_map/ppermute | solution.py:515
  371.5 58.1 %attend_back.1 = (bf16[2048,1024]{1,0:T(8,128)(2,1)}, bf16[2048,1024]{1,0:T(8,128)(2,1)}) custom-call(s32[8]{0:T(128)} %and_select_fusion.low_ref, bf16[2048,1024]{1,0:T(8,128)(2,1)} %convolution_convert_fusion.1.q_ref, bf16[2048,1024]{1,0:T(8,128)(2,1)} %convolution_convert_fusion.v_ref, bf16[2048,32]{1,0:T(8,128)(2,1)} %slice.314.code_ref, ...), custom_call_target="tpu_custom_call" | custom-call | flops 16106127360 | bytes 25165824 | tf_op jit(solution)/shard_map/attend_back/pallas_call | solution.py:215
  429.6 10.8 %fusion.64 = f32[2048,1024]{1,0:T(8,128)} fusion(bf16[2048,1024]{1,0:T(8,128)(2,1)} %get-tuple-element.76, bf16[1024,1024]{1,0:T(8,128)(2,1)} %bitcast.96), kind=kOutput, calls=%fused_computation.152 | convolution fusion | flops 4294967296 | bytes 14680064 | tf_op jit(solution)/shard_map/dot_general | solution.py:38
  440.4 5.8 convolution_convert_fusion.2
  446.2 5.7 convolution_convert_fusion.3
  451.9 12.9 %fusion.8 = (bf16[1024]{0:T(1024)(128)(2,1)S(1)}, f32[2048]{0:T(1024)S(1)}, bf16[1024]{0:T(1024)(128)(2,1)S(1)}, f32[2048,1024]{1,0:T(8,128)}) fusion(f32[2048]{0:T(1024)S(1)} %fusion.31, f32[2048]{0:T(1024)S(1)} %broadcast_multiply_fusion, bf16[512,1024]{1,0:T(8,128)(2,1)} %collective-permute-done.1, bf16[1024,1024]{1,0:T(8,128)(2,1)S(1)} %copy-done, ...), kind=kOutput, calls=%fused_computation.12 | convolution fusion | flops 4326420480 | bytes 27295744 | tf_op jit(solution)/shard_map/dot_general | solution.py:38
  466.2 174.5 %reduce_scatter.1 = (f32[128,1024]{1,0:T(8,128)}, f32[128,1024]{1,0:T(8,128)}, f32[32,1024]{1,0:T(8,128)}, f32[32,1024]{1,0:T(8,128)}, f32[32,1024]{1,0:T(8,128)}, /*index=5*/f32[8,1024]{1,0:T(8,128)}) custom-call(bf16[4,2,2,2,128,1024]{5,4,3,2,1,0:T(8,128)(2,1)} %bitcast.84, bf16[4,2,2,2,128,1024]{5,4,3,2,1,0:T(8,128)(2,1)} %bitcast.85, ...), custom_call_target="tpu_custom_call" | custom-call | tf_op jit(solution)/shard_map/reduce_scatter/pallas_call | solution.py:473
  640.7 8.3 %fusion.51 = (f32[2048]{0:T(1024)S(1)}, f32[2048,1024]{1,0:T(8,128)S(1)}) fusion(f32[2048]{0:T(1024)S(1)} %multiply_multiply_fusion, f32[2048]{0:T(1024)S(1)} %broadcast_multiply_fusion, bf16[512,1024]{1,0:T(8,128)(2,1)} %collective-permute-done.1, bf16[1024,1024]{1,0:T(8,128)(2,1)S(1)} %copy-done, bf16[512,1024]{1,0:T(8,128)(2,1)S(1)} %collective-permute-done, ...), kind=kLoop, calls=%fused_computation.139 | loop fusion | flops 27260928 | bytes 21008384 | tf_op jit(solution)/shard_map/transpose(jvp())/reduce_sum | solution.py:42
  649.7 7.2 %collective-permute-start.6 = (bf16[512,1024]{1,0:T(8,128)(2,1)S(1)}, bf16[512,1024]{1,0:T(8,128)(2,1)S(1)}, u32[]{:S(2)}, u32[]{:S(2)}) collective-permute-start(bf16[512,1024]{1,0:T(8,128)(2,1)S(1)} %get-tuple-element.106), channel_id=1, source_target_pairs={{0,1},{1,2},{2,3},{3,4},{4,5},{5,6},{6,7},{7,8},{8,9},{9,10},{10,1... | collective-permute-start | bytes 3145736 | tf_op jit(solution)/shard_map/ppermute | solution.py:521
  662.5 16.7 %collective-permute-done.6 = bf16[512,1024]{1,0:T(8,128)(2,1)S(1)} collective-permute-done((bf16[512,1024]{1,0:T(8,128)(2,1)S(1)}, bf16[512,1024]{1,0:T(8,128)(2,1)S(1)}, u32[]{:S(2)}, u32[]{:S(2)}) %collective-permute-start.6) | collective-permute-done | bytes 1048608 | tf_op jit(solution)/shard_map/ppermute | solution.py:521
  682.5 4.7 multiply_convert_fusion
  (205 shorter events, 102.7 us)
Async XLA Ops:
  7.2 92.7 %all-gather.5.cloned.1.call-start = ((), (), s32[]{:S(2)}) async-start(), calls=%async_computation | async-start | bytes 7028736 | tf_op jit(solution)/shard_map/all_gather | solution.py:538
  23.4 203.8 %all-gather.7.cloned.1.call-start = ((), (), s32[]{:S(2)}) async-start(), calls=%async_computation.1 | async-start | bytes 19464192 | tf_op jit(solution)/shard_map/all_gather | solution.py:550
  25.9 24.8 %collective-permute-start = (bf16[512,1024]{1,0:T(8,128)(2,1)}, bf16[512,1024]{1,0:T(8,128)(2,1)S(1)}, u32[]{:S(2)}, u32[]{:S(2)}) collective-permute-start(bf16[512,1024]{1,0:T(8,128)(2,1)} %get-tuple-element.115), channel_id=1, source_target_pairs={{0,1},{1,2},{2,3},{3,4},{4,5},{5,6},{6,7},{7,8},{8,9},{9,10},{10,1... | collective-permute-start | bytes 3145736 | tf_op jit(solution)/shard_map/ppermute | solution.py:515
  29.6 26.6 %collective-permute-start.1 = (bf16[512,1024]{1,0:T(8,128)(2,1)}, bf16[512,1024]{1,0:T(8,128)(2,1)}, u32[]{:S(2)}, u32[]{:S(2)}) collective-permute-start(bf16[512,1024]{1,0:T(8,128)(2,1)} %get-tuple-element.116), channel_id=1, source_target_pairs={{1,0},{2,1},{3,2},{4,3},{5,4},{6,5},{7,6},{8,7},{9,8},{10,9},{11,1... | collective-permute-start | bytes 3145736 | tf_op jit(solution)/shard_map/ppermute | solution.py:516
  185.0 27.4 %copy-start.2 = (bf16[1024,1024]{1,0:T(8,128)(2,1)S(1)}, bf16[1024,1024]{1,0:T(8,128)(2,1)}, u32[]{:S(2)}) copy-start(bf16[1024,1024]{1,0:T(8,128)(2,1)} %param.28) | copy-start | bytes 6291460
  185.0 29.9 %copy-start.29 = (f32[32,32]{1,0:T(8,128)S(1)}, f32[32,32]{1,0:T(8,128)}, u32[]{:S(2)}) copy-start(f32[32,32]{1,0:T(8,128)} %get-tuple-element.124) | copy-start | bytes 12292
  185.1 30.0 %copy-start.28 = (f32[32,32]{1,0:T(8,128)S(1)}, f32[32,32]{1,0:T(8,128)}, u32[]{:S(2)}) copy-start(f32[32,32]{1,0:T(8,128)} %get-tuple-element.122) | copy-start | bytes 12292
  185.1 30.0 %copy-start.27 = (f32[32,32]{1,0:T(8,128)S(1)}, f32[32,32]{1,0:T(8,128)}, u32[]{:S(2)}) copy-start(f32[32,32]{1,0:T(8,128)} %get-tuple-element.123) | copy-start | bytes 12292
  188.2 40.9 %collective-permute-start.2 = (bf16[512,1024]{1,0:T(8,128)(2,1)}, bf16[512,1024]{1,0:T(8,128)(2,1)}, u32[]{:S(2)}, u32[]{:S(2)}) collective-permute-start(bf16[512,1024]{1,0:T(8,128)(2,1)} %get-tuple-element.109), channel_id=1, source_target_pairs={{0,1},{1,2},{2,3},{3,4},{4,5},{5,6},{6,7},{7,8},{8,9},{9,10},{10,1... | collective-permute-start | bytes 3145736 | tf_op jit(solution)/shard_map/ppermute | solution.py:521
  190.7 67.7 %collective-permute-start.3 = (bf16[512,1024]{1,0:T(8,128)(2,1)}, bf16[512,1024]{1,0:T(8,128)(2,1)}, u32[]{:S(2)}, u32[]{:S(2)}) collective-permute-start(bf16[512,1024]{1,0:T(8,128)(2,1)} %get-tuple-element.110), channel_id=1, source_target_pairs={{1,0},{2,1},{3,2},{4,3},{5,4},{6,5},{7,6},{8,7},{9,8},{10,9},{11,1... | collective-permute-start | bytes 3145736 | tf_op jit(solution)/shard_map/ppermute | solution.py:520
  227.2 31.2 %copy-start.17 = (bf16[2048,1024]{1,0:T(8,128)(2,1)S(1)}, bf16[2048,1024]{1,0:T(8,128)(2,1)}, u32[]{:S(2)}) copy-start(bf16[2048,1024]{1,0:T(8,128)(2,1)} %get-tuple-element.70.comb_ref) | copy-start | bytes 12582916
  229.1 34.0 %copy-start.9 = (bf16[32,32,1024]{2,1,0:T(8,128)(2,1)}, bf16[32,32,1024]{2,1,0:T(8,128)(2,1)S(1)}, u32[]{:S(2)}) copy-start(bf16[32,32,1024]{2,1,0:T(8,128)(2,1)S(1)} %slice.281) | copy-start | bytes 6291460
  345.5 22.5 %collective-permute-start.4 = (bf16[512,1024]{1,0:T(8,128)(2,1)}, bf16[512,1024]{1,0:T(8,128)(2,1)}, u32[]{:S(2)}, u32[]{:S(2)}) collective-permute-start(bf16[512,1024]{1,0:T(8,128)(2,1)} %get-tuple-element.111), channel_id=1, source_target_pairs={{0,1},{1,2},{2,3},{3,4},{4,5},{5,6},{6,7},{7,8},{8,9},{9,10},{10,1... | collective-permute-start | bytes 3145736 | tf_op jit(solution)/shard_map/ppermute | solution.py:515
  347.4 20.6 %collective-permute-start.5 = (bf16[512,1024]{1,0:T(8,128)(2,1)}, bf16[512,1024]{1,0:T(8,128)(2,1)}, u32[]{:S(2)}, u32[]{:S(2)}) collective-permute-start(bf16[512,1024]{1,0:T(8,128)(2,1)} %get-tuple-element.112), channel_id=1, source_target_pairs={{1,0},{2,1},{3,2},{4,3},{5,4},{6,5},{7,6},{8,7},{9,8},{10,9},{11,1... | collective-permute-start | bytes 3145736 | tf_op jit(solution)/shard_map/ppermute | solution.py:516
  350.4 17.7 %copy-start.5 = (bf16[1024,1024]{1,0:T(8,128)(2,1)S(1)}, bf16[1024,1024]{1,0:T(8,128)(2,1)}, u32[]{:S(2)}) copy-start(bf16[1024,1024]{1,0:T(8,128)(2,1)} %copy-done.4) | copy-start | bytes 6291460
  466.2 174.5 %copy-start.26 = (f32[2048]{0:T(1024)S(1)}, f32[2048]{0:T(1024)}, u32[]{:S(2)}) copy-start(f32[2048]{0:T(1024)} %copy-done.25) | copy-start | bytes 24580
  649.5 12.1 %copy-start.19 = (f32[128,1024]{1,0:T(8,128)S(1)}, f32[128,1024]{1,0:T(8,128)}, u32[]{:S(2)}) copy-start(f32[128,1024]{1,0:T(8,128)} %get-tuple-element.83) | copy-start | bytes 1572868
  649.5 33.0 %copy-start.3 = (bf16[1024,1024]{1,0:T(8,128)(2,1)S(1)}, bf16[1024,1024]{1,0:T(8,128)(2,1)}, u32[]{:S(2)}) copy-start(bf16[1024,1024]{1,0:T(8,128)(2,1)} %param.28) | copy-start | bytes 6291460
  649.7 29.4 %collective-permute-start.6 = (bf16[512,1024]{1,0:T(8,128)(2,1)S(1)}, bf16[512,1024]{1,0:T(8,128)(2,1)S(1)}, u32[]{:S(2)}, u32[]{:S(2)}) collective-permute-start(bf16[512,1024]{1,0:T(8,128)(2,1)S(1)} %get-tuple-element.106), channel_id=1, source_target_pairs={{0,1},{1,2},{2,3},{3,4},{4,5},{5,6},{6,7},{7,8},{8,9},{9,10},{10,1... | collective-permute-start | bytes 3145736 | tf_op jit(solution)/shard_map/ppermute | solution.py:521
  657.0 25.5 %collective-permute-start.7 = (bf16[512,1024]{1,0:T(8,128)(2,1)S(1)}, bf16[512,1024]{1,0:T(8,128)(2,1)S(1)}, u32[]{:S(2)}, u32[]{:S(2)}) collective-permute-start(bf16[512,1024]{1,0:T(8,128)(2,1)S(1)} %get-tuple-element.107), channel_id=1, source_target_pairs={{1,0},{2,1},{3,2},{4,3},{5,4},{6,5},{7,6},{8,7},{9,8},{10,9},{11,1... | collective-permute-start | bytes 3145736 | tf_op jit(solution)/shard_map/ppermute | solution.py:520
  662.5 24.8 %copy-start.24 = (f32[32,1024]{1,0:T(8,128)S(1)}, f32[32,1024]{1,0:T(8,128)}, u32[]{:S(2)}) copy-start(f32[32,1024]{1,0:T(8,128)} %get-tuple-element.167) | copy-start | bytes 393220
  662.5 25.4 %copy-start.23 = (f32[32,1024]{1,0:T(8,128)S(1)}, f32[32,1024]{1,0:T(8,128)}, u32[]{:S(2)}) copy-start(f32[32,1024]{1,0:T(8,128)} %get-tuple-element.168) | copy-start | bytes 393220
  662.5 26.1 %copy-start.22 = (f32[32,1024]{1,0:T(8,128)S(1)}, f32[32,1024]{1,0:T(8,128)}, u32[]{:S(2)}) copy-start(f32[32,1024]{1,0:T(8,128)} %get-tuple-element.169) | copy-start | bytes 393220
  662.5 26.7 %copy-start.18 = (f32[128,1024]{1,0:T(8,128)S(1)}, f32[128,1024]{1,0:T(8,128)}, u32[]{:S(2)}) copy-start(f32[128,1024]{1,0:T(8,128)} %get-tuple-element.171) | copy-start | bytes 1572868
  (32 other events, 160.9 us)
Sparse Core Ops, SparseCore 0:
  23.5 76.3 all-gather.4
  102.8 124.3 all-gather.6

commit v3 on v2

--- a/solution.py
+++ b/solution.py
@@ -19,7 +19,12 @@
 SELF2 = -100000.0 * LOG2E
 NEG = -1e30
 SCALE = 1.0 / math.sqrt(DH)
-TILE = 256
+TILE = 512
+HALF = TILE // 2
+STEP = 128.0
+SHIFT = 1.5 * 2.0**30
+TAME = 3000.0
+PAIR = 2
 FREE = 99.0
 STRIP = 512
 ROWS = 1024
@@ -49,139 +54,264 @@
     return pullback(upstream)
 
 
-def prepare(q_ref, code_ref, spread_ref, unit_s, ask_s, key_s):
-    rows = q_ref.shape[0]
+def prepare(q, code_ref, spread, ask_s, key_s, h, at):
     lane = lax.broadcasted_iota(jnp.int32, (TILE, DH), 1)
     target = ((lane // 64) * 32 + lane % 16).astype(F32)
-    for i in range(rows // TILE):
-        at = pl.ds(i * TILE, TILE)
-        q = q_ref[at, :].astype(F32)
-        norm = lax.rsqrt(jnp.sum(q * q, axis=1, keepdims=True) + EPS_UNIT)
-        unit_s[at, :] = (q * (norm * (SCALE * LOG2E))).astype(BF16)
-        code = dot(code_ref[at, :], spread_ref[...])
-        here = code == target
-        ask_s[at, :] = jnp.where(here, 1.0, 0.0).astype(BF16)
-        key_s[at, :] = jnp.where(here | (code + 1.0 == target), 1.0, 0.0).astype(BF16)
-
-
-def attend_kernel(low_ref, q_ref, v_ref, code_ref, spread_ref, comb_ref, lse_ref, lone_ref, unit_s, ask_s, key_s, vt_s, acc_s):
+    wide = q.astype(F32)
+    square = jnp.sum(wide * wide, axis=1, keepdims=True)
+    code = dot(code_ref[:, at], spread, TN)
+    here = code == target
+    ask_s[h, at, :DH] = q
+    ask_s[h, at, DH:] = jnp.where(here, STEP, 0.0).astype(BF16)
+    key_s[h, at, :DH] = (wide * (lax.rsqrt(square + EPS_UNIT) * (SCALE * LOG2E))).astype(BF16)
+    key_s[h, at, DH:] = jnp.where(here | (code + 1.0 == target), 1.0, 0.0).astype(BF16)
+    return jnp.max(square)
+
+
+def lowest(info_ref, i):
+    start, stop = i * TILE, (i + 1) * TILE
+    one = (info_ref[0] < stop) & (info_ref[1] > start)
+    two = (info_ref[2] < stop) & (info_ref[3] > start)
+    begin = jnp.where(one, info_ref[0], jnp.where(two, info_ref[2], stop))
+    return lax.div(begin, TILE)
+
+
+def tile_rows(i):
+    return pl.ds(pl.multiple_of(i * TILE, TILE), TILE)
+
+
+def halves(i):
+    start = i * TILE
+    return [((0, pl.multiple_of(start, HALF), pl.multiple_of(start, HALF)), HALF),
+            ((HALF, pl.multiple_of(start + HALF, HALF), pl.multiple_of(start, HALF)), TILE)]
+
+
+def part_of(both):
+    count = (both + SHIFT) - SHIFT
+    return count, both - count
+
+
+def apart(left, right):
+    return dot(left[:, DH:], right[:, DH:], NT), dot(left[:, :DH], right[:, :DH], NT)
+
+
+def attend_kernel(low_ref, q_ref, v_ref, code_ref, spread_ref, comb_ref, lse_ref, lone_ref, ask_s, key_s, more_s, acc_s, top_s):
     rows = q_ref.shape[0]
-    prepare(q_ref, code_ref, spread_ref, unit_s, ask_s, key_s)
-    for i in range(rows // TILE):
-        at = pl.ds(i * TILE, TILE)
-        vt_s[:, at] = v_ref[at, :].astype(F32).T.astype(BF16)
-    key_at = lax.broadcasted_iota(jnp.int32, (TILE, TILE), 0)
-    ask_at = lax.broadcasted_iota(jnp.int32, (TILE, TILE), 1)
-    for i in range(rows // TILE):
-        at = pl.ds(i * TILE, TILE)
-        low = low_ref[i]
-
-        @pl.when(low <= i)
+    tiles = rows // TILE
+    heads = [slice(h * DH, (h + 1) * DH) for h in range(PAIR)]
+
+    def ready(i, largest):
+        def fill():
+            most = jnp.float32(0.0)
+            at = tile_rows(i)
+            for h, cols in enumerate(heads):
+                most = jnp.maximum(most, prepare(q_ref[at, cols], code_ref, spread_ref[:, cols], ask_s, key_s, h, at))
+                more_s[h, at, :DH] = v_ref[at, cols]
+                more_s[h, at, DH:] = jnp.ones((TILE, DH), BF16)
+            return most
+
+        return jnp.maximum(largest, lax.cond(lowest(low_ref, i) <= i, fill, lambda: jnp.float32(0.0)))
+
+    largest = lax.fori_loop(0, tiles, ready, jnp.float32(0.0))
+    tame = largest * (SCALE * LOG2E) ** 2 < TAME
+    ask_at = lax.broadcasted_iota(jnp.int32, (TILE, TILE), 0)
+    key_at = lax.broadcasted_iota(jnp.int32, (TILE, TILE), 1)
+
+    def finish(h, cols, at, top):
+        total = acc_s[h, :, DH:]
+        some = total > 0.0
+        safe = jnp.where(some, total, 1.0)
+        inverse = jnp.where(some, 1.0 / safe, 0.0)
+        comb_ref[at, cols] = (acc_s[h, :, :DH] * inverse).astype(BF16)
+        lse_ref[h, :, at] = (jnp.log2(safe) + top).T[:1]
+
+    def rows_of(i, carry):
+        at = tile_rows(i)
+        low = lowest(low_ref, i)
+
+        @pl.when((low <= i) & tame)
         def _():
-            q = q_ref[at, :]
-            ask = ask_s[at, :]
-            score = dot(unit_s[at, :], q, NT)
-            count = dot(key_s[at, :], ask, NT)
-            score = jnp.where(key_at == ask_at, SELF2, score)
-            score = jnp.where((key_at <= ask_at) & (count > 0.5), score, NEG)
-            top = jnp.max(score, axis=0, keepdims=True)
-            prob = count * jnp.exp2(score - top)
-            total = jnp.sum(prob, axis=0, keepdims=True)
-            acc_s[...] = dot(vt_s[:, at], prob.astype(BF16))
+            for h in range(PAIR):
+                acc_s[h] = jnp.zeros((TILE, 2 * DH), F32)
 
             def step(j, carry):
-                top, total = carry
-                key_rows = pl.ds(pl.multiple_of(j * TILE, TILE), TILE)
-                score = dot(unit_s[key_rows, :], q, NT)
-                count = dot(key_s[key_rows, :], ask, NT)
-                score = jnp.where(count > 0.5, score, NEG)
-                newer = jnp.maximum(top, jnp.max(score, axis=0, keepdims=True))
-                fade = jnp.exp2(top - newer)
-                prob = count * jnp.exp2(score - newer)
-                acc_s[...] = acc_s[...] * fade + dot(vt_s[:, key_rows], prob.astype(BF16))
-                return newer, total * fade + jnp.sum(prob, axis=0, keepdims=True)
-
-            top, total = lax.fori_loop(low, i, step, (top, total))
-            some = total > 0.0
-            safe = jnp.where(some, total, 1.0)
-            inverse = jnp.where(some, 1.0 / safe, 0.0)
-            comb_ref[at, :] = (acc_s[...] * inverse).T.astype(BF16)
-            lse_ref[0, :, at] = top + jnp.log2(safe)
-            lone_ref[0, :, at] = ROUNDS * jnp.exp2(SELF2 - jnp.maximum(top, SELF2)) * inverse
+                keys = tile_rows(j)
+                for h in range(PAIR):
+                    count, score = part_of(dot(ask_s[h, at, :], key_s[h, keys, :], NT))
+                    acc_s[h] += dot((count * jnp.exp2(score)).astype(BF16), more_s[h, keys, :])
+                return carry
+
+            lax.fori_loop(low, i, step, 0)
+            for h, cols in enumerate(heads):
+                for asks, span in halves(i):
+                    here = pl.ds(asks[0], HALF)
+                    there = pl.ds(asks[1], HALF)
+                    keys = pl.ds(asks[2], span)
+                    key_at = lax.broadcasted_iota(jnp.int32, (HALF, span), 1)
+                    ask_at = lax.broadcasted_iota(jnp.int32, (HALF, span), 0) + (span - HALF)
+                    count, score = part_of(dot(ask_s[h, there, :], key_s[h, keys, :], NT))
+                    prob = jnp.where(key_at < ask_at, count * jnp.exp2(score), 0.0).astype(BF16)
+                    acc_s[h, here, :] += dot(prob, more_s[h, keys, :])
+                    active = jnp.max(jnp.where(key_at == ask_at, count, 0.0), axis=1, keepdims=True) > 0.0
+                    lone = jnp.where(active & (acc_s[h, here, DH:] == 0.0), 1.0, 0.0)
+                    acc_s[h, here, :DH] += lone * v_ref[there, cols].astype(F32)
+                    acc_s[h, here, DH:] += lone
+                    lone_ref[h, :, there] = lone.T[:1]
+                finish(h, cols, at, 0.0)
+
+        @pl.when((low <= i) & jnp.logical_not(tame))
+        def _():
+            for h, cols in enumerate(heads):
+                count, score = apart(ask_s[h, at, :], key_s[h, at, :])
+                score = jnp.where(key_at == ask_at, SELF2, score)
+                score = jnp.where((key_at <= ask_at) & (count > 0.5), score, NEG)
+                top = jnp.max(score, axis=1, keepdims=True)
+                prob = count * jnp.exp2(score - top)
+                acc_s[h] = dot(prob.astype(BF16), more_s[h, at, :])
+                top_s[h] = jnp.broadcast_to(top, (TILE, DH))
+
+                def step(j, carry):
+                    keys = tile_rows(j)
+                    count, score = apart(ask_s[h, at, :], key_s[h, keys, :])
+                    score = jnp.where(count > 0.5, score, NEG)
+                    top = top_s[h]
+                    newer = jnp.maximum(top, jnp.max(score, axis=1, keepdims=True))
+                    fade = jnp.exp2(top - newer)
+                    prob = count * jnp.exp2(score - newer[:, :1])
+                    acc_s[h] = acc_s[h] * jnp.concatenate([fade, fade], axis=1) + dot(prob.astype(BF16), more_s[h, keys, :])
+                    top_s[h] = newer
+                    return carry
+
+                lax.fori_loop(low, i, step, 0)
+                total = acc_s[h, :, DH:]
+                own = STEP * ROUNDS * jnp.exp2(SELF2 - jnp.maximum(top_s[h], SELF2))
+                lone_ref[h, :, at] = jnp.where(total > 0.0, own / jnp.where(total > 0.0, total, 1.0), 0.0).T[:1]
+                finish(h, cols, at, top_s[h])
 
         @pl.when(low > i)
         def _():
-            comb_ref[at, :] = jnp.zeros((TILE, DH), BF16)
-            lse_ref[0, :, at] = jnp.zeros((1, TILE), F32)
-            lone_ref[0, :, at] = jnp.zeros((1, TILE), F32)
+            comb_ref[at, :] = jnp.zeros((TILE, PAIR * DH), BF16)
+            for h in range(PAIR):
+                lse_ref[h, :, at] = jnp.zeros((1, TILE), F32)
+                lone_ref[h, :, at] = jnp.zeros((1, TILE), F32)
+
+        return carry
+
+    lax.fori_loop(0, tiles, rows_of, 0)
 
 
 def back_kernel(
     low_ref, q_ref, v_ref, code_ref, spread_ref, comb_ref, above_ref, lse_ref, lone_ref,
-    dq_ref, dv_ref, unit_s, ask_s, key_s, dunit_s, dvalue_s, dask_s,
+    dq_ref, dv_ref, ask_s, key_s, dunit_s, dvalue_s, dask_s,
 ):
     rows = q_ref.shape[0]
-    prepare(q_ref, code_ref, spread_ref, unit_s, ask_s, key_s)
-    key_at = lax.broadcasted_iota(jnp.int32, (TILE, TILE), 0)
-    ask_at = lax.broadcasted_iota(jnp.int32, (TILE, TILE), 1)
-    dunit_s[...] = jnp.zeros(dunit_s.shape, F32)
-    dvalue_s[...] = jnp.zeros(dvalue_s.shape, F32)
-    dask_s[...] = jnp.zeros(dask_s.shape, F32)
-    for i in range(rows // TILE):
-        at = pl.ds(i * TILE, TILE)
-        low = low_ref[i]
-
-        @pl.when(low <= i)
+    tiles = rows // TILE
+    heads = [slice(h * DH, (h + 1) * DH) for h in range(PAIR)]
+
+    def ready(i, largest):
+        def fill():
+            most = jnp.float32(0.0)
+            at = tile_rows(i)
+            for h, cols in enumerate(heads):
+                most = jnp.maximum(most, prepare(q_ref[at, cols], code_ref, spread_ref[:, cols], ask_s, key_s, h, at))
+                for total in (dunit_s, dvalue_s, dask_s):
+                    total[h, at, :] = jnp.zeros((TILE, DH), F32)
+            return most
+
+        return jnp.maximum(largest, lax.cond(lowest(low_ref, i) <= i, fill, lambda: jnp.float32(0.0)))
+
+    largest = lax.fori_loop(0, tiles, ready, jnp.float32(0.0))
+    tame = largest * (SCALE * LOG2E) ** 2 < TAME
+
+    def pass_over(i, low, split):
+        at = tile_rows(i)
+        deltas = []
+        for h, cols in enumerate(heads):
+            mixed = above_ref[at, cols].astype(F32) * comb_ref[at, cols].astype(F32)
+            deltas.append(jnp.sum(mixed.T, axis=0, keepdims=True))
+
+        def step(j, carry):
+            keys = tile_rows(j)
+            for h, cols in enumerate(heads):
+                q, above, unit = q_ref[at, cols], above_ref[at, cols], key_s[h, keys, :DH]
+                count, score = split(key_s[h, keys, :], ask_s[h, at, :])
+                d_prob = dot(v_ref[keys, cols], above, NT)
+                prob = count * jnp.exp2(score - lse_ref[h, :, at])
+                d_score = (prob * (d_prob - carry[h])).astype(BF16)
+                dvalue_s[h, keys, :] += dot(prob.astype(BF16), above)
+                dunit_s[h, keys, :] += dot(d_score, q)
+                dask_s[h, at, :] += dot(d_score, unit, TN)
+            return carry
+
+        deltas = lax.fori_loop(low, i, step, tuple(deltas))
+        for h, cols in enumerate(heads):
+            for asks, span in halves(i):
+                there = pl.ds(asks[1], HALF)
+                keys = pl.ds(asks[2], span)
+                key_at = lax.broadcasted_iota(jnp.int32, (span, HALF), 0)
+                ask_at = lax.broadcasted_iota(jnp.int32, (span, HALF), 1) + (span - HALF)
+                q, above, unit = q_ref[there, cols], above_ref[there, cols], key_s[h, keys, :DH]
+                count, score = split(key_s[h, keys, :], ask_s[h, there, :])
+                d_prob = dot(v_ref[keys, cols], above, NT)
+                prob = count * jnp.exp2(score - lse_ref[h, :, there])
+                prob = jnp.where(key_at < ask_at, prob, 0.0)
+                d_score = (prob * (d_prob - deltas[h][:, asks[0] : asks[0] + HALF])).astype(BF16)
+                prob = jnp.where(key_at == ask_at, lone_ref[h, :, there], prob).astype(BF16)
+                dvalue_s[h, keys, :] += dot(prob, above)
+                dunit_s[h, keys, :] += dot(d_score, q)
+                dask_s[h, there, :] += dot(d_score, unit, TN)
+
+    def together(left, right):
+        return part_of(dot(left, right, NT))
+
+    def guarded(left, right):
+        count, score = apart(left, right)
+        return count, jnp.where(count > 0.5, score, NEG)
+
+    def rows_of(i, carry):
+        low = lowest(low_ref, i)
+
+        @pl.when((low <= i) & tame)
         def _():
-            q = q_ref[at, :]
-            ask = ask_s[at, :]
-            above = above_ref[at, :]
-            lse = lse_ref[0, :, at]
-            mixed = above.astype(F32) * comb_ref[at, :].astype(F32)
-            delta = jnp.sum(mixed.T, axis=0, keepdims=True)
-            score = dot(unit_s[at, :], q, NT)
-            count = dot(key_s[at, :], ask, NT)
-            d_prob = dot(v_ref[at, :], above, NT)
-            earlier = key_at < ask_at
-            prob = count * jnp.exp2(jnp.minimum(score - lse, 0.0))
-            prob = jnp.where(earlier, prob, 0.0)
-            d_score = (prob * (d_prob - delta)).astype(BF16)
-            prob = jnp.where(key_at == ask_at, lone_ref[0, :, at], prob).astype(BF16)
-            dvalue_s[at, :] += dot(prob, above)
-            dunit_s[at, :] += dot(d_score, q)
-            dask_s[at, :] += dot(d_score, unit_s[at, :], TN)
-
-            def step(j, carry):
-                key_rows = pl.ds(pl.multiple_of(j * TILE, TILE), TILE)
-                unit = unit_s[key_rows, :]
-                score = dot(unit, q, NT)
-                count = dot(key_s[key_rows, :], ask, NT)
-                d_prob = dot(v_ref[key_rows, :], above, NT)
-                prob = count * jnp.exp2(jnp.minimum(score - lse, 0.0))
-                d_score = (prob * (d_prob - delta)).astype(BF16)
-                dvalue_s[key_rows, :] += dot(prob.astype(BF16), above)
-                dunit_s[key_rows, :] += dot(d_score, q)
-                dask_s[at, :] += dot(d_score, unit, TN)
-                return carry
-
-            lax.fori_loop(low, i, step, 0)
-
-    for i in range(rows // TILE):
-        at = pl.ds(i * TILE, TILE)
-        q = q_ref[at, :].astype(F32)
-        norm = lax.rsqrt(jnp.sum(q * q, axis=1, keepdims=True) + EPS_UNIT)
-        d_unit = dunit_s[at, :] * SCALE
-        along = jnp.sum(q * d_unit, axis=1, keepdims=True)
-        d_q = dask_s[at, :] * (1.0 / LOG2E) + d_unit * norm - q * (norm * norm * norm * along)
-        dq_ref[at, :] = d_q.astype(BF16)
-        dv_ref[at, :] = dvalue_s[at, :].astype(BF16)
+            pass_over(i, low, together)
+
+        @pl.when((low <= i) & jnp.logical_not(tame))
+        def _():
+            pass_over(i, low, guarded)
+
+        return carry
+
+    lax.fori_loop(0, tiles, rows_of, 0)
+
+    def close(i, carry):
+        at = tile_rows(i)
+
+        @pl.when(lowest(low_ref, i) <= i)
+        def _():
+            for h, cols in enumerate(heads):
+                q = q_ref[at, cols].astype(F32)
+                norm = lax.rsqrt(jnp.sum(q * q, axis=1, keepdims=True) + EPS_UNIT)
+                d_unit = dunit_s[h, at, :] * SCALE
+                along = jnp.sum(q * d_unit, axis=1, keepdims=True)
+                d_q = dask_s[h, at, :] * (1.0 / LOG2E) + d_unit * norm - q * (norm * norm * norm * along)
+                dq_ref[at, cols] = d_q.astype(BF16)
+                dv_ref[at, cols] = dvalue_s[h, at, :].astype(BF16)
+
+        @pl.when(lowest(low_ref, i) > i)
+        def _():
+            dq_ref[at, :] = jnp.zeros((TILE, PAIR * DH), BF16)
+            dv_ref[at, :] = jnp.zeros((TILE, PAIR * DH), BF16)
+
+        return carry
+
+    lax.fori_loop(0, tiles, close, 0)
 
 
 def head_specs(rows):
-    by_head = pl.BlockSpec((rows, DH), lambda h, low: (0, h))
-    code = pl.BlockSpec((rows, ROUNDS * HEADS), lambda h, low: (0, 0))
-    spread = pl.BlockSpec((ROUNDS * HEADS, DH), lambda h, low: (0, h))
-    stat = pl.BlockSpec((1, 1, rows), lambda h, low: (h, 0, 0))
+    by_head = pl.BlockSpec((rows, PAIR * DH), lambda h, low: (0, h))
+    code = pl.BlockSpec((ROUNDS * HEADS, rows), lambda h, low: (0, 0))
+    spread = pl.BlockSpec((ROUNDS * HEADS, PAIR * DH), lambda h, low: (0, h))
+    stat = pl.BlockSpec((PAIR, 1, rows), lambda h, low: (h, 0, 0))
     return by_head, code, spread, stat
 
 
@@ -194,13 +324,14 @@
         attend_kernel,
         grid_spec=pltpu.PrefetchScalarGridSpec(
             num_scalar_prefetch=1,
-            grid=(HEADS,),
+            grid=(HEADS // PAIR,),
             in_specs=[by_head, by_head, code_spec, spread_spec],
             out_specs=[by_head, stat, stat],
-            scratch_shapes=[pltpu.VMEM((rows, DH), BF16)] * 3
-            + [pltpu.VMEM((DH, rows), BF16), pltpu.VMEM((DH, TILE), F32)],
+            scratch_shapes=[pltpu.VMEM((PAIR, rows, 2 * DH), BF16)] * 3
+            + [pltpu.VMEM((PAIR, TILE, 2 * DH), F32), pltpu.VMEM((PAIR, TILE, DH), F32)],
         ),
         out_shape=(wide, thin, thin),
+        compiler_params=pltpu.CompilerParams(vmem_limit_bytes=48 << 20),
         name="attend",
         cost_estimate=pl.CostEstimate(
             flops=HEADS * 20 * 3 * 2 * TILE * TILE * DH, bytes_accessed=rows * HEADS * DH * 6, transcendentals=HEADS * 20 * TILE * TILE
@@ -216,12 +347,13 @@
         back_kernel,
         grid_spec=pltpu.PrefetchScalarGridSpec(
             num_scalar_prefetch=1,
-            grid=(HEADS,),
+            grid=(HEADS // PAIR,),
             in_specs=[by_head, by_head, code_spec, spread_spec, by_head, by_head, stat, stat],
             out_specs=[by_head, by_head],
-            scratch_shapes=[pltpu.VMEM((rows, DH), BF16)] * 3 + [pltpu.VMEM((rows, DH), F32)] * 3,
+            scratch_shapes=[pltpu.VMEM((PAIR, rows, 2 * DH), BF16)] * 2 + [pltpu.VMEM((PAIR, rows, DH), F32)] * 3,
         ),
         out_shape=(wide, wide),
+        compiler_params=pltpu.CompilerParams(vmem_limit_bytes=48 << 20),
         name="attend_back",
         cost_estimate=pl.CostEstimate(
             flops=HEADS * 20 * 6 * 2 * TILE * TILE * DH, bytes_accessed=rows * HEADS * DH * 12, transcendentals=HEADS * 20 * TILE * TILE
@@ -481,18 +613,226 @@
     )(*[array.reshape(outer, side, side, core, *array.shape[1:]) for array in arrays])
 
 
-def block_of_rank(buckets, length):
-    slots = buckets.shape[-1]
-    place = lax.broadcasted_iota(jnp.int32, (1, 1, slots), 2)
-    bucket = lax.broadcasted_iota(jnp.int32, (1, BUCKETS, 1), 1)
-    one_hot = (buckets[:, None, :] == bucket) & (place < length)
-    first = lax.broadcasted_iota(jnp.int32, (slots, slots), 0)
-    second = lax.broadcasted_iota(jnp.int32, (slots, slots), 1)
-    before = dot(one_hot.astype(BF16).reshape(-1, slots), (first < second).astype(BF16)).reshape(one_hot.shape)
-    size = jnp.sum(one_hot.astype(F32), axis=2, keepdims=True)
-    offset = jnp.cumsum(size, axis=1) - size
-    rank = jnp.sum(jnp.where(one_hot, before + offset, 0.0), axis=1)
-    return jnp.where(place[0] < length, jnp.floor(rank * (1.0 / GROUP)), FREE)
+def rank_kernel(length_ref, target_ref, bucket_ref, block_ref, info_ref, before_s):
+    devices = length_ref.shape[0]
+    lists, slots = bucket_ref.shape
+    me = lax.axis_index("fsdp")
+    base = me * slots
+    window = 2 * slots
+
+    def look(s, carry):
+        start, mine, found, one, two = carry
+        size = length_ref[s]
+        target = target_ref[s]
+        middle = start + lax.shift_right_logical(size, 1)
+        inside = (middle >= base) & (middle < base + slots)
+        offset = start - base + slots // 2
+        entry = (offset, offset + size, target)
+        first, second = inside & (found == 0), inside & (found == 1)
+        one = tuple(jnp.where(first, new, old) for new, old in zip(entry, one))
+        two = tuple(jnp.where(second, new, old) for new, old in zip(entry, two))
+        return start + size, jnp.where(target == me, size, mine), found + inside.astype(jnp.int32), one, two
+
+    zero = jnp.int32(0)
+    nothing = (jnp.int32(window), jnp.int32(window), zero)
+    total, mine, found, one, two = lax.fori_loop(0, devices, look, (zero, zero, zero, nothing, nothing))
+    for k, value in enumerate((one[0], one[1], two[0], two[1], one[2], two[2], total, found)):
+        info_ref[k] = value
+
+    def fill(i, carry):
+        at = pl.ds(pl.multiple_of(i * DH, DH), DH)
+        first = lax.broadcasted_iota(jnp.int32, (DH, slots), 0) + i * DH
+        second = lax.broadcasted_iota(jnp.int32, (DH, slots), 1)
+        before_s[at, :] = jnp.where(first < second, 1.0, 0.0).astype(BF16)
+        return carry
+
+    lax.fori_loop(0, slots // DH, fill, 0)
+    left = lax.broadcasted_iota(jnp.int32, (DH, DH), 0)
+    right = lax.broadcasted_iota(jnp.int32, (DH, DH), 1)
+    smaller = jnp.where((left // BUCKETS == right // BUCKETS) & (right < left), 1.0, 0.0).astype(BF16)
+    many = DH // BUCKETS
+    bucket = lax.broadcasted_iota(jnp.int32, (many, BUCKETS, slots), 1)
+    live = lax.broadcasted_iota(jnp.int32, (many, BUCKETS, slots), 2) < mine
+    ranks = []
+    for g in range(lists // many):
+        here = (jnp.broadcast_to(bucket_ref[g * many : (g + 1) * many, :][:, None, :], bucket.shape) == bucket) & live
+        one_hot = jnp.where(here, 1.0, 0.0)
+        flat = one_hot.reshape(DH, slots).astype(BF16)
+        offset = jnp.sum(dot(smaller, flat), axis=1, keepdims=True)
+        place = (dot(flat, before_s[...]) + offset).reshape(many, BUCKETS, slots)
+        ranks.append(jnp.sum(one_hot * place, axis=1))
+    rank = jnp.concatenate(ranks, axis=0)
+    live = lax.broadcasted_iota(jnp.int32, (lists, slots), 1) < mine
+    block_ref[...] = jnp.where(live, jnp.floor(rank * (1.0 / GROUP)), FREE).astype(BF16)
+
+
+def rank_blocks(lengths, destination, buckets):
+    lists, slots = buckets.shape
+    smem = pl.BlockSpec(memory_space=pltpu.SMEM)
+    vmem = pl.BlockSpec(memory_space=pltpu.VMEM)
+    return pl.pallas_call(
+        rank_kernel,
+        in_specs=[smem, smem, vmem],
+        out_specs=[vmem, smem],
+        out_shape=[jax.ShapeDtypeStruct((lists, slots), BF16), jax.ShapeDtypeStruct((8,), jnp.int32)],
+        scratch_shapes=[pltpu.VMEM((slots, slots), BF16)],
+        compiler_params=pltpu.CompilerParams(vmem_limit_bytes=32 << 20),
+        name="rank_blocks",
+    )(lengths, destination, buckets)
+
+
+def project_kernel(
+    info_ref, head_ref, own_ref, tail_ref, gain_ref, shift_ref, w_s_ref, w_v_ref, one_ref, two_ref,
+    normed_ref, shared_ref, value_ref, code_ref,
+):
+    i = pl.program_id(0)
+    tile = own_ref.shape[0]
+    steps = pl.num_programs(0)
+
+    def go(ref):
+        normed = layer_norm(ref[...].astype(F32), gain_ref[...], shift_ref[...]).astype(BF16)
+        normed_ref[...] = normed
+        shared_ref[...] = dot(normed, w_s_ref[...]).astype(BF16)
+        value_ref[...] = dot(normed, w_v_ref[...]).astype(BF16)
+
+    @pl.when(i < steps // 4)
+    def _():
+        go(head_ref)
+
+    @pl.when((i >= steps // 4) & (i < steps - steps // 4))
+    def _():
+        go(own_ref)
+
+    @pl.when(i >= steps - steps // 4)
+    def _():
+        go(tail_ref)
+
+    @pl.when(i == 0)
+    def _():
+        lists, window = code_ref.shape
+        lane = lax.broadcasted_iota(jnp.int32, (lists, window), 1)
+        code = jnp.full((lists, window), FREE, F32)
+        for k, ref in enumerate((one_ref, two_ref)):
+            begin, end = info_ref[2 * k], info_ref[2 * k + 1]
+            rows = ref[0].astype(F32)
+            moved = pltpu.roll(jnp.concatenate([rows, rows], axis=1), lax.rem(begin, window), 1)
+            code = jnp.where((lane >= begin) & (lane < end), moved + 32.0 * k, code)
+        code_ref[...] = code.astype(BF16)
+
+
+def project(info, head, own, tail, gain, shift, w_s, w_v, blocks):
+    slots, width = own.shape
+    window = 2 * slots
+    lists = ROUNDS * HEADS
+    tile = 256
+    steps = window // tile
+    quarter = steps // 4
+    rows = pl.BlockSpec((tile, width), lambda i, info: (i, 0))
+    vector = pl.BlockSpec((1, width), lambda i, info: (0, 0))
+    matrix = pl.BlockSpec((width, width), lambda i, info: (0, 0), pipeline_mode=pl.Buffered(1))
+    wide = jax.ShapeDtypeStruct((window, width), BF16)
+    return pl.pallas_call(
+        project_kernel,
+        grid_spec=pltpu.PrefetchScalarGridSpec(
+            num_scalar_prefetch=1,
+            grid=(steps,),
+            in_specs=[
+                pl.BlockSpec((tile, width), lambda i, info: (jnp.minimum(i, quarter - 1), 0)),
+                pl.BlockSpec((tile, width), lambda i, info: (jnp.clip(i - quarter, 0, 2 * quarter - 1), 0)),
+                pl.BlockSpec((tile, width), lambda i, info: (jnp.clip(i - 3 * quarter, 0, quarter - 1), 0)),
+                vector, vector, matrix, matrix,
+                pl.BlockSpec((1, lists, slots), lambda i, info: (info[4], 0, 0)),
+                pl.BlockSpec((1, lists, slots), lambda i, info: (info[5], 0, 0)),
+            ],
+            out_specs=[rows, rows, rows, pl.BlockSpec((lists, window), lambda i, info: (0, 0))],
+        ),
+        out_shape=[wide, wide, wide, jax.ShapeDtypeStruct((lists, window), BF16)],
+        compiler_params=pltpu.CompilerParams(vmem_limit_bytes=40 << 20),
+        name="project",
+    )(info, head, own, tail, gain, shift, w_s, w_v, blocks, blocks)
+
+
+def gather_kernel(devices, arrays, *refs):
+    sources, outs = refs[:arrays], refs[arrays : 2 * arrays]
+    own_sem, sem_o, sem_a, sem_b, sem_c = refs[2 * arrays :]
+    outer, side, core = digits(devices)
+    (o, p, q, c), core_peer, q_peers, p_peers, o_peers = neighbours(devices)
+    greet([core_peer] + [d for _, d in q_peers] + [d for _, d in p_peers] + [d for _, d in o_peers])
+    half = sources[0].shape[-1] // 2
+    columns = (pl.ds(0, half), pl.ds(half, half))
+
+    def remote(src, dst, sems, slot, device):
+        return pltpu.make_async_remote_copy(
+            src_ref=src, dst_ref=dst, send_sem=sems.at[(0,) + slot], recv_sem=sems.at[(1,) + slot],
+            device_id=(device,), device_id_type=MESH,
+        )
+
+    copies, locals_, begun, first, second, last = [], [], {}, {}, {}, {}
+    for s in range(arrays):
+        locals_.append(pltpu.make_async_copy(sources[s], outs[s].at[o, p, q, c], own_sem.at[s]))
+        locals_[s].start()
+        for d, (k, device) in enumerate(o_peers):
+            begun[s, d] = remote(sources[s], outs[s].at[o, p, q, c], sem_o, (s, d), device)
+            begun[s, d].start()
+
+    def stage_a(s):
+        locals_[s].wait()
+        for d in range(outer - 1):
+            begun[s, d].wait_recv()
+        for h, peers in enumerate((q_peers, p_peers)):
+            piece = outs[s].at[:, p, q, c, :, columns[h]]
+            for d, (k, device) in enumerate(peers):
+                first[s, h, d] = remote(piece, piece, sem_a, (s, h, d), device)
+                first[s, h, d].start()
+
+    def stage_b(s):
+        for h, peers in enumerate((p_peers, q_peers)):
+            for d in range(side - 1):
+                first[s, h, d].wait_recv()
+            piece = outs[s].at[:, p, :, c, :, columns[h]] if h == 0 else outs[s].at[:, :, q, c, :, columns[h]]
+            for d, (k, device) in enumerate(peers):
+                second[s, h, d] = remote(piece, piece, sem_b, (s, h, d), device)
+                second[s, h, d].start()
+
+    def stage_c(s):
+        for h in range(2):
+            for d in range(side - 1):
+                second[s, h, d].wait_recv()
+        piece = outs[s].at[:, :, :, c]
+        last[s] = remote(piece, piece, sem_c, (s,), core_peer)
+        last[s].start()
+
+    for t in range(arrays + 2):
+        if t < arrays:
+            stage_a(t)
+        if 0 <= t - 1 < arrays:
+            stage_b(t - 1)
+        if 0 <= t - 2 < arrays:
+            stage_c(t - 2)
+    for s in range(arrays):
+        last[s].wait_recv()
+    for group in (begun, first, second, last):
+        for copy in group.values():
+            copy.wait_send()
+
+
+def gather(devices, arrays):
+    outer, side, core = digits(devices)
+    count = len(arrays)
+    dma = pltpu.SemaphoreType.DMA
+    anywhere = pl.BlockSpec(memory_space=pl.ANY)
+    outs = pl.pallas_call(
+        functools.partial(gather_kernel, devices, count),
+        out_shape=tuple(jax.ShapeDtypeStruct((outer, side, side, core) + array.shape, array.dtype) for array in arrays),
+        in_specs=[anywhere] * count,
+        out_specs=(anywhere,) * count,
+        scratch_shapes=[
+            dma((count,)), dma((2, count, outer - 1)), dma((2, count, 2, side - 1)), dma((2, count, 2, side - 1)), dma((2, count))
+        ],
+        compiler_params=pltpu.CompilerParams(collective_id=2, has_side_effects=True),
+        name="gather",
+    )(*arrays)
+    return [out.reshape((devices,) + array.shape) for out, array in zip(outs, arrays)]
 
 
 def body(
@@ -511,82 +851,61 @@
     down = [(i, i - 1) for i in range(1, devices)]
     up = [(i, i + 1) for i in range(devices - 1)]
 
+    def to_sides(head, tail):
+        return lax.ppermute(tail, "fsdp", up), lax.ppermute(head, "fsdp", down)
+
     def widen(own):
-        head = lax.ppermute(own[half:], "fsdp", up)
-        tail = lax.ppermute(own[:half], "fsdp", down)
+        head, tail = to_sides(own[:half], own[half:])
         return jnp.concatenate([head, own, tail], axis=0)
 
     def narrow(wide):
-        tail = lax.ppermute(wide[:half], "fsdp", down)
-        head = lax.ppermute(wide[half + slots :], "fsdp", up)
+        head, tail = to_sides(wide[:half], wide[half + slots :])
         return wide[half : half + slots], jnp.concatenate([head, tail], axis=0)
 
-    ends = jnp.cumsum(lengths)
-    starts = ends - lengths
-    middle = starts + lengths // 2
     base = me * slots
-    owner = jnp.zeros((devices,), jnp.int32).at[destination].set(jnp.arange(devices, dtype=jnp.int32))
-    mine = lengths[owner[me]]
-    block = block_of_rank(buckets[0], mine)
-
-    vectors = jnp.concatenate(
-        [gain_attend, shift_attend, gain_mixing, shift_mixing, bias_output, bias_reduce, bias_expand]
-    )
+    lists = ROUNDS * HEADS
+    block, info = rank_blocks(lengths, destination, buckets[0])
+    spot = jnp.arange(width, dtype=jnp.int32)
+    short = jnp.stack([gain_attend, shift_attend, gain_mixing, shift_mixing, bias_output, bias_reduce])
+    short = jnp.where(spot // part == me, jnp.tile(short, (1, devices)), 0.0)
+    many = hidden // devices
+    long = jnp.tile(bias_expand, width // many)[None]
+    long = jnp.where(spot[None] // many + (width // many) * jnp.arange(sides, dtype=jnp.int32)[:, None] == me, long, 0.0)
+    vectors = jnp.concatenate([short, long], axis=0)
     high = lax.reduce_precision(vectors, 8, 7)
     count = vectors.shape[0]
-    packed = jnp.zeros((8, width), BF16).at[0, :count].set(high.astype(BF16)).at[1, :count].set((vectors - high).astype(BF16))
-    first = lax.all_gather(
-        jnp.concatenate([w_shared, w_value, block.astype(BF16), packed], axis=0), "fsdp", axis=0, tiled=False
+    packed = jnp.concatenate(
+        [block, high.astype(BF16), (vectors - high).astype(BF16), jnp.zeros((24 - 2 * count, width), BF16)], axis=0
     )
-    lists = ROUNDS * HEADS
-    full_shared = first[:, :part].reshape(width, width)
-    full_value = first[:, part : 2 * part].reshape(width, width)
-    blocks_all = first[:, 2 * part : 2 * part + lists]
-    full_vectors = first[:, 2 * part + lists, :count].astype(F32) + first[:, 2 * part + lists + 1, :count].astype(F32)
-    gain_a, shift_a, gain_m, shift_m, bias_o, bias_r = (
-        full_vectors[:, k * part : (k + 1) * part].reshape(width) for k in range(6)
-    )
-    bias_e = full_vectors[:, 6 * part :].reshape(hidden)
     second_gather = lax.all_gather(
         jnp.concatenate(
             [w_reduce, w_output] + [w_expand[:, k * width : (k + 1) * width] for k in range(sides)], axis=0
         ),
         "fsdp", axis=0, tiled=False,
     )
+    full_shared, full_value, packed = gather(devices, [w_shared, w_value, packed])
+    full_shared, full_value = full_shared.reshape(width, width), full_value.reshape(width, width)
+    vectors = jnp.sum(packed[:, lists : lists + 2 * count].astype(F32), axis=0)
+    vectors = vectors[:count] + vectors[count:]
+    gain_a, shift_a, gain_m, shift_m, bias_o, bias_r = (vectors[k : k + 1] for k in range(6))
+    bias_e = vectors[6:].reshape(1, hidden)
     full_output = second_gather[:, sides * part : (sides + 1) * part].reshape(width, width)
-
-    inside = (middle >= base) & (middle < base + slots)
-    chosen = jnp.sum(inside.astype(jnp.int32))
-    lowest = jnp.minimum(jnp.argmax(inside).astype(jnp.int32), devices - 1)
-    code = jnp.full((window + slots, lists), FREE, F32)
-    begin = jnp.full((window + slots,), window, jnp.int32)
-    spot = jnp.arange(slots, dtype=jnp.int32)
-    for k in range(2):
-        s = jnp.minimum(lowest + k, devices - 1)
-        valid = chosen > k
-        offset = jnp.where(valid, starts[s] - (base - half), window)
-        rows = lax.dynamic_index_in_dim(blocks_all, destination[s], 0, keepdims=False).astype(F32).T
-        rows = jnp.where(rows < 50.0, rows + 32.0 * k, FREE)
-        code = lax.dynamic_update_slice(code, rows, (offset, 0))
-        begin = lax.dynamic_update_slice(begin, jnp.where(spot < lengths[s], offset, window), (offset,))
-    code = code[:window].astype(BF16)
-    lowest_row = jnp.min(begin[:window].reshape(-1, TILE), axis=1)
-    low = (lowest_row // TILE).astype(jnp.int32)
     lane = jnp.arange(HEADS * DH, dtype=jnp.int32)
     row = jnp.arange(lists, dtype=jnp.int32)[:, None]
     spread = (row == ((lane % 64) // 16) * HEADS + lane // DH).astype(BF16)
 
-    live = ((base + jnp.arange(slots, dtype=jnp.int32)) < ends[-1]).astype(F32)[:, None]
+    live = ((base + jnp.arange(slots, dtype=jnp.int32)) < info[6]).astype(F32)[:, None]
     slot_one = input_one.astype(F32)
     slot_two = input_two.astype(F32)
     above_one = live * upstream_one.astype(F32)
     above_two = live * upstream_two.astype(F32)
 
-    two_window = widen(input_two).astype(F32)
-    normed = layer_norm(two_window, gain_a, shift_a).astype(BF16)
-    shared = dot(normed, full_shared).astype(BF16)
-    values = dot(normed, full_value).astype(BF16)
-    combined_window, lse, lone = attend(low, shared, values, code, spread)
+    two_head, two_tail = to_sides(input_two[:half], input_two[half:])
+    two_window = jnp.concatenate([two_head, input_two, two_tail], axis=0).astype(F32)
+    normed, shared, values, code = project(
+        info, two_head, input_two, two_tail, gain_a, shift_a, full_shared, full_value, packed
+    )
+    combined_window, lse, lone = attend(info, shared, values, code, spread)
     own, other = narrow(combined_window)
     combined = own + other
     attended = dot(combined, full_output) + bias_o
@@ -595,7 +914,7 @@
     d_reduce = above_two.astype(BF16)
     grad_bias_reduce = jnp.sum(d_reduce, axis=0, dtype=F32)
     mixed, d_second, grad_reduce, grad_expand, grad_bias_expand = mixing(
-        second, d_reduce, second_gather, bias_e[None], bias_r[None], part
+        second, d_reduce, second_gather, bias_e, bias_r, part
     )
     out_two = slot_two + live * mixed
     d_one_mix, grad_gain_m, grad_shift_m = norm_back(out_one, gain_m, shift_m, d_second)
@@ -605,7 +924,7 @@
     grad_bias_output = jnp.sum(d_attend, axis=0, dtype=F32)
     d_combined = dot(d_attend, full_output, NT).astype(BF16)
     d_shared, d_values = attend_back(
-        low, shared, values, code, spread, combined_window, widen(d_combined), lse, lone
+        info, shared, values, code, spread, combined_window, widen(d_combined), lse, lone
     )
     grad_shared = dot(normed, d_shared, TN)
     grad_value = dot(normed, d_values, TN)

time: 702 us -> 615 us (0.88)
  the two profiles are of different devices: /device:TPU:13 before, /device:TPU:1 now
where the time goes in v3:
time: 615 us; the launch traced here: 608 us
  Pallas kernels  382 us (62%)
  matrix products  48.1 us (8%)
  starting transfers between devices  44.5 us (7%)
  other arithmetic  44.3 us (7%)
  waiting for transfers between devices  41.8 us (7%)
  local copies, waits for them, and re-layouts  31.6 us (5%)
  between operations  14.9 us (2%)
    pallas_call x1, Pallas kernels, reduce_scatter(): pl.pallas_call(functools.partial(reduce_kernel, devices, plan, len(arrays...  163 us
    pallas_call x1, Pallas kernels, gather(): pl.pallas_call(functools.partial(gather_kernel, devices, count), out_shap...  79.3 us
    pallas_call x1, Pallas kernels, mixing(): pl.pallas_call(mixing_kernel, grid=(hidden // STRIP,), in_specs=[fixed, f...  63.8 us
    dot_general x7, matrix products, dot(): return lax.dot_general(a, b, dims, preferred_element_type=F32)  48.1 us
    ppermute x8, starting transfers between devices, to_sides(): return (lax.ppermute(tail, 'fsdp', up), lax.ppermute(head, 'fsdp', down))  44.4 us
    ppermute x8, waiting for transfers between devices, to_sides(): return (lax.ppermute(tail, 'fsdp', up), lax.ppermute(head, 'fsdp', down))  41.8 us
    pallas_call x1, Pallas kernels, attend_back(): pl.pallas_call(back_kernel, grid_spec=pltpu.PrefetchScalarGridSpec(num_sc...  35.6 us
    pallas_call x1, Pallas kernels, attend(): pl.pallas_call(attend_kernel, grid_spec=pltpu.PrefetchScalarGridSpec(num_...  19.7 us
  transfers between devices with their start and end apart: 9, of which 4 were waited for; matrix products, arithmetic and copies ran while one was open for 6% of the time, Pallas kernels for 20%

profile of v3, /device:TPU:1, one launch (start us, length us, event | category | flops | bytes accessed | tf_op | source)
XLA Modules:
  0.0 607.7 jit_solution(5957017111342843131)
XLA Ops:
  16.5 4.6 collective-permute-start
  23.3 5.1 rank_blocks.1
  29.9 79.3 %gather.1 = (bf16[4,2,2,2,32,1024]{5,4,3,2,1,0:T(8,128)(2,1)}, bf16[4,2,2,2,32,1024]{5,4,3,2,1,0:T(8,128)(2,1)}, bf16[4,2,2,2,56,1024]{5,4,3,2,1,0:T(8,128)(2,1)}) custom-call(bf16[32,1024]{1,0:T(8,128)(2,1)} %refs_0_.1, bf16[32,1024]{1,0:T(8,128)(2,1)} %refs_1_.1, bf16[56,1024]{1,0:T(8,128)(2,1)} %maximum_maximum_fusion.refs_2_), custom_call_target="tpu_custom_call" | custom-call | tf_op jit(solution)/shard_map/gather/pallas_call | solution.py:824
  112.4 4.1 fusion.29
  119.7 15.9 %project.1 = (bf16[2048,1024]{1,0:T(8,128)(2,1)}, bf16[2048,1024]{1,0:T(8,128)(2,1)}, bf16[2048,1024]{1,0:T(8,128)(2,1)}, bf16[32,2048]{1,0:T(8,128)(2,1)S(1)}) custom-call(s32[8]{0:T(128)S(1)} %get-tuple-element.53.info_ref.low_ref, bf16[512,1024]{1,0:T(8,128)(2,1)S(1)} %collective-permute-done.head_ref, bf16[1024,1024]{1,0:T(8,128)(2,1)S(1)} %copy-done.2, ...), custom_call_target="tpu_custom_call" | custom-call | tf_op jit(solution)/shard_map/project/pallas_call | solution.py:734
  135.6 19.7 %attend.1 = (bf16[2048,1024]{1,0:T(8,128)(2,1)S(1)}, f32[8,1,2048]{2,1,0:T(1,128)S(1)}, f32[8,1,2048]{2,1,0:T(1,128)S(1)}) custom-call(s32[8]{0:T(128)S(1)} %get-tuple-element.53.info_ref.low_ref, bf16[2048,1024]{1,0:T(8,128)(2,1)} %get-tuple-element.58.q_ref, bf16[2048,1024]{1,0:T(8,128)(2,1)} %get-tuple-element.59.v_ref, ...), custom_call_target="tpu_custom_call" | custom-call | flops 32212254720 | bytes 12582912 | tf_op jit(solution)/shard_map/attend/pallas_call | solution.py:323
  158.7 25.1 %collective-permute-start.2 = (bf16[512,1024]{1,0:T(8,128)(2,1)}, bf16[512,1024]{1,0:T(8,128)(2,1)}, u32[]{:S(2)}, u32[]{:S(2)}) collective-permute-start(bf16[512,1024]{1,0:T(8,128)(2,1)} %get-tuple-element.95), channel_id=1, source_target_pairs={{0,1},{1,2},{2,3},{3,4},{4,5},{5,6},{6,7},{7,8},{8,9},{9,10},{10,1... | collective-permute-start | bytes 3145736 | tf_op jit(solution)/shard_map/ppermute | solution.py:855
  194.1 11.4 %collective-permute-done.2 = bf16[512,1024]{1,0:T(8,128)(2,1)} collective-permute-done((bf16[512,1024]{1,0:T(8,128)(2,1)}, bf16[512,1024]{1,0:T(8,128)(2,1)}, u32[]{:S(2)}, u32[]{:S(2)}) %collective-permute-start.2) | collective-permute-done | bytes 1048608 | tf_op jit(solution)/shard_map/ppermute | solution.py:855
  205.6 4.9 fusion.40
  213.1 63.8 %mixing.1 = (f32[1024,1024]{1,0:T(8,128)}, f32[1024,1024]{1,0:T(8,128)}, bf16[32,128,1024]{2,1,0:T(8,128)(2,1)}, bf16[32,128,1024]{2,1,0:T(8,128)(2,1)}, f32[1,4096]{1,0:T(1,128)}) custom-call(bf16[1024,1024]{1,0:T(8,128)(2,1)} %add_convert_fusion.1.second_ref, bf16[1024,1024]{1,0:T(8,128)(2,1)} %get-tuple-element.85.above_ref, ...), custom_call_target="tpu_custom_call" | custom-call | tf_op jit(solution)/shard_map/mixing/pallas_call | solution.py:405
  276.9 4.1 multiply_reduce_fusion
  281.6 4.0 fusion.33
  292.5 4.4 collective-permute-start.4
  301.0 6.8 %convolution_convert_fusion.2 = bf16[1024,1024]{1,0:T(8,128)(2,1)} fusion(bf16[1024,1024]{1,0:T(8,128)(2,1)} %copy-done.23, bf16[512,1024]{1,0:T(8,128)(2,1)} %collective-permute-done.3, bf16[512,1024]{1,0:T(8,128)(2,1)} %collective-permute-done.2, bf16[2048,1024]{1,0:T(8,128)(2,1)} %copy-done.8), kind=kOutput, calls=%fused_computation.31 | convolution fusion | flops 2154823680 | bytes 8388608 | tf_op jit(solution)/shard_map/dot_general | solution.py:43
  307.8 12.3 %collective-permute-done.4 = bf16[512,1024]{1,0:T(8,128)(2,1)} collective-permute-done((bf16[512,1024]{1,0:T(8,128)(2,1)}, bf16[512,1024]{1,0:T(8,128)(2,1)}, u32[]{:S(2)}, u32[]{:S(2)}) %collective-permute-start.4) | collective-permute-done | bytes 1048608 | tf_op jit(solution)/shard_map/ppermute | solution.py:855
  323.8 35.6 %attend_back.1 = (bf16[2048,1024]{1,0:T(8,128)(2,1)S(1)}, bf16[2048,1024]{1,0:T(8,128)(2,1)}) custom-call(s32[8]{0:T(128)S(1)} %get-tuple-element.53.info_ref.low_ref, bf16[2048,1024]{1,0:T(8,128)(2,1)} %get-tuple-element.58.q_ref, bf16[2048,1024]{1,0:T(8,128)(2,1)} %get-tuple-element.59.v_ref, bf16[32,2048]{1,0:T(8,128)(2,1)S(1)} %get-tuple-element.60.code_ref, ...), custom_call_target="tpu_custom_call" | custom-call | flops 64424509440 | bytes 25165824 | tf_op jit(solution)/shard_map/attend_back/pallas_call | solution.py:346
  359.5 9.3 %fusion.41 = f32[2048,1024]{1,0:T(8,128)} fusion(bf16[2048,1024]{1,0:T(8,128)(2,1)} %get-tuple-element.67, bf16[1024,1024]{1,0:T(8,128)(2,1)S(1)} %bitcast.63), kind=kOutput, calls=%fused_computation.113 | convolution fusion | flops 4294967296 | bytes 14680064 | tf_op jit(solution)/shard_map/dot_general | solution.py:43
  368.7 6.0 convolution_convert_fusion
  374.7 5.7 convolution_convert_fusion.1
  380.5 13.0 %fusion.7 = (bf16[1024]{0:T(1024)(128)(2,1)S(1)}, f32[2048]{0:T(1024)S(1)}, bf16[1024]{0:T(1024)(128)(2,1)S(1)}, f32[2048,1024]{1,0:T(8,128)}) fusion(f32[2048]{0:T(1024)S(1)} %copy-done.32, f32[2048]{0:T(1024)S(1)} %broadcast_multiply_fusion, bf16[512,1024]{1,0:T(8,128)(2,1)} %collective-permute-done.1.tail_ref, bf16[1024,1024]{1,0:T(8,128)(2,1)S(1)} %copy-done.2, ...), kind=kOutput, calls=%fused_computation.10 | convolution fusion | flops 4326420480 | bytes 27295744 | tf_op jit(solution)/shard_map/dot_general | solution.py:43
  394.8 163.1 %reduce_scatter.1 = (f32[128,1024]{1,0:T(8,128)}, f32[128,1024]{1,0:T(8,128)}, f32[32,1024]{1,0:T(8,128)}, f32[32,1024]{1,0:T(8,128)}, f32[32,1024]{1,0:T(8,128)}, /*index=5*/f32[8,1024]{1,0:T(8,128)}) custom-call(bf16[4,2,2,2,128,1024]{5,4,3,2,1,0:T(8,128)(2,1)} %bitcast.70, bf16[4,2,2,2,128,1024]{5,4,3,2,1,0:T(8,128)(2,1)} %bitcast.71, ...), custom_call_target="tpu_custom_call" | custom-call | tf_op jit(solution)/shard_map/reduce_scatter/pallas_call | solution.py:605
  557.9 8.3 %fusion.32 = (f32[2048]{0:T(1024)S(1)}, f32[2048,1024]{1,0:T(8,128)S(1)}) fusion(f32[2048]{0:T(1024)S(1)} %multiply_multiply_fusion, f32[2048]{0:T(1024)S(1)} %broadcast_multiply_fusion, bf16[512,1024]{1,0:T(8,128)(2,1)} %collective-permute-done.1.tail_ref, bf16[1024,1024]{1,0:T(8,128)(2,1)S(1)} %copy-done.2, ...), kind=kLoop, calls=%fused_computation.104 | loop fusion | flops 27260928 | bytes 21008384 | tf_op jit(solution)/shard_map/transpose(jvp())/reduce_sum | solution.py:47
  575.1 16.9 %collective-permute-done.6 = bf16[512,1024]{1,0:T(8,128)(2,1)S(1)} collective-permute-done((bf16[512,1024]{1,0:T(8,128)(2,1)S(1)}, bf16[512,1024]{1,0:T(8,128)(2,1)S(1)}, u32[]{:S(2)}, u32[]{:S(2)}) %collective-permute-start.6) | collective-permute-done | bytes 1048608 | tf_op jit(solution)/shard_map/ppermute | solution.py:855
  593.2 4.7 multiply_convert_fusion
  (161 shorter events, 64.7 us)
Async XLA Ops:
  7.2 21.9 %copy-start = (f32[128]{0:T(128)S(1)}, f32[128]{0:T(128)}, u32[]{:S(2)}) copy-start(f32[128]{0:T(128)} %param.38) | copy-start | bytes 1540
  7.3 16.0 %copy-start.10 = (s32[1,32,1024]{2,1,0:T(8,128)S(1)}, s32[1,32,1024]{2,1,0:T(8,128)}, u32[]{:S(2)}) copy-start(s32[1,32,1024]{2,1,0:T(8,128)} %param.27) | copy-start | bytes 393220
  7.3 16.0 %copy-start.13 = (s32[32]{0:T(128)S(1)}, s32[32]{0:T(128)}, u32[]{:S(2)}) copy-start(s32[32]{0:T(128)} %length_ref.1) | copy-start | bytes 388
  7.3 16.0 %copy-start.14 = (s32[32]{0:T(128)S(1)}, s32[32]{0:T(128)}, u32[]{:S(2)}) copy-start(s32[32]{0:T(128)} %target_ref.1) | copy-start | bytes 388
  7.3 184.9 %all-gather.3.cloned.1.call-start = ((), (), s32[]{:S(2)}) async-start(), calls=%async_computation | async-start | bytes 19464192 | tf_op jit(solution)/shard_map/all_gather | solution.py:880
  16.5 100.0 %copy-start.2 = (bf16[1024,1024]{1,0:T(8,128)(2,1)S(1)}, bf16[1024,1024]{1,0:T(8,128)(2,1)}, u32[]{:S(2)}) copy-start(bf16[1024,1024]{1,0:T(8,128)(2,1)} %own_ref.1) | copy-start | bytes 6291460
  16.5 100.0 %collective-permute-start = (bf16[512,1024]{1,0:T(8,128)(2,1)}, bf16[512,1024]{1,0:T(8,128)(2,1)S(1)}, u32[]{:S(2)}, u32[]{:S(2)}) collective-permute-start(bf16[512,1024]{1,0:T(8,128)(2,1)} %get-tuple-element.100), channel_id=1, source_target_pairs={{0,1},{1,2},{2,3},{3,4},{4,5},{5,6},{6,7},{7,8},{8,9},{9,10},{10,1... | collective-permute-start | bytes 3145736 | tf_op jit(solution)/shard_map/ppermute | solution.py:855
  21.1 95.4 %collective-permute-start.1 = (bf16[512,1024]{1,0:T(8,128)(2,1)}, bf16[512,1024]{1,0:T(8,128)(2,1)}, u32[]{:S(2)}, u32[]{:S(2)}) collective-permute-start(bf16[512,1024]{1,0:T(8,128)(2,1)} %get-tuple-element.99), channel_id=1, source_target_pairs={{1,0},{2,1},{3,2},{4,3},{5,4},{6,5},{7,6},{8,7},{9,8},{10,9},{11,1... | collective-permute-start | bytes 3145736 | tf_op jit(solution)/shard_map/ppermute | solution.py:855
  112.4 23.3 %copy-start.11 = (f32[1,1024]{1,0:T(1,128)}, f32[1,1024]{1,0:T(1,128)S(1)}, u32[]{:S(2)}) copy-start(f32[1,1024]{1,0:T(1,128)S(1)} %get-tuple-element.110.gain_ref) | copy-start | bytes 12292
  158.7 46.8 %collective-permute-start.2 = (bf16[512,1024]{1,0:T(8,128)(2,1)}, bf16[512,1024]{1,0:T(8,128)(2,1)}, u32[]{:S(2)}, u32[]{:S(2)}) collective-permute-start(bf16[512,1024]{1,0:T(8,128)(2,1)} %get-tuple-element.95), channel_id=1, source_target_pairs={{0,1},{1,2},{2,3},{3,4},{4,5},{5,6},{6,7},{7,8},{8,9},{9,10},{10,1... | collective-permute-start | bytes 3145736 | tf_op jit(solution)/shard_map/ppermute | solution.py:855
  183.9 21.7 %collective-permute-start.3 = (bf16[512,1024]{1,0:T(8,128)(2,1)}, bf16[512,1024]{1,0:T(8,128)(2,1)}, u32[]{:S(2)}, u32[]{:S(2)}) collective-permute-start(bf16[512,1024]{1,0:T(8,128)(2,1)} %get-tuple-element.96), channel_id=1, source_target_pairs={{1,0},{2,1},{3,2},{4,3},{5,4},{6,5},{7,6},{8,7},{9,8},{10,9},{11,1... | collective-permute-start | bytes 3145736 | tf_op jit(solution)/shard_map/ppermute | solution.py:855
  194.1 16.4 %copy-start.20 = (bf16[32,32,1024]{2,1,0:T(8,128)(2,1)}, bf16[32,32,1024]{2,1,0:T(8,128)(2,1)S(1)}, u32[]{:S(2)}) copy-start(bf16[32,32,1024]{2,1,0:T(8,128)(2,1)S(1)} %slice.212) | copy-start | bytes 6291460
  292.5 27.7 %collective-permute-start.4 = (bf16[512,1024]{1,0:T(8,128)(2,1)}, bf16[512,1024]{1,0:T(8,128)(2,1)}, u32[]{:S(2)}, u32[]{:S(2)}) collective-permute-start(bf16[512,1024]{1,0:T(8,128)(2,1)} %get-tuple-element.97), channel_id=1, source_target_pairs={{0,1},{1,2},{2,3},{3,4},{4,5},{5,6},{6,7},{7,8},{8,9},{9,10},{10,1... | collective-permute-start | bytes 3145736 | tf_op jit(solution)/shard_map/ppermute | solution.py:855
  296.9 23.3 %collective-permute-start.5 = (bf16[512,1024]{1,0:T(8,128)(2,1)}, bf16[512,1024]{1,0:T(8,128)(2,1)}, u32[]{:S(2)}, u32[]{:S(2)}) collective-permute-start(bf16[512,1024]{1,0:T(8,128)(2,1)} %get-tuple-element.98), channel_id=1, source_target_pairs={{1,0},{2,1},{3,2},{4,3},{5,4},{6,5},{7,6},{8,7},{9,8},{10,9},{11,1... | collective-permute-start | bytes 3145736 | tf_op jit(solution)/shard_map/ppermute | solution.py:855
  301.0 19.2 %copy-start.18 = (bf16[1024,1024]{1,0:T(8,128)(2,1)S(1)}, bf16[1024,1024]{1,0:T(8,128)(2,1)}, u32[]{:S(2)}) copy-start(bf16[1024,1024]{1,0:T(8,128)(2,1)} %copy-done.17) | copy-start | bytes 6291460
  323.8 35.6 %copy-start.7 = (bf16[4,2,2,2,32,1024]{5,4,3,2,1,0:T(8,128)(2,1)S(1)}, bf16[4,2,2,2,32,1024]{5,4,3,2,1,0:T(8,128)(2,1)}, u32[]{:S(2)}) copy-start(bf16[4,2,2,2,32,1024]{5,4,3,2,1,0:T(8,128)(2,1)} %get-tuple-element.57) | copy-start | bytes 6291460
  566.8 26.4 %copy-start.16 = (bf16[1024,1024]{1,0:T(8,128)(2,1)S(1)}, bf16[1024,1024]{1,0:T(8,128)(2,1)}, u32[]{:S(2)}) copy-start(bf16[1024,1024]{1,0:T(8,128)(2,1)} %param.24) | copy-start | bytes 6291460
  567.0 25.0 %collective-permute-start.6 = (bf16[512,1024]{1,0:T(8,128)(2,1)S(1)}, bf16[512,1024]{1,0:T(8,128)(2,1)S(1)}, u32[]{:S(2)}, u32[]{:S(2)}) collective-permute-start(bf16[512,1024]{1,0:T(8,128)(2,1)S(1)} %get-tuple-element.92), channel_id=1, source_target_pairs={{0,1},{1,2},{2,3},{3,4},{4,5},{5,6},{6,7},{7,8},{8,9},{9,10},{10,1... | collective-permute-start | bytes 3145736 | tf_op jit(solution)/shard_map/ppermute | solution.py:855
  569.0 24.1 %collective-permute-start.7 = (bf16[512,1024]{1,0:T(8,128)(2,1)S(1)}, bf16[512,1024]{1,0:T(8,128)(2,1)S(1)}, u32[]{:S(2)}, u32[]{:S(2)}) collective-permute-start(bf16[512,1024]{1,0:T(8,128)(2,1)S(1)} %get-tuple-element.93), channel_id=1, source_target_pairs={{1,0},{2,1},{3,2},{4,3},{5,4},{6,5},{7,6},{8,7},{9,8},{10,9},{11,1... | collective-permute-start | bytes 3145736 | tf_op jit(solution)/shard_map/ppermute | solution.py:855
  574.2 26.4 %copy-start.1 = (f32[128]{0:T(128)S(1)}, f32[128]{0:T(128)}, u32[]{:S(2)}) copy-start(f32[128]{0:T(128)} %param.38) | copy-start | bytes 1540
  575.1 22.8 %copy-start.29 = (f32[32,1024]{1,0:T(8,128)S(1)}, f32[32,1024]{1,0:T(8,128)}, u32[]{:S(2)}) copy-start(f32[32,1024]{1,0:T(8,128)} %get-tuple-element.143) | copy-start | bytes 393220
  575.1 23.4 %copy-start.28 = (f32[32,1024]{1,0:T(8,128)S(1)}, f32[32,1024]{1,0:T(8,128)}, u32[]{:S(2)}) copy-start(f32[32,1024]{1,0:T(8,128)} %get-tuple-element.144) | copy-start | bytes 393220
  575.1 24.1 %copy-start.27 = (f32[32,1024]{1,0:T(8,128)S(1)}, f32[32,1024]{1,0:T(8,128)}, u32[]{:S(2)}) copy-start(f32[32,1024]{1,0:T(8,128)} %get-tuple-element.145) | copy-start | bytes 393220
  575.1 24.8 %copy-start.25 = (f32[128,1024]{1,0:T(8,128)S(1)}, f32[128,1024]{1,0:T(8,128)}, u32[]{:S(2)}) copy-start(f32[128,1024]{1,0:T(8,128)} %get-tuple-element.147) | copy-start | bytes 1572868
  (26 other events, 209.8 us)
Sparse Core Ops, SparseCore 0:
  13.6 159.4 all-gather.2

commit v4 on v3

--- a/solution.py
+++ b/solution.py
@@ -27,8 +27,6 @@
 PAIR = 2
 FREE = 99.0
 STRIP = 512
-ROWS = 1024
-LAG = 1
 CURVE = math.sqrt(2.0 / math.pi)
 MESH = pl.DeviceIdType.MESH
 
@@ -361,77 +359,6 @@
     )(low, shared, values, code, spread, combined, above, lse, lone)
 
 
-def mixing_kernel(second_ref, above_ref, expand_ref, reduce_ref, bias_e_ref, bias_r_ref,
-                  out_ref, back_ref, grad_r_ref, grad_e_ref, grad_b_ref, act_s, pre_s):
-    step = pl.program_id(0)
-    rows, width = second_ref.shape
-    w_e = expand_ref[...].reshape(width, STRIP)
-    w_r = reduce_ref[...].reshape(STRIP, width)
-    bias = bias_e_ref[...]
-
-    @pl.when(step == 0)
-    def _():
-        out_ref[...] = jnp.broadcast_to(bias_r_ref[...], out_ref.shape)
-        back_ref[...] = jnp.zeros(back_ref.shape, F32)
-
-    def strip(i, total):
-        at = pl.ds(pl.multiple_of(i * ROWS, ROWS), ROWS)
-        pre = dot(second_ref[at, :], w_e) + bias
-        square = pre * pre
-        curve = jnp.tanh(CURVE * pre * (1.0 + 0.044715 * square))
-        hinge = 0.5 * (1.0 + curve)
-        act = (pre * hinge).astype(BF16)
-        slope = hinge + 0.5 * pre * (1.0 - curve * curve) * (CURVE * (1.0 + 3 * 0.044715 * square))
-        d_pre_wide = dot(above_ref[at, :], w_r, NT) * slope
-        d_pre = d_pre_wide.astype(BF16)
-        act_s[at, :] = act
-        pre_s[at, :] = d_pre
-        out_ref[at, :] += dot(act, w_r)
-        back_ref[at, :] += dot(d_pre, w_e, NT)
-        return total + jnp.sum(d_pre.astype(F32), axis=0, keepdims=True)
-
-    grad_b_ref[...] = lax.fori_loop(0, rows // ROWS, strip, jnp.zeros((1, STRIP), F32))
-    grad_r_ref[...] = dot(act_s[...], above_ref[...], TN).astype(BF16).reshape(grad_r_ref.shape)
-    grad_e_ref[...] = dot(second_ref[...], pre_s[...], TN).astype(BF16).reshape(grad_e_ref.shape)
-
-
-def mixing(second, above, gathered, bias_e, bias_r, part):
-    rows, width = second.shape
-    devices = gathered.shape[0]
-    hidden = bias_e.shape[1]
-    many = hidden // devices
-    per = width // STRIP
-    fixed = pl.BlockSpec((rows, width), lambda i: (0, 0), pipeline_mode=pl.Buffered(1))
-    return pl.pallas_call(
-        mixing_kernel,
-        grid=(hidden // STRIP,),
-        in_specs=[
-            fixed, fixed,
-            pl.BlockSpec((devices, part, STRIP), lambda i: (0, many // part + 1 + i // per, i % per)),
-            pl.BlockSpec((STRIP // many, many, width), lambda i: (i, 0, 0)),
-            pl.BlockSpec((1, STRIP), lambda i: (0, i)),
-            pl.BlockSpec((1, width), lambda i: (0, 0)),
-        ],
-        out_specs=[
-            pl.BlockSpec((rows, width), lambda i: (0, 0)),
-            pl.BlockSpec((rows, width), lambda i: (0, 0)),
-            pl.BlockSpec((STRIP // many, many, width), lambda i: (i, 0, 0)),
-            pl.BlockSpec((devices, part, STRIP), lambda i: (0, i // per, i % per)),
-            pl.BlockSpec((1, STRIP), lambda i: (0, i)),
-        ],
-        out_shape=[
-            jax.ShapeDtypeStruct((rows, width), F32),
-            jax.ShapeDtypeStruct((rows, width), F32),
-            jax.ShapeDtypeStruct((devices, many, width), BF16),
-            jax.ShapeDtypeStruct((devices, hidden // width * part, width), BF16),
-            jax.ShapeDtypeStruct((1, hidden), F32),
-        ],
-        scratch_shapes=[pltpu.VMEM((rows, STRIP), BF16)] * 2,
-        compiler_params=pltpu.CompilerParams(vmem_limit_bytes=56 << 20),
-        name="mixing",
-    )(second, above, gathered, gathered, bias_e, bias_r)
-
-
 def digits(devices):
     side = 2
     while 8 * side * side < devices:
@@ -452,10 +379,14 @@
         return ((o_ * side + p_) * side + q_) * core + c_
 
     core_peer = at(o, p, q, 1 - c)
-    q_peers = [lax.rem(q + d, side) for d in range(1, side)]
-    p_peers = [lax.rem(p + d, side) for d in range(1, side)]
-    o_peers = [lax.rem(o + d, outer) for d in range(1, outer)]
-    return (o, p, q, c), core_peer, [(k, at(o, p, k, c)) for k in q_peers], [(k, at(o, k, q, c)) for k in p_peers], [(k, at(k, p, q, c)) for k in o_peers]
+    q_peers = [(k, at(o, p, k, c)) for k in (lax.rem(q + d, side) for d in range(1, side))]
+    p_peers = [(k, at(o, k, q, c)) for k in (lax.rem(p + d, side) for d in range(1, side))]
+    o_peers = [(k, at(k, p, q, c)) for k in (lax.rem(o + d, outer) for d in range(1, outer))]
+    return (o, p, q, c), core_peer, q_peers, p_peers, o_peers
+
+
+def peers_of(where):
+    return [where[1]] + [device for group in where[2:] for _, device in group]
 
 
 def greet(peers):
@@ -465,152 +396,692 @@
     pl.semaphore_wait(barrier, len(peers))
 
 
-def reduce_kernel(devices, plan, arrays, *refs):
-    outer, side, core = digits(devices)
-    sources, outs = refs[:arrays], refs[arrays : 2 * arrays]
-    rest = refs[2 * arrays :]
-    count = len(plan)
-    own = rest[:count]
-    landed_c = rest[count : 2 * count]
-    landed_a = rest[2 * count : 4 * count]
-    landed_b = rest[4 * count : 5 * count]
-    landed_o = rest[5 * count : 6 * count]
-    load_sem, sem_c, sem_a, sem_b, sem_o = rest[6 * count :]
-    (o, p, q, c), core_peer, q_peers, p_peers, o_peers = neighbours(devices)
-    greet([core_peer] + [d for _, d in q_peers] + [d for _, d in p_peers] + [d for _, d in o_peers])
-    width = own[0].shape[-1]
-    half = width // 2
-    columns = (pl.ds(0, half), pl.ds(half, half))
-
-    def remote(src, dst, sems, slot, device):
-        return pltpu.make_async_remote_copy(
-            src_ref=src, dst_ref=dst, send_sem=sems.at[(0,) + slot], recv_sem=sems.at[(1,) + slot],
-            device_id=(device,), device_id_type=MESH,
+def remote(src, dst, sems, slot, device):
+    return pltpu.make_async_remote_copy(
+        src_ref=src, dst_ref=dst, send_sem=sems.at[(0,) + slot], recv_sem=sems.at[(1,) + slot],
+        device_id=(device,), device_id_type=MESH,
+    )
+
+
+class Scatter:
+    def __init__(self, devices, where, slot, boxes, sems, other, mine, load=None):
+        self.outer, self.side, _ = digits(devices)
+        (self.o, self.p, self.q, self.c), self.core_peer, self.q_peers, self.p_peers, self.o_peers = where
+        self.slot = slot
+        self.box_c, box_a0, box_a1, self.box_b, self.box_o = boxes
+        self.box_a = (box_a0, box_a1)
+        self.sem_c, self.sem_a, self.sem_b, self.sem_o = sems
+        self.other, self.mine, self.load = other, mine, load
+        half = self.box_o.shape[-1] // 2
+        self.columns = (pl.ds(0, half), pl.ds(half, half))
+
+    def core(self):
+        return remote(self.other(), self.box_c, self.sem_c, (self.slot,), self.core_peer)
+
+    def first(self, h, d):
+        k, device = (self.q_peers, self.p_peers)[h][d]
+        spot = (slice(None), slice(None), k) if h == 0 else (slice(None), k, slice(None))
+        return remote(self.mine(spot, self.columns[h]), self.box_a[h].at[d], self.sem_a, (self.slot, h, d), device)
+
+    def second(self, h, d):
+        k, device = (self.p_peers, self.q_peers)[h][d]
+        return remote(
+            self.box_a[h].at[0, :, k], self.box_b.at[d, :, :, self.columns[h]], self.sem_b, (self.slot, h, d), device
         )
 
-    loads, to_core, first, second, third = {}, {}, {}, {}, {}
-    for s, (k, row, rows) in enumerate(plan):
-        at = pl.ds(row, rows)
-        to_core[s] = remote(sources[k].at[:, :, :, 1 - c, at, :], landed_c[s], sem_c, (s,), core_peer)
-        to_core[s].start()
-        loads[s] = pltpu.make_async_copy(sources[k].at[:, :, :, c, at, :], own[s], load_sem.at[s])
-        loads[s].start()
-
-    def stage_core(s):
-        loads[s].wait()
-        to_core[s].wait_recv()
-        mine, other = own[s], landed_c[s]
+    def third(self, d):
+        k, device = self.o_peers[d]
+        return remote(self.box_b.at[0, k], self.box_o.at[d], self.sem_o, (self.slot, d), device)
+
+    def begin(self):
+        self.core().start()
+        if self.load is not None:
+            self.load().start()
+
+    def stage_core(self):
+        if self.load is not None:
+            self.load().wait()
+        self.core().wait_recv()
+        side = self.side
 
         def add(i, carry):
-            a, b, d = i // (side * side), (i // side) % side, i % side
-            mine[a, b, d] = mine[a, b, d] + other[a, b, d]
+            spot = (lax.div(i, side * side), lax.rem(lax.div(i, side), side), lax.rem(i, side))
+            ref = self.mine(spot, slice(None))
+            ref[...] = ref[...] + self.box_c[spot]
             return carry
 
-        lax.fori_loop(0, outer * side * side, add, 0)
+        lax.fori_loop(0, self.outer * side * side, add, 0)
         for h in range(2):
             for d in range(side - 1):
-                if h == 0:
-                    k, device = q_peers[d]
-                    src = mine.at[:, :, k, :, columns[h]]
-                else:
-                    k, device = p_peers[d]
-                    src = mine.at[:, k, :, :, columns[h]]
-                first[s, h, d] = remote(src, landed_a[2 * s + h].at[d], sem_a, (s, h, d), device)
-                first[s, h, d].start()
-
-    def stage_first(s):
-        mine = own[s]
+                self.first(h, d).start()
+
+    def stage_first(self):
+        side = self.side
         for h in range(2):
-            box = landed_a[2 * s + h]
+            box = self.box_a[h]
             for d in range(side - 1):
-                first[s, h, d].wait_recv()
+                self.first(h, d).wait_recv()
 
             def add(i, carry):
-                a, b = i // side, i % side
-                total = mine[a, b, q, :, columns[h]] if h == 0 else mine[a, p, b, :, columns[h]]
+                a, b = lax.div(i, side), lax.rem(i, side)
+                total = self.mine((a, b, self.q) if h == 0 else (a, self.p, b), self.columns[h])[...]
                 for d in range(side - 1):
                     total = total + box[d, a, b]
                 box[0, a, b] = total
                 return carry
 
-            lax.fori_loop(0, outer * side, add, 0)
+            lax.fori_loop(0, self.outer * side, add, 0)
             for d in range(side - 1):
-                k, device = (p_peers if h == 0 else q_peers)[d]
-                second[s, h, d] = remote(
-                    box.at[0, :, k], landed_b[s].at[d, :, :, columns[h]], sem_b, (s, h, d), device
-                )
-                second[s, h, d].start()
-
-    def stage_second(s):
-        box = landed_b[s]
+                self.second(h, d).start()
+
+    def stage_second(self):
+        box = self.box_b
         for h in range(2):
-            part = landed_a[2 * s + h]
-            k = p if h == 0 else q
-            for d in range(side - 1):
-                second[s, h, d].wait_recv()
+            k = self.p if h == 0 else self.q
+            for d in range(self.side - 1):
+                self.second(h, d).wait_recv()
 
             def add(a, carry):
-                total = part[0, a, k]
-                for d in range(side - 1):
-                    total = total + box[d, a, :, columns[h]]
-                box[0, a, :, columns[h]] = total
+                total = self.box_a[h][0, a, k]
+                for d in range(self.side - 1):
+                    total = total + box[d, a, :, self.columns[h]]
+                box[0, a, :, self.columns[h]] = total
                 return carry
 
-            lax.fori_loop(0, outer, add, 0)
-        for d in range(outer - 1):
-            k, device = o_peers[d]
-            third[s, d] = remote(box.at[0, k], landed_o[s].at[d], sem_o, (s, d), device)
-            third[s, d].start()
-
-    def stage_third(s):
-        k, row, rows = plan[s]
-        total = landed_b[s][0, o].astype(F32)
-        for d in range(outer - 1):
-            third[s, d].wait_recv()
-            total = total + landed_o[s][d].astype(F32)
-        outs[k][pl.ds(row, rows), :] = total
-
-    for t in range(count + 3 * LAG):
-        if t < count:
-            stage_core(t)
-        if 0 <= t - LAG < count:
-            stage_first(t - LAG)
-        if 0 <= t - 2 * LAG < count:
-            stage_second(t - 2 * LAG)
-        if 0 <= t - 3 * LAG < count:
-            stage_third(t - 3 * LAG)
-    for copies in (to_core, first, second, third):
-        for copy in copies.values():
+            lax.fori_loop(0, self.outer, add, 0)
+        for d in range(self.outer - 1):
+            self.third(d).start()
+
+    def stage_third(self):
+        total = self.box_b[0, self.o].astype(F32)
+        for d in range(self.outer - 1):
+            self.third(d).wait_recv()
+            total = total + self.box_o[d].astype(F32)
+        return total
+
+    def sent_first(self):
+        self.core().wait_send()
+        for h in range(2):
+            for d in range(self.side - 1):
+                self.first(h, d).wait_send()
+
+    def sent_last(self):
+        for h in range(2):
+            for d in range(self.side - 1):
+                self.second(h, d).wait_send()
+        for d in range(self.outer - 1):
+            self.third(d).wait_send()
+
+
+def boxes_for(devices, rows, width):
+    outer, side, _ = digits(devices)
+    half = width // 2
+    return [
+        pltpu.VMEM((outer, side, side, rows, width), BF16),
+        pltpu.VMEM((side - 1, outer, side, rows, half), BF16),
+        pltpu.VMEM((side - 1, outer, side, rows, half), BF16),
+        pltpu.VMEM((side - 1, outer, rows, width), BF16),
+        pltpu.VMEM((outer - 1, rows, width), BF16),
+    ]
+
+
+def sems_for(devices, count):
+    outer, side, _ = digits(devices)
+    dma = pltpu.SemaphoreType.DMA
+    return [dma((2, count)), dma((2, count, 2, side - 1)), dma((2, count, 2, side - 1)), dma((2, count, outer - 1))]
+
+
+def mixing_kernel(
+    devices, hidden_steps, second_ref, above_ref, expand_ref, reduce_ref, bias_e_ref, bias_r_ref,
+    out_ref, back_ref, grad_r_ref, grad_b_ref, grad_e_ref, rest_e_ref, above_b_ref, act_s, pre_s, grad_s, *rest,
+):
+    step = pl.program_id(0)
+    rows, width = second_ref.shape
+    strip = act_s.shape[1]
+    per = width // strip
+    slices = (len(rest) - 4) // 5
+    sems = rest[5 * slices :]
+    where = neighbours(devices)
+    (o, p, q, c), core_peer, q_peers, p_peers, o_peers = where
+    part = grad_s.shape[-2]
+
+    def mover(k):
+        def other():
+            return grad_s.at[k % 2, :, :, :, 1 - c]
+
+        def mine(spot, cols):
+            return grad_s.at[(k % 2,) + tuple(spot) + (c, slice(None), cols)]
+
+        return Scatter(devices, where, k, rest[5 * k : 5 * k + 5], sems, other, mine)
+
+    movers = [mover(k) for k in range(slices)]
+    w_e = expand_ref[...].reshape(width, strip)
+    w_r = reduce_ref[...].reshape(strip, width)
+
+    @pl.when(step == 0)
+    def _():
+        greet(peers_of(where))
+        out_ref[...] = jnp.broadcast_to(bias_r_ref[...], out_ref.shape)
+        back_ref[...] = jnp.zeros(back_ref.shape, F32)
+        above_b_ref[...] = jnp.sum(above_ref[...].astype(F32), axis=0, keepdims=True)
+
+    pre = dot(second_ref[...], w_e) + bias_e_ref[...]
+    square = pre * pre
+    curve = jnp.tanh(CURVE * pre * (1.0 + 0.044715 * square))
+    hinge = 0.5 * (1.0 + curve)
+    act_s[...] = (pre * hinge).astype(BF16)
+    slope = hinge + 0.5 * pre * (1.0 - curve * curve) * (CURVE * (1.0 + 3 * 0.044715 * square))
+    d_pre = (dot(above_ref[...], w_r, NT) * slope).astype(BF16)
+    pre_s[...] = d_pre
+    grad_b_ref[...] = jnp.sum(d_pre.astype(F32), axis=0, keepdims=True)
+    out_ref[...] += dot(act_s[...], w_r)
+    back_ref[...] += dot(d_pre, w_e, NT)
+    grad_r_ref[...] = dot(act_s[...], above_ref[...], TN).astype(BF16).reshape(grad_r_ref.shape)
+    grad_e = dot(second_ref[...], pre_s[...], TN).astype(BF16)
+    for k in range(slices):
+        for j in range(per):
+            @pl.when(step == k * per + j)
+            def _():
+                if j == 0 and k >= 2:
+                    movers[k - 2].sent_first()
+                grad_s[k % 2, :, :, :, :, :, j * strip : (j + 1) * strip] = grad_e.reshape(grad_s.shape[1:-1] + (strip,))
+                if j == per - 1:
+                    movers[k].begin()
+
+    @pl.when(step >= slices * per)
+    def _():
+        rest_e_ref[...] = grad_e.reshape(rest_e_ref.shape)
+
+    def close(k):
+        grad_e_ref[k * part : (k + 1) * part, :] = movers[k].stage_third()
+
+    final = hidden_steps - 1
+    late = []
+    for k in range(slices):
+        for number, action in enumerate((movers[k].stage_core, movers[k].stage_first, movers[k].stage_second, functools.partial(close, k))):
+            when = (k + 1) * per + number
+            if when > final:
+                late.append((when, -k, action))
+            else:
+                pl.when(step == when)(action)
+
+    @pl.when(step == final)
+    def _():
+        for _, _, action in sorted(late, key=lambda entry: entry[:2]):
+            action()
+        for k in range(max(0, slices - 2), slices):
+            movers[k].sent_first()
+        for k in range(slices):
+            movers[k].sent_last()
+
+
+def mixing(devices, second, above, gathered, bias_e, bias_r, part):
+    rows, width = second.shape
+    hidden = bias_e.shape[1]
+    many = hidden // devices
+    sides = hidden // width
+    strip = STRIP
+    per = width // strip
+    outer, side, core = digits(devices)
+    fixed = pl.BlockSpec((rows, width), lambda i: (0, 0), pipeline_mode=pl.Buffered(1))
+    whole = pl.BlockSpec(memory_space=pltpu.VMEM)
+    scratch = [pltpu.VMEM((rows, strip), BF16)] * 2 + [pltpu.VMEM((2, outer, side, side, core, part, width), BF16)]
+    slices = sides - 1
+    for k in range(slices):
+        scratch += boxes_for(devices, part, width)
+    return pl.pallas_call(
+        functools.partial(mixing_kernel, devices, hidden // strip),
+        grid=(hidden // strip,),
+        in_specs=[
+            fixed, fixed,
+            pl.BlockSpec((devices, part, strip), lambda i: (0, many // part + 1 + i // per, i % per)),
+            pl.BlockSpec((strip // many, many, width), lambda i: (i, 0, 0)),
+            pl.BlockSpec((1, strip), lambda i: (0, i)),
+            pl.BlockSpec((1, width), lambda i: (0, 0)),
+        ],
+        out_specs=[
+            fixed,
+            fixed,
+            pl.BlockSpec((strip // many, many, width), lambda i: (i, 0, 0)),
+            pl.BlockSpec((1, strip), lambda i: (0, i)),
+            pl.BlockSpec((slices * part, width), lambda i: (0, 0)),
+            pl.BlockSpec((devices, part, strip), lambda i: (0, 0, jnp.maximum(i - slices * per, 0))),
+            pl.BlockSpec((1, width), lambda i: (0, 0)),
+        ],
+        out_shape=[
+            jax.ShapeDtypeStruct((rows, width), F32),
+            jax.ShapeDtypeStruct((rows, width), F32),
+            jax.ShapeDtypeStruct((devices, many, width), BF16),
+            jax.ShapeDtypeStruct((1, hidden), F32),
+            jax.ShapeDtypeStruct((slices * part, width), F32),
+            jax.ShapeDtypeStruct((devices, part, width), BF16),
+            jax.ShapeDtypeStruct((1, width), F32),
+        ],
+        scratch_shapes=scratch + sems_for(devices, slices),
+        compiler_params=pltpu.CompilerParams(collective_id=3, has_side_effects=True, vmem_limit_bytes=57 << 20),
+        name="mixing",
+    )(second, above, gathered, gathered, bias_e, bias_r)
+
+
+def turn_kernel(
+    devices, grad_r_ref, grad_e_ref, out_one_ref, d_second_ref, mixed_ref, two_ref, above_ref, combined_ref, live_ref, gain_ref, w_o_ref,
+    bias_r_ref, bias_e_ref,
+    wide_ref, grad_one_ref, one_ref, res_two_ref, grad_o_ref, small_ref, part_e_ref, part_r_ref,
+    attend_s, load_sem, halo_sem, *rest,
+):
+    slots, width = two_ref.shape
+    half = slots // 2
+    tile = 256
+    part = part_e_ref.shape[0]
+    where = neighbours(devices)
+    (o, p, q, c), *_ = where
+    me = lax.axis_index("fsdp")
+    owns, rest = rest[:2], rest[2:]
+    sems = rest[-4:]
+
+    def distant(source, row, rows, k):
+        at = pl.ds(row, rows)
+
+        def other():
+            return source.at[:, :, :, 1 - c, at, :]
+
+        def mine(spot, cols):
+            return owns[k].at[tuple(spot) + (slice(None), cols)]
+
+        def load():
+            return pltpu.make_async_copy(source.at[:, :, :, c, at, :], owns[k], load_sem.at[k])
+
+        return Scatter(devices, where, k, rest[5 * k : 5 * k + 5], sems, other, mine, load)
+
+    movers = [distant(grad_e_ref, 0, part, 0), distant(grad_r_ref, 0, part_r_ref.shape[0], 1)]
+    last = devices - 1
+    left, right = lax.rem(me + last, devices), lax.rem(me + 1, devices)
+    greet(peers_of(where) + [left, right])
+    for mover in movers:
+        mover.begin()
+
+    def to_left():
+        return remote(wide_ref.at[half : 2 * half], wide_ref.at[half + slots :], halo_sem, (0,), left)
+
+    def to_right():
+        return remote(wide_ref.at[2 * half : 3 * half], wide_ref.at[:half], halo_sem, (1,), right)
+
+    small_ref[...] = jnp.zeros(small_ref.shape, F32)
+    gain = gain_ref[...]
+
+    def norm_tile(i, carry):
+        at = pl.ds(pl.multiple_of(i * tile, tile), tile)
+        live = live_ref[at, :]
+        values = out_one_ref[at, :]
+        above = d_second_ref[at, :]
+        center = values - jnp.mean(values, axis=1, keepdims=True)
+        scale = lax.rsqrt(jnp.mean(center * center, axis=1, keepdims=True) + EPS_NORM)
+        center = center * scale
+        small_ref[2:3, :] += jnp.sum(above * center, axis=0, keepdims=True)
+        small_ref[3:4, :] += jnp.sum(above, axis=0, keepdims=True)
+        above = above * gain
+        mean = jnp.mean(above, axis=1, keepdims=True)
+        along = jnp.mean(above * center, axis=1, keepdims=True)
+        total = live * (above_ref[at, :].astype(F32) + scale * (above - mean - center * along))
+        low = total.astype(BF16)
+        grad_one_ref[at, :] = low
+        attend_s[at, :] = low
+        small_ref[4:5, :] += jnp.sum(low.astype(F32), axis=0, keepdims=True)
+        wide_ref[pl.ds(pl.multiple_of(half + i * tile, tile), tile), :] = dot(low, w_o_ref[...], NT).astype(BF16)
+        return carry
+
+    lax.fori_loop(0, half // tile, norm_tile, 0)
+
+    @pl.when(me > 0)
+    def _():
+        to_left().start()
+
+    movers[0].stage_core()
+    lax.fori_loop(half // tile, slots // tile, norm_tile, 0)
+
+    @pl.when(me < last)
+    def _():
+        to_right().start()
+
+    movers[1].stage_core()
+
+    def finish_tile(i, carry):
+        at = pl.ds(pl.multiple_of(i * tile, tile), tile)
+        live = live_ref[at, :]
+        one_ref[at, :] = (live * out_one_ref[at, :]).astype(BF16)
+        res_two_ref[at, :] = (live * (two_ref[at, :].astype(F32) + mixed_ref[at, :])).astype(BF16)
+        return carry
+
+    lax.fori_loop(0, slots // tile, finish_tile, 0)
+    movers[0].stage_first()
+
+    def weights(i, carry):
+        cols = pl.ds(pl.multiple_of(i * tile, tile), tile)
+        many = tile // part
+        grad_o_ref[pl.ds(pl.multiple_of(i * many, many), many)] = (
+            dot(combined_ref[:, cols], attend_s[...], TN).astype(BF16).reshape(many, part, width)
+        )
+        return carry
+
+    lax.fori_loop(0, width // tile, weights, 0)
+    movers[1].stage_first()
+    movers[0].stage_second()
+    small_ref[5:6, :] = bias_r_ref[...]
+    for k in range(bias_e_ref.shape[1] // width):
+        small_ref[6 + k : 7 + k, :] = bias_e_ref[:, k * width : (k + 1) * width]
+    movers[1].stage_second()
+    part_e_ref[...] = movers[0].stage_third()
+    part_r_ref[...] = movers[1].stage_third()
+
+    @pl.when(me > 0)
+    def _():
+        to_right().wait_recv()
+        to_left().wait_send()
+
+    @pl.when(me == 0)
+    def _():
+        wide_ref[:half] = jnp.zeros((half, width), BF16)
+
+    @pl.when(me < last)
+    def _():
+        to_left().wait_recv()
+        to_right().wait_send()
+
+    @pl.when(me == last)
+    def _():
+        wide_ref[half + slots :] = jnp.zeros((half, width), BF16)
+
+    for mover in movers:
+        mover.sent_first()
+        mover.sent_last()
+
+
+def turn(devices, grad_r, grad_e, out_one, d_second, mixed, two, above, combined, live, gain, w_o, bias_r, bias_e):
+    slots, width = two.shape
+    outer, side, core = digits(devices)
+    part, many = grad_e.shape[1], grad_r.shape[1]
+    vmem = pl.BlockSpec(memory_space=pltpu.VMEM)
+    anywhere = pl.BlockSpec(memory_space=pl.ANY)
+    dma = pltpu.SemaphoreType.DMA
+    sizes = [part, many // 2]
+    scratch = [pltpu.VMEM((slots, width), BF16), dma((2,)), dma((2, 2))]
+    scratch += [pltpu.VMEM((outer, side, side, rows, width), BF16) for rows in sizes]
+    for rows in sizes:
+        scratch += boxes_for(devices, rows, width)
+    shape = (outer, side, side, core)
+    rows_low = jax.ShapeDtypeStruct((slots, width), BF16)
+    return pl.pallas_call(
+        functools.partial(turn_kernel, devices),
+        in_specs=[anywhere, anywhere] + [vmem] * 11,
+        out_specs=(vmem,) * 8,
+        out_shape=(
+            jax.ShapeDtypeStruct((2 * slots, width), BF16), rows_low, rows_low, rows_low,
+            jax.ShapeDtypeStruct((devices, part, width), BF16),
+            jax.ShapeDtypeStruct((16, width), F32),
+            jax.ShapeDtypeStruct((part, width), F32),
+            jax.ShapeDtypeStruct((many // 2, width), F32),
+        ),
+        scratch_shapes=scratch + sems_for(devices, len(sizes)),
+        compiler_params=pltpu.CompilerParams(collective_id=5, has_side_effects=True, vmem_limit_bytes=57 << 20),
+        name="turn",
+    )(
+        grad_r.reshape(shape + grad_r.shape[1:]), grad_e.reshape(shape + grad_e.shape[1:]),
+        out_one, d_second, mixed, two, above, combined, live, gain, w_o, bias_r, bias_e,
+    )
+
+
+def tail_kernel(
+    devices, grad_r_ref, grad_o_ref, d_shared_ref, d_value_ref, normed_ref, head_ref, own_ref, end_ref, above_ref, live_ref,
+    gain_ref, w_s_ref, w_v_ref, small_ref,
+    back_ref, out_s_ref, out_v_ref, out_o_ref, out_r_ref, thin_ref, long_ref,
+    side_s, side_in, vector_s, vector_in, grad_s, load_sem, halo_sem, vector_sem, *rest,
+):
+    window, width = normed_ref.shape
+    slots = own_ref.shape[0]
+    half = slots // 2
+    part = out_s_ref.shape[0]
+    many = 2 * out_r_ref.shape[0]
+    tile = 256
+    where = neighbours(devices)
+    (o, p, q, c), core_peer, q_peers, p_peers, o_peers = where
+    me = lax.axis_index("fsdp")
+    outer, side, core = digits(devices)
+    owns, rest = rest[:2], rest[2:]
+    sems = rest[-4:]
+
+    def distant(source, row, rows, k):
+        at = pl.ds(row, rows)
+
+        def other():
+            return source.at[:, :, :, 1 - c, at, :]
+
+        def mine(spot, cols):
+            return owns[k].at[tuple(spot) + (slice(None), cols)]
+
+        def load():
+            return pltpu.make_async_copy(source.at[:, :, :, c, at, :], owns[k], load_sem.at[k])
+
+        return Scatter(devices, where, k, rest[5 * k : 5 * k + 5], sems, other, mine, load)
+
+    def near(j, k):
+        def other():
+            return grad_s.at[j, :, :, :, 1 - c]
+
+        def mine(spot, cols):
+            return grad_s.at[(j,) + tuple(spot) + (c, slice(None), cols)]
+
+        return Scatter(devices, where, k, rest[5 * k : 5 * k + 5], sems, other, mine)
+
+    movers = [
+        distant(grad_r_ref, many // 2, many // 2, 0), distant(grad_o_ref, 0, part, 1), near(0, 2), near(1, 3),
+    ]
+    last = devices - 1
+    left, right = lax.rem(me + last, devices), lax.rem(me + 1, devices)
+    greet(peers_of(where) + [left, right])
+    for k in range(2):
+        movers[k].begin()
+
+    def to_left():
+        return remote(side_s.at[0], side_in.at[1], halo_sem, (0,), left)
+
+    def to_right():
+        return remote(side_s.at[1], side_in.at[0], halo_sem, (1,), right)
+
+    vector_s[...] = small_ref[...]
+    gain = gain_ref[...]
+
+    def norm_tile(ref, row, at):
+        values = ref[pl.ds(row, tile), :].astype(F32)
+        above = dot(d_shared_ref[at, :], w_s_ref[...], NT) + dot(d_value_ref[at, :], w_v_ref[...], NT)
+        center = values - jnp.mean(values, axis=1, keepdims=True)
+        scale = lax.rsqrt(jnp.mean(center * center, axis=1, keepdims=True) + EPS_NORM)
+        center = center * scale
+        vector_s[0:1, :] += jnp.sum(above * center, axis=0, keepdims=True)
+        vector_s[1:2, :] += jnp.sum(above, axis=0, keepdims=True)
+        above = above * gain
+        mean = jnp.mean(above, axis=1, keepdims=True)
+        along = jnp.mean(above * center, axis=1, keepdims=True)
+        return scale * (above - mean - center * along)
+
+    def side_tiles(i, carry):
+        row = pl.multiple_of(i * tile, tile)
+        side_s[0, pl.ds(row, tile), :] = norm_tile(head_ref, row, pl.ds(row, tile)).astype(BF16)
+        at = pl.ds(pl.multiple_of(half + slots + i * tile, tile), tile)
+        side_s[1, pl.ds(row, tile), :] = norm_tile(end_ref, row, at).astype(BF16)
+        return carry
+
+    lax.fori_loop(0, half // tile, side_tiles, 0)
+
+    @pl.when(me > 0)
+    def _():
+        to_left().start()
+
+    @pl.when(me < last)
+    def _():
+        to_right().start()
+
+    movers[0].stage_core()
+
+    def weights(j, ref):
+        wide = tile // part
+
+        def strip(i, carry):
+            cols = pl.ds(pl.multiple_of(i * tile, tile), tile)
+            block = dot(normed_ref[:, cols], ref[...], TN).astype(BF16).reshape(wide // core, core, part, width)
+            for k in range(wide // core):
+                index = i * (wide // core) + k
+                spot = (lax.div(index, side * side), lax.rem(lax.div(index, side), side), lax.rem(index, side))
+                grad_s[(j,) + spot] = block[k]
+            return carry
+
+        lax.fori_loop(0, width // tile, strip, 0)
+
+    weights(0, d_shared_ref)
+    movers[2].begin()
+    movers[1].stage_core()
+    movers[0].stage_first()
+    weights(1, d_value_ref)
+    movers[3].begin()
+    movers[1].stage_first()
+    movers[0].stage_second()
+    movers[2].stage_core()
+
+    def own_tiles(i, carry):
+        row = pl.multiple_of(i * tile, tile)
+        at = pl.ds(pl.multiple_of(half + i * tile, tile), tile)
+        here = pl.ds(row, tile)
+        total = above_ref[here, :].astype(F32) + norm_tile(own_ref, row, at)
+        back_ref[here, :] = (live_ref[here, :] * total).astype(BF16)
+        return carry
+
+    lax.fori_loop(0, slots // tile, own_tiles, 0)
+
+    def vector_copies(stage):
+        group = ([(0, core_peer)], q_peers, p_peers, o_peers)[stage]
+        base = (0, 1, side, 2 * side - 1)[stage]
+        return [
+            remote(vector_s if stage == 0 else vector_in.at[base - 1], vector_in.at[base + d], vector_sem, (base + d,), device)
+            for d, (_, device) in enumerate(group)
+        ]
+
+    def vector_stage(stage):
+        base = (0, 1, side, 2 * side - 1)[stage]
+        copies = vector_copies(stage)
+        total = vector_s[...] if stage == 0 else vector_in[base - 1]
+        for d, copy in enumerate(copies):
+            copy.wait_recv()
+            total = total + vector_in[base + d]
+        vector_in[base + len(copies) - 1] = total
+
+    for copy in vector_copies(0):
+        copy.start()
+    movers[3].stage_core()
+    movers[1].stage_second()
+    out_r_ref[...] = movers[0].stage_third()
+    movers[2].stage_first()
+    vector_stage(0)
+    for copy in vector_copies(1):
+        copy.start()
+    movers[3].stage_first()
+    out_o_ref[...] = movers[1].stage_third()
+    movers[2].stage_second()
+    vector_stage(1)
+    for copy in vector_copies(2):
+        copy.start()
+    movers[3].stage_second()
+    vector_stage(2)
+    for copy in vector_copies(3):
+        copy.start()
+
+    @pl.when(me > 0)
+    def _():
+        to_right().wait_recv()
+
+    @pl.when(me == 0)
+    def _():
+        side_in[0] = jnp.zeros((half, width), BF16)
+
+    @pl.when(me < last)
+    def _():
+        to_left().wait_recv()
+
+    @pl.when(me == last)
+    def _():
+        side_in[1] = jnp.zeros((half, width), BF16)
+
+    for k in range(2):
+        at = slice(k * half, (k + 1) * half)
+        back_ref[at, :] = (back_ref[at, :].astype(F32) + side_in[k].astype(F32)).astype(BF16)
+    out_s_ref[...] = movers[2].stage_third()
+    vector_stage(3)
+    out_v_ref[...] = movers[3].stage_third()
+    vectors = 2 * side + outer - 3
+    total = vector_in[vectors]
+    thin_ref[...] = pltpu.roll(total, lax.rem(width - me * part, width), 1)[:, :DH]
+    each = long_ref.shape[1]
+    long_rows = [total[6 + k : 7 + k, :] for k in range(devices * each // width)]
+    mine = lax.div(me * each, width)
+    chosen = long_rows[0]
+    for k in range(1, len(long_rows)):
+        chosen = jnp.where(mine == k, long_rows[k], chosen)
+    long_ref[...] = pltpu.roll(chosen, lax.rem(width - lax.rem(me * each, width), width), 1)[:, :each]
+    for stage in range(4):
+        for copy in vector_copies(stage):
             copy.wait_send()
 
-
-def reduce_scatter(devices, arrays, cuts):
+    @pl.when(me > 0)
+    def _():
+        to_left().wait_send()
+
+    @pl.when(me < last)
+    def _():
+        to_right().wait_send()
+
+    for mover in movers:
+        mover.sent_first()
+        mover.sent_last()
+
+
+def tail(devices, grad_r, grad_o, d_shared, d_values, normed, head, own, end, above, live, gain, w_s, w_v, small):
+    window, width = normed.shape
+    slots = own.shape[0]
     outer, side, core = digits(devices)
-    plan = []
-    for k, array in enumerate(arrays):
-        rows = array.shape[1] // cuts[k]
-        plan += [(k, i * rows, rows) for i in range(cuts[k])]
-    width = arrays[0].shape[2]
-    half = width // 2
-    count = len(plan)
-    vmem = pltpu.VMEM
-    scratch = [vmem((outer, side, side, r, width), BF16) for _, _, r in plan]
-    scratch += [vmem((outer, side, side, r, width), BF16) for _, _, r in plan]
-    for _, _, r in plan:
-        scratch += [vmem((side - 1, outer, side, r, half), BF16)] * 2
-    scratch += [vmem((side - 1, outer, r, width), BF16) for _, _, r in plan]
-    scratch += [vmem((outer - 1, r, width), BF16) for _, _, r in plan]
+    part, many = grad_o.shape[1], grad_r.shape[1]
+    each = many
+    vmem = pl.BlockSpec(memory_space=pltpu.VMEM)
+    anywhere = pl.BlockSpec(memory_space=pl.ANY)
     dma = pltpu.SemaphoreType.DMA
-    scratch += [dma((count,)), dma((2, count)), dma((2, count, 2, side - 1)), dma((2, count, 2, side - 1)), dma((2, count, outer - 1))]
+    sizes = [many // 2, part, part, part]
+    scratch = [
+        pltpu.VMEM((2, slots // 2, width), BF16), pltpu.VMEM((2, slots // 2, width), BF16),
+        pltpu.VMEM((16, width), F32), pltpu.VMEM((2 * side + outer - 2, 16, width), F32),
+        pltpu.VMEM((2, outer, side, side, core, part, width), BF16),
+        dma((2,)), dma((2, 2)), dma((2, 2 * side + outer - 2)),
+    ]
+    scratch += [pltpu.VMEM((outer, side, side, rows, width), BF16) for rows in sizes[:2]]
+    for rows in sizes:
+        scratch += boxes_for(devices, rows, width)
+    shape = (outer, side, side, core)
     return pl.pallas_call(
-        functools.partial(reduce_kernel, devices, plan, len(arrays)),
-        out_shape=tuple(jax.ShapeDtypeStruct(array.shape[1:], F32) for array in arrays),
-        in_specs=[pl.BlockSpec(memory_space=pl.ANY)] * len(arrays),
-        out_specs=tuple(pl.BlockSpec(memory_space=pltpu.VMEM) for _ in arrays),
-        scratch_shapes=scratch,
-        compiler_params=pltpu.CompilerParams(collective_id=1, has_side_effects=True, vmem_limit_bytes=56 << 20),
-        name="reduce_scatter",
-    )(*[array.reshape(outer, side, side, core, *array.shape[1:]) for array in arrays])
+        functools.partial(tail_kernel, devices),
+        in_specs=[anywhere, anywhere] + [vmem] * 12,
+        out_specs=(vmem,) * 7,
+        out_shape=(
+            jax.ShapeDtypeStruct((slots, width), BF16),
+            jax.ShapeDtypeStruct((part, width), F32),
+            jax.ShapeDtypeStruct((part, width), F32),
+            jax.ShapeDtypeStruct((part, width), F32),
+            jax.ShapeDtypeStruct((many // 2, width), F32),
+            jax.ShapeDtypeStruct((16, DH), F32),
+            jax.ShapeDtypeStruct((1, each), F32),
+        ),
+        scratch_shapes=scratch + sems_for(devices, len(sizes)),
+        compiler_params=pltpu.CompilerParams(collective_id=4, has_side_effects=True, vmem_limit_bytes=57 << 20),
+        name="tail",
+    )(
+        grad_r.reshape(shape + grad_r.shape[1:]), grad_o.reshape(shape + grad_o.shape[1:]),
+        d_shared, d_values, normed, head, own, end, above, live, gain, w_s, w_v, small,
+    )
 
 
 def rank_kernel(length_ref, target_ref, bucket_ref, block_ref, info_ref, before_s):
@@ -853,10 +1324,6 @@
 
     def to_sides(head, tail):
         return lax.ppermute(tail, "fsdp", up), lax.ppermute(head, "fsdp", down)
-
-    def widen(own):
-        head, tail = to_sides(own[:half], own[half:])
-        return jnp.concatenate([head, own, tail], axis=0)
 
     def narrow(wide):
         head, tail = to_sides(wide[:half], wide[half + slots :])
@@ -897,11 +1364,7 @@
     live = ((base + jnp.arange(slots, dtype=jnp.int32)) < info[6]).astype(F32)[:, None]
     slot_one = input_one.astype(F32)
     slot_two = input_two.astype(F32)
-    above_one = live * upstream_one.astype(F32)
-    above_two = live * upstream_two.astype(F32)
-
     two_head, two_tail = to_sides(input_two[:half], input_two[half:])
-    two_window = jnp.concatenate([two_head, input_two, two_tail], axis=0).astype(F32)
     normed, shared, values, code = project(
         info, two_head, input_two, two_tail, gain_a, shift_a, full_shared, full_value, packed
     )
@@ -911,64 +1374,38 @@
     attended = dot(combined, full_output) + bias_o
     out_one = slot_one + live * attended
     second = layer_norm(out_one, gain_m, shift_m).astype(BF16)
-    d_reduce = above_two.astype(BF16)
-    grad_bias_reduce = jnp.sum(d_reduce, axis=0, dtype=F32)
-    mixed, d_second, grad_reduce, grad_expand, grad_bias_expand = mixing(
-        second, d_reduce, second_gather, bias_e, bias_r, part
+    d_reduce = (live * upstream_two.astype(F32)).astype(BF16)
+    mixed, d_second, grad_reduce, grad_bias_expand, grad_expand, last_expand, grad_bias_reduce = mixing(
+        devices, second, d_reduce, second_gather, bias_e, bias_r, part
     )
-    out_two = slot_two + live * mixed
-    d_one_mix, grad_gain_m, grad_shift_m = norm_back(out_one, gain_m, shift_m, d_second)
-    total_one = above_one + d_one_mix
-    d_attend = (live * total_one).astype(BF16)
-    grad_output = dot(combined, d_attend, TN)
-    grad_bias_output = jnp.sum(d_attend, axis=0, dtype=F32)
-    d_combined = dot(d_attend, full_output, NT).astype(BF16)
+    d_combined, grad_one, result_one, result_two, grad_output, small, last_expand, first_reduce = turn(
+        devices, grad_reduce, last_expand, out_one, d_second, mixed, input_two, upstream_one, combined, live, gain_m,
+        full_output, grad_bias_reduce, grad_bias_expand,
+    )
     d_shared, d_values = attend_back(
-        info, shared, values, code, spread, combined_window, widen(d_combined), lse, lone
+        info, shared, values, code, spread, combined_window, d_combined, lse, lone
     )
-    grad_shared = dot(normed, d_shared, TN)
-    grad_value = dot(normed, d_values, TN)
-    d_normed = dot(d_shared, full_shared, NT) + dot(d_values, full_value, NT)
-    d_two_window, grad_gain_a, grad_shift_a = norm_back(two_window, gain_a, shift_a, d_normed)
-    own, other = narrow(d_two_window.astype(BF16))
-    back_two = above_two + own.astype(F32) + other.astype(F32)
-
-    def split(whole):
-        return whole.astype(BF16).reshape(devices, -1, width)
-
-    small = jnp.concatenate(
-        [
-            member.reshape(devices, -1)
-            for member in (
-                grad_gain_a, grad_shift_a, grad_gain_m, grad_shift_m, grad_bias_output, grad_bias_reduce, grad_bias_expand
-            )
-        ],
-        axis=1,
+    grad_two, grad_shared, grad_value, grad_output, grad_reduce, thin, long = tail(
+        devices, grad_reduce, grad_output, d_shared, d_values, normed,
+        two_head, input_two, two_tail, upstream_two, live, gain_a, full_shared, full_value, small,
     )
-    small = jnp.zeros((devices, 8, width), BF16).at[:, 0, : small.shape[1]].set(small.astype(BF16))
-    grad_reduce, grad_expand, grad_output, grad_shared, grad_value, small = reduce_scatter(
-        devices,
-        (grad_reduce, grad_expand, split(grad_output), split(grad_shared), split(grad_value), small),
-        (2, 2, 1, 1, 1, 1),
-    )
-    small = small[0]
     return (
-        (live * out_one).astype(BF16),
-        (live * out_two).astype(BF16),
-        (live * total_one).astype(BF16),
-        (live * back_two).astype(BF16),
+        result_one,
+        result_two,
+        grad_one,
+        grad_two,
         grad_shared,
         grad_value,
         grad_output,
-        jnp.concatenate([grad_expand[k * part : (k + 1) * part] for k in range(sides)], axis=1),
-        grad_reduce,
-        small[:part],
-        small[part : 2 * part],
-        small[2 * part : 3 * part],
-        small[3 * part : 4 * part],
-        small[4 * part : 5 * part],
-        small[6 * part : 6 * part + hidden // devices],
-        small[5 * part : 6 * part],
+        jnp.concatenate([grad_expand[k * part : (k + 1) * part] for k in range(sides - 1)] + [last_expand], axis=1),
+        jnp.concatenate([first_reduce, grad_reduce], axis=0),
+        thin[0, :part],
+        thin[1, :part],
+        thin[2, :part],
+        thin[3, :part],
+        thin[4, :part],
+        long.reshape(-1),
+        thin[5, :part],
     )
 
 

time: 615 us -> 595 us (0.967)
  the two profiles are of different devices: /device:TPU:1 before, /device:TPU:0 now
where the time goes in v4:
time: 595 us; the launch traced here: 589 us
  Pallas kernels  486 us (82%)
  local copies, waits for them, and re-layouts  35.9 us (6%)
  starting transfers between devices  30.2 us (5%)
  other arithmetic  17.3 us (3%)
  between operations  14.9 us (3%)
    pallas_call x1, Pallas kernels, tail(): pl.pallas_call(functools.partial(tail_kernel, devices), in_specs=[anywher...  146 us
    pallas_call x1, Pallas kernels, mixing(): pl.pallas_call(functools.partial(mixing_kernel, devices, hidden // strip)...  101 us
    pallas_call x1, Pallas kernels, gather(): pl.pallas_call(functools.partial(gather_kernel, devices, count), out_shap...  82.9 us
    pallas_call x1, Pallas kernels, turn(): pl.pallas_call(functools.partial(turn_kernel, devices), in_specs=[anywher...  78.8 us
    pallas_call x1, Pallas kernels, attend_back(): pl.pallas_call(back_kernel, grid_spec=pltpu.PrefetchScalarGridSpec(num_sc...  35.8 us
    ppermute x4, starting transfers between devices, to_sides(): return (lax.ppermute(tail, 'fsdp', up), lax.ppermute(head, 'fsdp', down))  30.1 us
    unnamed x85, local copies, waits for them, and re-layouts  25.1 us
    pallas_call x1, Pallas kernels, attend(): pl.pallas_call(attend_kernel, grid_spec=pltpu.PrefetchScalarGridSpec(num_...  20 us
  transfers between devices with their start and end apart: 5, of which 0 were waited for; matrix products, arithmetic and copies ran while one was open for 3% of the time, Pallas kernels for 21%

profile of v4, /device:TPU:0, one launch (start us, length us, event | category | flops | bytes accessed | tf_op | source)
XLA Modules:
  0.0 588.7 jit_solution(5031091653162286833)
XLA Ops:
  13.6 3.0 fusion.20
  16.6 2.4 collective-permute-start
  20.6 5.1 rank_blocks.1
  26.6 82.9 %gather.1 = (bf16[4,2,2,2,32,1024]{5,4,3,2,1,0:T(8,128)(2,1)}, bf16[4,2,2,2,32,1024]{5,4,3,2,1,0:T(8,128)(2,1)}, bf16[4,2,2,2,56,1024]{5,4,3,2,1,0:T(8,128)(2,1)}) custom-call(bf16[32,1024]{1,0:T(8,128)(2,1)} %refs_0_.1, bf16[32,1024]{1,0:T(8,128)(2,1)} %refs_1_.1, bf16[56,1024]{1,0:T(8,128)(2,1)} %maximum_maximum_fusion.refs_2_), custom_call_target="tpu_custom_call" | custom-call | tf_op jit(solution)/shard_map/gather/pallas_call | solution.py:1295
  109.6 1.7 convert_reduce_fusion
  112.0 3.4 copy-done.3
  115.4 1.8 copy-done.4
  117.2 1.6 copy-done.5
  118.8 16.0 %project.1 = (bf16[2048,1024]{1,0:T(8,128)(2,1)}, bf16[2048,1024]{1,0:T(8,128)(2,1)}, bf16[2048,1024]{1,0:T(8,128)(2,1)}, bf16[32,2048]{1,0:T(8,128)(2,1)S(1)}) custom-call(s32[8]{0:T(128)S(1)} %get-tuple-element.52.info_ref.low_ref, bf16[512,1024]{1,0:T(8,128)(2,1)S(1)} %collective-permute-done.head_ref, bf16[1024,1024]{1,0:T(8,128)(2,1)S(1)} %copy-done.2, ...), custom_call_target="tpu_custom_call" | custom-call | tf_op jit(solution)/shard_map/project/pallas_call | solution.py:1205
  134.9 20.0 %attend.1 = (bf16[2048,1024]{1,0:T(8,128)(2,1)S(1)}, f32[8,1,2048]{2,1,0:T(1,128)S(1)}, f32[8,1,2048]{2,1,0:T(1,128)S(1)}) custom-call(s32[8]{0:T(128)S(1)} %get-tuple-element.52.info_ref.low_ref, bf16[2048,1024]{1,0:T(8,128)(2,1)} %get-tuple-element.57.q_ref, bf16[2048,1024]{1,0:T(8,128)(2,1)} %get-tuple-element.58.v_ref, ...), custom_call_target="tpu_custom_call" | custom-call | flops 32212254720 | bytes 12582912 | tf_op jit(solution)/shard_map/attend/pallas_call | solution.py:321
  154.9 2.0 copy-done.8
  158.0 25.1 %collective-permute-start.2 = (bf16[512,1024]{1,0:T(8,128)(2,1)}, bf16[512,1024]{1,0:T(8,128)(2,1)S(1)}, u32[]{:S(2)}, u32[]{:S(2)}) collective-permute-start(bf16[512,1024]{1,0:T(8,128)(2,1)} %get-tuple-element.88), channel_id=1, source_target_pairs={{0,1},{1,2},{2,3},{3,4},{4,5},{5,6},{6,7},{7,8},{8,9},{9,10},{10,1... | collective-permute-start | bytes 3145736 | tf_op jit(solution)/shard_map/ppermute | solution.py:1326
  186.6 1.5 fusion.live_ref
  188.1 3.3 multiply_convert_fusion.above_ref
  191.4 3.5 maximum_add_fusion.combined_ref
  195.0 1.9 slice.125
  197.2 4.6 fusion.23
  202.5 2.1 add_convert_fusion.second_ref
  204.6 101.4 %mixing.1 = (f32[1024,1024]{1,0:T(8,128)}, f32[1024,1024]{1,0:T(8,128)}, bf16[32,128,1024]{2,1,0:T(8,128)(2,1)}, f32[1,4096]{1,0:T(1,128)}, f32[96,1024]{1,0:T(8...) custom-call(bf16[1024,1024]{1,0:T(8,128)(2,1)} %add_convert_fusion.second_ref, ...), custom_call_target="tpu_custom_call" | custom-call | tf_op jit(solution)/shard_map/mixing/pallas_call | solution.py:632
  307.0 78.8 %turn.1 = (bf16[2048,1024]{1,0:T(8,128)(2,1)}, bf16[1024,1024]{1,0:T(8,128)(2,1)}, bf16[1024,1024]{1,0:T(8,128)(2,1)}, bf16[1024,1024]{1,0:T(8,128)(2,1)}, bf16[...) custom-call(bf16[4,2,2,2,128,1024]{5,4,3,2,1,0:T(8,128)(2,1)} %bitcast.51, ...), custom_call_target="tpu_custom_call" | custom-call | tf_op jit(solution)/shard_map/turn/pallas_call | solution.py:813
  385.9 35.8 %attend_back.1 = (bf16[2048,1024]{1,0:T(8,128)(2,1)S(1)}, bf16[2048,1024]{1,0:T(8,128)(2,1)}) custom-call(s32[8]{0:T(128)S(1)} %get-tuple-element.52.info_ref.low_ref, bf16[2048,1024]{1,0:T(8,128)(2,1)} %get-tuple-element.57.q_ref, bf16[2048,1024]{1,0:T(8,128)(2,1)} %get-tuple-element.58.v_ref, bf16[32,2048]{1,0:T(8,128)(2,1)S(1)} %get-tuple-element.59.code_ref, ...), custom_call_target="tpu_custom_call" | custom-call | flops 64424509440 | bytes 25165824 | tf_op jit(solution)/shard_map/attend_back/pallas_call | solution.py:344
  421.7 2.0 copy-done.6
  423.7 145.7 %tail.1 = (bf16[1024,1024]{1,0:T(8,128)(2,1)}, f32[32,1024]{1,0:T(8,128)}, f32[32,1024]{1,0:T(8,128)}, f32[32,1024]{1,0:T(8,128)}, f32[64,1024]{1,0:T(8,128)}, /*index=5*/f32[16,128]{1,0:T(8,128)}, f32[1,128]{1,0:T(1,128)}) custom-call(bf16[4,2,2,2,128,1024]{5,4,3,2,1,0:T(8,128)(2,1)} %bitcast.52, bf16[4,2,2,2,32,1024]{5,4,3,2,1,0:T(8,128)(2,1)} %bitcast.55, ...), custom_call_target="tpu_custom_call" | custom-call | tf_op jit(solution)/shard_map/tail/pallas_call | solution.py:1065
  570.9 1.8 pad_maximum_fusion.1
  (116 shorter events, 26.1 us)
Async XLA Ops:
  7.2 18.6 %copy-start = (f32[128]{0:T(128)S(1)}, f32[128]{0:T(128)}, u32[]{:S(2)}) copy-start(f32[128]{0:T(128)} %param.36) | copy-start | bytes 1540
  7.2 13.1 %copy-start.28 = (f32[32]{0:T(128)S(1)}, f32[32]{0:T(128)}, u32[]{:S(2)}) copy-start(f32[32]{0:T(128)} %param.31) | copy-start | bytes 388
  7.2 13.1 %copy-start.29 = (f32[32]{0:T(128)S(1)}, f32[32]{0:T(128)}, u32[]{:S(2)}) copy-start(f32[32]{0:T(128)} %param.32) | copy-start | bytes 388
  7.2 13.1 %copy-start.30 = (f32[32]{0:T(128)S(1)}, f32[32]{0:T(128)}, u32[]{:S(2)}) copy-start(f32[32]{0:T(128)} %param.33) | copy-start | bytes 388
  7.2 13.1 %copy-start.31 = (f32[32]{0:T(128)S(1)}, f32[32]{0:T(128)}, u32[]{:S(2)}) copy-start(f32[32]{0:T(128)} %param.34) | copy-start | bytes 388
  7.2 13.1 %copy-start.32 = (f32[32]{0:T(128)S(1)}, f32[32]{0:T(128)}, u32[]{:S(2)}) copy-start(f32[32]{0:T(128)} %param.35) | copy-start | bytes 388
  7.3 13.1 %copy-start.33 = (f32[32]{0:T(128)S(1)}, f32[32]{0:T(128)}, u32[]{:S(2)}) copy-start(f32[32]{0:T(128)} %param.37) | copy-start | bytes 388
  7.3 13.4 %copy-start.10 = (s32[1,32,1024]{2,1,0:T(8,128)S(1)}, s32[1,32,1024]{2,1,0:T(8,128)}, u32[]{:S(2)}) copy-start(s32[1,32,1024]{2,1,0:T(8,128)} %param.25) | copy-start | bytes 393220
  7.3 13.4 %copy-start.12 = (s32[32]{0:T(128)S(1)}, s32[32]{0:T(128)}, u32[]{:S(2)}) copy-start(s32[32]{0:T(128)} %length_ref.1) | copy-start | bytes 388
  7.3 13.3 %copy-start.13 = (s32[32]{0:T(128)S(1)}, s32[32]{0:T(128)}, u32[]{:S(2)}) copy-start(s32[32]{0:T(128)} %target_ref.1) | copy-start | bytes 388
  7.3 187.7 %all-gather.3.cloned.1.call-start = ((), (), s32[]{:S(2)}) async-start(), calls=%async_computation | async-start | bytes 19464192 | tf_op jit(solution)/shard_map/all_gather | solution.py:1347
  9.2 102.8 %copy-start.2 = (bf16[1024,1024]{1,0:T(8,128)(2,1)S(1)}, bf16[1024,1024]{1,0:T(8,128)(2,1)}, u32[]{:S(2)}) copy-start(bf16[1024,1024]{1,0:T(8,128)(2,1)} %own_ref.3) | copy-start | bytes 6291460
  16.6 95.4 %collective-permute-start = (bf16[512,1024]{1,0:T(8,128)(2,1)}, bf16[512,1024]{1,0:T(8,128)(2,1)S(1)}, u32[]{:S(2)}, u32[]{:S(2)}) collective-permute-start(bf16[512,1024]{1,0:T(8,128)(2,1)} %get-tuple-element.91), channel_id=1, source_target_pairs={{0,1},{1,2},{2,3},{3,4},{4,5},{5,6},{6,7},{7,8},{8,9},{9,10},{10,1... | collective-permute-start | bytes 3145736 | tf_op jit(solution)/shard_map/ppermute | solution.py:1326
  19.0 93.0 %collective-permute-start.1 = (bf16[512,1024]{1,0:T(8,128)(2,1)}, bf16[512,1024]{1,0:T(8,128)(2,1)}, u32[]{:S(2)}, u32[]{:S(2)}) collective-permute-start(bf16[512,1024]{1,0:T(8,128)(2,1)} %get-tuple-element.90), channel_id=1, source_target_pairs={{1,0},{2,1},{3,2},{4,3},{5,4},{6,5},{7,6},{8,7},{9,8},{10,9},{11,1... | collective-permute-start | bytes 3145736 | tf_op jit(solution)/shard_map/ppermute | solution.py:1326
  111.9 22.9 %copy-start.11 = (f32[1,1024]{1,0:T(1,128)}, f32[1,1024]{1,0:T(1,128)S(1)}, u32[]{:S(2)}) copy-start(f32[1,1024]{1,0:T(1,128)S(1)} %get-tuple-element.100.gain_ref) | copy-start | bytes 12292
  112.0 90.5 %copy-start.27 = (f32[1,1024]{1,0:T(1,128)}, f32[1,1024]{1,0:T(1,128)S(1)}, u32[]{:S(2)}) copy-start(f32[1,1024]{1,0:T(1,128)S(1)} %get-tuple-element.97.gain_ref) | copy-start | bytes 12292
  112.0 22.9 %copy-start.7 = (bf16[512,1024]{1,0:T(8,128)(2,1)}, bf16[512,1024]{1,0:T(8,128)(2,1)S(1)}, u32[]{:S(2)}) copy-start(bf16[512,1024]{1,0:T(8,128)(2,1)S(1)} %collective-permute-done.head_ref) | copy-start | bytes 3145732
  158.0 33.5 %collective-permute-start.2 = (bf16[512,1024]{1,0:T(8,128)(2,1)}, bf16[512,1024]{1,0:T(8,128)(2,1)S(1)}, u32[]{:S(2)}, u32[]{:S(2)}) collective-permute-start(bf16[512,1024]{1,0:T(8,128)(2,1)} %get-tuple-element.88), channel_id=1, source_target_pairs={{0,1},{1,2},{2,3},{3,4},{4,5},{5,6},{6,7},{7,8},{8,9},{9,10},{10,1... | collective-permute-start | bytes 3145736 | tf_op jit(solution)/shard_map/ppermute | solution.py:1326
  183.1 8.3 %collective-permute-start.3 = (bf16[512,1024]{1,0:T(8,128)(2,1)S(1)}, bf16[512,1024]{1,0:T(8,128)(2,1)}, u32[]{:S(2)}, u32[]{:S(2)}) collective-permute-start(bf16[512,1024]{1,0:T(8,128)(2,1)S(1)} %get-tuple-element.89), channel_id=1, source_target_pairs={{1,0},{2,1},{3,2},{4,3},{5,4},{6,5},{7,6},{8,7},{9,8},{10,9},{11,1... | collective-permute-start | bytes 3145736 | tf_op jit(solution)/shard_map/ppermute | solution.py:1326
  185.0 6.4 %copy-start.9 = (bf16[2048,1024]{1,0:T(8,128)(2,1)S(1)}, bf16[2048,1024]{1,0:T(8,128)(2,1)}, u32[]{:S(2)}) copy-start(bf16[2048,1024]{1,0:T(8,128)(2,1)} %copy-done.8) | copy-start | bytes 12582916
  423.7 147.2 %copy-start.22 = (f32[64,1024]{1,0:T(8,128)S(1)}, f32[64,1024]{1,0:T(8,128)}, u32[]{:S(2)}) copy-start(f32[64,1024]{1,0:T(8,128)} %get-tuple-element.84) | copy-start | bytes 786436
  423.7 149.0 %copy-start.26 = (f32[32,1024]{1,0:T(8,128)S(1)}, f32[32,1024]{1,0:T(8,128)}, u32[]{:S(2)}) copy-start(f32[32,1024]{1,0:T(8,128)} %get-tuple-element.83) | copy-start | bytes 393220
  423.7 149.8 %copy-start.19 = (bf16[1024,1024]{1,0:T(8,128)(2,1)S(1)}, bf16[1024,1024]{1,0:T(8,128)(2,1)}, u32[]{:S(2)}) copy-start(bf16[1024,1024]{1,0:T(8,128)(2,1)} %get-tuple-element.127) | copy-start | bytes 6291460
  574.9 6.6 %copy-start.1 = (f32[128]{0:T(128)S(1)}, f32[128]{0:T(128)}, u32[]{:S(2)}) copy-start(f32[128]{0:T(128)} %param.36) | copy-start | bytes 1540
  (16 other events, 47.3 us)
Sparse Core Ops, SparseCore 0:
  13.7 157.9 all-gather.2

commit v5 on v4

--- a/solution.py
+++ b/solution.py
@@ -513,15 +513,53 @@
             self.third(d).wait_send()
 
 
-def boxes_for(devices, rows, width):
-    outer, side, _ = digits(devices)
+class Unit(Scatter):
+    def __init__(self, unit, devices, *rest, **named):
+        super().__init__(devices, *rest, **named)
+        self.planes, self.outer, self.unit = self.outer, 1, unit
+
+    def third(self, d=None):
+        if d is not None:
+            return remote(self.box_b.at[0, 0], self.box_o.at[d], self.sem_o, (self.slot, d), self.core_peer)
+        me = lax.axis_index("fsdp")
+        device = me + (self.unit - self.o) * (self.side * self.side * 2)
+        d = lax.rem(self.o - self.unit + 2 * self.planes - 1, self.planes)
+        return remote(self.box_b.at[0, 0], self.box_o.at[d], self.sem_o, (self.slot, d), device)
+
+    def stage_second(self):
+        super().stage_second()
+
+        @pl.when(self.o != self.unit)
+        def _():
+            self.third().start()
+
+    def close(self, ref):
+        @pl.when(self.o == self.unit)
+        def _():
+            total = self.box_b[0, 0].astype(F32)
+            for d in range(self.planes - 1):
+                self.third(d).wait_recv()
+                total = total + self.box_o[d].astype(F32)
+            ref[...] = total
+
+    def sent_last(self):
+        super().sent_last()
+
+        @pl.when(self.o != self.unit)
+        def _():
+            self.third().wait_send()
+
+
+def boxes_for(devices, rows, width, unit=False):
+    planes, side, _ = digits(devices)
+    outer = 1 if unit else planes
     half = width // 2
     return [
         pltpu.VMEM((outer, side, side, rows, width), BF16),
         pltpu.VMEM((side - 1, outer, side, rows, half), BF16),
         pltpu.VMEM((side - 1, outer, side, rows, half), BF16),
         pltpu.VMEM((side - 1, outer, rows, width), BF16),
-        pltpu.VMEM((outer - 1, rows, width), BF16),
+        pltpu.VMEM((planes - 1, rows, width), BF16),
     ]
 
 
@@ -533,14 +571,14 @@
 
 def mixing_kernel(
     devices, hidden_steps, second_ref, above_ref, expand_ref, reduce_ref, bias_e_ref, bias_r_ref,
-    out_ref, back_ref, grad_r_ref, grad_b_ref, grad_e_ref, rest_e_ref, above_b_ref, act_s, pre_s, grad_s, *rest,
+    out_ref, back_ref, grad_b_ref, grad_e_ref, rest_e_ref, rest_r_ref, grad_r_ref, above_b_ref, act_s, pre_s, grad_s, unit_s, *rest,
 ):
     step = pl.program_id(0)
     rows, width = second_ref.shape
     strip = act_s.shape[1]
     per = width // strip
-    slices = (len(rest) - 4) // 5
-    sems = rest[5 * slices :]
+    slices = (len(rest) - 4) // 10
+    sems = rest[10 * slices :]
     where = neighbours(devices)
     (o, p, q, c), core_peer, q_peers, p_peers, o_peers = where
     part = grad_s.shape[-2]
@@ -554,7 +592,18 @@
 
         return Scatter(devices, where, k, rest[5 * k : 5 * k + 5], sems, other, mine)
 
+    def unit(k):
+        def other():
+            return unit_s.at[k % 2, :, :, :, 1 - c]
+
+        def mine(spot, cols):
+            return unit_s.at[(k % 2,) + tuple(spot) + (c, slice(None), cols)]
+
+        slot = slices + k
+        return Unit(k, devices, where, slot, rest[5 * slot : 5 * slot + 5], sems, other, mine)
+
     movers = [mover(k) for k in range(slices)]
+    units = [unit(k) for k in range(slices)]
     w_e = expand_ref[...].reshape(width, strip)
     w_r = reduce_ref[...].reshape(strip, width)
 
@@ -576,7 +625,7 @@
     grad_b_ref[...] = jnp.sum(d_pre.astype(F32), axis=0, keepdims=True)
     out_ref[...] += dot(act_s[...], w_r)
     back_ref[...] += dot(d_pre, w_e, NT)
-    grad_r_ref[...] = dot(act_s[...], above_ref[...], TN).astype(BF16).reshape(grad_r_ref.shape)
+    grad_r = dot(act_s[...], above_ref[...], TN).astype(BF16)
     grad_e = dot(second_ref[...], pre_s[...], TN).astype(BF16)
     for k in range(slices):
         for j in range(per):
@@ -584,13 +633,18 @@
             def _():
                 if j == 0 and k >= 2:
                     movers[k - 2].sent_first()
+                    units[k - 2].sent_first()
+                half = unit_s.shape[2] // per
+                unit_s[k % 2, 0, j * half : (j + 1) * half] = grad_r.reshape((half,) + unit_s.shape[3:])
                 grad_s[k % 2, :, :, :, :, :, j * strip : (j + 1) * strip] = grad_e.reshape(grad_s.shape[1:-1] + (strip,))
                 if j == per - 1:
                     movers[k].begin()
+                    units[k].begin()
 
     @pl.when(step >= slices * per)
     def _():
         rest_e_ref[...] = grad_e.reshape(rest_e_ref.shape)
+        rest_r_ref[...] = grad_r.reshape(rest_r_ref.shape)
 
     def close(k):
         grad_e_ref[k * part : (k + 1) * part, :] = movers[k].stage_third()
@@ -598,21 +652,28 @@
     final = hidden_steps - 1
     late = []
     for k in range(slices):
-        for number, action in enumerate((movers[k].stage_core, movers[k].stage_first, movers[k].stage_second, functools.partial(close, k))):
+        finish = functools.partial(units[k].close, grad_r_ref)
+        for number, actions in enumerate((
+            (movers[k].stage_core, units[k].stage_core), (movers[k].stage_first, units[k].stage_first),
+            (movers[k].stage_second, units[k].stage_second), (functools.partial(close, k), finish),
+        )):
             when = (k + 1) * per + number
-            if when > final:
-                late.append((when, -k, action))
-            else:
-                pl.when(step == when)(action)
+            for order, action in enumerate(actions):
+                if when > final:
+                    late.append((when, -k, order, action))
+                else:
+                    pl.when(step == when)(action)
 
     @pl.when(step == final)
     def _():
-        for _, _, action in sorted(late, key=lambda entry: entry[:2]):
+        for *_, action in sorted(late, key=lambda entry: entry[:3]):
             action()
         for k in range(max(0, slices - 2), slices):
             movers[k].sent_first()
+            units[k].sent_first()
         for k in range(slices):
             movers[k].sent_last()
+            units[k].sent_last()
 
 
 def mixing(devices, second, above, gathered, bias_e, bias_r, part):
@@ -627,8 +688,11 @@
     whole = pl.BlockSpec(memory_space=pltpu.VMEM)
     scratch = [pltpu.VMEM((rows, strip), BF16)] * 2 + [pltpu.VMEM((2, outer, side, side, core, part, width), BF16)]
     slices = sides - 1
+    scratch += [pltpu.VMEM((2, 1, side, side, core, many, width), BF16)]
     for k in range(slices):
         scratch += boxes_for(devices, part, width)
+    for k in range(slices):
+        scratch += boxes_for(devices, many, width, unit=True)
     return pl.pallas_call(
         functools.partial(mixing_kernel, devices, hidden // strip),
         grid=(hidden // strip,),
@@ -642,22 +706,24 @@
         out_specs=[
             fixed,
             fixed,
-            pl.BlockSpec((strip // many, many, width), lambda i: (i, 0, 0)),
             pl.BlockSpec((1, strip), lambda i: (0, i)),
             pl.BlockSpec((slices * part, width), lambda i: (0, 0)),
             pl.BlockSpec((devices, part, strip), lambda i: (0, 0, jnp.maximum(i - slices * per, 0))),
+            pl.BlockSpec((strip // many, many, width), lambda i: (jnp.maximum(i - slices * per, 0), 0, 0)),
+            pl.BlockSpec((many, width), lambda i: (0, 0)),
             pl.BlockSpec((1, width), lambda i: (0, 0)),
         ],
         out_shape=[
             jax.ShapeDtypeStruct((rows, width), F32),
             jax.ShapeDtypeStruct((rows, width), F32),
-            jax.ShapeDtypeStruct((devices, many, width), BF16),
             jax.ShapeDtypeStruct((1, hidden), F32),
             jax.ShapeDtypeStruct((slices * part, width), F32),
             jax.ShapeDtypeStruct((devices, part, width), BF16),
+            jax.ShapeDtypeStruct((devices // outer, many, width), BF16),
+            jax.ShapeDtypeStruct((many, width), F32),
             jax.ShapeDtypeStruct((1, width), F32),
         ],
-        scratch_shapes=scratch + sems_for(devices, slices),
+        scratch_shapes=scratch + sems_for(devices, 2 * slices),
         compiler_params=pltpu.CompilerParams(collective_id=3, has_side_effects=True, vmem_limit_bytes=57 << 20),
         name="mixing",
     )(second, above, gathered, gathered, bias_e, bias_r)
@@ -665,7 +731,7 @@
 
 def turn_kernel(
     devices, grad_r_ref, grad_e_ref, out_one_ref, d_second_ref, mixed_ref, two_ref, above_ref, combined_ref, live_ref, gain_ref, w_o_ref,
-    bias_r_ref, bias_e_ref,
+    bias_r_ref, bias_e_ref, first_r_ref,
     wide_ref, grad_one_ref, one_ref, res_two_ref, grad_o_ref, small_ref, part_e_ref, part_r_ref,
     attend_s, load_sem, halo_sem, *rest,
 ):
@@ -679,7 +745,7 @@
     owns, rest = rest[:2], rest[2:]
     sems = rest[-4:]
 
-    def distant(source, row, rows, k):
+    def distant(source, row, rows, k, unit=0):
         at = pl.ds(row, rows)
 
         def other():
@@ -691,9 +757,11 @@
         def load():
             return pltpu.make_async_copy(source.at[:, :, :, c, at, :], owns[k], load_sem.at[k])
 
-        return Scatter(devices, where, k, rest[5 * k : 5 * k + 5], sems, other, mine, load)
-
-    movers = [distant(grad_e_ref, 0, part, 0), distant(grad_r_ref, 0, part_r_ref.shape[0], 1)]
+        group = (devices, where, k, rest[5 * k : 5 * k + 5], sems, other, mine, load)
+        return Unit(unit, *group) if unit else Scatter(*group)
+
+    outer = digits(devices)[0]
+    movers = [distant(grad_e_ref, 0, part, 0), distant(grad_r_ref, 0, part_r_ref.shape[0], 1, outer - 1)]
     last = devices - 1
     left, right = lax.rem(me + last, devices), lax.rem(me + 1, devices)
     greet(peers_of(where) + [left, right])
@@ -771,7 +839,8 @@
         small_ref[6 + k : 7 + k, :] = bias_e_ref[:, k * width : (k + 1) * width]
     movers[1].stage_second()
     part_e_ref[...] = movers[0].stage_third()
-    part_r_ref[...] = movers[1].stage_third()
+    part_r_ref[...] = first_r_ref[...]
+    movers[1].close(part_r_ref)
 
     @pl.when(me > 0)
     def _():
@@ -796,57 +865,54 @@
         mover.sent_last()
 
 
-def turn(devices, grad_r, grad_e, out_one, d_second, mixed, two, above, combined, live, gain, w_o, bias_r, bias_e):
+def turn(devices, grad_r, grad_e, out_one, d_second, mixed, two, above, combined, live, gain, w_o, bias_r, bias_e, first_r):
     slots, width = two.shape
     outer, side, core = digits(devices)
     part, many = grad_e.shape[1], grad_r.shape[1]
     vmem = pl.BlockSpec(memory_space=pltpu.VMEM)
     anywhere = pl.BlockSpec(memory_space=pl.ANY)
     dma = pltpu.SemaphoreType.DMA
-    sizes = [part, many // 2]
     scratch = [pltpu.VMEM((slots, width), BF16), dma((2,)), dma((2, 2))]
-    scratch += [pltpu.VMEM((outer, side, side, rows, width), BF16) for rows in sizes]
-    for rows in sizes:
-        scratch += boxes_for(devices, rows, width)
+    scratch += [pltpu.VMEM((outer, side, side, part, width), BF16), pltpu.VMEM((1, side, side, many, width), BF16)]
+    scratch += boxes_for(devices, part, width) + boxes_for(devices, many, width, unit=True)
     shape = (outer, side, side, core)
     rows_low = jax.ShapeDtypeStruct((slots, width), BF16)
     return pl.pallas_call(
         functools.partial(turn_kernel, devices),
-        in_specs=[anywhere, anywhere] + [vmem] * 11,
+        in_specs=[anywhere, anywhere] + [vmem] * 12,
         out_specs=(vmem,) * 8,
         out_shape=(
             jax.ShapeDtypeStruct((2 * slots, width), BF16), rows_low, rows_low, rows_low,
             jax.ShapeDtypeStruct((devices, part, width), BF16),
             jax.ShapeDtypeStruct((16, width), F32),
             jax.ShapeDtypeStruct((part, width), F32),
-            jax.ShapeDtypeStruct((many // 2, width), F32),
+            jax.ShapeDtypeStruct((many, width), F32),
         ),
-        scratch_shapes=scratch + sems_for(devices, len(sizes)),
+        scratch_shapes=scratch + sems_for(devices, 2),
         compiler_params=pltpu.CompilerParams(collective_id=5, has_side_effects=True, vmem_limit_bytes=57 << 20),
         name="turn",
     )(
-        grad_r.reshape(shape + grad_r.shape[1:]), grad_e.reshape(shape + grad_e.shape[1:]),
-        out_one, d_second, mixed, two, above, combined, live, gain, w_o, bias_r, bias_e,
+        grad_r.reshape((1,) + shape[1:] + grad_r.shape[1:]), grad_e.reshape(shape + grad_e.shape[1:]),
+        out_one, d_second, mixed, two, above, combined, live, gain, w_o, bias_r, bias_e, first_r,
     )
 
 
 def tail_kernel(
-    devices, grad_r_ref, grad_o_ref, d_shared_ref, d_value_ref, normed_ref, head_ref, own_ref, end_ref, above_ref, live_ref,
+    devices, grad_o_ref, d_shared_ref, d_value_ref, normed_ref, head_ref, own_ref, end_ref, above_ref, live_ref,
     gain_ref, w_s_ref, w_v_ref, small_ref,
-    back_ref, out_s_ref, out_v_ref, out_o_ref, out_r_ref, thin_ref, long_ref,
+    back_ref, out_s_ref, out_v_ref, out_o_ref, thin_ref, long_ref,
     side_s, side_in, vector_s, vector_in, grad_s, load_sem, halo_sem, vector_sem, *rest,
 ):
     window, width = normed_ref.shape
     slots = own_ref.shape[0]
     half = slots // 2
     part = out_s_ref.shape[0]
-    many = 2 * out_r_ref.shape[0]
     tile = 256
     where = neighbours(devices)
     (o, p, q, c), core_peer, q_peers, p_peers, o_peers = where
     me = lax.axis_index("fsdp")
     outer, side, core = digits(devices)
-    owns, rest = rest[:2], rest[2:]
+    owns, rest = rest[:1], rest[1:]
     sems = rest[-4:]
 
     def distant(source, row, rows, k):
@@ -873,13 +939,12 @@
         return Scatter(devices, where, k, rest[5 * k : 5 * k + 5], sems, other, mine)
 
     movers = [
-        distant(grad_r_ref, many // 2, many // 2, 0), distant(grad_o_ref, 0, part, 1), near(0, 2), near(1, 3),
+        distant(grad_o_ref, 0, part, 0), near(0, 1), near(1, 2),
     ]
     last = devices - 1
     left, right = lax.rem(me + last, devices), lax.rem(me + 1, devices)
     greet(peers_of(where) + [left, right])
-    for k in range(2):
-        movers[k].begin()
+    movers[0].begin()
 
     def to_left():
         return remote(side_s.at[0], side_in.at[1], halo_sem, (0,), left)
@@ -937,14 +1002,12 @@
         lax.fori_loop(0, width // tile, strip, 0)
 
     weights(0, d_shared_ref)
-    movers[2].begin()
-    movers[1].stage_core()
+    movers[1].begin()
     movers[0].stage_first()
     weights(1, d_value_ref)
-    movers[3].begin()
-    movers[1].stage_first()
+    movers[2].begin()
     movers[0].stage_second()
-    movers[2].stage_core()
+    movers[1].stage_core()
 
     def own_tiles(i, carry):
         row = pl.multiple_of(i * tile, tile)
@@ -975,20 +1038,18 @@
 
     for copy in vector_copies(0):
         copy.start()
-    movers[3].stage_core()
-    movers[1].stage_second()
-    out_r_ref[...] = movers[0].stage_third()
-    movers[2].stage_first()
+    movers[2].stage_core()
+    movers[1].stage_first()
+    out_o_ref[...] = movers[0].stage_third()
     vector_stage(0)
     for copy in vector_copies(1):
         copy.start()
-    movers[3].stage_first()
-    out_o_ref[...] = movers[1].stage_third()
-    movers[2].stage_second()
+    movers[2].stage_first()
+    movers[1].stage_second()
     vector_stage(1)
     for copy in vector_copies(2):
         copy.start()
-    movers[3].stage_second()
+    movers[2].stage_second()
     vector_stage(2)
     for copy in vector_copies(3):
         copy.start()
@@ -1012,9 +1073,9 @@
     for k in range(2):
         at = slice(k * half, (k + 1) * half)
         back_ref[at, :] = (back_ref[at, :].astype(F32) + side_in[k].astype(F32)).astype(BF16)
-    out_s_ref[...] = movers[2].stage_third()
+    out_s_ref[...] = movers[1].stage_third()
     vector_stage(3)
-    out_v_ref[...] = movers[3].stage_third()
+    out_v_ref[...] = movers[2].stage_third()
     vectors = 2 * side + outer - 3
     total = vector_in[vectors]
     thin_ref[...] = pltpu.roll(total, lax.rem(width - me * part, width), 1)[:, :DH]
@@ -1042,36 +1103,35 @@
         mover.sent_last()
 
 
-def tail(devices, grad_r, grad_o, d_shared, d_values, normed, head, own, end, above, live, gain, w_s, w_v, small):
+def tail(devices, grad_o, d_shared, d_values, normed, head, own, end, above, live, gain, w_s, w_v, small, hidden):
     window, width = normed.shape
     slots = own.shape[0]
     outer, side, core = digits(devices)
-    part, many = grad_o.shape[1], grad_r.shape[1]
-    each = many
+    part = grad_o.shape[1]
+    each = hidden // devices
     vmem = pl.BlockSpec(memory_space=pltpu.VMEM)
     anywhere = pl.BlockSpec(memory_space=pl.ANY)
     dma = pltpu.SemaphoreType.DMA
-    sizes = [many // 2, part, part, part]
+    sizes = [part, part, part]
     scratch = [
         pltpu.VMEM((2, slots // 2, width), BF16), pltpu.VMEM((2, slots // 2, width), BF16),
         pltpu.VMEM((16, width), F32), pltpu.VMEM((2 * side + outer - 2, 16, width), F32),
         pltpu.VMEM((2, outer, side, side, core, part, width), BF16),
-        dma((2,)), dma((2, 2)), dma((2, 2 * side + outer - 2)),
+        dma((1,)), dma((2, 2)), dma((2, 2 * side + outer - 2)),
     ]
-    scratch += [pltpu.VMEM((outer, side, side, rows, width), BF16) for rows in sizes[:2]]
+    scratch += [pltpu.VMEM((outer, side, side, rows, width), BF16) for rows in sizes[:1]]
     for rows in sizes:
         scratch += boxes_for(devices, rows, width)
     shape = (outer, side, side, core)
     return pl.pallas_call(
         functools.partial(tail_kernel, devices),
-        in_specs=[anywhere, anywhere] + [vmem] * 12,
-        out_specs=(vmem,) * 7,
+        in_specs=[anywhere] + [vmem] * 12,
+        out_specs=(vmem,) * 6,
         out_shape=(
             jax.ShapeDtypeStruct((slots, width), BF16),
             jax.ShapeDtypeStruct((part, width), F32),
             jax.ShapeDtypeStruct((part, width), F32),
             jax.ShapeDtypeStruct((part, width), F32),
-            jax.ShapeDtypeStruct((many // 2, width), F32),
             jax.ShapeDtypeStruct((16, DH), F32),
             jax.ShapeDtypeStruct((1, each), F32),
         ),
@@ -1079,12 +1139,12 @@
         compiler_params=pltpu.CompilerParams(collective_id=4, has_side_effects=True, vmem_limit_bytes=57 << 20),
         name="tail",
     )(
-        grad_r.reshape(shape + grad_r.shape[1:]), grad_o.reshape(shape + grad_o.shape[1:]),
+        grad_o.reshape(shape + grad_o.shape[1:]),
         d_shared, d_values, normed, head, own, end, above, live, gain, w_s, w_v, small,
     )
 
 
-def rank_kernel(length_ref, target_ref, bucket_ref, block_ref, info_ref, before_s):
+def find_ranks(length_ref, target_ref, bucket_ref, packed_ref, info_ref, before_s):
     devices = length_ref.shape[0]
     lists, slots = bucket_ref.shape
     me = lax.axis_index("fsdp")
@@ -1134,22 +1194,7 @@
         ranks.append(jnp.sum(one_hot * place, axis=1))
     rank = jnp.concatenate(ranks, axis=0)
     live = lax.broadcasted_iota(jnp.int32, (lists, slots), 1) < mine
-    block_ref[...] = jnp.where(live, jnp.floor(rank * (1.0 / GROUP)), FREE).astype(BF16)
-
-
-def rank_blocks(lengths, destination, buckets):
-    lists, slots = buckets.shape
-    smem = pl.BlockSpec(memory_space=pltpu.SMEM)
-    vmem = pl.BlockSpec(memory_space=pltpu.VMEM)
-    return pl.pallas_call(
-        rank_kernel,
-        in_specs=[smem, smem, vmem],
-        out_specs=[vmem, smem],
-        out_shape=[jax.ShapeDtypeStruct((lists, slots), BF16), jax.ShapeDtypeStruct((8,), jnp.int32)],
-        scratch_shapes=[pltpu.VMEM((slots, slots), BF16)],
-        compiler_params=pltpu.CompilerParams(vmem_limit_bytes=32 << 20),
-        name="rank_blocks",
-    )(lengths, destination, buckets)
+    packed_ref[:lists, :] = jnp.where(live, jnp.floor(rank * (1.0 / GROUP)), FREE).astype(BF16)
 
 
 def project_kernel(
@@ -1223,9 +1268,10 @@
     )(info, head, own, tail, gain, shift, w_s, w_v, blocks, blocks)
 
 
-def gather_kernel(devices, arrays, *refs):
-    sources, outs = refs[:arrays], refs[arrays : 2 * arrays]
-    own_sem, sem_o, sem_a, sem_b, sem_c = refs[2 * arrays :]
+def gather_kernel(devices, arrays, length_ref, target_ref, bucket_ref, vector_ref, *refs):
+    sources, outs, info_ref = refs[: arrays - 1], refs[arrays - 1 : 2 * arrays - 1], refs[2 * arrays - 1]
+    packed_s, before_s, own_sem, sem_o, sem_a, sem_b, sem_c = refs[2 * arrays :]
+    sources = sources + (packed_s,)
     outer, side, core = digits(devices)
     (o, p, q, c), core_peer, q_peers, p_peers, o_peers = neighbours(devices)
     greet([core_peer] + [d for _, d in q_peers] + [d for _, d in p_peers] + [d for _, d in o_peers])
@@ -1240,6 +1286,9 @@
 
     copies, locals_, begun, first, second, last = [], [], {}, {}, {}, {}
     for s in range(arrays):
+        if s == arrays - 1:
+            find_ranks(length_ref, target_ref, bucket_ref, packed_s, info_ref, before_s)
+            packed_s[bucket_ref.shape[0] :, :] = vector_ref[...]
         locals_.append(pltpu.make_async_copy(sources[s], outs[s].at[o, p, q, c], own_sem.at[s]))
         locals_[s].start()
         for d, (k, device) in enumerate(o_peers):
@@ -1287,23 +1336,30 @@
             copy.wait_send()
 
 
-def gather(devices, arrays):
+def gather(devices, lengths, destination, buckets, vectors, arrays):
     outer, side, core = digits(devices)
-    count = len(arrays)
+    lists, slots = buckets.shape
+    packed = jax.ShapeDtypeStruct((lists + vectors.shape[0], slots), BF16)
+    shapes = [jax.ShapeDtypeStruct(array.shape, array.dtype) for array in arrays] + [packed]
+    count = len(shapes)
     dma = pltpu.SemaphoreType.DMA
     anywhere = pl.BlockSpec(memory_space=pl.ANY)
+    smem = pl.BlockSpec(memory_space=pltpu.SMEM)
+    vmem = pl.BlockSpec(memory_space=pltpu.VMEM)
     outs = pl.pallas_call(
         functools.partial(gather_kernel, devices, count),
-        out_shape=tuple(jax.ShapeDtypeStruct((outer, side, side, core) + array.shape, array.dtype) for array in arrays),
-        in_specs=[anywhere] * count,
-        out_specs=(anywhere,) * count,
+        out_shape=tuple(jax.ShapeDtypeStruct((outer, side, side, core) + shape.shape, shape.dtype) for shape in shapes)
+        + (jax.ShapeDtypeStruct((8,), jnp.int32),),
+        in_specs=[smem, smem, vmem, vmem] + [anywhere] * (count - 1),
+        out_specs=(anywhere,) * count + (smem,),
         scratch_shapes=[
-            dma((count,)), dma((2, count, outer - 1)), dma((2, count, 2, side - 1)), dma((2, count, 2, side - 1)), dma((2, count))
+            pltpu.VMEM(packed.shape, BF16), pltpu.VMEM((slots, slots), BF16),
+            dma((count,)), dma((2, count, outer - 1)), dma((2, count, 2, side - 1)), dma((2, count, 2, side - 1)), dma((2, count)),
         ],
-        compiler_params=pltpu.CompilerParams(collective_id=2, has_side_effects=True),
+        compiler_params=pltpu.CompilerParams(collective_id=2, has_side_effects=True, vmem_limit_bytes=32 << 20),
         name="gather",
-    )(*arrays)
-    return [out.reshape((devices,) + array.shape) for out, array in zip(outs, arrays)]
+    )(lengths, destination, buckets, vectors, *arrays)
+    return [out.reshape((devices,) + shape.shape) for out, shape in zip(outs, shapes)] + [outs[-1]]
 
 
 def body(
@@ -1331,7 +1387,6 @@
 
     base = me * slots
     lists = ROUNDS * HEADS
-    block, info = rank_blocks(lengths, destination, buckets[0])
     spot = jnp.arange(width, dtype=jnp.int32)
     short = jnp.stack([gain_attend, shift_attend, gain_mixing, shift_mixing, bias_output, bias_reduce])
     short = jnp.where(spot // part == me, jnp.tile(short, (1, devices)), 0.0)
@@ -1342,7 +1397,7 @@
     high = lax.reduce_precision(vectors, 8, 7)
     count = vectors.shape[0]
     packed = jnp.concatenate(
-        [block, high.astype(BF16), (vectors - high).astype(BF16), jnp.zeros((24 - 2 * count, width), BF16)], axis=0
+        [high.astype(BF16), (vectors - high).astype(BF16), jnp.zeros((24 - 2 * count, width), BF16)], axis=0
     )
     second_gather = lax.all_gather(
         jnp.concatenate(
@@ -1350,7 +1405,7 @@
         ),
         "fsdp", axis=0, tiled=False,
     )
-    full_shared, full_value, packed = gather(devices, [w_shared, w_value, packed])
+    full_shared, full_value, packed, info = gather(devices, lengths, destination, buckets[0], packed, [w_shared, w_value])
     full_shared, full_value = full_shared.reshape(width, width), full_value.reshape(width, width)
     vectors = jnp.sum(packed[:, lists : lists + 2 * count].astype(F32), axis=0)
     vectors = vectors[:count] + vectors[count:]
@@ -1363,7 +1418,6 @@
 
     live = ((base + jnp.arange(slots, dtype=jnp.int32)) < info[6]).astype(F32)[:, None]
     slot_one = input_one.astype(F32)
-    slot_two = input_two.astype(F32)
     two_head, two_tail = to_sides(input_two[:half], input_two[half:])
     normed, shared, values, code = project(
         info, two_head, input_two, two_tail, gain_a, shift_a, full_shared, full_value, packed
@@ -1375,19 +1429,19 @@
     out_one = slot_one + live * attended
     second = layer_norm(out_one, gain_m, shift_m).astype(BF16)
     d_reduce = (live * upstream_two.astype(F32)).astype(BF16)
-    mixed, d_second, grad_reduce, grad_bias_expand, grad_expand, last_expand, grad_bias_reduce = mixing(
+    mixed, d_second, grad_bias_expand, grad_expand, last_expand, last_reduce, grad_reduce, grad_bias_reduce = mixing(
         devices, second, d_reduce, second_gather, bias_e, bias_r, part
     )
-    d_combined, grad_one, result_one, result_two, grad_output, small, last_expand, first_reduce = turn(
-        devices, grad_reduce, last_expand, out_one, d_second, mixed, input_two, upstream_one, combined, live, gain_m,
-        full_output, grad_bias_reduce, grad_bias_expand,
+    d_combined, grad_one, result_one, result_two, grad_output, small, last_expand, grad_reduce = turn(
+        devices, last_reduce, last_expand, out_one, d_second, mixed, input_two, upstream_one, combined, live, gain_m,
+        full_output, grad_bias_reduce, grad_bias_expand, grad_reduce,
     )
     d_shared, d_values = attend_back(
         info, shared, values, code, spread, combined_window, d_combined, lse, lone
     )
-    grad_two, grad_shared, grad_value, grad_output, grad_reduce, thin, long = tail(
-        devices, grad_reduce, grad_output, d_shared, d_values, normed,
-        two_head, input_two, two_tail, upstream_two, live, gain_a, full_shared, full_value, small,
+    grad_two, grad_shared, grad_value, grad_output, thin, long = tail(
+        devices, grad_output, d_shared, d_values, normed,
+        two_head, input_two, two_tail, upstream_two, live, gain_a, full_shared, full_value, small, hidden,
     )
     return (
         result_one,
@@ -1398,7 +1452,7 @@
         grad_value,
         grad_output,
         jnp.concatenate([grad_expand[k * part : (k + 1) * part] for k in range(sides - 1)] + [last_expand], axis=1),
-        jnp.concatenate([first_reduce, grad_reduce], axis=0),
+        grad_reduce,
         thin[0, :part],
         thin[1, :part],
         thin[2, :part],

time: 595 us -> 602 us (1.012)
  starting transfers between devices: 30.2 us -> 7.5 us
  waiting for transfers between devices: 0.03 us -> 19.5 us
  Pallas kernels: 486 us -> 505 us
    pallas_call x1, Pallas kernels: 101 us -> 131 us  [mixing(): pl.pallas_call(functools.partial(mixing_kernel, devices, hidden // strip)...]
    ppermute x4, starting transfers between devices: 30.1 us -> 7.46 us  [to_sides(): return (lax.ppermute(tail, 'fsdp', up), lax.ppermute(head, 'fsdp', down))]
    ppermute x4, waiting for transfers between devices: 0.01 us -> 19.5 us  [to_sides(): return (lax.ppermute(tail, 'fsdp', up), lax.ppermute(head, 'fsdp', down))]
    pallas_call x1, Pallas kernels: 78.8 us -> 72 us  [turn(): pl.pallas_call(functools.partial(turn_kernel, devices), in_specs=[anywher...]
    unnamed x85 -> x88, local copies, waits for them, and re-layouts: 25.1 us -> 19 us
  transfers between devices with their start and end apart: 5 -> 5, of which waited for: 0 -> 1; matrix products, arithmetic and copies ran while one was open for 3% -> 3% of each run, Pallas kernels for 21% -> 20%
where the time goes in v5:
time: 602 us; the launch traced here: 596 us
  Pallas kernels  505 us (84%)
  local copies, waits for them, and re-layouts  31.7 us (5%)
  waiting for transfers between devices  19.5 us (3%)
  between operations  14.8 us (2%)
  other arithmetic  13.3 us (2%)
  starting transfers between devices  7.5 us (1%)
    pallas_call x1, Pallas kernels, tail(): pl.pallas_call(functools.partial(tail_kernel, devices), in_specs=[anywher...  144 us
    pallas_call x1, Pallas kernels, mixing(): pl.pallas_call(functools.partial(mixing_kernel, devices, hidden // strip)...  131 us
    pallas_call x1, Pallas kernels, gather(): pl.pallas_call(functools.partial(gather_kernel, devices, count), out_shap...  86.4 us
    pallas_call x1, Pallas kernels, turn(): pl.pallas_call(functools.partial(turn_kernel, devices), in_specs=[anywher...  72 us
    pallas_call x1, Pallas kernels, attend_back(): pl.pallas_call(back_kernel, grid_spec=pltpu.PrefetchScalarGridSpec(num_sc...  35.6 us
    pallas_call x1, Pallas kernels, attend(): pl.pallas_call(attend_kernel, grid_spec=pltpu.PrefetchScalarGridSpec(num_...  19.7 us
    ppermute x4, waiting for transfers between devices, to_sides(): return (lax.ppermute(tail, 'fsdp', up), lax.ppermute(head, 'fsdp', down))  19.5 us
    unnamed x88, local copies, waits for them, and re-layouts  19 us
  transfers between devices with their start and end apart: 5, of which 1 were waited for; matrix products, arithmetic and copies ran while one was open for 3% of the time, Pallas kernels for 20%

profile of v5, /device:TPU:0, one launch (start us, length us, event | category | flops | bytes accessed | tf_op | source)
XLA Modules:
  0.0 596.3 jit_solution(8609491370480098362)
XLA Ops:
  13.7 3.0 fusion.20
  16.7 2.4 collective-permute-start
  22.5 86.4 %gather.1 = (bf16[4,2,2,2,32,1024]{5,4,3,2,1,0:T(8,128)(2,1)S(1)}, bf16[4,2,2,2,32,1024]{5,4,3,2,1,0:T(8,128)(2,1)S(1)}, bf16[4,2,2,2,56,1024]{5,4,3,2,1,0:T(8,128)(2,1)S(1)}, s32[8]{0:T(128)S(1)}) custom-call(s32[32]{0:T(128)S(1)} %copy-done.13, s32[32]{0:T(128)S(1)} %copy-done.14, s32[32,1024]{1,0:T(8,128)S(1)} %bitcast.47, ...), custom_call_target="tpu_custom_call" | custom-call | tf_op jit(solution)/shard_map/gather/pallas_call | solution.py:1349
  110.2 16.1 %project.1 = (bf16[2048,1024]{1,0:T(8,128)(2,1)}, bf16[2048,1024]{1,0:T(8,128)(2,1)}, bf16[2048,1024]{1,0:T(8,128)(2,1)}, bf16[32,2048]{1,0:T(8,128)(2,1)S(1)}) custom-call(s32[8]{0:T(128)S(1)} %get-tuple-element.51.info_ref.low_ref, bf16[512,1024]{1,0:T(8,128)(2,1)S(1)} %collective-permute-done.head_ref, bf16[1024,1024]{1,0:T(8,128)(2,1)S(1)} %copy-done.2, ...), custom_call_target="tpu_custom_call" | custom-call | tf_op jit(solution)/shard_map/project/pallas_call | solution.py:1250
  126.3 19.7 %attend.1 = (bf16[2048,1024]{1,0:T(8,128)(2,1)S(1)}, f32[8,1,2048]{2,1,0:T(1,128)S(1)}, f32[8,1,2048]{2,1,0:T(1,128)S(1)}) custom-call(s32[8]{0:T(128)S(1)} %get-tuple-element.51.info_ref.low_ref, bf16[2048,1024]{1,0:T(8,128)(2,1)} %get-tuple-element.55.q_ref, bf16[2048,1024]{1,0:T(8,128)(2,1)} %get-tuple-element.56.v_ref, ...), custom_call_target="tpu_custom_call" | custom-call | flops 32212254720 | bytes 12582912 | tf_op jit(solution)/shard_map/attend/pallas_call | solution.py:321
  146.0 2.0 copy-done.5
  149.1 2.5 collective-permute-start.2
  155.1 1.5 fusion.live_ref
  156.6 3.3 multiply_convert_fusion.above_ref
  159.9 19.5 %collective-permute-done.3 = bf16[512,1024]{1,0:T(8,128)(2,1)} collective-permute-done((bf16[512,1024]{1,0:T(8,128)(2,1)S(1)}, bf16[512,1024]{1,0:T(8,128)(2,1)}, u32[]{:S(2)}, u32[]{:S(2)}) %collective-permute-start.3) | collective-permute-done | bytes 1048608 | tf_op jit(solution)/shard_map/ppermute | solution.py:1382
  179.4 3.5 maximum_add_fusion.combined_ref
  182.9 1.9 slice.125
  185.2 4.6 fusion.23
  190.4 2.1 add_convert_fusion.second_ref
  192.5 131.4 %mixing.1 = (f32[1024,1024]{1,0:T(8,128)}, f32[1024,1024]{1,0:T(8,128)}, f32[1,4096]{1,0:T(1,128)}, f32[96,1024]{1,0:T(8,128)}, bf16[32,32,1024]{2,1,0:T(8,128)(...) custom-call(bf16[1024,1024]{1,0:T(8,128)(2,1)} %add_convert_fusion.second_ref, ...), custom_call_target="tpu_custom_call" | custom-call | tf_op jit(solution)/shard_map/mixing/pallas_call | solution.py:696
  324.9 72.0 %turn.1 = (bf16[2048,1024]{1,0:T(8,128)(2,1)}, bf16[1024,1024]{1,0:T(8,128)(2,1)}, bf16[1024,1024]{1,0:T(8,128)(2,1)}, bf16[1024,1024]{1,0:T(8,128)(2,1)}, bf16[...) custom-call(bf16[1,2,2,2,128,1024]{5,4,3,2,1,0:T(8,128)(2,1)} %bitcast.55, ...), custom_call_target="tpu_custom_call" | custom-call | tf_op jit(solution)/shard_map/turn/pallas_call | solution.py:880
  396.9 35.6 %attend_back.1 = (bf16[2048,1024]{1,0:T(8,128)(2,1)S(1)}, bf16[2048,1024]{1,0:T(8,128)(2,1)}) custom-call(s32[8]{0:T(128)S(1)} %get-tuple-element.51.info_ref.low_ref, bf16[2048,1024]{1,0:T(8,128)(2,1)} %get-tuple-element.55.q_ref, bf16[2048,1024]{1,0:T(8,128)(2,1)} %get-tuple-element.56.v_ref, bf16[32,2048]{1,0:T(8,128)(2,1)S(1)} %get-tuple-element.57.code_ref, ...), custom_call_target="tpu_custom_call" | custom-call | flops 64424509440 | bytes 25165824 | tf_op jit(solution)/shard_map/attend_back/pallas_call | solution.py:344
  432.6 2.0 copy-done.7
  434.5 143.8 %tail.1 = (bf16[1024,1024]{1,0:T(8,128)(2,1)}, f32[32,1024]{1,0:T(8,128)}, f32[32,1024]{1,0:T(8,128)}, f32[32,1024]{1,0:T(8,128)}, f32[16,128]{1,0:T(8,128)}, /*index=5*/f32[1,128]{1,0:T(1,128)}) custom-call(bf16[4,2,2,2,32,1024]{5,4,3,2,1,0:T(8,128)(2,1)} %bitcast.53, bf16[2048,1024]{1,0:T(8,128)(2,1)} %copy-done.7, ...), custom_call_target="tpu_custom_call" | custom-call | tf_op jit(solution)/shard_map/tail/pallas_call | solution.py:1126
  578.3 1.4 slice_bitcast_fusion.1
  580.6 1.3 copy.52
  581.9 1.3 copy.53
  583.3 1.3 copy.54
  584.7 1.3 copy.55
  (117 shorter events, 21.6 us)
Async XLA Ops:
  7.2 15.0 %copy-start = (f32[128]{0:T(128)S(1)}, f32[128]{0:T(128)}, u32[]{:S(2)}) copy-start(f32[128]{0:T(128)} %param.36) | copy-start | bytes 1540
  7.2 13.2 %copy-start.29 = (f32[32]{0:T(128)S(1)}, f32[32]{0:T(128)}, u32[]{:S(2)}) copy-start(f32[32]{0:T(128)} %param.31) | copy-start | bytes 388
  7.2 13.2 %copy-start.30 = (f32[32]{0:T(128)S(1)}, f32[32]{0:T(128)}, u32[]{:S(2)}) copy-start(f32[32]{0:T(128)} %param.32) | copy-start | bytes 388
  7.2 13.2 %copy-start.31 = (f32[32]{0:T(128)S(1)}, f32[32]{0:T(128)}, u32[]{:S(2)}) copy-start(f32[32]{0:T(128)} %param.33) | copy-start | bytes 388
  7.2 13.2 %copy-start.32 = (f32[32]{0:T(128)S(1)}, f32[32]{0:T(128)}, u32[]{:S(2)}) copy-start(f32[32]{0:T(128)} %param.34) | copy-start | bytes 388
  7.3 15.2 %copy-start.9 = (s32[1,32,1024]{2,1,0:T(8,128)S(1)}, s32[1,32,1024]{2,1,0:T(8,128)}, u32[]{:S(2)}) copy-start(s32[1,32,1024]{2,1,0:T(8,128)} %param.25) | copy-start | bytes 393220
  7.3 15.2 %copy-start.13 = (s32[32]{0:T(128)S(1)}, s32[32]{0:T(128)}, u32[]{:S(2)}) copy-start(s32[32]{0:T(128)} %length_ref.1) | copy-start | bytes 388
  7.3 15.2 %copy-start.14 = (s32[32]{0:T(128)S(1)}, s32[32]{0:T(128)}, u32[]{:S(2)}) copy-start(s32[32]{0:T(128)} %target_ref.1) | copy-start | bytes 388
  7.3 15.2 %copy-start.10 = (bf16[32,1024]{1,0:T(8,128)(2,1)S(1)}, bf16[32,1024]{1,0:T(8,128)(2,1)}, u32[]{:S(2)}) copy-start(bf16[32,1024]{1,0:T(8,128)(2,1)} %refs_0_.1) | copy-start | bytes 196612
  7.3 15.2 %copy-start.11 = (bf16[32,1024]{1,0:T(8,128)(2,1)S(1)}, bf16[32,1024]{1,0:T(8,128)(2,1)}, u32[]{:S(2)}) copy-start(bf16[32,1024]{1,0:T(8,128)(2,1)} %refs_1_.1) | copy-start | bytes 196612
  7.3 175.6 %all-gather.3.cloned.1.call-start = ((), (), s32[]{:S(2)}) async-start(), calls=%async_computation | async-start | bytes 19464192 | tf_op jit(solution)/shard_map/all_gather | solution.py:1402
  8.4 101.8 %copy-start.2 = (bf16[1024,1024]{1,0:T(8,128)(2,1)S(1)}, bf16[1024,1024]{1,0:T(8,128)(2,1)}, u32[]{:S(2)}) copy-start(bf16[1024,1024]{1,0:T(8,128)(2,1)} %own_ref.3) | copy-start | bytes 6291460
  16.7 93.5 %collective-permute-start = (bf16[512,1024]{1,0:T(8,128)(2,1)}, bf16[512,1024]{1,0:T(8,128)(2,1)S(1)}, u32[]{:S(2)}, u32[]{:S(2)}) collective-permute-start(bf16[512,1024]{1,0:T(8,128)(2,1)} %get-tuple-element.89), channel_id=1, source_target_pairs={{0,1},{1,2},{2,3},{3,4},{4,5},{5,6},{6,7},{7,8},{8,9},{9,10},{10,1... | collective-permute-start | bytes 3145736 | tf_op jit(solution)/shard_map/ppermute | solution.py:1382
  19.1 91.1 %collective-permute-start.1 = (bf16[512,1024]{1,0:T(8,128)(2,1)}, bf16[512,1024]{1,0:T(8,128)(2,1)}, u32[]{:S(2)}, u32[]{:S(2)}) collective-permute-start(bf16[512,1024]{1,0:T(8,128)(2,1)} %get-tuple-element.88), channel_id=1, source_target_pairs={{1,0},{2,1},{3,2},{4,3},{5,4},{6,5},{7,6},{8,7},{9,8},{10,9},{11,1... | collective-permute-start | bytes 3145736 | tf_op jit(solution)/shard_map/ppermute | solution.py:1382
  108.9 17.4 %copy-start.3 = (bf16[4,2,2,2,32,1024]{5,4,3,2,1,0:T(8,128)(2,1)}, bf16[4,2,2,2,32,1024]{5,4,3,2,1,0:T(8,128)(2,1)S(1)}, u32[]{:S(2)}) copy-start(bf16[4,2,2,2,32,1024]{5,4,3,2,1,0:T(8,128)(2,1)S(1)} %get-tuple-element.53) | copy-start | bytes 6291460
  108.9 17.4 %copy-start.4 = (bf16[4,2,2,2,32,1024]{5,4,3,2,1,0:T(8,128)(2,1)}, bf16[4,2,2,2,32,1024]{5,4,3,2,1,0:T(8,128)(2,1)S(1)}, u32[]{:S(2)}) copy-start(bf16[4,2,2,2,32,1024]{5,4,3,2,1,0:T(8,128)(2,1)S(1)} %get-tuple-element.54) | copy-start | bytes 6291460
  110.1 16.2 %copy-start.12 = (f32[1,1024]{1,0:T(1,128)}, f32[1,1024]{1,0:T(1,128)S(1)}, u32[]{:S(2)}) copy-start(f32[1,1024]{1,0:T(1,128)S(1)} %get-tuple-element.98.gain_ref) | copy-start | bytes 12292
  110.2 80.2 %copy-start.28 = (f32[1,1024]{1,0:T(1,128)}, f32[1,1024]{1,0:T(1,128)S(1)}, u32[]{:S(2)}) copy-start(f32[1,1024]{1,0:T(1,128)S(1)} %get-tuple-element.95.gain_ref) | copy-start | bytes 12292
  110.2 16.1 %copy-start.8 = (bf16[512,1024]{1,0:T(8,128)(2,1)}, bf16[512,1024]{1,0:T(8,128)(2,1)S(1)}, u32[]{:S(2)}) copy-start(bf16[512,1024]{1,0:T(8,128)(2,1)S(1)} %collective-permute-done.head_ref) | copy-start | bytes 3145732
  149.1 10.8 %collective-permute-start.2 = (bf16[512,1024]{1,0:T(8,128)(2,1)}, bf16[512,1024]{1,0:T(8,128)(2,1)S(1)}, u32[]{:S(2)}, u32[]{:S(2)}) collective-permute-start(bf16[512,1024]{1,0:T(8,128)(2,1)} %get-tuple-element.86), channel_id=1, source_target_pairs={{0,1},{1,2},{2,3},{3,4},{4,5},{5,6},{6,7},{7,8},{8,9},{9,10},{10,1... | collective-permute-start | bytes 3145736 | tf_op jit(solution)/shard_map/ppermute | solution.py:1382
  151.6 27.8 %collective-permute-start.3 = (bf16[512,1024]{1,0:T(8,128)(2,1)S(1)}, bf16[512,1024]{1,0:T(8,128)(2,1)}, u32[]{:S(2)}, u32[]{:S(2)}) collective-permute-start(bf16[512,1024]{1,0:T(8,128)(2,1)S(1)} %get-tuple-element.87), channel_id=1, source_target_pairs={{1,0},{2,1},{3,2},{4,3},{5,4},{6,5},{7,6},{8,7},{9,8},{10,9},{11,1... | collective-permute-start | bytes 3145736 | tf_op jit(solution)/shard_map/ppermute | solution.py:1382
  153.5 25.9 %copy-start.6 = (bf16[2048,1024]{1,0:T(8,128)(2,1)S(1)}, bf16[2048,1024]{1,0:T(8,128)(2,1)}, u32[]{:S(2)}) copy-start(bf16[2048,1024]{1,0:T(8,128)(2,1)} %copy-done.5) | copy-start | bytes 12582916
  434.5 145.2 %copy-start.27 = (f32[32,1024]{1,0:T(8,128)S(1)}, f32[32,1024]{1,0:T(8,128)}, u32[]{:S(2)}) copy-start(f32[32,1024]{1,0:T(8,128)} %get-tuple-element.82) | copy-start | bytes 393220
  434.5 146.1 %copy-start.20 = (bf16[1024,1024]{1,0:T(8,128)(2,1)S(1)}, bf16[1024,1024]{1,0:T(8,128)(2,1)}, u32[]{:S(2)}) copy-start(bf16[1024,1024]{1,0:T(8,128)(2,1)} %get-tuple-element.125) | copy-start | bytes 6291460
  (17 other events, 77.7 us)
Sparse Core Ops, SparseCore 0:
  13.8 156.1 all-gather.2

commit v6 on v4

--- a/solution.py
+++ b/solution.py
@@ -24,9 +24,10 @@
 STEP = 128.0
 SHIFT = 1.5 * 2.0**30
 TAME = 3000.0
-PAIR = 2
+PAIR = 4
 FREE = 99.0
 STRIP = 512
+AFTER = (1, 4, 6, 8)
 CURVE = math.sqrt(2.0 / math.pi)
 MESH = pl.DeviceIdType.MESH
 
@@ -45,11 +46,6 @@
     center = values - jnp.mean(values, axis=-1, keepdims=True)
     spread = jnp.mean(center * center, axis=-1, keepdims=True)
     return center * lax.rsqrt(spread + EPS_NORM) * gain + shift
-
-
-def norm_back(values, gain, shift, upstream):
-    outcome, pullback = jax.vjp(layer_norm, values, gain, shift)
-    return pullback(upstream)
 
 
 def prepare(q, code_ref, spread, ask_s, key_s, h, at):
@@ -329,7 +325,7 @@
             + [pltpu.VMEM((PAIR, TILE, 2 * DH), F32), pltpu.VMEM((PAIR, TILE, DH), F32)],
         ),
         out_shape=(wide, thin, thin),
-        compiler_params=pltpu.CompilerParams(vmem_limit_bytes=48 << 20),
+        compiler_params=pltpu.CompilerParams(vmem_limit_bytes=57 << 20),
         name="attend",
         cost_estimate=pl.CostEstimate(
             flops=HEADS * 20 * 3 * 2 * TILE * TILE * DH, bytes_accessed=rows * HEADS * DH * 6, transcendentals=HEADS * 20 * TILE * TILE
@@ -351,7 +347,7 @@
             scratch_shapes=[pltpu.VMEM((PAIR, rows, 2 * DH), BF16)] * 2 + [pltpu.VMEM((PAIR, rows, DH), F32)] * 3,
         ),
         out_shape=(wide, wide),
-        compiler_params=pltpu.CompilerParams(vmem_limit_bytes=48 << 20),
+        compiler_params=pltpu.CompilerParams(vmem_limit_bytes=57 << 20),
         name="attend_back",
         cost_estimate=pl.CostEstimate(
             flops=HEADS * 20 * 6 * 2 * TILE * TILE * DH, bytes_accessed=rows * HEADS * DH * 12, transcendentals=HEADS * 20 * TILE * TILE
@@ -532,8 +528,8 @@
 
 
 def mixing_kernel(
-    devices, hidden_steps, second_ref, above_ref, expand_ref, reduce_ref, bias_e_ref, bias_r_ref,
-    out_ref, back_ref, grad_r_ref, grad_b_ref, grad_e_ref, rest_e_ref, above_b_ref, act_s, pre_s, grad_s, *rest,
+    devices, second_ref, above_ref, expand_ref, reduce_ref, bias_e_ref, bias_r_ref,
+    out_ref, back_ref, grad_r_ref, grad_b_ref, grad_e_ref, above_b_ref, act_s, pre_s, grad_s, *rest,
 ):
     step = pl.program_id(0)
     rows, width = second_ref.shape
@@ -565,6 +561,26 @@
         back_ref[...] = jnp.zeros(back_ref.shape, F32)
         above_b_ref[...] = jnp.sum(above_ref[...].astype(F32), axis=0, keepdims=True)
 
+    def close(k):
+        grad_e_ref[k * part : (k + 1) * part, :] = movers[k].stage_third()
+
+    final = slices * per - 1
+    timed, late = [], []
+    for k in range(slices):
+        begun = 2 * ((k + 1) * per - 1) + 1
+        for after, action in zip(
+            AFTER, (movers[k].stage_core, movers[k].stage_first, movers[k].stage_second, functools.partial(close, k))
+        ):
+            if begun + after > 2 * final + 1:
+                late.append(action)
+            else:
+                timed.append((begun + after, action))
+
+    def stages(point):
+        for when, action in timed:
+            if when % 2 == point:
+                pl.when(step == when // 2)(action)
+
     pre = dot(second_ref[...], w_e) + bias_e_ref[...]
     square = pre * pre
     curve = jnp.tanh(CURVE * pre * (1.0 + 0.044715 * square))
@@ -574,6 +590,7 @@
     d_pre = (dot(above_ref[...], w_r, NT) * slope).astype(BF16)
     pre_s[...] = d_pre
     grad_b_ref[...] = jnp.sum(d_pre.astype(F32), axis=0, keepdims=True)
+    stages(0)
     out_ref[...] += dot(act_s[...], w_r)
     back_ref[...] += dot(d_pre, w_e, NT)
     grad_r_ref[...] = dot(act_s[...], above_ref[...], TN).astype(BF16).reshape(grad_r_ref.shape)
@@ -588,26 +605,11 @@
                 if j == per - 1:
                     movers[k].begin()
 
-    @pl.when(step >= slices * per)
-    def _():
-        rest_e_ref[...] = grad_e.reshape(rest_e_ref.shape)
-
-    def close(k):
-        grad_e_ref[k * part : (k + 1) * part, :] = movers[k].stage_third()
-
-    final = hidden_steps - 1
-    late = []
-    for k in range(slices):
-        for number, action in enumerate((movers[k].stage_core, movers[k].stage_first, movers[k].stage_second, functools.partial(close, k))):
-            when = (k + 1) * per + number
-            if when > final:
-                late.append((when, -k, action))
-            else:
-                pl.when(step == when)(action)
+    stages(1)
 
     @pl.when(step == final)
     def _():
-        for _, _, action in sorted(late, key=lambda entry: entry[:2]):
+        for action in late:
             action()
         for k in range(max(0, slices - 2), slices):
             movers[k].sent_first()
@@ -626,11 +628,10 @@
     fixed = pl.BlockSpec((rows, width), lambda i: (0, 0), pipeline_mode=pl.Buffered(1))
     whole = pl.BlockSpec(memory_space=pltpu.VMEM)
     scratch = [pltpu.VMEM((rows, strip), BF16)] * 2 + [pltpu.VMEM((2, outer, side, side, core, part, width), BF16)]
-    slices = sides - 1
-    for k in range(slices):
+    for k in range(sides):
         scratch += boxes_for(devices, part, width)
     return pl.pallas_call(
-        functools.partial(mixing_kernel, devices, hidden // strip),
+        functools.partial(mixing_kernel, devices),
         grid=(hidden // strip,),
         in_specs=[
             fixed, fixed,
@@ -644,8 +645,7 @@
             fixed,
             pl.BlockSpec((strip // many, many, width), lambda i: (i, 0, 0)),
             pl.BlockSpec((1, strip), lambda i: (0, i)),
-            pl.BlockSpec((slices * part, width), lambda i: (0, 0)),
-            pl.BlockSpec((devices, part, strip), lambda i: (0, 0, jnp.maximum(i - slices * per, 0))),
+            pl.BlockSpec((sides * part, width), lambda i: (0, 0)),
             pl.BlockSpec((1, width), lambda i: (0, 0)),
         ],
         out_shape=[
@@ -653,52 +653,130 @@
             jax.ShapeDtypeStruct((rows, width), F32),
             jax.ShapeDtypeStruct((devices, many, width), BF16),
             jax.ShapeDtypeStruct((1, hidden), F32),
-            jax.ShapeDtypeStruct((slices * part, width), F32),
-            jax.ShapeDtypeStruct((devices, part, width), BF16),
+            jax.ShapeDtypeStruct((sides * part, width), F32),
             jax.ShapeDtypeStruct((1, width), F32),
         ],
-        scratch_shapes=scratch + sems_for(devices, slices),
+        scratch_shapes=scratch + sems_for(devices, sides),
         compiler_params=pltpu.CompilerParams(collective_id=3, has_side_effects=True, vmem_limit_bytes=57 << 20),
         name="mixing",
     )(second, above, gathered, gathered, bias_e, bias_r)
 
 
+def join_kernel(
+    devices, window_ref, first_ref, final_ref, one_ref, above_ref, live_ref, w_ref, bias_ref, gain_ref, shift_ref,
+    combined_ref, out_ref, second_ref, reduce_ref, side_in, part_s, halo_sem,
+):
+    slots, width = one_ref.shape
+    half = slots // 2
+    tile = 256
+    me = lax.axis_index("fsdp")
+    last = devices - 1
+    left, right = lax.rem(me + last, devices), lax.rem(me + 1, devices)
+    greet([left, right])
+
+    def to_left():
+        return remote(window_ref.at[:half], side_in.at[1], halo_sem, (0,), left)
+
+    def to_right():
+        return remote(window_ref.at[half + slots :], side_in.at[0], halo_sem, (1,), right)
+
+    @pl.when(me > 0)
+    def _():
+        to_left().start()
+
+    @pl.when(me < last)
+    def _():
+        to_right().start()
+
+    @pl.when(me == 0)
+    def _():
+        side_in[0] = jnp.zeros((half, width), BF16)
+
+    @pl.when(me == last)
+    def _():
+        side_in[1] = jnp.zeros((half, width), BF16)
+
+    w_o = w_ref[...].reshape(width, width)
+
+    owns = (first_ref, final_ref)
+
+    def before(side, i, carry):
+        here = pl.ds(pl.multiple_of(i * tile, tile), tile)
+        at = pl.ds(pl.multiple_of(side * half + i * tile, tile), tile)
+        part_s[at, :] = dot(owns[side][here, :], w_o)
+        reduce_ref[at, :] = (live_ref[at, :] * above_ref[at, :].astype(F32)).astype(BF16)
+        return carry
+
+    for side in range(2):
+        lax.fori_loop(0, half // tile, functools.partial(before, side), 0)
+
+    def after(side, i, carry):
+        here = pl.ds(pl.multiple_of(i * tile, tile), tile)
+        at = pl.ds(pl.multiple_of(side * half + i * tile, tile), tile)
+        other = side_in[side, here, :]
+        combined_ref[at, :] = owns[side][here, :] + other
+        attended = part_s[at, :] + dot(other, w_o) + bias_ref[...]
+        out = one_ref[at, :].astype(F32) + live_ref[at, :] * attended
+        out_ref[at, :] = out
+        second_ref[at, :] = layer_norm(out, gain_ref[...], shift_ref[...]).astype(BF16)
+        return carry
+
+    @pl.when(me > 0)
+    def _():
+        to_right().wait_recv()
+
+    lax.fori_loop(0, half // tile, functools.partial(after, 0), 0)
+
+    @pl.when(me < last)
+    def _():
+        to_left().wait_recv()
+
+    lax.fori_loop(0, half // tile, functools.partial(after, 1), 0)
+
+    @pl.when(me > 0)
+    def _():
+        to_left().wait_send()
+
+    @pl.when(me < last)
+    def _():
+        to_right().wait_send()
+
+
+def join(devices, window, one, above, live, gathered, bias, gain, shift, part, sides):
+    slots, width = one.shape
+    dma = pltpu.SemaphoreType.DMA
+    rows = pl.BlockSpec((slots, width), lambda i: (0, 0))
+    thin = pl.BlockSpec((1, width), lambda i: (0, 0))
+    low = jax.ShapeDtypeStruct((slots, width), BF16)
+    return pl.pallas_call(
+        functools.partial(join_kernel, devices),
+        grid=(1,),
+        in_specs=[
+            pl.BlockSpec(memory_space=pl.ANY),
+            pl.BlockSpec((slots // 2, width), lambda i: (1, 0)), pl.BlockSpec((slots // 2, width), lambda i: (2, 0)), rows, rows, pl.BlockSpec((slots, 1), lambda i: (0, 0)),
+            pl.BlockSpec((devices, part, width), lambda i: (0, sides, 0)), thin, thin, thin,
+        ],
+        out_specs=[rows] * 4,
+        out_shape=[low, jax.ShapeDtypeStruct((slots, width), F32), low, low],
+        scratch_shapes=[pltpu.VMEM((2, slots // 2, width), BF16), pltpu.VMEM((slots, width), F32), dma((2, 2))],
+        compiler_params=pltpu.CompilerParams(collective_id=6, has_side_effects=True, vmem_limit_bytes=57 << 20),
+        name="join",
+    )(window, window, window, one, above, live, gathered, bias, gain, shift)
+
+
 def turn_kernel(
-    devices, grad_r_ref, grad_e_ref, out_one_ref, d_second_ref, mixed_ref, two_ref, above_ref, combined_ref, live_ref, gain_ref, w_o_ref,
+    devices, out_one_ref, d_second_ref, mixed_ref, two_ref, above_ref, combined_ref, live_ref, gain_ref, w_o_ref,
     bias_r_ref, bias_e_ref,
-    wide_ref, grad_one_ref, one_ref, res_two_ref, grad_o_ref, small_ref, part_e_ref, part_r_ref,
-    attend_s, load_sem, halo_sem, *rest,
+    wide_ref, grad_one_ref, one_ref, res_two_ref, grad_o_ref, small_ref, attend_s, halo_sem,
 ):
     slots, width = two_ref.shape
     half = slots // 2
     tile = 256
-    part = part_e_ref.shape[0]
-    where = neighbours(devices)
-    (o, p, q, c), *_ = where
+    part = grad_o_ref.shape[1]
     me = lax.axis_index("fsdp")
-    owns, rest = rest[:2], rest[2:]
-    sems = rest[-4:]
-
-    def distant(source, row, rows, k):
-        at = pl.ds(row, rows)
-
-        def other():
-            return source.at[:, :, :, 1 - c, at, :]
-
-        def mine(spot, cols):
-            return owns[k].at[tuple(spot) + (slice(None), cols)]
-
-        def load():
-            return pltpu.make_async_copy(source.at[:, :, :, c, at, :], owns[k], load_sem.at[k])
-
-        return Scatter(devices, where, k, rest[5 * k : 5 * k + 5], sems, other, mine, load)
-
-    movers = [distant(grad_e_ref, 0, part, 0), distant(grad_r_ref, 0, part_r_ref.shape[0], 1)]
     last = devices - 1
     left, right = lax.rem(me + last, devices), lax.rem(me + 1, devices)
-    greet(peers_of(where) + [left, right])
-    for mover in movers:
-        mover.begin()
+    greet([left, right])
 
     def to_left():
         return remote(wide_ref.at[half : 2 * half], wide_ref.at[half + slots :], halo_sem, (0,), left)
@@ -736,14 +814,11 @@
     def _():
         to_left().start()
 
-    movers[0].stage_core()
     lax.fori_loop(half // tile, slots // tile, norm_tile, 0)
 
     @pl.when(me < last)
     def _():
         to_right().start()
-
-    movers[1].stage_core()
 
     def finish_tile(i, carry):
         at = pl.ds(pl.multiple_of(i * tile, tile), tile)
@@ -753,7 +828,6 @@
         return carry
 
     lax.fori_loop(0, slots // tile, finish_tile, 0)
-    movers[0].stage_first()
 
     def weights(i, carry):
         cols = pl.ds(pl.multiple_of(i * tile, tile), tile)
@@ -764,14 +838,9 @@
         return carry
 
     lax.fori_loop(0, width // tile, weights, 0)
-    movers[1].stage_first()
-    movers[0].stage_second()
     small_ref[5:6, :] = bias_r_ref[...]
     for k in range(bias_e_ref.shape[1] // width):
         small_ref[6 + k : 7 + k, :] = bias_e_ref[:, k * width : (k + 1) * width]
-    movers[1].stage_second()
-    part_e_ref[...] = movers[0].stage_third()
-    part_r_ref[...] = movers[1].stage_third()
 
     @pl.when(me > 0)
     def _():
@@ -791,43 +860,25 @@
     def _():
         wide_ref[half + slots :] = jnp.zeros((half, width), BF16)
 
-    for mover in movers:
-        mover.sent_first()
-        mover.sent_last()
-
-
-def turn(devices, grad_r, grad_e, out_one, d_second, mixed, two, above, combined, live, gain, w_o, bias_r, bias_e):
+
+def turn(devices, out_one, d_second, mixed, two, above, combined, live, gain, w_o, bias_r, bias_e):
     slots, width = two.shape
-    outer, side, core = digits(devices)
-    part, many = grad_e.shape[1], grad_r.shape[1]
+    part = width // devices
     vmem = pl.BlockSpec(memory_space=pltpu.VMEM)
-    anywhere = pl.BlockSpec(memory_space=pl.ANY)
-    dma = pltpu.SemaphoreType.DMA
-    sizes = [part, many // 2]
-    scratch = [pltpu.VMEM((slots, width), BF16), dma((2,)), dma((2, 2))]
-    scratch += [pltpu.VMEM((outer, side, side, rows, width), BF16) for rows in sizes]
-    for rows in sizes:
-        scratch += boxes_for(devices, rows, width)
-    shape = (outer, side, side, core)
     rows_low = jax.ShapeDtypeStruct((slots, width), BF16)
     return pl.pallas_call(
         functools.partial(turn_kernel, devices),
-        in_specs=[anywhere, anywhere] + [vmem] * 11,
-        out_specs=(vmem,) * 8,
+        in_specs=[vmem] * 11,
+        out_specs=(vmem,) * 6,
         out_shape=(
             jax.ShapeDtypeStruct((2 * slots, width), BF16), rows_low, rows_low, rows_low,
             jax.ShapeDtypeStruct((devices, part, width), BF16),
             jax.ShapeDtypeStruct((16, width), F32),
-            jax.ShapeDtypeStruct((part, width), F32),
-            jax.ShapeDtypeStruct((many // 2, width), F32),
         ),
-        scratch_shapes=scratch + sems_for(devices, len(sizes)),
+        scratch_shapes=[pltpu.VMEM((slots, width), BF16), pltpu.SemaphoreType.DMA((2, 2))],
         compiler_params=pltpu.CompilerParams(collective_id=5, has_side_effects=True, vmem_limit_bytes=57 << 20),
         name="turn",
-    )(
-        grad_r.reshape(shape + grad_r.shape[1:]), grad_e.reshape(shape + grad_e.shape[1:]),
-        out_one, d_second, mixed, two, above, combined, live, gain, w_o, bias_r, bias_e,
-    )
+    )(out_one, d_second, mixed, two, above, combined, live, gain, w_o, bias_r, bias_e)
 
 
 def tail_kernel(
@@ -840,13 +891,13 @@
     slots = own_ref.shape[0]
     half = slots // 2
     part = out_s_ref.shape[0]
-    many = 2 * out_r_ref.shape[0]
+    many = out_r_ref.shape[0]
     tile = 256
     where = neighbours(devices)
     (o, p, q, c), core_peer, q_peers, p_peers, o_peers = where
     me = lax.axis_index("fsdp")
     outer, side, core = digits(devices)
-    owns, rest = rest[:2], rest[2:]
+    owns, rest = rest[:3], rest[3:]
     sems = rest[-4:]
 
     def distant(source, row, rows, k):
@@ -873,12 +924,13 @@
         return Scatter(devices, where, k, rest[5 * k : 5 * k + 5], sems, other, mine)
 
     movers = [
-        distant(grad_r_ref, many // 2, many // 2, 0), distant(grad_o_ref, 0, part, 1), near(0, 2), near(1, 3),
+        distant(grad_r_ref, 0, many // 2, 0), distant(grad_r_ref, many // 2, many // 2, 1), distant(grad_o_ref, 0, part, 2),
+        near(0, 3), near(1, 4),
     ]
     last = devices - 1
     left, right = lax.rem(me + last, devices), lax.rem(me + 1, devices)
     greet(peers_of(where) + [left, right])
-    for k in range(2):
+    for k in range(3):
         movers[k].begin()
 
     def to_left():
@@ -937,14 +989,14 @@
         lax.fori_loop(0, width // tile, strip, 0)
 
     weights(0, d_shared_ref)
-    movers[2].begin()
+    movers[3].begin()
     movers[1].stage_core()
     movers[0].stage_first()
     weights(1, d_value_ref)
-    movers[3].begin()
+    movers[4].begin()
+    movers[2].stage_core()
     movers[1].stage_first()
     movers[0].stage_second()
-    movers[2].stage_core()
 
     def own_tiles(i, carry):
         row = pl.multiple_of(i * tile, tile)
@@ -976,19 +1028,22 @@
     for copy in vector_copies(0):
         copy.start()
     movers[3].stage_core()
+    movers[2].stage_first()
     movers[1].stage_second()
-    out_r_ref[...] = movers[0].stage_third()
-    movers[2].stage_first()
+    out_r_ref[: many // 2, :] = movers[0].stage_third()
     vector_stage(0)
     for copy in vector_copies(1):
         copy.start()
+    movers[4].stage_core()
     movers[3].stage_first()
-    out_o_ref[...] = movers[1].stage_third()
     movers[2].stage_second()
+    out_r_ref[many // 2 :, :] = movers[1].stage_third()
     vector_stage(1)
     for copy in vector_copies(2):
         copy.start()
+    movers[4].stage_first()
     movers[3].stage_second()
+    out_o_ref[...] = movers[2].stage_third()
     vector_stage(2)
     for copy in vector_copies(3):
         copy.start()
@@ -1012,9 +1067,10 @@
     for k in range(2):
         at = slice(k * half, (k + 1) * half)
         back_ref[at, :] = (back_ref[at, :].astype(F32) + side_in[k].astype(F32)).astype(BF16)
-    out_s_ref[...] = movers[2].stage_third()
+    movers[4].stage_second()
+    out_s_ref[...] = movers[3].stage_third()
     vector_stage(3)
-    out_v_ref[...] = movers[3].stage_third()
+    out_v_ref[...] = movers[4].stage_third()
     vectors = 2 * side + outer - 3
     total = vector_in[vectors]
     thin_ref[...] = pltpu.roll(total, lax.rem(width - me * part, width), 1)[:, :DH]
@@ -1051,14 +1107,14 @@
     vmem = pl.BlockSpec(memory_space=pltpu.VMEM)
     anywhere = pl.BlockSpec(memory_space=pl.ANY)
     dma = pltpu.SemaphoreType.DMA
-    sizes = [many // 2, part, part, part]
+    sizes = [many // 2, many // 2, part, part, part]
     scratch = [
         pltpu.VMEM((2, slots // 2, width), BF16), pltpu.VMEM((2, slots // 2, width), BF16),
         pltpu.VMEM((16, width), F32), pltpu.VMEM((2 * side + outer - 2, 16, width), F32),
         pltpu.VMEM((2, outer, side, side, core, part, width), BF16),
-        dma((2,)), dma((2, 2)), dma((2, 2 * side + outer - 2)),
+        dma((3,)), dma((2, 2)), dma((2, 2 * side + outer - 2)),
     ]
-    scratch += [pltpu.VMEM((outer, side, side, rows, width), BF16) for rows in sizes[:2]]
+    scratch += [pltpu.VMEM((outer, side, side, rows, width), BF16) for rows in sizes[:3]]
     for rows in sizes:
         scratch += boxes_for(devices, rows, width)
     shape = (outer, side, side, core)
@@ -1071,7 +1127,7 @@
             jax.ShapeDtypeStruct((part, width), F32),
             jax.ShapeDtypeStruct((part, width), F32),
             jax.ShapeDtypeStruct((part, width), F32),
-            jax.ShapeDtypeStruct((many // 2, width), F32),
+            jax.ShapeDtypeStruct((many, width), F32),
             jax.ShapeDtypeStruct((16, DH), F32),
             jax.ShapeDtypeStruct((1, each), F32),
         ),
@@ -1084,7 +1140,7 @@
     )
 
 
-def rank_kernel(length_ref, target_ref, bucket_ref, block_ref, info_ref, before_s):
+def find_ranks(length_ref, target_ref, bucket_ref, packed_ref, info_ref, before_s):
     devices = length_ref.shape[0]
     lists, slots = bucket_ref.shape
     me = lax.axis_index("fsdp")
@@ -1134,22 +1190,7 @@
         ranks.append(jnp.sum(one_hot * place, axis=1))
     rank = jnp.concatenate(ranks, axis=0)
     live = lax.broadcasted_iota(jnp.int32, (lists, slots), 1) < mine
-    block_ref[...] = jnp.where(live, jnp.floor(rank * (1.0 / GROUP)), FREE).astype(BF16)
-
-
-def rank_blocks(lengths, destination, buckets):
-    lists, slots = buckets.shape
-    smem = pl.BlockSpec(memory_space=pltpu.SMEM)
-    vmem = pl.BlockSpec(memory_space=pltpu.VMEM)
-    return pl.pallas_call(
-        rank_kernel,
-        in_specs=[smem, smem, vmem],
-        out_specs=[vmem, smem],
-        out_shape=[jax.ShapeDtypeStruct((lists, slots), BF16), jax.ShapeDtypeStruct((8,), jnp.int32)],
-        scratch_shapes=[pltpu.VMEM((slots, slots), BF16)],
-        compiler_params=pltpu.CompilerParams(vmem_limit_bytes=32 << 20),
-        name="rank_blocks",
-    )(lengths, destination, buckets)
+    packed_ref[:lists, :] = jnp.where(live, jnp.floor(rank * (1.0 / GROUP)), FREE).astype(BF16)
 
 
 def project_kernel(
@@ -1223,28 +1264,58 @@
     )(info, head, own, tail, gain, shift, w_s, w_v, blocks, blocks)
 
 
-def gather_kernel(devices, arrays, *refs):
-    sources, outs = refs[:arrays], refs[arrays : 2 * arrays]
-    own_sem, sem_o, sem_a, sem_b, sem_c = refs[2 * arrays :]
+def gather_kernel(devices, arrays, length_ref, target_ref, bucket_ref, vector_ref, rows_ref, *refs):
+    sources, outs, (info_ref, head_ref, end_ref) = refs[: arrays - 1], refs[arrays - 1 : 2 * arrays - 1], refs[2 * arrays - 1 : 2 * arrays + 2]
+    packed_s, before_s, own_sem, sem_o, sem_a, sem_b, sem_c, halo_sem, edge_sem = refs[2 * arrays + 2 :]
+    sources = sources + (packed_s,)
     outer, side, core = digits(devices)
     (o, p, q, c), core_peer, q_peers, p_peers, o_peers = neighbours(devices)
-    greet([core_peer] + [d for _, d in q_peers] + [d for _, d in p_peers] + [d for _, d in o_peers])
+    me = lax.axis_index("fsdp")
+    last_device = devices - 1
+    left, right = lax.rem(me + last_device, devices), lax.rem(me + 1, devices)
+    greet([core_peer] + [d for _, d in q_peers] + [d for _, d in p_peers] + [d for _, d in o_peers] + [left, right])
     half = sources[0].shape[-1] // 2
+    border = head_ref.shape[0]
+
+    def to_left():
+        return remote(rows_ref.at[:border], end_ref, halo_sem, (0,), left)
+
+    def to_right():
+        return remote(rows_ref.at[border:], head_ref, halo_sem, (1,), right)
+
+    def blank(ref):
+        return pltpu.make_async_copy(before_s.at[:border], ref, edge_sem.at[0])
+
     columns = (pl.ds(0, half), pl.ds(half, half))
 
-    def remote(src, dst, sems, slot, device):
-        return pltpu.make_async_remote_copy(
-            src_ref=src, dst_ref=dst, send_sem=sems.at[(0,) + slot], recv_sem=sems.at[(1,) + slot],
-            device_id=(device,), device_id_type=MESH,
-        )
-
-    copies, locals_, begun, first, second, last = [], [], {}, {}, {}, {}
+    locals_, begun, first, second, last = [], {}, {}, {}, {}
     for s in range(arrays):
+        if s == arrays - 1:
+            find_ranks(length_ref, target_ref, bucket_ref, packed_s, info_ref, before_s)
+            packed_s[bucket_ref.shape[0] :, :] = vector_ref[...]
         locals_.append(pltpu.make_async_copy(sources[s], outs[s].at[o, p, q, c], own_sem.at[s]))
         locals_[s].start()
         for d, (k, device) in enumerate(o_peers):
             begun[s, d] = remote(sources[s], outs[s].at[o, p, q, c], sem_o, (s, d), device)
             begun[s, d].start()
+
+    @pl.when(me > 0)
+    def _():
+        to_left().start()
+
+    @pl.when(me < last_device)
+    def _():
+        to_right().start()
+
+    before_s[:border, :] = jnp.zeros((border, before_s.shape[1]), BF16)
+
+    @pl.when(me == 0)
+    def _():
+        blank(head_ref).start()
+
+    @pl.when(me == last_device)
+    def _():
+        blank(end_ref).start()
 
     def stage_a(s):
         locals_[s].wait()
@@ -1282,28 +1353,56 @@
             stage_c(t - 2)
     for s in range(arrays):
         last[s].wait_recv()
+
+    @pl.when(me > 0)
+    def _():
+        to_right().wait_recv()
+        to_left().wait_send()
+
+    @pl.when(me == 0)
+    def _():
+        blank(head_ref).wait()
+
+    @pl.when(me < last_device)
+    def _():
+        to_left().wait_recv()
+        to_right().wait_send()
+
+    @pl.when(me == last_device)
+    def _():
+        blank(end_ref).wait()
+
     for group in (begun, first, second, last):
         for copy in group.values():
             copy.wait_send()
 
 
-def gather(devices, arrays):
+def gather(devices, lengths, destination, buckets, vectors, rows, arrays):
     outer, side, core = digits(devices)
-    count = len(arrays)
+    lists, slots = buckets.shape
+    packed = jax.ShapeDtypeStruct((lists + vectors.shape[0], slots), BF16)
+    shapes = [jax.ShapeDtypeStruct(array.shape, array.dtype) for array in arrays] + [packed]
+    count = len(shapes)
     dma = pltpu.SemaphoreType.DMA
     anywhere = pl.BlockSpec(memory_space=pl.ANY)
+    smem = pl.BlockSpec(memory_space=pltpu.SMEM)
+    vmem = pl.BlockSpec(memory_space=pltpu.VMEM)
     outs = pl.pallas_call(
         functools.partial(gather_kernel, devices, count),
-        out_shape=tuple(jax.ShapeDtypeStruct((outer, side, side, core) + array.shape, array.dtype) for array in arrays),
-        in_specs=[anywhere] * count,
-        out_specs=(anywhere,) * count,
+        out_shape=tuple(jax.ShapeDtypeStruct((outer, side, side, core) + shape.shape, shape.dtype) for shape in shapes)
+        + (jax.ShapeDtypeStruct((8,), jnp.int32),)
+        + (jax.ShapeDtypeStruct((slots // 2, rows.shape[1]), BF16),) * 2,
+        in_specs=[smem, smem, vmem, vmem] + [anywhere] * count,
+        out_specs=(anywhere,) * count + (smem, anywhere, anywhere),
         scratch_shapes=[
-            dma((count,)), dma((2, count, outer - 1)), dma((2, count, 2, side - 1)), dma((2, count, 2, side - 1)), dma((2, count))
+            pltpu.VMEM(packed.shape, BF16), pltpu.VMEM((slots, slots), BF16),
+            dma((count,)), dma((2, count, outer - 1)), dma((2, count, 2, side - 1)), dma((2, count, 2, side - 1)), dma((2, count)),
+            dma((2, 2)), dma((1,)),
         ],
-        compiler_params=pltpu.CompilerParams(collective_id=2, has_side_effects=True),
+        compiler_params=pltpu.CompilerParams(collective_id=2, has_side_effects=True, vmem_limit_bytes=32 << 20),
         name="gather",
-    )(*arrays)
-    return [out.reshape((devices,) + array.shape) for out, array in zip(outs, arrays)]
+    )(lengths, destination, buckets, vectors, rows, *arrays)
+    return [out.reshape((devices,) + shape.shape) for out, shape in zip(outs, shapes)] + list(outs[count:])
 
 
 def body(
@@ -1319,19 +1418,8 @@
     part = w_shared.shape[0]
     hidden = w_expand.shape[1]
     sides = hidden // width
-    down = [(i, i - 1) for i in range(1, devices)]
-    up = [(i, i + 1) for i in range(devices - 1)]
-
-    def to_sides(head, tail):
-        return lax.ppermute(tail, "fsdp", up), lax.ppermute(head, "fsdp", down)
-
-    def narrow(wide):
-        head, tail = to_sides(wide[:half], wide[half + slots :])
-        return wide[half : half + slots], jnp.concatenate([head, tail], axis=0)
-
     base = me * slots
     lists = ROUNDS * HEADS
-    block, info = rank_blocks(lengths, destination, buckets[0])
     spot = jnp.arange(width, dtype=jnp.int32)
     short = jnp.stack([gain_attend, shift_attend, gain_mixing, shift_mixing, bias_output, bias_reduce])
     short = jnp.where(spot // part == me, jnp.tile(short, (1, devices)), 0.0)
@@ -1342,7 +1430,7 @@
     high = lax.reduce_precision(vectors, 8, 7)
     count = vectors.shape[0]
     packed = jnp.concatenate(
-        [block, high.astype(BF16), (vectors - high).astype(BF16), jnp.zeros((24 - 2 * count, width), BF16)], axis=0
+        [high.astype(BF16), (vectors - high).astype(BF16), jnp.zeros((24 - 2 * count, width), BF16)], axis=0
     )
     second_gather = lax.all_gather(
         jnp.concatenate(
@@ -1350,7 +1438,9 @@
         ),
         "fsdp", axis=0, tiled=False,
     )
-    full_shared, full_value, packed = gather(devices, [w_shared, w_value, packed])
+    full_shared, full_value, packed, info, two_head, two_tail = gather(
+        devices, lengths, destination, buckets[0], packed, input_two, [w_shared, w_value]
+    )
     full_shared, full_value = full_shared.reshape(width, width), full_value.reshape(width, width)
     vectors = jnp.sum(packed[:, lists : lists + 2 * count].astype(F32), axis=0)
     vectors = vectors[:count] + vectors[count:]
@@ -1362,25 +1452,18 @@
     spread = (row == ((lane % 64) // 16) * HEADS + lane // DH).astype(BF16)
 
     live = ((base + jnp.arange(slots, dtype=jnp.int32)) < info[6]).astype(F32)[:, None]
-    slot_one = input_one.astype(F32)
-    slot_two = input_two.astype(F32)
-    two_head, two_tail = to_sides(input_two[:half], input_two[half:])
     normed, shared, values, code = project(
         info, two_head, input_two, two_tail, gain_a, shift_a, full_shared, full_value, packed
     )
     combined_window, lse, lone = attend(info, shared, values, code, spread)
-    own, other = narrow(combined_window)
-    combined = own + other
-    attended = dot(combined, full_output) + bias_o
-    out_one = slot_one + live * attended
-    second = layer_norm(out_one, gain_m, shift_m).astype(BF16)
-    d_reduce = (live * upstream_two.astype(F32)).astype(BF16)
-    mixed, d_second, grad_reduce, grad_bias_expand, grad_expand, last_expand, grad_bias_reduce = mixing(
+    combined, out_one, second, d_reduce = join(
+        devices, combined_window, input_one, upstream_two, live, second_gather, bias_o, gain_m, shift_m, part, sides
+    )
+    mixed, d_second, grad_reduce, grad_bias_expand, grad_expand, grad_bias_reduce = mixing(
         devices, second, d_reduce, second_gather, bias_e, bias_r, part
     )
-    d_combined, grad_one, result_one, result_two, grad_output, small, last_expand, first_reduce = turn(
-        devices, grad_reduce, last_expand, out_one, d_second, mixed, input_two, upstream_one, combined, live, gain_m,
-        full_output, grad_bias_reduce, grad_bias_expand,
+    d_combined, grad_one, result_one, result_two, grad_output, small = turn(
+        devices, out_one, d_second, mixed, input_two, upstream_one, combined, live, gain_m, full_output, grad_bias_reduce, grad_bias_expand
     )
     d_shared, d_values = attend_back(
         info, shared, values, code, spread, combined_window, d_combined, lse, lone
@@ -1397,8 +1480,8 @@
         grad_shared,
         grad_value,
         grad_output,
-        jnp.concatenate([grad_expand[k * part : (k + 1) * part] for k in range(sides - 1)] + [last_expand], axis=1),
-        jnp.concatenate([first_reduce, grad_reduce], axis=0),
+        jnp.concatenate([grad_expand[k * part : (k + 1) * part] for k in range(sides)], axis=1),
+        grad_reduce,
         thin[0, :part],
         thin[1, :part],
         thin[2, :part],

time: 595 us -> 592 us (level)
  Pallas kernels: 486 us -> 523 us
  starting transfers between devices: 30.2 us -> 0.04 us
  other arithmetic: 17.3 us -> 5.04 us
  waiting for transfers between devices: 0.03 us -> 6.36 us
    ppermute x4 -> x0, starting transfers between devices: 30.1 us -> none  [to_sides(): return (lax.ppermute(tail, 'fsdp', up), lax.ppermute(head, 'fsdp', down))]
    pallas_call x1, Pallas kernels: 35.8 us -> 54.4 us  [attend_back(): pl.pallas_call(back_kernel, grid_spec=pltpu.PrefetchScalarGridSpec(num_sc...]
    pallas_call x1, Pallas kernels: 146 us -> 160 us  [tail(): pl.pallas_call(functools.partial(tail_kernel, devices), in_specs=[anywher...]
    pallas_call x3, Pallas kernels: 185 us -> 174 us  [the longest x1 132 us: mixing(): pl.pallas_call(functools.partial(mixing_kernel, devices), grid=(hidden //...]
    pallas_call x1, Pallas kernels: 82.9 us -> 92 us  [gather(): pl.pallas_call(functools.partial(gather_kernel, devices, count), out_shap...]
    pallas_call x1, Pallas kernels: 20 us -> 28.4 us  [attend(): pl.pallas_call(attend_kernel, grid_spec=pltpu.PrefetchScalarGridSpec(num_...]
    all_gather x1, waiting for transfers between devices: 0.01 us -> 6.35 us  [body(): lax.all_gather(jnp.concatenate([w_reduce, w_output] + [w_expand[:, k * wi...]
    unnamed x85 -> x76, local copies, waits for them, and re-layouts: 25.1 us -> 28.7 us
  transfers between devices with their start and end apart: 5 -> 1, of which waited for: 0 -> 1; matrix products, arithmetic and copies ran while one was open for 3% -> 1% of each run, Pallas kernels for 21% -> 23%
where the time goes in v6:
time: 592 us; the launch traced here: 587 us
  Pallas kernels  523 us (88%)
  local copies, waits for them, and re-layouts  37.5 us (6%)
  between operations  14.5 us (2%)
  waiting for transfers between devices  6.36 us (1%)
    pallas_call x1, Pallas kernels, tail(): pl.pallas_call(functools.partial(tail_kernel, devices), in_specs=[anywher...  160 us
    pallas_call x1, Pallas kernels, mixing(): pl.pallas_call(functools.partial(mixing_kernel, devices), grid=(hidden //...  132 us
    pallas_call x1, Pallas kernels, gather(): pl.pallas_call(functools.partial(gather_kernel, devices, count), out_shap...  92 us
    pallas_call x1, Pallas kernels, attend_back(): pl.pallas_call(back_kernel, grid_spec=pltpu.PrefetchScalarGridSpec(num_sc...  54.4 us
    unnamed x76, local copies, waits for them, and re-layouts  28.7 us
    pallas_call x1, Pallas kernels, attend(): pl.pallas_call(attend_kernel, grid_spec=pltpu.PrefetchScalarGridSpec(num_...  28.4 us
    pallas_call x1, Pallas kernels, turn(): pl.pallas_call(functools.partial(turn_kernel, devices), in_specs=[vmem] *...  24.6 us
    pallas_call x1, Pallas kernels, join(): pl.pallas_call(functools.partial(join_kernel, devices), grid=(1,), in_spe...  17.5 us
  transfers between devices with their start and end apart: 1, of which 1 were waited for; matrix products, arithmetic and copies ran while one was open for 1% of the time, Pallas kernels for 23%

profile of v6, /device:TPU:0, one launch (start us, length us, event | category | flops | bytes accessed | tf_op | source)
XLA Modules:
  0.0 587.0 jit_solution(16675839337524598518)
XLA Ops:
  14.7 92.0 %gather.1 = (bf16[4,2,2,2,32,1024]{5,4,3,2,1,0:T(8,128)(2,1)S(1)}, bf16[4,2,2,2,32,1024]{5,4,3,2,1,0:T(8,128)(2,1)S(1)}, bf16[4,2,2,2,56,1024]{5,4,3,2,1,0:T(8,1...) custom-call(s32[32]{0:T(128)S(1)} %copy-done.16, s32[32]{0:T(128)S(1)} %copy-done.17, ...), custom_call_target="tpu_custom_call" | custom-call | tf_op jit(solution)/shard_map/gather/pallas_call | solution.py:1390
  106.8 1.9 copy-done.3
  108.7 1.3 copy-done.5
  110.0 1.3 copy-done.7
  112.9 1.8 convert_reduce_fusion
  116.0 2.3 copy-done.4
  118.4 1.6 copy-done.6
  120.0 1.6 copy-done.8
  121.6 15.0 %project.1 = (bf16[2048,1024]{1,0:T(8,128)(2,1)}, bf16[2048,1024]{1,0:T(8,128)(2,1)}, bf16[2048,1024]{1,0:T(8,128)(2,1)}, bf16[32,2048]{1,0:T(8,128)(2,1)S(1)}) custom-call(s32[8]{0:T(128)S(1)} %get-tuple-element.54.info_ref.low_ref, bf16[512,1024]{1,0:T(8,128)(2,1)S(1)} %get-tuple-element.55.head_ref, bf16[1024,1024]{1,0:T(8,128)(2,1)S(1)} %copy-done.2, ...), custom_call_target="tpu_custom_call" | custom-call | tf_op jit(solution)/shard_map/project/pallas_call | solution.py:1246
  136.6 1.6 fusion.live_ref
  138.8 28.4 %attend.1 = (bf16[2048,1024]{1,0:T(8,128)(2,1)}, f32[8,1,2048]{2,1,0:T(1,128)}, f32[8,1,2048]{2,1,0:T(1,128)}) custom-call(s32[8]{0:T(128)} %copy-done.18, bf16[2048,1024]{1,0:T(8,128)(2,1)} %get-tuple-element.60.q_ref, bf16[2048,1024]{1,0:T(8,128)(2,1)} %get-tuple-element.61.v_ref, bf16[32,2048]{1,0:T(8,128)(2,1)} %copy-done.19, ...), custom_call_target="tpu_custom_call" | custom-call | flops 32212254720 | bytes 12582912 | tf_op jit(solution)/shard_map/attend/pallas_call | solution.py:317
  167.3 6.3 %all-gather.3.cloned.1.call-done = bf16[9216,1024]{1,0:T(8,128)(2,1)} async-done(((bf16[288,1024]{1,0:T(8,128)(2,1)}), bf16[9216,1024]{1,0:T(8,128)(2,1)}) %all-gather.3.cloned.1.call-update) | async-done | bytes 18874384 | tf_op jit(solution)/shard_map/all_gather | solution.py:1435
  173.6 3.2 slice.114
  176.8 17.5 %join.1 = (bf16[1024,1024]{1,0:T(8,128)(2,1)}, f32[1024,1024]{1,0:T(8,128)}, bf16[1024,1024]{1,0:T(8,128)(2,1)}, bf16[1024,1024]{1,0:T(8,128)(2,1)}) custom-call(bf16[2048,1024]{1,0:T(8,128)(2,1)} %get-tuple-element.63.window_ref.first_ref.final_ref.comb_ref, bf16[2048,1024]{1,0:T(8,128)(2,1)} %get-tuple-element.63.window_ref.first_ref.final_ref.comb_ref, ...), custom_call_target="tpu_custom_call" | custom-call | tf_op jit(solution)/shard_map/join/pallas_call | solution.py:751
  194.3 132.0 %mixing.1 = (f32[1024,1024]{1,0:T(8,128)}, f32[1024,1024]{1,0:T(8,128)}, bf16[32,128,1024]{2,1,0:T(8,128)(2,1)}, f32[1,4096]{1,0:T(1,128)}, f32[128,1024]{1,0:T(8,128)}, /*index=5*/f32[1,1024]{1,0:T(1,128)}) custom-call(bf16[1024,1024]{1,0:T(8,128)(2,1)} %get-tuple-element.65.second_ref, bf16[1024,1024]{1,0:T(8,128)(2,1)} %get-tuple-element.66.above_ref, ...), custom_call_target="tpu_custom_call" | custom-call | tf_op jit(solution)/shard_map/mixing/pallas_call | solution.py:633
  326.2 1.1 fusion.18
  327.4 24.6 %turn.1 = (bf16[2048,1024]{1,0:T(8,128)(2,1)}, bf16[1024,1024]{1,0:T(8,128)(2,1)}, bf16[1024,1024]{1,0:T(8,128)(2,1)}, bf16[1024,1024]{1,0:T(8,128)(2,1)}, bf16[...) custom-call(f32[1024,1024]{1,0:T(8,128)} %get-tuple-element.64.out_one_ref, f32[1024,1024]{1,0:T(8,128)} %get-tuple-element.67.d_second_ref, ...), custom_call_target="tpu_custom_call" | custom-call | tf_op jit(solution)/shard_map/turn/pallas_call | solution.py:869
  352.0 54.4 %attend_back.1 = (bf16[2048,1024]{1,0:T(8,128)(2,1)}, bf16[2048,1024]{1,0:T(8,128)(2,1)}) custom-call(s32[8]{0:T(128)} %copy-done.18, bf16[2048,1024]{1,0:T(8,128)(2,1)} %get-tuple-element.60.q_ref, bf16[2048,1024]{1,0:T(8,128)(2,1)} %get-tuple-element.61.v_ref, bf16[32,2048]{1,0:T(8,128)(2,1)} %copy-done.19, bf16[32,1024]{1,0:T(8,128)(2,1)} %fusion.1.spread_ref, ...), custom_call_target="tpu_custom_call" | custom-call | flops 64424509440 | bytes 25165824 | tf_op jit(solution)/shard_map/attend_back/pallas_call | solution.py:340
  406.5 159.5 %tail.1 = (bf16[1024,1024]{1,0:T(8,128)(2,1)}, f32[32,1024]{1,0:T(8,128)}, f32[32,1024]{1,0:T(8,128)}, f32[32,1024]{1,0:T(8,128)}, f32[128,1024]{1,0:T(8,128)}, /*index=5*/f32[16,128]{1,0:T(8,128)}, f32[1,128]{1,0:T(1,128)}) custom-call(bf16[4,2,2,2,128,1024]{5,4,3,2,1,0:T(8,128)(2,1)} %bitcast.46, bf16[4,2,2,2,32,1024]{5,4,3,2,1,0:T(8,128)(2,1)} %bitcast.48, ...), custom_call_target="tpu_custom_call" | custom-call | tf_op jit(solution)/shard_map/tail/pallas_call | solution.py:1121
  566.0 1.4 slice_bitcast_fusion.1
  568.3 1.3 copy.50
  570.6 1.3 copy.51
  573.0 1.3 copy.52
  575.3 1.3 copy.53
  (88 shorter events, 18.2 us)
Async XLA Ops:
  7.2 7.3 %copy-start = (f32[128]{0:T(128)S(1)}, f32[128]{0:T(128)}, u32[]{:S(2)}) copy-start(f32[128]{0:T(128)} %param.36) | copy-start | bytes 1540
  7.2 7.5 %copy-start.12 = (s32[1,32,1024]{2,1,0:T(8,128)S(1)}, s32[1,32,1024]{2,1,0:T(8,128)}, u32[]{:S(2)}) copy-start(s32[1,32,1024]{2,1,0:T(8,128)} %param.25) | copy-start | bytes 393220
  7.2 7.5 %copy-start.2 = (bf16[1024,1024]{1,0:T(8,128)(2,1)S(1)}, bf16[1024,1024]{1,0:T(8,128)(2,1)}, u32[]{:S(2)}) copy-start(bf16[1024,1024]{1,0:T(8,128)(2,1)} %own_ref.3) | copy-start | bytes 6291460
  7.2 7.5 %copy-start.16 = (s32[32]{0:T(128)S(1)}, s32[32]{0:T(128)}, u32[]{:S(2)}) copy-start(s32[32]{0:T(128)} %length_ref.1) | copy-start | bytes 388
  7.2 7.5 %copy-start.17 = (s32[32]{0:T(128)S(1)}, s32[32]{0:T(128)}, u32[]{:S(2)}) copy-start(s32[32]{0:T(128)} %target_ref.1) | copy-start | bytes 388
  7.2 7.5 %copy-start.13 = (bf16[32,1024]{1,0:T(8,128)(2,1)S(1)}, bf16[32,1024]{1,0:T(8,128)(2,1)}, u32[]{:S(2)}) copy-start(bf16[32,1024]{1,0:T(8,128)(2,1)} %refs_0_.1) | copy-start | bytes 196612
  7.3 7.5 %copy-start.14 = (bf16[32,1024]{1,0:T(8,128)(2,1)S(1)}, bf16[32,1024]{1,0:T(8,128)(2,1)}, u32[]{:S(2)}) copy-start(bf16[32,1024]{1,0:T(8,128)(2,1)} %refs_1_.1) | copy-start | bytes 196612
  7.3 166.3 %all-gather.3.cloned.1.call-start = ((), (), s32[]{:S(2)}) async-start(), calls=%async_computation | async-start | bytes 19464192 | tf_op jit(solution)/shard_map/all_gather | solution.py:1435
  106.8 1.9 copy-start.3
  112.3 24.3 %copy-start.9 = (bf16[512,1024]{1,0:T(8,128)(2,1)}, bf16[512,1024]{1,0:T(8,128)(2,1)S(1)}, u32[]{:S(2)}) copy-start(bf16[512,1024]{1,0:T(8,128)(2,1)S(1)} %get-tuple-element.55.head_ref) | copy-start | bytes 3145732
  112.3 24.3 %copy-start.18 = (s32[8]{0:T(128)}, s32[8]{0:T(128)S(1)}, u32[]{:S(2)}) copy-start(s32[8]{0:T(128)S(1)} %get-tuple-element.54.info_ref.low_ref) | copy-start | bytes 100
  112.9 3.1 copy-start.11
  116.0 20.6 %copy-start.15 = (f32[1,1024]{1,0:T(1,128)}, f32[1,1024]{1,0:T(1,128)S(1)}, u32[]{:S(2)}) copy-start(f32[1,1024]{1,0:T(1,128)S(1)} %get-tuple-element.101.gain_ref) | copy-start | bytes 12292
  116.0 2.4 copy-start.4
  136.6 2.2 copy-start.19
  406.5 161.8 %copy-start.22 = (bf16[1024,1024]{1,0:T(8,128)(2,1)S(1)}, bf16[1024,1024]{1,0:T(8,128)(2,1)}, u32[]{:S(2)}) copy-start(bf16[1024,1024]{1,0:T(8,128)(2,1)} %get-tuple-element.126) | copy-start | bytes 6291460
  568.3 2.3 copy-start.21
  570.6 2.3 copy-start.20
  573.0 2.3 copy-start.23
  573.0 7.0 %copy-start.1 = (f32[128]{0:T(128)S(1)}, f32[128]{0:T(128)}, u32[]{:S(2)}) copy-start(f32[128]{0:T(128)} %param.36) | copy-start | bytes 1540
  575.3 2.0 copy-start.27
  575.3 2.7 copy-start.26
  575.3 3.3 copy-start.25
  575.3 4.1 copy-start.29
  (7 other events, 9.0 us)
Sparse Core Ops, SparseCore 0:
  13.6 159.9 all-gather.2

commit v7 on v6

--- a/solution.py
+++ b/solution.py
@@ -21,13 +21,15 @@
 SCALE = 1.0 / math.sqrt(DH)
 TILE = 512
 HALF = TILE // 2
+KEYS = 256
+MANY = TILE // KEYS
 STEP = 128.0
 SHIFT = 1.5 * 2.0**30
 TAME = 3000.0
 PAIR = 4
 FREE = 99.0
 STRIP = 512
-AFTER = (1, 4, 6, 8)
+AFTER = (2, 4, 6, 8)
 CURVE = math.sqrt(2.0 / math.pi)
 MESH = pl.DeviceIdType.MESH
 
@@ -67,7 +69,7 @@
     one = (info_ref[0] < stop) & (info_ref[1] > start)
     two = (info_ref[2] < stop) & (info_ref[3] > start)
     begin = jnp.where(one, info_ref[0], jnp.where(two, info_ref[2], stop))
-    return lax.div(begin, TILE)
+    return lax.div(begin, KEYS)
 
 
 def tile_rows(i):
@@ -104,7 +106,7 @@
                 more_s[h, at, DH:] = jnp.ones((TILE, DH), BF16)
             return most
 
-        return jnp.maximum(largest, lax.cond(lowest(low_ref, i) <= i, fill, lambda: jnp.float32(0.0)))
+        return jnp.maximum(largest, lax.cond(lowest(low_ref, i) <= (i + 1) * MANY - 1, fill, lambda: jnp.float32(0.0)))
 
     largest = lax.fori_loop(0, tiles, ready, jnp.float32(0.0))
     tame = largest * (SCALE * LOG2E) ** 2 < TAME
@@ -123,19 +125,19 @@
         at = tile_rows(i)
         low = lowest(low_ref, i)
 
-        @pl.when((low <= i) & tame)
+        @pl.when((low < (i + 1) * MANY) & tame)
         def _():
             for h in range(PAIR):
                 acc_s[h] = jnp.zeros((TILE, 2 * DH), F32)
 
             def step(j, carry):
-                keys = tile_rows(j)
+                keys = pl.ds(pl.multiple_of(j * KEYS, KEYS), KEYS)
                 for h in range(PAIR):
                     count, score = part_of(dot(ask_s[h, at, :], key_s[h, keys, :], NT))
                     acc_s[h] += dot((count * jnp.exp2(score)).astype(BF16), more_s[h, keys, :])
                 return carry
 
-            lax.fori_loop(low, i, step, 0)
+            lax.fori_loop(low, i * MANY, step, 0)
             for h, cols in enumerate(heads):
                 for asks, span in halves(i):
                     here = pl.ds(asks[0], HALF)
@@ -153,7 +155,7 @@
                     lone_ref[h, :, there] = lone.T[:1]
                 finish(h, cols, at, 0.0)
 
-        @pl.when((low <= i) & jnp.logical_not(tame))
+        @pl.when((low < (i + 1) * MANY) & jnp.logical_not(tame))
         def _():
             for h, cols in enumerate(heads):
                 count, score = apart(ask_s[h, at, :], key_s[h, at, :])
@@ -165,7 +167,7 @@
                 top_s[h] = jnp.broadcast_to(top, (TILE, DH))
 
                 def step(j, carry):
-                    keys = tile_rows(j)
+                    keys = pl.ds(pl.multiple_of(j * KEYS, KEYS), KEYS)
                     count, score = apart(ask_s[h, at, :], key_s[h, keys, :])
                     score = jnp.where(count > 0.5, score, NEG)
                     top = top_s[h]
@@ -176,13 +178,13 @@
                     top_s[h] = newer
                     return carry
 
-                lax.fori_loop(low, i, step, 0)
+                lax.fori_loop(low, i * MANY, step, 0)
                 total = acc_s[h, :, DH:]
                 own = STEP * ROUNDS * jnp.exp2(SELF2 - jnp.maximum(top_s[h], SELF2))
                 lone_ref[h, :, at] = jnp.where(total > 0.0, own / jnp.where(total > 0.0, total, 1.0), 0.0).T[:1]
                 finish(h, cols, at, top_s[h])
 
-        @pl.when(low > i)
+        @pl.when(low >= (i + 1) * MANY)
         def _():
             comb_ref[at, :] = jnp.zeros((TILE, PAIR * DH), BF16)
             for h in range(PAIR):
@@ -195,10 +197,36 @@
 
 
 def back_kernel(
-    low_ref, q_ref, v_ref, code_ref, spread_ref, comb_ref, above_ref, lse_ref, lone_ref,
-    dq_ref, dv_ref, ask_s, key_s, dunit_s, dvalue_s, dask_s,
+    low_ref, q_ref, v_ref, code_ref, spread_ref, comb_ref, above_ref, lse_ref, lone_ref, *rest,
 ):
+    count = (len(rest) - 8) // 2
+    sources, (dq_ref, dv_ref, *targets) = rest[:count], rest[count : 2 * count + 2]
+    ask_s, key_s, dunit_s, dvalue_s, dask_s, sem = rest[2 * count + 2 :]
     rows = q_ref.shape[0]
+    width = q_ref.shape[1] * (HEADS // PAIR)
+
+    def copies():
+        started = []
+        for source, target in zip(sources, targets):
+            for k in range(target.shape[1] // width):
+                part = source.shape[0] * width // target.shape[1]
+                started.append(
+                    pltpu.make_async_copy(
+                        source.at[k * part : (k + 1) * part, :], target.at[:, k * width : (k + 1) * width], sem.at[len(started)]
+                    )
+                )
+        return started
+
+    @pl.when(pl.program_id(0) == 0)
+    def _():
+        for copy in copies():
+            copy.start()
+
+    @pl.when(pl.program_id(0) == pl.num_programs(0) - 1)
+    def _():
+        for copy in copies():
+            copy.wait()
+
     tiles = rows // TILE
     heads = [slice(h * DH, (h + 1) * DH) for h in range(PAIR)]
 
@@ -212,7 +240,7 @@
                     total[h, at, :] = jnp.zeros((TILE, DH), F32)
             return most
 
-        return jnp.maximum(largest, lax.cond(lowest(low_ref, i) <= i, fill, lambda: jnp.float32(0.0)))
+        return jnp.maximum(largest, lax.cond(lowest(low_ref, i) <= (i + 1) * MANY - 1, fill, lambda: jnp.float32(0.0)))
 
     largest = lax.fori_loop(0, tiles, ready, jnp.float32(0.0))
     tame = largest * (SCALE * LOG2E) ** 2 < TAME
@@ -225,7 +253,7 @@
             deltas.append(jnp.sum(mixed.T, axis=0, keepdims=True))
 
         def step(j, carry):
-            keys = tile_rows(j)
+            keys = pl.ds(pl.multiple_of(j * KEYS, KEYS), KEYS)
             for h, cols in enumerate(heads):
                 q, above, unit = q_ref[at, cols], above_ref[at, cols], key_s[h, keys, :DH]
                 count, score = split(key_s[h, keys, :], ask_s[h, at, :])
@@ -237,7 +265,7 @@
                 dask_s[h, at, :] += dot(d_score, unit, TN)
             return carry
 
-        deltas = lax.fori_loop(low, i, step, tuple(deltas))
+        deltas = lax.fori_loop(low, i * MANY, step, tuple(deltas))
         for h, cols in enumerate(heads):
             for asks, span in halves(i):
                 there = pl.ds(asks[1], HALF)
@@ -265,11 +293,11 @@
     def rows_of(i, carry):
         low = lowest(low_ref, i)
 
-        @pl.when((low <= i) & tame)
+        @pl.when((low < (i + 1) * MANY) & tame)
         def _():
             pass_over(i, low, together)
 
-        @pl.when((low <= i) & jnp.logical_not(tame))
+        @pl.when((low < (i + 1) * MANY) & jnp.logical_not(tame))
         def _():
             pass_over(i, low, guarded)
 
@@ -280,7 +308,7 @@
     def close(i, carry):
         at = tile_rows(i)
 
-        @pl.when(lowest(low_ref, i) <= i)
+        @pl.when(lowest(low_ref, i) <= (i + 1) * MANY - 1)
         def _():
             for h, cols in enumerate(heads):
                 q = q_ref[at, cols].astype(F32)
@@ -291,7 +319,7 @@
                 dq_ref[at, cols] = d_q.astype(BF16)
                 dv_ref[at, cols] = dvalue_s[h, at, :].astype(BF16)
 
-        @pl.when(lowest(low_ref, i) > i)
+        @pl.when(lowest(low_ref, i) > (i + 1) * MANY - 1)
         def _():
             dq_ref[at, :] = jnp.zeros((TILE, PAIR * DH), BF16)
             dv_ref[at, :] = jnp.zeros((TILE, PAIR * DH), BF16)
@@ -333,7 +361,7 @@
     )(low, shared, values, code, spread)
 
 
-def attend_back(low, shared, values, code, spread, combined, above, lse, lone):
+def attend_back(low, shared, values, code, spread, combined, above, lse, lone, sources, shapes):
     rows = shared.shape[0]
     by_head, code_spec, spread_spec, stat = head_specs(rows)
     wide = jax.ShapeDtypeStruct((rows, HEADS * DH), BF16)
@@ -342,17 +370,19 @@
         grid_spec=pltpu.PrefetchScalarGridSpec(
             num_scalar_prefetch=1,
             grid=(HEADS // PAIR,),
-            in_specs=[by_head, by_head, code_spec, spread_spec, by_head, by_head, stat, stat],
-            out_specs=[by_head, by_head],
-            scratch_shapes=[pltpu.VMEM((PAIR, rows, 2 * DH), BF16)] * 2 + [pltpu.VMEM((PAIR, rows, DH), F32)] * 3,
+            in_specs=[by_head, by_head, code_spec, spread_spec, by_head, by_head, stat, stat]
+            + [pl.BlockSpec(memory_space=pl.ANY)] * len(sources),
+            out_specs=[by_head, by_head] + [pl.BlockSpec(memory_space=pltpu.HBM)] * len(sources),
+            scratch_shapes=[pltpu.VMEM((PAIR, rows, 2 * DH), BF16)] * 2 + [pltpu.VMEM((PAIR, rows, DH), F32)] * 3
+            + [pltpu.SemaphoreType.DMA((16,))],
         ),
-        out_shape=(wide, wide),
+        out_shape=(wide, wide) + tuple(jax.ShapeDtypeStruct(shape, source.dtype) for shape, source in zip(shapes, sources)),
         compiler_params=pltpu.CompilerParams(vmem_limit_bytes=57 << 20),
         name="attend_back",
         cost_estimate=pl.CostEstimate(
             flops=HEADS * 20 * 6 * 2 * TILE * TILE * DH, bytes_accessed=rows * HEADS * DH * 12, transcendentals=HEADS * 20 * TILE * TILE
         ),
-    )(low, shared, values, code, spread, combined, above, lse, lone)
+    )(low, shared, values, code, spread, combined, above, lse, lone, *sources)
 
 
 def digits(devices):
@@ -572,7 +602,7 @@
             AFTER, (movers[k].stage_core, movers[k].stage_first, movers[k].stage_second, functools.partial(close, k))
         ):
             if begun + after > 2 * final + 1:
-                late.append(action)
+                late.append((begun + after, -k, action))
             else:
                 timed.append((begun + after, action))
 
@@ -609,7 +639,7 @@
 
     @pl.when(step == final)
     def _():
-        for action in late:
+        for *_, action in sorted(late, key=lambda entry: entry[:2]):
             action()
         for k in range(max(0, slices - 2), slices):
             movers[k].sent_first()
@@ -1385,6 +1415,7 @@
     count = len(shapes)
     dma = pltpu.SemaphoreType.DMA
     anywhere = pl.BlockSpec(memory_space=pl.ANY)
+    hbm = pl.BlockSpec(memory_space=pltpu.HBM)
     smem = pl.BlockSpec(memory_space=pltpu.SMEM)
     vmem = pl.BlockSpec(memory_space=pltpu.VMEM)
     outs = pl.pallas_call(
@@ -1393,7 +1424,7 @@
         + (jax.ShapeDtypeStruct((8,), jnp.int32),)
         + (jax.ShapeDtypeStruct((slots // 2, rows.shape[1]), BF16),) * 2,
         in_specs=[smem, smem, vmem, vmem] + [anywhere] * count,
-        out_specs=(anywhere,) * count + (smem, anywhere, anywhere),
+        out_specs=(hbm,) * count + (smem, hbm, hbm),
         scratch_shapes=[
             pltpu.VMEM(packed.shape, BF16), pltpu.VMEM((slots, slots), BF16),
             dma((count,)), dma((2, count, outer - 1)), dma((2, count, 2, side - 1)), dma((2, count, 2, side - 1)), dma((2, count)),
@@ -1465,8 +1496,10 @@
     d_combined, grad_one, result_one, result_two, grad_output, small = turn(
         devices, out_one, d_second, mixed, input_two, upstream_one, combined, live, gain_m, full_output, grad_bias_reduce, grad_bias_expand
     )
-    d_shared, d_values = attend_back(
-        info, shared, values, code, spread, combined_window, d_combined, lse, lone
+    rows = (slots, width)
+    d_shared, d_values, grad_one, result_one, result_two, grad_expand = attend_back(
+        info, shared, values, code, spread, combined_window, d_combined, lse, lone,
+        (grad_one, result_one, result_two, grad_expand), (rows, rows, rows, (part, hidden)),
     )
     grad_two, grad_shared, grad_value, grad_output, grad_reduce, thin, long = tail(
         devices, grad_reduce, grad_output, d_shared, d_values, normed,
@@ -1480,7 +1513,7 @@
         grad_shared,
         grad_value,
         grad_output,
-        jnp.concatenate([grad_expand[k * part : (k + 1) * part] for k in range(sides)], axis=1),
+        grad_expand,
         grad_reduce,
         thin[0, :part],
         thin[1, :part],

time: 592 us -> 748 us (1.26)
  Pallas kernels: 523 us -> 674 us
    pallas_call x1, Pallas kernels: 54.4 us -> 230 us  [attend_back(): pl.pallas_call(back_kernel, grid_spec=pltpu.PrefetchScalarGridSpec(num_sc...]
    pallas_call x1, Pallas kernels: 132 us -> 116 us  [mixing(): pl.pallas_call(functools.partial(mixing_kernel, devices), grid=(hidden //...]
    pallas_call x1, Pallas kernels: 160 us -> 151 us  [tail(): pl.pallas_call(functools.partial(tail_kernel, devices), in_specs=[anywher...]
    pallas_call x1, Pallas kernels: 17.5 us -> 25 us  [join(): pl.pallas_call(functools.partial(join_kernel, devices), grid=(1,), in_spe...]
    unnamed x76 -> x65, local copies, waits for them, and re-layouts: 28.7 us -> 23.5 us
  transfers between devices with their start and end apart: 1 -> 1, of which waited for: 1 -> 1; matrix products, arithmetic and copies ran while one was open for 1% -> 1% of each run, Pallas kernels for 23% -> 17%
where the time goes in v7:
time: 748 us; the launch traced here: 738 us
  Pallas kernels  674 us (90%)
  local copies, waits for them, and re-layouts  31.2 us (4%)
  between operations  14.6 us (2%)
  waiting for transfers between devices  13.8 us (2%)
    pallas_call x1, Pallas kernels, attend_back(): pl.pallas_call(back_kernel, grid_spec=pltpu.PrefetchScalarGridSpec(num_sc...  230 us
    pallas_call x1, Pallas kernels, tail(): pl.pallas_call(functools.partial(tail_kernel, devices), in_specs=[anywher...  151 us
    pallas_call x1, Pallas kernels, mixing(): pl.pallas_call(functools.partial(mixing_kernel, devices), grid=(hidden //...  116 us
    pallas_call x1, Pallas kernels, gather(): pl.pallas_call(functools.partial(gather_kernel, devices, count), out_shap...  92 us
    pallas_call x1, Pallas kernels, join(): pl.pallas_call(functools.partial(join_kernel, devices), grid=(1,), in_spe...  25 us
    pallas_call x1, Pallas kernels, turn(): pl.pallas_call(functools.partial(turn_kernel, devices), in_specs=[vmem] *...  24.4 us
    unnamed x65, local copies, waits for them, and re-layouts  23.5 us
    pallas_call x1, Pallas kernels, attend(): pl.pallas_call(attend_kernel, grid_spec=pltpu.PrefetchScalarGridSpec(num_...  21 us
  transfers between devices with their start and end apart: 1, of which 1 were waited for; matrix products, arithmetic and copies ran while one was open for 1% of the time, Pallas kernels for 17%

profile of v7, /device:TPU:0, one launch (start us, length us, event | category | flops | bytes accessed | tf_op | source)
XLA Modules:
  0.0 738.3 jit_solution(13010926434067812590)
XLA Ops:
  7.3 1.1 constant_dynamic-update-slice_fusion.1
  8.4 0.8 constant_dynamic-update-slice_fusion
  10.1 0.8 slice_dynamic-update-slice_fusion.2
  14.7 92.0 %gather.1 = (bf16[4,2,2,2,32,1024]{5,4,3,2,1,0:T(8,128)(2,1)S(1)}, bf16[4,2,2,2,32,1024]{5,4,3,2,1,0:T(8,128)(2,1)S(1)}, bf16[4,2,2,2,56,1024]{5,4,3,2,1,0:T(8,1...) custom-call(s32[32]{0:T(128)S(1)} %copy-done.16, s32[32]{0:T(128)S(1)} %copy-done.17, ...), custom_call_target="tpu_custom_call" | custom-call | tf_op jit(solution)/shard_map/gather/pallas_call | solution.py:1421
  106.8 1.9 copy-done.3
  108.6 1.3 copy-done.5
  110.0 1.4 copy-done.7
  111.3 1.0 copy-done.10
  113.0 1.8 convert_reduce_fusion
  116.1 2.3 copy-done.4
  118.4 1.6 copy-done.6
  120.0 1.6 copy-done.8
  121.6 15.0 %project.1 = (bf16[2048,1024]{1,0:T(8,128)(2,1)}, bf16[2048,1024]{1,0:T(8,128)(2,1)}, bf16[2048,1024]{1,0:T(8,128)(2,1)}, bf16[32,2048]{1,0:T(8,128)(2,1)S(1)}) custom-call(s32[8]{0:T(128)S(1)} %get-tuple-element.58.info_ref.low_ref, bf16[512,1024]{1,0:T(8,128)(2,1)S(1)} %get-tuple-element.59.head_ref, bf16[1024,1024]{1,0:T(8,128)(2,1)S(1)} %copy-done.2, ...), custom_call_target="tpu_custom_call" | custom-call | tf_op jit(solution)/shard_map/project/pallas_call | solution.py:1276
  136.7 1.6 fusion.live_ref
  138.8 21.0 %attend.1 = (bf16[2048,1024]{1,0:T(8,128)(2,1)}, f32[8,1,2048]{2,1,0:T(1,128)}, f32[8,1,2048]{2,1,0:T(1,128)}) custom-call(s32[8]{0:T(128)} %copy-done.18, bf16[2048,1024]{1,0:T(8,128)(2,1)} %get-tuple-element.64.q_ref, bf16[2048,1024]{1,0:T(8,128)(2,1)} %get-tuple-element.65.v_ref, bf16[32,2048]{1,0:T(8,128)(2,1)} %copy-done.19, ...), custom_call_target="tpu_custom_call" | custom-call | flops 32212254720 | bytes 12582912 | tf_op jit(solution)/shard_map/attend/pallas_call | solution.py:345
  159.9 13.7 %all-gather.3.cloned.1.call-done = bf16[9216,1024]{1,0:T(8,128)(2,1)} async-done(((bf16[288,1024]{1,0:T(8,128)(2,1)}), bf16[9216,1024]{1,0:T(8,128)(2,1)}) %all-gather.3.cloned.1.call-update) | async-done | bytes 18874384 | tf_op jit(solution)/shard_map/all_gather | solution.py:1466
  173.6 3.2 slice.98
  176.8 25.0 %join.1 = (bf16[1024,1024]{1,0:T(8,128)(2,1)}, f32[1024,1024]{1,0:T(8,128)}, bf16[1024,1024]{1,0:T(8,128)(2,1)}, bf16[1024,1024]{1,0:T(8,128)(2,1)}) custom-call(bf16[2048,1024]{1,0:T(8,128)(2,1)} %get-tuple-element.67.window_ref.first_ref.final_ref.comb_ref, bf16[2048,1024]{1,0:T(8,128)(2,1)} %get-tuple-element.67.window_ref.first_ref.final_ref.comb_ref, ...), custom_call_target="tpu_custom_call" | custom-call | tf_op jit(solution)/shard_map/join/pallas_call | solution.py:781
  201.8 116.1 %mixing.1 = (f32[1024,1024]{1,0:T(8,128)}, f32[1024,1024]{1,0:T(8,128)}, bf16[32,128,1024]{2,1,0:T(8,128)(2,1)}, f32[1,4096]{1,0:T(1,128)}, f32[128,1024]{1,0:T(8,128)}, /*index=5*/f32[1,1024]{1,0:T(1,128)}) custom-call(bf16[1024,1024]{1,0:T(8,128)(2,1)} %get-tuple-element.69.second_ref, bf16[1024,1024]{1,0:T(8,128)(2,1)} %get-tuple-element.70.above_ref, ...), custom_call_target="tpu_custom_call" | custom-call | tf_op jit(solution)/shard_map/mixing/pallas_call | solution.py:663
  317.9 24.4 %turn.1 = (bf16[2048,1024]{1,0:T(8,128)(2,1)}, bf16[1024,1024]{1,0:T(8,128)(2,1)}, bf16[1024,1024]{1,0:T(8,128)(2,1)}, bf16[1024,1024]{1,0:T(8,128)(2,1)}, bf16[...) custom-call(f32[1024,1024]{1,0:T(8,128)} %get-tuple-element.68.out_one_ref, f32[1024,1024]{1,0:T(8,128)} %get-tuple-element.71.d_second_ref, ...), custom_call_target="tpu_custom_call" | custom-call | tf_op jit(solution)/shard_map/turn/pallas_call | solution.py:899
  342.3 230.1 %attend_back.1 = (bf16[2048,1024]{1,0:T(8,128)(2,1)}, bf16[2048,1024]{1,0:T(8,128)(2,1)}, bf16[1024,1024]{1,0:T(8,128)(2,1)}, bf16[1024,1024]{1,0:T(8,128)(2,1)}...) custom-call(s32[8]{0:T(128)} %copy-done.18, bf16[2048,1024]{1,0:T(8,128)(2,1)} %get-tuple-element.64.q_ref, ...), custom_call_target="tpu_custom_call" | custom-call | flops 64424509440 | bytes 25165824 | tf_op jit(solution)/shard_map/attend_back/pallas_call | solution.py:368
  572.4 150.9 %tail.1 = (bf16[1024,1024]{1,0:T(8,128)(2,1)}, f32[32,1024]{1,0:T(8,128)}, f32[32,1024]{1,0:T(8,128)}, f32[32,1024]{1,0:T(8,128)}, f32[128,1024]{1,0:T(8,128)}, /*index=5*/f32[16,128]{1,0:T(8,128)}, f32[1,128]{1,0:T(1,128)}) custom-call(bf16[4,2,2,2,128,1024]{5,4,3,2,1,0:T(8,128)(2,1)} %bitcast.46, bf16[4,2,2,2,32,1024]{5,4,3,2,1,0:T(8,128)(2,1)} %bitcast.48, ...), custom_call_target="tpu_custom_call" | custom-call | tf_op jit(solution)/shard_map/tail/pallas_call | solution.py:1151
  723.3 1.4 slice_bitcast_fusion.1
  724.8 3.2 copy.47
  (75 shorter events, 10.5 us)
Async XLA Ops:
  7.2 7.3 copy-start
  7.2 7.5 %copy-start.12 = (s32[1,32,1024]{2,1,0:T(8,128)S(1)}, s32[1,32,1024]{2,1,0:T(8,128)}, u32[]{:S(2)}) copy-start(s32[1,32,1024]{2,1,0:T(8,128)} %param.25) | copy-start | bytes 393220
  7.2 7.5 %copy-start.2 = (bf16[1024,1024]{1,0:T(8,128)(2,1)S(1)}, bf16[1024,1024]{1,0:T(8,128)(2,1)}, u32[]{:S(2)}) copy-start(bf16[1024,1024]{1,0:T(8,128)(2,1)} %own_ref.3) | copy-start | bytes 6291460
  7.2 7.5 %copy-start.16 = (s32[32]{0:T(128)S(1)}, s32[32]{0:T(128)}, u32[]{:S(2)}) copy-start(s32[32]{0:T(128)} %length_ref.1) | copy-start | bytes 388
  7.2 7.5 %copy-start.17 = (s32[32]{0:T(128)S(1)}, s32[32]{0:T(128)}, u32[]{:S(2)}) copy-start(s32[32]{0:T(128)} %target_ref.1) | copy-start | bytes 388
  7.2 7.5 %copy-start.13 = (bf16[32,1024]{1,0:T(8,128)(2,1)S(1)}, bf16[32,1024]{1,0:T(8,128)(2,1)}, u32[]{:S(2)}) copy-start(bf16[32,1024]{1,0:T(8,128)(2,1)} %refs_0_.1) | copy-start | bytes 196612
  7.3 7.5 %copy-start.14 = (bf16[32,1024]{1,0:T(8,128)(2,1)S(1)}, bf16[32,1024]{1,0:T(8,128)(2,1)}, u32[]{:S(2)}) copy-start(bf16[32,1024]{1,0:T(8,128)(2,1)} %refs_1_.1) | copy-start | bytes 196612
  7.3 166.4 %all-gather.3.cloned.1.call-start = ((), (), s32[]{:S(2)}) async-start(), calls=%async_computation | async-start | bytes 19464192 | tf_op jit(solution)/shard_map/all_gather | solution.py:1466
  106.8 1.9 copy-start.3
  110.0 1.4 copy-start.7
  112.3 24.3 %copy-start.9 = (bf16[512,1024]{1,0:T(8,128)(2,1)}, bf16[512,1024]{1,0:T(8,128)(2,1)S(1)}, u32[]{:S(2)}) copy-start(bf16[512,1024]{1,0:T(8,128)(2,1)S(1)} %get-tuple-element.59.head_ref) | copy-start | bytes 3145732
  112.3 24.3 %copy-start.18 = (s32[8]{0:T(128)}, s32[8]{0:T(128)S(1)}, u32[]{:S(2)}) copy-start(s32[8]{0:T(128)S(1)} %get-tuple-element.58.info_ref.low_ref) | copy-start | bytes 100
  113.0 3.1 copy-start.11
  116.1 20.6 %copy-start.15 = (f32[1,1024]{1,0:T(1,128)}, f32[1,1024]{1,0:T(1,128)S(1)}, u32[]{:S(2)}) copy-start(f32[1,1024]{1,0:T(1,128)S(1)} %get-tuple-element.105.gain_ref) | copy-start | bytes 12292
  116.1 2.3 copy-start.4
  118.4 1.6 copy-start.6
  120.0 1.6 copy-start.8
  136.6 2.2 copy-start.19
  724.7 6.5 copy-start.1
  724.7 3.2 copy-start.24
  724.7 3.9 copy-start.23
  724.7 4.5 copy-start.22
  724.8 5.2 copy-start.21
  724.8 5.9 copy-start.25
  (3 other events, 3.1 us)
Sparse Core Ops, SparseCore 0:
  13.6 159.9 all-gather.2

commit v8 on v6

--- a/solution.py
+++ b/solution.py
@@ -21,13 +21,15 @@
 SCALE = 1.0 / math.sqrt(DH)
 TILE = 512
 HALF = TILE // 2
+KEYS = 256
+MANY = TILE // KEYS
 STEP = 128.0
 SHIFT = 1.5 * 2.0**30
 TAME = 3000.0
 PAIR = 4
 FREE = 99.0
 STRIP = 512
-AFTER = (1, 4, 6, 8)
+AFTER = (2, 4, 6, 8)
 CURVE = math.sqrt(2.0 / math.pi)
 MESH = pl.DeviceIdType.MESH
 
@@ -67,7 +69,7 @@
     one = (info_ref[0] < stop) & (info_ref[1] > start)
     two = (info_ref[2] < stop) & (info_ref[3] > start)
     begin = jnp.where(one, info_ref[0], jnp.where(two, info_ref[2], stop))
-    return lax.div(begin, TILE)
+    return lax.div(begin, KEYS)
 
 
 def tile_rows(i):
@@ -104,7 +106,7 @@
                 more_s[h, at, DH:] = jnp.ones((TILE, DH), BF16)
             return most
 
-        return jnp.maximum(largest, lax.cond(lowest(low_ref, i) <= i, fill, lambda: jnp.float32(0.0)))
+        return jnp.maximum(largest, lax.cond(lowest(low_ref, i) <= (i + 1) * MANY - 1, fill, lambda: jnp.float32(0.0)))
 
     largest = lax.fori_loop(0, tiles, ready, jnp.float32(0.0))
     tame = largest * (SCALE * LOG2E) ** 2 < TAME
@@ -123,19 +125,19 @@
         at = tile_rows(i)
         low = lowest(low_ref, i)
 
-        @pl.when((low <= i) & tame)
+        @pl.when((low < (i + 1) * MANY) & tame)
         def _():
             for h in range(PAIR):
                 acc_s[h] = jnp.zeros((TILE, 2 * DH), F32)
 
             def step(j, carry):
-                keys = tile_rows(j)
+                keys = pl.ds(pl.multiple_of(j * KEYS, KEYS), KEYS)
                 for h in range(PAIR):
                     count, score = part_of(dot(ask_s[h, at, :], key_s[h, keys, :], NT))
                     acc_s[h] += dot((count * jnp.exp2(score)).astype(BF16), more_s[h, keys, :])
                 return carry
 
-            lax.fori_loop(low, i, step, 0)
+            lax.fori_loop(low, i * MANY, step, 0)
             for h, cols in enumerate(heads):
                 for asks, span in halves(i):
                     here = pl.ds(asks[0], HALF)
@@ -153,7 +155,7 @@
                     lone_ref[h, :, there] = lone.T[:1]
                 finish(h, cols, at, 0.0)
 
-        @pl.when((low <= i) & jnp.logical_not(tame))
+        @pl.when((low < (i + 1) * MANY) & jnp.logical_not(tame))
         def _():
             for h, cols in enumerate(heads):
                 count, score = apart(ask_s[h, at, :], key_s[h, at, :])
@@ -165,7 +167,7 @@
                 top_s[h] = jnp.broadcast_to(top, (TILE, DH))
 
                 def step(j, carry):
-                    keys = tile_rows(j)
+                    keys = pl.ds(pl.multiple_of(j * KEYS, KEYS), KEYS)
                     count, score = apart(ask_s[h, at, :], key_s[h, keys, :])
                     score = jnp.where(count > 0.5, score, NEG)
                     top = top_s[h]
@@ -176,13 +178,13 @@
                     top_s[h] = newer
                     return carry
 
-                lax.fori_loop(low, i, step, 0)
+                lax.fori_loop(low, i * MANY, step, 0)
                 total = acc_s[h, :, DH:]
                 own = STEP * ROUNDS * jnp.exp2(SELF2 - jnp.maximum(top_s[h], SELF2))
                 lone_ref[h, :, at] = jnp.where(total > 0.0, own / jnp.where(total > 0.0, total, 1.0), 0.0).T[:1]
                 finish(h, cols, at, top_s[h])
 
-        @pl.when(low > i)
+        @pl.when(low >= (i + 1) * MANY)
         def _():
             comb_ref[at, :] = jnp.zeros((TILE, PAIR * DH), BF16)
             for h in range(PAIR):
@@ -212,7 +214,7 @@
                     total[h, at, :] = jnp.zeros((TILE, DH), F32)
             return most
 
-        return jnp.maximum(largest, lax.cond(lowest(low_ref, i) <= i, fill, lambda: jnp.float32(0.0)))
+        return jnp.maximum(largest, lax.cond(lowest(low_ref, i) <= (i + 1) * MANY - 1, fill, lambda: jnp.float32(0.0)))
 
     largest = lax.fori_loop(0, tiles, ready, jnp.float32(0.0))
     tame = largest * (SCALE * LOG2E) ** 2 < TAME
@@ -225,7 +227,7 @@
             deltas.append(jnp.sum(mixed.T, axis=0, keepdims=True))
 
         def step(j, carry):
-            keys = tile_rows(j)
+            keys = pl.ds(pl.multiple_of(j * KEYS, KEYS), KEYS)
             for h, cols in enumerate(heads):
                 q, above, unit = q_ref[at, cols], above_ref[at, cols], key_s[h, keys, :DH]
                 count, score = split(key_s[h, keys, :], ask_s[h, at, :])
@@ -237,7 +239,7 @@
                 dask_s[h, at, :] += dot(d_score, unit, TN)
             return carry
 
-        deltas = lax.fori_loop(low, i, step, tuple(deltas))
+        deltas = lax.fori_loop(low, i * MANY, step, tuple(deltas))
         for h, cols in enumerate(heads):
             for asks, span in halves(i):
                 there = pl.ds(asks[1], HALF)
@@ -265,11 +267,11 @@
     def rows_of(i, carry):
         low = lowest(low_ref, i)
 
-        @pl.when((low <= i) & tame)
+        @pl.when((low < (i + 1) * MANY) & tame)
         def _():
             pass_over(i, low, together)
 
-        @pl.when((low <= i) & jnp.logical_not(tame))
+        @pl.when((low < (i + 1) * MANY) & jnp.logical_not(tame))
         def _():
             pass_over(i, low, guarded)
 
@@ -280,7 +282,7 @@
     def close(i, carry):
         at = tile_rows(i)
 
-        @pl.when(lowest(low_ref, i) <= i)
+        @pl.when(lowest(low_ref, i) <= (i + 1) * MANY - 1)
         def _():
             for h, cols in enumerate(heads):
                 q = q_ref[at, cols].astype(F32)
@@ -291,7 +293,7 @@
                 dq_ref[at, cols] = d_q.astype(BF16)
                 dv_ref[at, cols] = dvalue_s[h, at, :].astype(BF16)
 
-        @pl.when(lowest(low_ref, i) > i)
+        @pl.when(lowest(low_ref, i) > (i + 1) * MANY - 1)
         def _():
             dq_ref[at, :] = jnp.zeros((TILE, PAIR * DH), BF16)
             dv_ref[at, :] = jnp.zeros((TILE, PAIR * DH), BF16)
@@ -572,7 +574,7 @@
             AFTER, (movers[k].stage_core, movers[k].stage_first, movers[k].stage_second, functools.partial(close, k))
         ):
             if begun + after > 2 * final + 1:
-                late.append(action)
+                late.append((begun + after, -k, action))
             else:
                 timed.append((begun + after, action))
 
@@ -609,7 +611,7 @@
 
     @pl.when(step == final)
     def _():
-        for action in late:
+        for *_, action in sorted(late, key=lambda entry: entry[:2]):
             action()
         for k in range(max(0, slices - 2), slices):
             movers[k].sent_first()
@@ -1385,6 +1387,7 @@
     count = len(shapes)
     dma = pltpu.SemaphoreType.DMA
     anywhere = pl.BlockSpec(memory_space=pl.ANY)
+    hbm = pl.BlockSpec(memory_space=pltpu.HBM)
     smem = pl.BlockSpec(memory_space=pltpu.SMEM)
     vmem = pl.BlockSpec(memory_space=pltpu.VMEM)
     outs = pl.pallas_call(
@@ -1393,13 +1396,13 @@
         + (jax.ShapeDtypeStruct((8,), jnp.int32),)
         + (jax.ShapeDtypeStruct((slots // 2, rows.shape[1]), BF16),) * 2,
         in_specs=[smem, smem, vmem, vmem] + [anywhere] * count,
-        out_specs=(anywhere,) * count + (smem, anywhere, anywhere),
+        out_specs=(hbm,) * count + (smem, hbm, hbm),
         scratch_shapes=[
             pltpu.VMEM(packed.shape, BF16), pltpu.VMEM((slots, slots), BF16),
             dma((count,)), dma((2, count, outer - 1)), dma((2, count, 2, side - 1)), dma((2, count, 2, side - 1)), dma((2, count)),
             dma((2, 2)), dma((1,)),
         ],
-        compiler_params=pltpu.CompilerParams(collective_id=2, has_side_effects=True, vmem_limit_bytes=32 << 20),
+        compiler_params=pltpu.CompilerParams(collective_id=2, has_side_effects=True, vmem_limit_bytes=57 << 20),
         name="gather",
     )(lengths, destination, buckets, vectors, rows, *arrays)
     return [out.reshape((devices,) + shape.shape) for out, shape in zip(outs, shapes)] + list(outs[count:])

time: 592 us -> 579 us (0.978)
  Pallas kernels: 523 us -> 497 us
  waiting for transfers between devices: 6.36 us -> 16.1 us
    pallas_call x1, Pallas kernels: 54.4 us -> 36.6 us  [attend_back(): pl.pallas_call(back_kernel, grid_spec=pltpu.PrefetchScalarGridSpec(num_sc...]
    pallas_call x1, Pallas kernels: 132 us -> 120 us  [mixing(): pl.pallas_call(functools.partial(mixing_kernel, devices), grid=(hidden //...]
    all_gather x1, waiting for transfers between devices: 6.35 us -> 16.1 us  [body(): lax.all_gather(jnp.concatenate([w_reduce, w_output] + [w_expand[:, k * wi...]
    pallas_call x1, Pallas kernels: 160 us -> 167 us  [tail(): pl.pallas_call(functools.partial(tail_kernel, devices), in_specs=[anywher...]
    pallas_call x1, Pallas kernels: 28.4 us -> 21 us  [attend(): pl.pallas_call(attend_kernel, grid_spec=pltpu.PrefetchScalarGridSpec(num_...]
    unnamed x76 -> x58, local copies, waits for them, and re-layouts: 28.7 us -> 26.2 us
where the time goes in v8:
time: 579 us; the launch traced here: 569 us
  Pallas kernels  497 us (86%)
  local copies, waits for them, and re-layouts  35.7 us (6%)
  waiting for transfers between devices  16.1 us (3%)
  between operations  14.4 us (2%)
    pallas_call x1, Pallas kernels, tail(): pl.pallas_call(functools.partial(tail_kernel, devices), in_specs=[anywher...  167 us
    pallas_call x1, Pallas kernels, mixing(): pl.pallas_call(functools.partial(mixing_kernel, devices), grid=(hidden //...  120 us
    pallas_call x1, Pallas kernels, gather(): pl.pallas_call(functools.partial(gather_kernel, devices, count), out_shap...  92.3 us
    pallas_call x1, Pallas kernels, attend_back(): pl.pallas_call(back_kernel, grid_spec=pltpu.PrefetchScalarGridSpec(num_sc...  36.6 us
    pallas_call x1, Pallas kernels, turn(): pl.pallas_call(functools.partial(turn_kernel, devices), in_specs=[vmem] *...  26.4 us
    unnamed x58, local copies, waits for them, and re-layouts  26.2 us
    pallas_call x1, Pallas kernels, attend(): pl.pallas_call(attend_kernel, grid_spec=pltpu.PrefetchScalarGridSpec(num_...  21 us
    pallas_call x1, Pallas kernels, join(): pl.pallas_call(functools.partial(join_kernel, devices), grid=(1,), in_spe...  17.9 us
  transfers between devices with their start and end apart: 1, of which 1 were waited for; matrix products, arithmetic and copies ran while one was open for 1% of the time, Pallas kernels for 23%

profile of v8, /device:TPU:0, one launch (start us, length us, event | category | flops | bytes accessed | tf_op | source)
XLA Modules:
  0.0 568.5 jit_solution(13904806540250645791)
XLA Ops:
  15.1 92.3 %gather.1 = (bf16[4,2,2,2,32,1024]{5,4,3,2,1,0:T(8,128)(2,1)}, bf16[4,2,2,2,32,1024]{5,4,3,2,1,0:T(8,128)(2,1)}, bf16[4,2,2,2,56,1024]{5,4,3,2,1,0:T(8,128)(2,1)...) custom-call(s32[32]{0:T(128)} %length_ref.1, s32[32]{0:T(128)} %target_ref.1, ...), custom_call_target="tpu_custom_call" | custom-call | tf_op jit(solution)/shard_map/gather/pallas_call | solution.py:1393
  107.4 1.4 slice.83
  108.7 1.7 convert_reduce_fusion
  111.7 2.0 copy-done.3
  113.7 1.6 copy-done.4
  115.3 2.2 copy-done.5
  117.6 1.5 copy-done.7
  119.8 14.9 %project.1 = (bf16[2048,1024]{1,0:T(8,128)(2,1)}, bf16[2048,1024]{1,0:T(8,128)(2,1)}, bf16[2048,1024]{1,0:T(8,128)(2,1)}, bf16[32,2048]{1,0:T(8,128)(2,1)S(1)}) custom-call(s32[8]{0:T(128)S(1)} %copy-done.9, bf16[512,1024]{1,0:T(8,128)(2,1)S(1)} %copy-done.6, bf16[1024,1024]{1,0:T(8,128)(2,1)S(1)} %copy-done.2, bf16[512,1024]{1,0:T(8,128)(2,1)S(1)} %copy-done.7, ...), custom_call_target="tpu_custom_call" | custom-call | tf_op jit(solution)/shard_map/project/pallas_call | solution.py:1248
  135.3 1.5 fusion.live_ref
  137.5 21.0 %attend.1 = (bf16[2048,1024]{1,0:T(8,128)(2,1)}, f32[8,1,2048]{2,1,0:T(1,128)}, f32[8,1,2048]{2,1,0:T(1,128)}) custom-call(s32[8]{0:T(128)} %get-tuple-element.54.info_ref.low_ref, bf16[2048,1024]{1,0:T(8,128)(2,1)} %get-tuple-element.60.q_ref, bf16[2048,1024]{1,0:T(8,128)(2,1)} %get-tuple-element.61.v_ref, bf16[32,2048]{1,0:T(8,128)(2,1)} %copy-done.10, ...), custom_call_target="tpu_custom_call" | custom-call | flops 32212254720 | bytes 12582912 | tf_op jit(solution)/shard_map/attend/pallas_call | solution.py:319
  158.5 16.1 %all-gather.3.cloned.1.call-done = bf16[9216,1024]{1,0:T(8,128)(2,1)} async-done(((bf16[288,1024]{1,0:T(8,128)(2,1)}), bf16[9216,1024]{1,0:T(8,128)(2,1)}) %all-gather.3.cloned.1.call-update) | async-done | bytes 18874384 | tf_op jit(solution)/shard_map/all_gather | solution.py:1438
  174.6 3.2 slice.114
  177.8 17.9 %join.1 = (bf16[1024,1024]{1,0:T(8,128)(2,1)}, f32[1024,1024]{1,0:T(8,128)}, bf16[1024,1024]{1,0:T(8,128)(2,1)}, bf16[1024,1024]{1,0:T(8,128)(2,1)}) custom-call(bf16[2048,1024]{1,0:T(8,128)(2,1)} %get-tuple-element.63.window_ref.first_ref.final_ref.comb_ref, bf16[2048,1024]{1,0:T(8,128)(2,1)} %get-tuple-element.63.window_ref.first_ref.final_ref.comb_ref, ...), custom_call_target="tpu_custom_call" | custom-call | tf_op jit(solution)/shard_map/join/pallas_call | solution.py:753
  195.7 120.1 %mixing.1 = (f32[1024,1024]{1,0:T(8,128)}, f32[1024,1024]{1,0:T(8,128)}, bf16[32,128,1024]{2,1,0:T(8,128)(2,1)}, f32[1,4096]{1,0:T(1,128)}, f32[128,1024]{1,0:T(8,128)}, /*index=5*/f32[1,1024]{1,0:T(1,128)}) custom-call(bf16[1024,1024]{1,0:T(8,128)(2,1)} %get-tuple-element.65.second_ref, bf16[1024,1024]{1,0:T(8,128)(2,1)} %get-tuple-element.66.above_ref, ...), custom_call_target="tpu_custom_call" | custom-call | tf_op jit(solution)/shard_map/mixing/pallas_call | solution.py:635
  315.8 1.1 fusion.18
  317.0 26.4 %turn.1 = (bf16[2048,1024]{1,0:T(8,128)(2,1)}, bf16[1024,1024]{1,0:T(8,128)(2,1)}, bf16[1024,1024]{1,0:T(8,128)(2,1)}, bf16[1024,1024]{1,0:T(8,128)(2,1)}, bf16[...) custom-call(f32[1024,1024]{1,0:T(8,128)} %get-tuple-element.64.out_one_ref, f32[1024,1024]{1,0:T(8,128)} %get-tuple-element.67.d_second_ref, ...), custom_call_target="tpu_custom_call" | custom-call | tf_op jit(solution)/shard_map/turn/pallas_call | solution.py:871
  343.4 36.6 %attend_back.1 = (bf16[2048,1024]{1,0:T(8,128)(2,1)}, bf16[2048,1024]{1,0:T(8,128)(2,1)}) custom-call(s32[8]{0:T(128)} %get-tuple-element.54.info_ref.low_ref, bf16[2048,1024]{1,0:T(8,128)(2,1)} %get-tuple-element.60.q_ref, bf16[2048,1024]{1,0:T(8,128)(2,1)} %get-tuple-element.61.v_ref, bf16[32,2048]{1,0:T(8,128)(2,1)} %copy-done.10, ...), custom_call_target="tpu_custom_call" | custom-call | flops 64424509440 | bytes 25165824 | tf_op jit(solution)/shard_map/attend_back/pallas_call | solution.py:342
  380.0 167.5 %tail.1 = (bf16[1024,1024]{1,0:T(8,128)(2,1)}, f32[32,1024]{1,0:T(8,128)}, f32[32,1024]{1,0:T(8,128)}, f32[32,1024]{1,0:T(8,128)}, f32[128,1024]{1,0:T(8,128)}, /*index=5*/f32[16,128]{1,0:T(8,128)}, f32[1,128]{1,0:T(1,128)}) custom-call(bf16[4,2,2,2,128,1024]{5,4,3,2,1,0:T(8,128)(2,1)} %bitcast.45, bf16[4,2,2,2,32,1024]{5,4,3,2,1,0:T(8,128)(2,1)} %bitcast.47, ...), custom_call_target="tpu_custom_call" | custom-call | tf_op jit(solution)/shard_map/tail/pallas_call | solution.py:1123
  547.5 1.4 slice_bitcast_fusion.1
  549.8 1.3 copy.50
  551.1 1.0 copy-done.12
  552.1 1.3 copy.51
  554.5 1.3 copy.52
  556.8 1.3 copy.53
  (70 shorter events, 17.3 us)
Async XLA Ops:
  7.2 7.1 %copy-start = (f32[128]{0:T(128)S(1)}, f32[128]{0:T(128)}, u32[]{:S(2)}) copy-start(f32[128]{0:T(128)} %param.36) | copy-start | bytes 1540
  7.2 167.4 %all-gather.3.cloned.1.call-start = ((), (), s32[]{:S(2)}) async-start(), calls=%async_computation | async-start | bytes 19464192 | tf_op jit(solution)/shard_map/all_gather | solution.py:1438
  12.4 0.8 copy-start.15
  15.1 96.6 %copy-start.2 = (bf16[1024,1024]{1,0:T(8,128)(2,1)S(1)}, bf16[1024,1024]{1,0:T(8,128)(2,1)}, u32[]{:S(2)}) copy-start(bf16[1024,1024]{1,0:T(8,128)(2,1)} %own_ref.3) | copy-start | bytes 6291460
  107.4 4.3 copy-start.6
  111.7 23.0 %copy-start.8 = (f32[1,1024]{1,0:T(1,128)}, f32[1,1024]{1,0:T(1,128)S(1)}, u32[]{:S(2)}) copy-start(f32[1,1024]{1,0:T(1,128)S(1)} %get-tuple-element.101.gain_ref) | copy-start | bytes 12292
  111.7 2.0 copy-start.3
  113.7 1.6 copy-start.4
  115.3 2.2 copy-start.5
  117.6 1.5 copy-start.7
  119.1 0.7 copy-start.9
  134.7 0.7 copy-start.10
  380.0 169.8 %copy-start.13 = (bf16[1024,1024]{1,0:T(8,128)(2,1)S(1)}, bf16[1024,1024]{1,0:T(8,128)(2,1)}, u32[]{:S(2)}) copy-start(bf16[1024,1024]{1,0:T(8,128)(2,1)} %get-tuple-element.126) | copy-start | bytes 6291460
  549.8 2.3 copy-start.12
  552.1 2.3 copy-start.11
  554.4 2.3 copy-start.14
  554.5 7.0 %copy-start.1 = (f32[128]{0:T(128)S(1)}, f32[128]{0:T(128)}, u32[]{:S(2)}) copy-start(f32[128]{0:T(128)} %param.36) | copy-start | bytes 1540
  556.8 1.3 copy-start.19
  556.8 2.0 copy-start.18
  556.8 2.7 copy-start.17
  556.8 3.3 copy-start.16
  556.8 4.1 copy-start.20
Sparse Core Ops, SparseCore 0:
  13.4 161.1 all-gather.2
